TPU v7x, 128 devices: a whole 4x4x4 slice. The times are simulated.
128 devices in a mesh: pop: 32 (over y, x_lo, z), mp: 4 (over x_hi, core).
Axes of the slice: x: 4 (x_hi: 2, x_lo: 2; x = x_hi * 2 + x_lo), y: 4, z: 4, core: 2. Of those that a mesh axis runs over, the one named last changes fastest.
Arguments:
- token_ids: int32 [384, 4, 16], P('pop'), may hold values from 0 to 255
- fitness_ranks: int32 [384], P('pop'), may hold values from 0 to 575, as said below
- embedding: bfloat16 [256, 4096], P(None, 'mp'), may hold values from -6 to 6
- mix_weights: bfloat16 [2, 4096, 4096], P(None, 'mp'), may hold values from -0.09375 to 0.09375
- factors_in: bfloat16 [2, 384, 4, 4096], P(None, 'pop', None, 'mp'), may hold values from -6 to 6
- factors_out: bfloat16 [2, 384, 4, 4096], P(None, 'pop'), may hold values from -6 to 6
- decay_rates: float32 [2, 4096], P(None, 'mp'), may hold values from 0.2 to 0.98
- norm_gain: float32 [2, 4096], P(None, 'mp'), may hold values from 0.1 to 1.9
- reward_dir: float32 [4096], P('mp'), may hold values from -6 to 6
Outputs:
- final_features: bfloat16 [384, 4, 4096], P('pop', None, 'mp')
- scores: float32 [384, 4], P('pop')
- weight_step: float32 [2, 4096, 4096], P(None, 'mp', 'pop')
Inputs may be any that keep to these rules, and one draw needn't show every extreme that they name: `fitness_ranks`: ranks may repeat.
All inputs are finite; a program needn't handle non-finite values.
Results may differ from a plain program's by a relative error of at most 0.023.
Values may be sent and summed in bfloat16 or wider, within the bound.
No kernel may reach another device: no remote copies, remote signals or barrier semaphores. Data moves between devices by JAX's collectives and lax.ppermute only.
A program may use at most 128 MiB of HBM per device.

v0:
```python
import jax
import jax.numpy as jnp
from jax import lax
from jax.experimental import pallas as pl
from jax.experimental.pallas import tpu as pltpu
from jax.sharding import Mesh
from jax.sharding import PartitionSpec as P

noise_scale = 0.25
norm_eps = 1e-06
spread_eps = 1e-05

POP = ("y", "xl", "z")
MP = ("xh", "c")
CHUNKS = 3
f32 = jnp.float32
bf16 = jnp.bfloat16
SMEM = pl.BlockSpec(memory_space=pltpu.SMEM)
VMEM = pl.BlockSpec(memory_space=pltpu.VMEM)


def params(mib=48):
    return pltpu.CompilerParams(vmem_limit_bytes=mib * 1024 * 1024)


def swap(value, axis):
    return lax.ppermute(value, axis, [(0, 1), (1, 0)])


def shift(value, axis, by):
    n = lax.axis_size(axis)
    return lax.ppermute(value, axis, [(i, (i + by) % n) for i in range(n)])


def mp_parts(value):
    both = lax.ppermute(value, MP, [(i, 3 - i) for i in range(4)])
    return value, swap(value, "c"), swap(value, "xh"), both


def dot(a, b, ca, cb, precision=None):
    return lax.dot_general(
        a, b, (((ca,), (cb,)), ((), ())), preferred_element_type=f32, precision=precision
    )


def regroup(factors, first, second):
    layers, members, ranks, width = factors.shape
    blocks = width // 128

    def kernel(in_ref, out_ref):
        for m in range(members):
            rows = jnp.concatenate(
                [in_ref[l, m].astype(f32) for l in range(layers)], axis=0
            ).astype(bf16)
            lo = m * layers * ranks
            for b in range(blocks):
                out_ref[b, lo : lo + layers * ranks, :] = rows[:, b * 128 : (b + 1) * 128]

    return pl.pallas_call(
        kernel,
        out_shape=jax.ShapeDtypeStruct((blocks, members * layers * ranks, 128), bf16),
        in_specs=[VMEM],
        out_specs=VMEM,
        compiler_params=params(),
        name=first,
    )(factors)


def table_partial(layer, where, embedding, weights):
    vocab, width = embedding.shape
    full = weights.shape[2]
    piece = full // 16

    def kernel(where_ref, e_ref, wp_ref, wo_ref, peer_ref, own_ref):
        peer_ref[0] = jnp.dot(e_ref[...], wp_ref[0], preferred_element_type=f32).astype(bf16)
        own_ref[0] = jnp.dot(e_ref[...], wo_ref[0], preferred_element_type=f32).astype(bf16)

    def block(rel, where_ref, flip):
        z, xh, c = where_ref[0], where_ref[1], where_ref[2]
        owner = (xh ^ rel) * 2 + (c ^ flip)
        return owner * 4 + z

    return pl.pallas_call(
        kernel,
        grid_spec=pltpu.PrefetchScalarGridSpec(
            num_scalar_prefetch=1,
            grid=(2,),
            in_specs=[
                pl.BlockSpec((vocab, width), lambda r, s: (0, 0)),
                pl.BlockSpec((1, width, piece), lambda r, s: (layer, 0, block(r, s, 1))),
                pl.BlockSpec((1, width, piece), lambda r, s: (layer, 0, block(r, s, 0))),
            ],
            out_specs=[pl.BlockSpec((1, vocab, piece), lambda r, s: (r, 0, 0))] * 2,
        ),
        out_shape=[jax.ShapeDtypeStruct((2, vocab, piece), bf16)] * 2,
        compiler_params=params(),
        name="table",
        cost_estimate=pl.CostEstimate(
            flops=2 * vocab * width * piece * 4, bytes_accessed=width * piece * 8, transcendentals=0
        ),
    )(where, embedding, weights, weights)


def member_of(shape, per, dim):
    return lax.broadcasted_iota(jnp.int32, shape, dim) // per


def low_kernel(onehot, embedding, factors):
    rows = onehot.shape[0]
    per_chunk = rows // CHUNKS
    group = factors.shape[1] // CHUNKS

    def kernel(o_ref, e_ref, a_ref, out_ref):
        for k in range(CHUNKS):
            x = jnp.dot(
                o_ref[k * per_chunk : (k + 1) * per_chunk, :], e_ref[...], preferred_element_type=f32
            ).astype(bf16)
            total = jnp.zeros((group, per_chunk), f32)
            for b in range(factors.shape[0]):
                total += dot(
                    a_ref[b, k * group : (k + 1) * group, :], x[:, b * 128 : (b + 1) * 128], 1, 1
                )
            out_ref[:, k * per_chunk : (k + 1) * per_chunk] = diagonal(total)

    return pl.pallas_call(
        kernel,
        out_shape=jax.ShapeDtypeStruct((8, rows), f32),
        in_specs=[VMEM] * 3,
        out_specs=VMEM,
        compiler_params=params(),
        name="low",
    )(onehot, embedding, factors)


def diagonal(total):
    group, cols = total.shape
    row_member = member_of((group, cols), 8, 0)
    col_member = (lax.broadcasted_iota(jnp.int32, (group, cols), 1) % 16) // 4
    kept = jnp.where(row_member == col_member, total, 0.0)
    out = kept[0:8]
    for m in range(1, group // 8):
        out = out + kept[m * 8 : (m + 1) * 8]
    return out


def spread(low, layer, group):
    cols = low.shape[1]
    row = lax.broadcasted_iota(jnp.int32, (group, cols), 0)
    col_member = (lax.broadcasted_iota(jnp.int32, (group, cols), 1) % 16) // 4
    keep = (row // 8 == col_member) & ((row % 8) // 4 == layer)
    tiled = jnp.concatenate([low] * (group // 8), axis=0)
    return jnp.where(keep, tiled, 0.0).astype(bf16)


def first_layer(chunk, where, coef, onehot, tables, lows, out_factors, in_factors, decay, gain):
    rows = onehot.shape[0] // CHUNKS
    group = out_factors.shape[1] // CHUNKS
    width = decay.shape[1]
    steps = 16
    per = rows // steps

    def kernel(where_ref, o_ref, t0, t1, t2, t3, l0, l1, l2, l3, b_ref, a_ref, d_ref, g_ref,
               lifted_ref, stats_ref, square):
        z = where_ref[0]
        low = (l0[...] + l1[...] + l2[...] + l3[...]) * coef
        spread_low = spread(low, 0, group)
        square[...] = jnp.zeros_like(square)
        total = jnp.zeros((group, rows), f32)
        for k, table in enumerate((t0, t1, t2, t3)):
            blk = (z - k + 4) % 4
            cols = pl.ds(pl.multiple_of(blk * 256, 256), 256)
            factor = jnp.concatenate([b_ref[2 * blk], b_ref[2 * blk + 1]], axis=1)
            u = jnp.dot(o_ref[...], table[...], preferred_element_type=f32) + dot(
                spread_low, factor, 0, 0
            )
            d = d_ref[:, cols]
            g = g_ref[:, cols]
            rest = 1.0 - d
            h = jnp.zeros((per, 256), f32)
            for t in range(steps):
                span = slice(t * per, (t + 1) * per)
                h = d * h + rest * u[span]
                lifted_ref[span, cols] = (h * g).astype(bf16)
                hh = h * h
                square[span] += hh[:, :128] + hh[:, 128:]
            factor_in = jnp.concatenate([a_ref[2 * blk], a_ref[2 * blk + 1]], axis=1)
            total += dot(factor_in, lifted_ref[:, cols], 1, 1)
        sums = dot(jnp.ones((8, 128), f32), square[...], 1, 1, lax.Precision.HIGHEST)
        low_next = diagonal(total)
        row = lax.broadcasted_iota(jnp.int32, (8, rows), 0)
        stats_ref[...] = jnp.where(row < 4, sums, low_next)

    sl = lambda a, n: lax.slice_in_dim(a, chunk * n, (chunk + 1) * n, axis=0)
    lc = [lax.slice_in_dim(a, chunk * rows, (chunk + 1) * rows, axis=1) for a in lows]
    mid = lambda a: lax.slice_in_dim(a, chunk * group, (chunk + 1) * group, axis=1)
    return pl.pallas_call(
        kernel,
        out_shape=[
            jax.ShapeDtypeStruct((rows, width), bf16),
            jax.ShapeDtypeStruct((8, rows), f32),
        ],
        in_specs=[SMEM] + [VMEM] * 13,
        out_specs=[VMEM, VMEM],
        scratch_shapes=[pltpu.VMEM((rows, 128), f32)],
        compiler_params=params(),
        name="first_layer",
        cost_estimate=pl.CostEstimate(flops=2000000000, bytes_accessed=4000000, transcendentals=0),
    )(where, sl(onehot, rows), *tables, *lc, mid(out_factors), mid(in_factors), decay, gain)


def product(where, rel, lifted, lifted_peer, weights, weights_peer, out_dtype):
    rows, width = lifted.shape
    blocks = 4
    piece = width // blocks

    def kernel(where_ref, a_ref, b_ref, wa_ref, wb_ref, out_ref):
        out_ref[...] = (
            jnp.dot(a_ref[...], wa_ref[0], preferred_element_type=f32)
            + jnp.dot(b_ref[...], wb_ref[0], preferred_element_type=f32)
        ).astype(out_dtype)

    return pl.pallas_call(
        kernel,
        grid_spec=pltpu.PrefetchScalarGridSpec(
            num_scalar_prefetch=1,
            grid=(blocks,),
            in_specs=[
                pl.BlockSpec((rows, width), lambda n, s: (0, 0)),
                pl.BlockSpec((rows, width), lambda n, s: (0, 0)),
                pl.BlockSpec(
                    (1, width, piece),
                    lambda n, s: (1, 0, ((s[1] ^ rel) * 2 + s[2]) * blocks + n),
                ),
                pl.BlockSpec((1, width, piece), lambda n, s: (rel, 0, n)),
            ],
            out_specs=pl.BlockSpec((rows, piece), lambda n, s: (0, n)),
        ),
        out_shape=jax.ShapeDtypeStruct((rows, width), out_dtype),
        compiler_params=params(),
        name="product",
        cost_estimate=pl.CostEstimate(
            flops=4 * rows * width * width, bytes_accessed=6 * width * width, transcendentals=0
        ),
    )(where, lifted, lifted_peer, weights, weights_peer)


def second_layer(chunk, where, coef, full_width, onehot, embedding, tables, lows, stats, lifted,
                 own, other, out_factors, decay, gain, reward):
    rows = lifted.shape[0]
    group = out_factors.shape[1] // CHUNKS
    width = decay.shape[1]
    steps = 16
    per = rows // steps

    def kernel(where_ref, o_ref, e_ref, t0, t1, t2, t3, l0, l1, l2, l3, s0, s1, s2, s3, lifted_ref,
               own_ref, other_ref, b_ref, d_ref, g_ref, r_ref,
               stats_ref, hidden_ref, last_ref, square, lr, xr):
        z = where_ref[0]
        from_hidden = l0[...] + l1[...] + l2[...] + l3[...]
        so_far = s0[...] + s1[...] + s2[...] + s3[...]
        norm = lax.rsqrt(so_far[0:1] / full_width + norm_eps)
        low = (from_hidden + norm * so_far) * coef
        spread_low = spread(low, 1, group)
        norm_col = jnp.transpose(jnp.broadcast_to(norm, (8, rows)))[:, 0:1]
        square[...] = jnp.zeros_like(square)
        lr[...] = jnp.zeros_like(lr)
        xr[...] = jnp.zeros_like(xr)
        for k, table in enumerate((t0, t1, t2, t3)):
            blk = (z - k + 4) % 4
            cols = pl.ds(pl.multiple_of(blk * 256, 256), 256)
            factor = jnp.concatenate([b_ref[2 * blk], b_ref[2 * blk + 1]], axis=1)
            both = own_ref[:, cols] + other_ref[:, cols].astype(f32)
            u = (
                jnp.dot(o_ref[...], table[...], preferred_element_type=f32)
                + dot(spread_low, factor, 0, 0)
                + norm_col * both
            )
            x = jnp.dot(o_ref[...], e_ref[:, cols], preferred_element_type=f32)
            x = (x + norm_col * lifted_ref[:, cols].astype(f32)).astype(bf16)
            d = d_ref[:, cols]
            g = g_ref[:, cols]
            r = r_ref[:, cols]
            rest = 1.0 - d
            h = jnp.zeros((per, 256), f32)
            xrr = x.astype(f32) * r
            xr[...] += xrr[:, :128] + xrr[:, 128:]
            gr = g * r
            for t in range(steps):
                span = slice(t * per, (t + 1) * per)
                h = d * h + rest * u[span]
                hr = h * gr
                hh = h * h
                square[span] += hh[:, :128] + hh[:, 128:]
                lr[span] += hr[:, :128] + hr[:, 128:]
            hidden_ref[:, cols] = x[(steps - 1) * per :].astype(f32)
            last_ref[:, cols] = h * g
        ones = jnp.ones((8, 128), f32)
        sums = [dot(ones, a[...], 1, 1, lax.Precision.HIGHEST) for a in (square, lr, xr)]
        row = lax.broadcasted_iota(jnp.int32, (8, rows), 0)
        stats_ref[...] = jnp.where(row == 0, sums[0], jnp.where(row == 1, sums[1], sums[2]))

    sl = lambda a, n: lax.slice_in_dim(a, chunk * n, (chunk + 1) * n, axis=0)
    lc = [lax.slice_in_dim(a, chunk * rows, (chunk + 1) * rows, axis=1) for a in lows]
    mid = lambda a: lax.slice_in_dim(a, chunk * group, (chunk + 1) * group, axis=1)
    return pl.pallas_call(
        kernel,
        out_shape=[
            jax.ShapeDtypeStruct((8, rows), f32),
            jax.ShapeDtypeStruct((per, width), f32),
            jax.ShapeDtypeStruct((per, width), f32),
        ],
        in_specs=[SMEM] + [VMEM] * 21,
        out_specs=[VMEM] * 3,
        scratch_shapes=[pltpu.VMEM((rows, 128), f32)] * 3,
        compiler_params=params(),
        name="second_layer",
        cost_estimate=pl.CostEstimate(flops=2000000000, bytes_accessed=4000000, transcendentals=0),
    )(where, sl(onehot, rows), embedding, *tables, *lc, *stats, lifted, own, other,
      mid(out_factors), decay, gain, reward)


def step_kernel(where, ins, outs, width):
    pops, k, cols = outs.shape
    halves = len(ins)
    per_half = width // halves

    def kernel(where_ref, outs_ref, *refs):
        in_refs = refs[:8]
        out_ref, paired = refs[8], refs[9]
        z, y, xl = where_ref[0], where_ref[3], where_ref[4]
        half = (lax.broadcasted_iota(jnp.int32, (k, cols), 0) % 8) // 4
        for half_idx in range(2):
            total = [jnp.zeros((2 * cols, 128), f32) for _ in range(4)]
            for dy in range(4):
                for dz in range(4):
                    for dx in range(2):
                        at = (dz * 2 + dx) * k
                        pop = ((y - dy + 4) % 4) * 8 + (xl ^ dx) * 4 + (z - dz + 4) % 4
                        o = outs_ref[pop]
                        zero = jnp.zeros_like(o)
                        paired[at : at + k, 0:cols] = jnp.where(half == 0, o, zero)
                        paired[at : at + k, cols : 2 * cols] = jnp.where(half == 1, o, zero)
                flipped = paired[...]
                for b in range(4):
                    parts = [
                        in_refs[dy][dz, dx, b] if half_idx == 0 else in_refs[4 + dz][dy, dx, b]
                        for dz in range(4)
                        for dx in range(2)
                    ]
                    a = jnp.concatenate(parts, axis=0)
                    total[b] += dot(flipped, a, 0, 0)
            for b in range(4):
                lo = half_idx * per_half + b * 128
                out = jnp.transpose(total[b])
                out_ref[0, lo : lo + 128, :] = out[:, :cols]
                out_ref[1, lo : lo + 128, :] = out[:, cols:]

    return pl.pallas_call(
        kernel,
        out_shape=jax.ShapeDtypeStruct((2, width, cols), f32),
        in_specs=[SMEM] + [VMEM] * 9,
        out_specs=VMEM,
        scratch_shapes=[pltpu.VMEM((8 * k, 2 * cols), bf16)],
        compiler_params=params(56),
        name="weight_step",
        cost_estimate=pl.CostEstimate(flops=2000000000, bytes_accessed=8000000, transcendentals=0),
    )(where, outs, *ins[0], *ins[1])


def ring_copies(value, axis):
    return [value] + [shift(value, axis, j) for j in range(1, lax.axis_size(axis))]


def shards(
    token_ids,
    fitness_ranks,
    embedding,
    mix_weights,
    factors_in,
    factors_out,
    decay_rates,
    norm_gain,
    reward_dir,
):
    members, seq_count, step_count = token_ids.shape
    vocab, width = embedding.shape
    full_width = mix_weights.shape[2]
    rank_count = factors_in.shape[2]
    pop_count = lax.axis_size(POP)
    members_all = members * pop_count
    coef = noise_scale * (full_width * rank_count) ** (-0.5)
    y, xl, z = (lax.axis_index(a) for a in POP)
    xh, c = (lax.axis_index(a) for a in MP)
    where = jnp.stack([z, xh, c, y, xl]).astype(jnp.int32)
    rows_all = members * seq_count * step_count
    rows = rows_all // CHUNKS

    tables = []
    for layer in range(2):
        peer, own = table_partial(layer, where, embedding, mix_weights)
        pair = own.astype(f32) + swap(peer, "c").astype(f32)
        crossing = swap(pair[1].astype(bf16), "xh")
        table = (pair[0] + crossing.astype(f32)).astype(bf16)
        tables.append(ring_copies(table, "z"))

    order = token_ids.reshape(CHUNKS, -1, step_count).transpose(0, 2, 1).reshape(-1)
    onehot = (order[:, None] == jnp.arange(vocab, dtype=jnp.int32)[None, :]).astype(bf16)
    a_blocks = regroup(factors_in, "regroup_in", 0)
    b_blocks = regroup(factors_out, "regroup_out", 0)
    b_own = lax.dynamic_slice_in_dim(b_blocks, (xh * 2 + c) * 8, 8, 0)
    lows = mp_parts(low_kernel(onehot, embedding, a_blocks))

    peer_cols = [
        lax.dynamic_slice(mix_weights, (1, 0, ((xh ^ rel) * 2 + (1 - c)) * width), (1, width, width))
        for rel in range(2)
    ]
    weights_peer = swap(jnp.concatenate(peer_cols, axis=0), "c")

    decay = [decay_rates[l : l + 1] for l in range(2)]
    gain = [norm_gain[l : l + 1] for l in range(2)]
    lifted, stats, sent, own_half, peers = [], [], [], [], []
    for k in range(CHUNKS):
        up, st = first_layer(
            k, where, coef, onehot, tables_of(tables, 0), lows, b_own, a_blocks, decay[0], gain[0]
        )
        lifted.append(up)
        peers.append(swap(up, "c"))
        stats.append(mp_parts(st))
    for k in range(CHUNKS):
        half = product(where, 1, lifted[k], peers[k], mix_weights, weights_peer, bf16)
        sent.append(swap(half, "xh"))
    for k in range(CHUNKS):
        own_half.append(product(where, 0, lifted[k], peers[k], mix_weights, weights_peer, f32))

    pair_in = jnp.stack([a_blocks, swap(a_blocks, "xl")])
    first, second = pair_in[:, :4], pair_in[:, 4:]
    first_z = jnp.stack(ring_copies(first, "z"))
    second_y = jnp.stack(ring_copies(second, "y"))
    first_zy = ring_copies(first_z, "y")
    second_yz = ring_copies(second_y, "z")
    half_rows = b_blocks.shape[1] // 2
    my_rows = lax.dynamic_slice_in_dim(b_blocks, c * half_rows, half_rows, 1)
    mine = lax.all_to_all(my_rows, POP, 0, 0, tiled=True)
    theirs = swap(mine, "c")
    outs = jnp.where(
        c == 0, jnp.concatenate([mine, theirs], axis=1), jnp.concatenate([theirs, mine], axis=1)
    )
    ranks_every = lax.all_gather(fitness_ranks, POP, tiled=True)
    shares_all = ranks_every.astype(f32) / members_all
    rank_mean = jnp.mean(shares_all)
    rank_spread = jnp.mean((shares_all - rank_mean) * (shares_all - rank_mean)) + spread_eps
    shaped = (shares_all - rank_mean) * lax.rsqrt(rank_spread)
    shaped = shaped * (members_all * rank_count) ** (-0.5)
    shaped_rows = jnp.repeat(shaped.reshape(pop_count, members), 2 * rank_count, axis=1)
    outs = (outs.astype(f32) * shaped_rows[:, :, None]).astype(bf16)
    weight_step = step_kernel(where, [first_zy, second_yz], outs, width)

    finals, terms = [], []
    for k in range(CHUNKS):
        st, hidden, last = second_layer(
            k, where, coef, full_width, onehot, embedding, tables_of(tables, 1), lows, stats[k],
            lifted[k], own_half[k], sent[k], b_own, decay[1], gain[1], reward_dir[None],
        )
        so_far = sum(mp_parts(st))
        norm = lax.rsqrt(so_far[0] / full_width + norm_eps)
        terms.append(so_far[2] + norm * so_far[1])
        tail = norm[-last.shape[0] :]
        finals.append((hidden + last * tail[:, None]).astype(bf16))
    final_features = jnp.concatenate(finals, axis=0).reshape(members, seq_count, width)
    scores = jnp.mean(jnp.stack(terms).reshape(CHUNKS, step_count, -1), axis=1)
    scores = scores.reshape(members, seq_count) * full_width ** (-0.5)
    return (final_features, scores, weight_step)


def tables_of(tables, layer):
    return tables[layer]


def solution(mesh):
    fine = Mesh(mesh.devices.reshape(4, 2, 4, 2, 2), POP + MP)
    return jax.shard_map(
        shards,
        mesh=fine,
        in_specs=(
            P(POP, None, None),
            P(POP),
            P(None, MP),
            P(None, MP, None),
            P(None, POP, None, MP),
            P(None, POP, None, None),
            P(None, MP),
            P(None, MP),
            P(MP),
        ),
        out_specs=(P(POP, None, MP), P(POP, None), P(None, MP, POP)),
        check_vma=False,
    )
```

profile of v0, /device:TPU:1, one launch (start us, length us, event | category | flops | bytes accessed | tf_op | source)
XLA Modules:
  0.0 216.4 jit_solution(6315739767684459981)
XLA Ops:
  7.0 3.3 %collective-permute-start.7 = (f32[8,768]{1,0:T(8,128)S(1)}, f32[8,768]{1,0:T(8,128)S(1)}, u32[]{:S(2)}, u32[]{:S(2)}) collective-permute-start(f32[8,768]{1,0:T(8,128)S(1)} %low.1), channel_id=1, source_target_pairs={{0,3},{1,2},{2,1},{3,0},{4,7},{5,6},{6,5},{7,4},{8,11},{9,10},{10,... | collective-permute-start | bytes 73736 | tf_op jit(solution)/shard_map/ppermute | solution.py:36
  11.9 8.2 %all-to-all-start = ((bf16[32,48,128]{2,1,0:T(8,128)(2,1)}), bf16[32,48,128]{2,1,0:T(8,128)(2,1)}, u32[]{:S(2)}, u32[]{:S(2)}) async-start(bf16[32,48,128]{2,1,0:T(8,128)(2,1)} %constant_dynamic-slice_fusion.2), calls=%async_computation | async-start | bytes 786432 | tf_op jit(solution)/shard_map/all_to_all | solution.py:443
  27.5 14.9 %all-reduce = s32[384]{0:T(512)S(1)} all-reduce(s32[384]{0:T(512)S(1)} %dynamic-update-slice), channel_id=1, replica_groups=mesh['y'=4,'xl'=2,'z'=4,'xh'=2,'c'=2] {'y','xl','z'}, use_global_device_ids=true, to_apply=%add | all-reduce | flops 384 | bytes 3072
  50.6 4.7 %collective-permute-start.8 = (bf16[2,256,256]{2,1,0:T(8,128)(2,1)S(1)}, bf16[2,256,256]{2,1,0:T(8,128)(2,1)S(1)}, u32[]{:S(2)}, u32[]{:S(2)}) collective-permute-start(bf16[2,256,256]{2,1,0:T(8,128)(2,1)S(1)} %get-tuple-element.25), channel_id=1, source_target_pairs={{0,1},{1,0},{2,3},{3,2},{4,5},{5,4},{6,7},{7,6},{8,9},{9,8},{10,11... | collective-permute-start | bytes 786440 | tf_op jit(solution)/shard_map/ppermute | solution.py:27
  68.3 3.7 %collective-permute-done.42 = bf16[2,4,96,128]{3,2,1,0:T(8,128)(2,1)S(1)} collective-permute-done((bf16[2,4,96,128]{3,2,1,0:T(8,128)(2,1)S(1)}, bf16[2,4,96,128]{3,2,1,0:T(8,128)(2,1)S(1)}, u32[]{:S(2)}, u32[]{:S(2)}) %collective-permute-start.42) | collective-permute-done | bytes 196640 | tf_op jit(solution)/shard_map/ppermute | solution.py:32
  80.8 3.7 %collective-permute-start.38 = (bf16[32,48,128]{2,1,0:T(8,128)(2,1)}, bf16[32,48,128]{2,1,0:T(8,128)(2,1)}, u32[]{:S(2)}, u32[]{:S(2)}) collective-permute-start(bf16[32,48,128]{2,1,0:T(8,128)(2,1)} %all-to-all-done), channel_id=1, source_target_pairs={{0,1},{1,0},{2,3},{3,2},{4,5},{5,4},{6,7},{7,6},{8,9},{9,8},{10,11... | collective-permute-start | bytes 1179656 | tf_op jit(solution)/shard_map/ppermute | solution.py:27
  91.1 3.6 %collective-permute-done.43.refs_1_ = bf16[4,2,4,96,128]{4,3,2,1,0:T(8,128)(2,1)} collective-permute-done((bf16[4,2,4,96,128]{4,3,2,1,0:T(8,128)(2,1)}, bf16[4,2,4,96,128]{4,3,2,1,0:T(8,128)(2,1)}, u32[]{:S(2)}, u32[]{:S(2)}) %collective-permute-start.43) | collective-permute-done | bytes 786464 | tf_op jit(solution)/shard_map/ppermute | solution.py:32
  95.8 15.8 %collective-permute-done.44.refs_2_ = bf16[4,2,4,96,128]{4,3,2,1,0:T(8,128)(2,1)} collective-permute-done((bf16[4,2,4,96,128]{4,3,2,1,0:T(8,128)(2,1)}, bf16[4,2,4,96,128]{4,3,2,1,0:T(8,128)(2,1)}, u32[]{:S(2)}, u32[]{:S(2)}) %collective-permute-start.44) | collective-permute-done | bytes 786464 | tf_op jit(solution)/shard_map/ppermute | solution.py:32
  117.3 5.7 %collective-permute-start.25 = (bf16[256,1024]{1,0:T(8,128)(2,1)S(1)}, bf16[256,1024]{1,0:T(8,128)(2,1)S(1)}, u32[]{:S(2)}, u32[]{:S(2)}) collective-permute-start(bf16[256,1024]{1,0:T(8,128)(2,1)S(1)} %get-tuple-element.32.a_ref.lifted_ref), channel_id=1, source_target_pairs={{0,1},{1,0},{2,3},{3,2},{4,5},{5,4},{6,7},{7,6},{8,9},{9,8},{10,11... | collective-permute-start | bytes 1572872 | tf_op jit(solution)/shard_map/ppermute | solution.py:27
  125.8 4.5 %product.7 = bf16[256,1024]{1,0:T(8,128)(2,1)S(1)} custom-call(s32[5]{0:T(128)S(1)} %stack.74.where_ref, bf16[256,1024]{1,0:T(8,128)(2,1)S(1)} %get-tuple-element.27.a_ref.lifted_ref, bf16[256,1024]{1,0:T(8,128)(2,1)S(1)} %collective-permute-done.16.b_ref, bf16[2,1024,4096]{2,1,0:T(8,128)(2,1)} %wa_ref.11, bf16[2,1024,1024]{2,1,0:T(8,128)(2,1)} %collective-permute-done.17.wb_ref), custom_call_target="tpu_custom_call" | custom-call | flops 1073741824 | bytes 6291456 | tf_op jit(solution)/shard_map/product/pallas_call | solution.py:222
  134.2 3.3 %collective-permute-start.18 = (bf16[256,1024]{1,0:T(8,128)(2,1)S(1)}, bf16[256,1024]{1,0:T(8,128)(2,1)S(1)}, u32[]{:S(2)}, u32[]{:S(2)}) collective-permute-start(bf16[256,1024]{1,0:T(8,128)(2,1)S(1)} %product.7), channel_id=1, source_target_pairs={{0,2},{2,0},{1,3},{3,1},{4,6},{6,4},{5,7},{7,5},{8,10},{10,8},{9,1... | collective-permute-start | bytes 1572872 | tf_op jit(solution)/shard_map/ppermute | solution.py:27
  137.5 8.0 %weight_step.1 = f32[2,1024,128]{2,1,0:T(8,128)} custom-call(s32[5]{0:T(128)} %copy-done.4, bf16[32,96,128]{2,1,0:T(8,128)(2,1)} %multiply_convert_fusion.outs_ref, bf16[4,2,4,96,128]{4,3,2,1,0:T(8,128)(2,1)} %pad_maximum_fusion.1.refs_0_, bf16[4,2,4,96,128]{4,3,2,1,0:T(8,128)(2,1)} %collective-permute-done.43.refs_1_, ...), custom_call_target="tpu_custom_call" | custom-call | flops 2000000000 | bytes 8000000 | tf_op jit(solution)/shard_map/weight_step/pallas_call | solution.py:358
  145.5 4.5 %product.9 = bf16[256,1024]{1,0:T(8,128)(2,1)S(1)} custom-call(s32[5]{0:T(128)S(1)} %copy-done.5, bf16[256,1024]{1,0:T(8,128)(2,1)S(1)} %get-tuple-element.32.a_ref.lifted_ref, bf16[256,1024]{1,0:T(8,128)(2,1)S(1)} %collective-permute-done.25.b_ref, bf16[2,1024,4096]{2,1,0:T(8,128)(2,1)} %wa_ref.11, bf16[2,1024,1024]{2,1,0:T(8,128)(2,1)} %collective-permute-done.17.wb_ref), custom_call_target="tpu_custom_call" | custom-call | flops 1073741824 | bytes 6291456 | tf_op jit(solution)/shard_map/product/pallas_call | solution.py:222
  150.1 4.4 %product.6.own_ref = f32[256,1024]{1,0:T(8,128)S(1)} custom-call(s32[5]{0:T(128)S(1)} %copy-done.5, bf16[256,1024]{1,0:T(8,128)(2,1)S(1)} %get-tuple-element.27.a_ref.lifted_ref, bf16[256,1024]{1,0:T(8,128)(2,1)S(1)} %collective-permute-done.16.b_ref, bf16[2,1024,4096]{2,1,0:T(8,128)(2,1)} %wa_ref.11, bf16[2,1024,1024]{2,1,0:T(8,128)(2,1)} %collective-permute-done.17.wb_ref), custom_call_target="tpu_custom_call" | custom-call | flops 1073741824 | bytes 6291456 | tf_op jit(solution)/shard_map/product/pallas_call | solution.py:222
  154.5 3.0 %collective-permute-start.4 = (bf16[256,256]{1,0:T(8,128)(2,1)S(1)}, bf16[256,256]{1,0:T(8,128)(2,1)S(1)}, u32[]{:S(2)}, u32[]{:S(2)}) collective-permute-start(bf16[256,256]{1,0:T(8,128)(2,1)S(1)} %fusion.4.t0), channel_id=1, source_target_pairs={{0,12},{4,0},{8,4},{12,8},{1,13},{5,1},{9,5},{13,9},{2,14},{6,2},{... | collective-permute-start | bytes 393224 | tf_op jit(solution)/shard_map/ppermute | solution.py:32
  157.6 4.5 %product.11 = bf16[256,1024]{1,0:T(8,128)(2,1)S(1)} custom-call(s32[5]{0:T(128)S(1)} %copy-done.5, bf16[256,1024]{1,0:T(8,128)(2,1)S(1)} %get-tuple-element.37.a_ref.lifted_ref, bf16[256,1024]{1,0:T(8,128)(2,1)S(1)} %collective-permute-done.33.b_ref, bf16[2,1024,4096]{2,1,0:T(8,128)(2,1)} %wa_ref.11, bf16[2,1024,1024]{2,1,0:T(8,128)(2,1)} %collective-permute-done.17.wb_ref), custom_call_target="tpu_custom_call" | custom-call | flops 1073741824 | bytes 6291456 | tf_op jit(solution)/shard_map/product/pallas_call | solution.py:222
  162.0 7.7 %collective-permute-start.13 = (f32[8,256]{1,0:T(8,128)S(1)}, f32[8,256]{1,0:T(8,128)S(1)}, u32[]{:S(2)}, u32[]{:S(2)}) collective-permute-start(f32[8,256]{1,0:T(8,128)S(1)} %get-tuple-element.26.s0), channel_id=1, source_target_pairs={{0,1},{1,0},{2,3},{3,2},{4,5},{5,4},{6,7},{7,6},{8,9},{9,8},{10,11... | collective-permute-start | bytes 24584 | tf_op jit(solution)/shard_map/ppermute | solution.py:27
  169.8 3.3 %collective-permute-start.34 = (bf16[256,1024]{1,0:T(8,128)(2,1)S(1)}, bf16[256,1024]{1,0:T(8,128)(2,1)S(1)}, u32[]{:S(2)}, u32[]{:S(2)}) collective-permute-start(bf16[256,1024]{1,0:T(8,128)(2,1)S(1)} %product.11), channel_id=1, source_target_pairs={{0,2},{2,0},{1,3},{3,1},{4,6},{6,4},{5,7},{7,5},{8,10},{10,8},{9,1... | collective-permute-start | bytes 1572872 | tf_op jit(solution)/shard_map/ppermute | solution.py:27
  173.0 4.4 %product.8.own_ref = f32[256,1024]{1,0:T(8,128)S(1)} custom-call(s32[5]{0:T(128)S(1)} %copy-done.5, bf16[256,1024]{1,0:T(8,128)(2,1)S(1)} %get-tuple-element.32.a_ref.lifted_ref, bf16[256,1024]{1,0:T(8,128)(2,1)S(1)} %collective-permute-done.25.b_ref, bf16[2,1024,4096]{2,1,0:T(8,128)(2,1)} %wa_ref.11, bf16[2,1024,1024]{2,1,0:T(8,128)(2,1)} %collective-permute-done.17.wb_ref), custom_call_target="tpu_custom_call" | custom-call | flops 1073741824 | bytes 6291456 | tf_op jit(solution)/shard_map/product/pallas_call | solution.py:222
  177.8 3.5 %collective-permute-start.15 = (f32[8,256]{1,0:T(8,128)S(1)}, f32[8,256]{1,0:T(8,128)S(1)}, u32[]{:S(2)}, u32[]{:S(2)}) collective-permute-start(f32[8,256]{1,0:T(8,128)S(1)} %get-tuple-element.26.s0), channel_id=1, source_target_pairs={{0,3},{1,2},{2,1},{3,0},{4,7},{5,6},{6,5},{7,4},{8,11},{9,10},{10,... | collective-permute-start | bytes 24584 | tf_op jit(solution)/shard_map/ppermute | solution.py:36
  181.3 4.4 %product.10.own_ref = f32[256,1024]{1,0:T(8,128)S(1)} custom-call(s32[5]{0:T(128)S(1)} %copy-done.5, bf16[256,1024]{1,0:T(8,128)(2,1)S(1)} %get-tuple-element.37.a_ref.lifted_ref, bf16[256,1024]{1,0:T(8,128)(2,1)S(1)} %collective-permute-done.33.b_ref, bf16[2,1024,4096]{2,1,0:T(8,128)(2,1)} %wa_ref.11, bf16[2,1024,1024]{2,1,0:T(8,128)(2,1)} %collective-permute-done.17.wb_ref), custom_call_target="tpu_custom_call" | custom-call | flops 1073741824 | bytes 6291456 | tf_op jit(solution)/shard_map/product/pallas_call | solution.py:222
  186.1 3.0 %collective-permute-start.23 = (f32[8,256]{1,0:T(8,128)S(1)}, f32[8,256]{1,0:T(8,128)S(1)}, u32[]{:S(2)}, u32[]{:S(2)}) collective-permute-start(f32[8,256]{1,0:T(8,128)S(1)} %get-tuple-element.31.s0), channel_id=1, source_target_pairs={{0,2},{2,0},{1,3},{3,1},{4,6},{6,4},{5,7},{7,5},{8,10},{10,8},{9,1... | collective-permute-start | bytes 24584 | tf_op jit(solution)/shard_map/ppermute | solution.py:27
  191.6 2.9 %collective-permute-start.31 = (f32[8,256]{1,0:T(8,128)S(1)}, f32[8,256]{1,0:T(8,128)S(1)}, u32[]{:S(2)}, u32[]{:S(2)}) collective-permute-start(f32[8,256]{1,0:T(8,128)S(1)} %get-tuple-element.36.s0), channel_id=1, source_target_pairs={{0,2},{2,0},{1,3},{3,1},{4,6},{6,4},{5,7},{7,5},{8,10},{10,8},{9,1... | collective-permute-start | bytes 24584 | tf_op jit(solution)/shard_map/ppermute | solution.py:27
  210.8 3.6 %collective-permute-done.37 = f32[8,256]{1,0:T(8,128)S(1)} collective-permute-done((f32[8,256]{1,0:T(8,128)S(1)}, f32[8,256]{1,0:T(8,128)S(1)}, u32[]{:S(2)}, u32[]{:S(2)}) %collective-permute-start.37) | collective-permute-done | bytes 8224 | tf_op jit(solution)/shard_map/ppermute | solution.py:36
  (203 shorter events, 84.8 us)
Async XLA Ops:
  1.7 53.7 %collective-permute-start.39 = (bf16[8,96,128]{2,1,0:T(8,128)(2,1)S(1)}, bf16[8,96,128]{2,1,0:T(8,128)(2,1)S(1)}, u32[]{:S(2)}, u32[]{:S(2)}) collective-permute-start(bf16[8,96,128]{2,1,0:T(8,128)(2,1)S(1)} %regroup_in.1.a_ref), channel_id=1, source_target_pairs={{0,16},{16,0},{1,17},{17,1},{2,18},{18,2},{3,19},{19,3},{4,20},{20... | collective-permute-start | bytes 589832 | tf_op jit(solution)/shard_map/ppermute | solution.py:27
  7.0 43.6 %collective-permute-start.7 = (f32[8,768]{1,0:T(8,128)S(1)}, f32[8,768]{1,0:T(8,128)S(1)}, u32[]{:S(2)}, u32[]{:S(2)}) collective-permute-start(f32[8,768]{1,0:T(8,128)S(1)} %low.1), channel_id=1, source_target_pairs={{0,3},{1,2},{2,1},{3,0},{4,7},{5,6},{6,5},{7,4},{8,11},{9,10},{10,... | collective-permute-start | bytes 73736 | tf_op jit(solution)/shard_map/ppermute | solution.py:36
  10.4 50.0 %collective-permute-start.6 = (f32[8,768]{1,0:T(8,128)S(1)}, f32[8,768]{1,0:T(8,128)S(1)}, u32[]{:S(2)}, u32[]{:S(2)}) collective-permute-start(f32[8,768]{1,0:T(8,128)S(1)} %low.1), channel_id=1, source_target_pairs={{0,2},{2,0},{1,3},{3,1},{4,6},{6,4},{5,7},{7,5},{8,10},{10,8},{9,1... | collective-permute-start | bytes 73736 | tf_op jit(solution)/shard_map/ppermute | solution.py:27
  10.9 49.9 %collective-permute-start.5 = (f32[8,768]{1,0:T(8,128)S(1)}, f32[8,768]{1,0:T(8,128)S(1)}, u32[]{:S(2)}, u32[]{:S(2)}) collective-permute-start(f32[8,768]{1,0:T(8,128)S(1)} %low.1), channel_id=1, source_target_pairs={{0,1},{1,0},{2,3},{3,2},{4,5},{5,4},{6,7},{7,6},{8,9},{9,8},{10,11... | collective-permute-start | bytes 73736 | tf_op jit(solution)/shard_map/ppermute | solution.py:27
  11.9 67.9 %all-to-all-start = ((bf16[32,48,128]{2,1,0:T(8,128)(2,1)}), bf16[32,48,128]{2,1,0:T(8,128)(2,1)}, u32[]{:S(2)}, u32[]{:S(2)}) async-start(bf16[32,48,128]{2,1,0:T(8,128)(2,1)} %constant_dynamic-slice_fusion.2), calls=%async_computation | async-start | bytes 786432 | tf_op jit(solution)/shard_map/all_to_all | solution.py:443
  25.2 97.8 %collective-permute-start.17 = (bf16[2,1024,1024]{2,1,0:T(8,128)(2,1)}, bf16[2,1024,1024]{2,1,0:T(8,128)(2,1)}, u32[]{:S(2)}, u32[]{:S(2)}) collective-permute-start(bf16[2,1024,1024]{2,1,0:T(8,128)(2,1)} %pad_maximum_fusion), channel_id=1, source_target_pairs={{0,1},{1,0},{2,3},{3,2},{4,5},{5,4},{6,7},{7,6},{8,9},{9,8},{10,11... | collective-permute-start | bytes 12582920 | tf_op jit(solution)/shard_map/ppermute | solution.py:27
  67.9 10.1 %collective-permute-start.10 = (bf16[256,256]{1,0:T(8,128)(2,1)S(1)}, bf16[256,256]{1,0:T(8,128)(2,1)S(1)}, u32[]{:S(2)}, u32[]{:S(2)}) collective-permute-start(bf16[256,256]{1,0:T(8,128)(2,1)S(1)} %fusion.2.t0), channel_id=1, source_target_pairs={{0,4},{4,8},{8,12},{12,0},{1,5},{5,9},{9,13},{13,1},{2,6},{6,10},{... | collective-permute-start | bytes 393224 | tf_op jit(solution)/shard_map/ppermute | solution.py:32
  75.0 11.3 %collective-permute-start.48 = (bf16[2,4,96,128]{3,2,1,0:T(8,128)(2,1)S(1)}, bf16[2,4,96,128]{3,2,1,0:T(8,128)(2,1)S(1)}, u32[]{:S(2)}, u32[]{:S(2)}) collective-permute-start(bf16[2,4,96,128]{3,2,1,0:T(8,128)(2,1)S(1)} %get-tuple-element.52), channel_id=1, source_target_pairs={{0,96},{32,0},{64,32},{96,64},{1,97},{33,1},{65,33},{97,65},{2,98}... | collective-permute-start | bytes 589832 | tf_op jit(solution)/shard_map/ppermute | solution.py:32
  78.0 16.6 %collective-permute-start.43 = (bf16[4,2,4,96,128]{4,3,2,1,0:T(8,128)(2,1)}, bf16[4,2,4,96,128]{4,3,2,1,0:T(8,128)(2,1)}, u32[]{:S(2)}, u32[]{:S(2)}) collective-permute-start(bf16[4,2,4,96,128]{4,3,2,1,0:T(8,128)(2,1)} %pad_maximum_fusion.1.refs_0_), channel_id=1, source_target_pairs={{0,32},{32,64},{64,96},{96,0},{1,33},{33,65},{65,97},{97,1},{2,34}... | collective-permute-start | bytes 2359304 | tf_op jit(solution)/shard_map/ppermute | solution.py:32
  78.8 32.8 %collective-permute-start.44 = (bf16[4,2,4,96,128]{4,3,2,1,0:T(8,128)(2,1)}, bf16[4,2,4,96,128]{4,3,2,1,0:T(8,128)(2,1)}, u32[]{:S(2)}, u32[]{:S(2)}) collective-permute-start(bf16[4,2,4,96,128]{4,3,2,1,0:T(8,128)(2,1)} %pad_maximum_fusion.1.refs_0_), channel_id=1, source_target_pairs={{0,64},{32,96},{64,0},{96,32},{1,65},{33,97},{65,1},{97,33},{2,66}... | collective-permute-start | bytes 2359304 | tf_op jit(solution)/shard_map/ppermute | solution.py:32
  87.7 29.6 %collective-permute-start.45 = (bf16[4,2,4,96,128]{4,3,2,1,0:T(8,128)(2,1)}, bf16[4,2,4,96,128]{4,3,2,1,0:T(8,128)(2,1)}, u32[]{:S(2)}, u32[]{:S(2)}) collective-permute-start(bf16[4,2,4,96,128]{4,3,2,1,0:T(8,128)(2,1)} %pad_maximum_fusion.1.refs_0_), channel_id=1, source_target_pairs={{0,96},{32,0},{64,32},{96,64},{1,97},{33,1},{65,33},{97,65},{2,98}... | collective-permute-start | bytes 2359304 | tf_op jit(solution)/shard_map/ppermute | solution.py:32
  90.6 39.6 %collective-permute-start.49 = (bf16[4,2,4,96,128]{4,3,2,1,0:T(8,128)(2,1)S(1)}, bf16[4,2,4,96,128]{4,3,2,1,0:T(8,128)(2,1)S(1)}, u32[]{:S(2)}, u32[]{:S(2)}) collective-permute-start(bf16[4,2,4,96,128]{4,3,2,1,0:T(8,128)(2,1)S(1)} %pad_maximum_fusion.2.refs_4_), channel_id=1, source_target_pairs={{0,4},{4,8},{8,12},{12,0},{1,5},{5,9},{9,13},{13,1},{2,6},{6,10},{... | collective-permute-start | bytes 2359304 | tf_op jit(solution)/shard_map/ppermute | solution.py:32
  94.6 36.2 %collective-permute-start.50 = (bf16[4,2,4,96,128]{4,3,2,1,0:T(8,128)(2,1)S(1)}, bf16[4,2,4,96,128]{4,3,2,1,0:T(8,128)(2,1)S(1)}, u32[]{:S(2)}, u32[]{:S(2)}) collective-permute-start(bf16[4,2,4,96,128]{4,3,2,1,0:T(8,128)(2,1)S(1)} %pad_maximum_fusion.2.refs_4_), channel_id=1, source_target_pairs={{0,8},{4,12},{8,0},{12,4},{1,9},{5,13},{9,1},{13,5},{2,10},{6,14},... | collective-permute-start | bytes 2359304 | tf_op jit(solution)/shard_map/ppermute | solution.py:32
  111.6 21.7 %collective-permute-start.51 = (bf16[4,2,4,96,128]{4,3,2,1,0:T(8,128)(2,1)S(1)}, bf16[4,2,4,96,128]{4,3,2,1,0:T(8,128)(2,1)S(1)}, u32[]{:S(2)}, u32[]{:S(2)}) collective-permute-start(bf16[4,2,4,96,128]{4,3,2,1,0:T(8,128)(2,1)S(1)} %pad_maximum_fusion.2.refs_4_), channel_id=1, source_target_pairs={{0,12},{4,0},{8,4},{12,8},{1,13},{5,1},{9,5},{13,9},{2,14},{6,2},{... | collective-permute-start | bytes 2359304 | tf_op jit(solution)/shard_map/ppermute | solution.py:32
  117.3 28.2 %collective-permute-start.25 = (bf16[256,1024]{1,0:T(8,128)(2,1)S(1)}, bf16[256,1024]{1,0:T(8,128)(2,1)S(1)}, u32[]{:S(2)}, u32[]{:S(2)}) collective-permute-start(bf16[256,1024]{1,0:T(8,128)(2,1)S(1)} %get-tuple-element.32.a_ref.lifted_ref), channel_id=1, source_target_pairs={{0,1},{1,0},{2,3},{3,2},{4,5},{5,4},{6,7},{7,6},{8,9},{9,8},{10,11... | collective-permute-start | bytes 1572872 | tf_op jit(solution)/shard_map/ppermute | solution.py:27
  123.0 31.6 %collective-permute-start.33 = (bf16[256,1024]{1,0:T(8,128)(2,1)S(1)}, bf16[256,1024]{1,0:T(8,128)(2,1)S(1)}, u32[]{:S(2)}, u32[]{:S(2)}) collective-permute-start(bf16[256,1024]{1,0:T(8,128)(2,1)S(1)} %get-tuple-element.37.a_ref.lifted_ref), channel_id=1, source_target_pairs={{0,1},{1,0},{2,3},{3,2},{4,5},{5,4},{6,7},{7,6},{8,9},{9,8},{10,11... | collective-permute-start | bytes 1572872 | tf_op jit(solution)/shard_map/ppermute | solution.py:27
  130.2 31.8 %collective-permute-start.2 = (bf16[256,256]{1,0:T(8,128)(2,1)S(1)}, bf16[256,256]{1,0:T(8,128)(2,1)S(1)}, u32[]{:S(2)}, u32[]{:S(2)}) collective-permute-start(bf16[256,256]{1,0:T(8,128)(2,1)S(1)} %fusion.4.t0), channel_id=1, source_target_pairs={{0,4},{4,8},{8,12},{12,0},{1,5},{5,9},{9,13},{13,1},{2,6},{6,10},{... | collective-permute-start | bytes 393224 | tf_op jit(solution)/shard_map/ppermute | solution.py:32
  130.8 39.0 %collective-permute-start.3 = (bf16[256,256]{1,0:T(8,128)(2,1)S(1)}, bf16[256,256]{1,0:T(8,128)(2,1)S(1)}, u32[]{:S(2)}, u32[]{:S(2)}) collective-permute-start(bf16[256,256]{1,0:T(8,128)(2,1)S(1)} %fusion.4.t0), channel_id=1, source_target_pairs={{0,8},{4,12},{8,0},{12,4},{1,9},{5,13},{9,1},{13,5},{2,10},{6,14},... | collective-permute-start | bytes 393224 | tf_op jit(solution)/shard_map/ppermute | solution.py:32
  134.2 54.9 %collective-permute-start.18 = (bf16[256,1024]{1,0:T(8,128)(2,1)S(1)}, bf16[256,1024]{1,0:T(8,128)(2,1)S(1)}, u32[]{:S(2)}, u32[]{:S(2)}) collective-permute-start(bf16[256,1024]{1,0:T(8,128)(2,1)S(1)} %product.7), channel_id=1, source_target_pairs={{0,2},{2,0},{1,3},{3,1},{4,6},{6,4},{5,7},{7,5},{8,10},{10,8},{9,1... | collective-permute-start | bytes 1572872 | tf_op jit(solution)/shard_map/ppermute | solution.py:27
  150.0 45.2 %collective-permute-start.26 = (bf16[256,1024]{1,0:T(8,128)(2,1)S(1)}, bf16[256,1024]{1,0:T(8,128)(2,1)S(1)}, u32[]{:S(2)}, u32[]{:S(2)}) collective-permute-start(bf16[256,1024]{1,0:T(8,128)(2,1)S(1)} %product.9), channel_id=1, source_target_pairs={{0,2},{2,0},{1,3},{3,1},{4,6},{6,4},{5,7},{7,5},{8,10},{10,8},{9,1... | collective-permute-start | bytes 1572872 | tf_op jit(solution)/shard_map/ppermute | solution.py:27
  154.5 23.0 %collective-permute-start.4 = (bf16[256,256]{1,0:T(8,128)(2,1)S(1)}, bf16[256,256]{1,0:T(8,128)(2,1)S(1)}, u32[]{:S(2)}, u32[]{:S(2)}) collective-permute-start(bf16[256,256]{1,0:T(8,128)(2,1)S(1)} %fusion.4.t0), channel_id=1, source_target_pairs={{0,12},{4,0},{8,4},{12,8},{1,13},{5,1},{9,5},{13,9},{2,14},{6,2},{... | collective-permute-start | bytes 393224 | tf_op jit(solution)/shard_map/ppermute | solution.py:32
  162.0 15.8 %collective-permute-start.13 = (f32[8,256]{1,0:T(8,128)S(1)}, f32[8,256]{1,0:T(8,128)S(1)}, u32[]{:S(2)}, u32[]{:S(2)}) collective-permute-start(f32[8,256]{1,0:T(8,128)S(1)} %get-tuple-element.26.s0), channel_id=1, source_target_pairs={{0,1},{1,0},{2,3},{3,2},{4,5},{5,4},{6,7},{7,6},{8,9},{9,8},{10,11... | collective-permute-start | bytes 24584 | tf_op jit(solution)/shard_map/ppermute | solution.py:27
  169.8 31.1 %collective-permute-start.34 = (bf16[256,1024]{1,0:T(8,128)(2,1)S(1)}, bf16[256,1024]{1,0:T(8,128)(2,1)S(1)}, u32[]{:S(2)}, u32[]{:S(2)}) collective-permute-start(bf16[256,1024]{1,0:T(8,128)(2,1)S(1)} %product.11), channel_id=1, source_target_pairs={{0,2},{2,0},{1,3},{3,1},{4,6},{6,4},{5,7},{7,5},{8,10},{10,8},{9,1... | collective-permute-start | bytes 1572872 | tf_op jit(solution)/shard_map/ppermute | solution.py:27
  195.2 10.4 %collective-permute-start.19 = (f32[8,256]{1,0:T(8,128)S(1)}, f32[8,256]{1,0:T(8,128)S(1)}, u32[]{:S(2)}, u32[]{:S(2)}) collective-permute-start(f32[8,256]{1,0:T(8,128)S(1)} %get-tuple-element.30), channel_id=1, source_target_pairs={{0,1},{1,0},{2,3},{3,2},{4,5},{5,4},{6,7},{7,6},{8,9},{9,8},{10,11... | collective-permute-start | bytes 24584 | tf_op jit(solution)/shard_map/ppermute | solution.py:27
  (52 other events, 498.3 us)
where the time goes:
time: 217 us; the launch traced here: 216 us
  starting transfers between devices  90.5 us (42%)
  Pallas kernels  52.6 us (24%)
  waiting for transfers between devices  32.1 us (15%)
  blocking collectives  14.9 us (7%)
  local copies, waits for them, and re-layouts  11.8 us (5%)
  other arithmetic  11.2 us (5%)
  between operations  3.16 us (1%)
    ppermute x27, starting transfers between devices, swap(): return lax.ppermute(value, axis, [(0, 1), (1, 0)])  50.9 us
    pallas_call x6, Pallas kernels, product(): pl.pallas_call(kernel, grid_spec=pltpu.PrefetchScalarGridSpec(num_scalar_...  26.7 us
    ppermute x18, waiting for transfers between devices, shift(): return lax.ppermute(value, axis, [(i, (i + by) % n) for i in range(n)])  26.5 us
    ppermute x18, starting transfers between devices, shift(): return lax.ppermute(value, axis, [(i, (i + by) % n) for i in range(n)])  21.1 us
    unnamed x1, blocking collectives  14.9 us
    ppermute x7, starting transfers between devices, mp_parts(): both = lax.ppermute(value, MP, [(i, 3 - i) for i in range(4)])  10.4 us
    all_to_all x1, starting transfers between devices, shards(): mine = lax.all_to_all(my_rows, POP, 0, 0, tiled=True)  8.17 us
    pallas_call x1, Pallas kernels, step_kernel(): pl.pallas_call(kernel, out_shape=jax.ShapeDtypeStruct((2, width, cols), f...  8.03 us
  transfers between devices with their start and end apart: 53, of which 11 were waited for; matrix products, arithmetic and copies ran while one was open for 8% of the time, Pallas kernels for 24%

commit v1 on v0

--- a/solution.py
+++ b/solution.py
@@ -32,9 +32,13 @@
     return lax.ppermute(value, axis, [(i, (i + by) % n) for i in range(n)])
 
 
+def after(value, *earlier):
+    return lax.optimization_barrier((value, *earlier))[0]
+
+
 def mp_parts(value):
-    both = lax.ppermute(value, MP, [(i, 3 - i) for i in range(4)])
-    return value, swap(value, "c"), swap(value, "xh"), both
+    pair = value + swap(value, "c")
+    return pair, swap(pair, "xh")
 
 
 def dot(a, b, ca, cb, precision=None):
@@ -66,7 +70,7 @@
     )(factors)
 
 
-def table_partial(layer, where, embedding, weights):
+def table_partial(layer, part_at, where, embedding, weights):
     vocab, width = embedding.shape
     full = weights.shape[2]
     piece = full // 16
@@ -75,10 +79,9 @@
         peer_ref[0] = jnp.dot(e_ref[...], wp_ref[0], preferred_element_type=f32).astype(bf16)
         own_ref[0] = jnp.dot(e_ref[...], wo_ref[0], preferred_element_type=f32).astype(bf16)
 
-    def block(rel, where_ref, flip):
-        z, xh, c = where_ref[0], where_ref[1], where_ref[2]
-        owner = (xh ^ rel) * 2 + (c ^ flip)
-        return owner * 4 + z
+    def block(rel, s, flip):
+        owner = (s[1] ^ rel) * 2 + (s[2] ^ flip)
+        return owner * 4 + s[part_at]
 
     return pl.pallas_call(
         kernel,
@@ -159,10 +162,10 @@
     steps = 16
     per = rows // steps
 
-    def kernel(where_ref, o_ref, t0, t1, t2, t3, l0, l1, l2, l3, b_ref, a_ref, d_ref, g_ref,
+    def kernel(where_ref, o_ref, t0, t1, t2, t3, l0, l1, b_ref, a_ref, d_ref, g_ref,
                lifted_ref, stats_ref, square):
         z = where_ref[0]
-        low = (l0[...] + l1[...] + l2[...] + l3[...]) * coef
+        low = (l0[...] + l1[...]) * coef
         spread_low = spread(low, 0, group)
         square[...] = jnp.zeros_like(square)
         total = jnp.zeros((group, rows), f32)
@@ -190,133 +193,154 @@
         row = lax.broadcasted_iota(jnp.int32, (8, rows), 0)
         stats_ref[...] = jnp.where(row < 4, sums, low_next)
 
-    sl = lambda a, n: lax.slice_in_dim(a, chunk * n, (chunk + 1) * n, axis=0)
-    lc = [lax.slice_in_dim(a, chunk * rows, (chunk + 1) * rows, axis=1) for a in lows]
-    mid = lambda a: lax.slice_in_dim(a, chunk * group, (chunk + 1) * group, axis=1)
-    return pl.pallas_call(
-        kernel,
+    whole = lambda a: pl.BlockSpec(a.shape, lambda i, n=a.ndim: (0,) * n)
+    at_col = pl.BlockSpec((8, rows), lambda i: (0, chunk))
+    mid = pl.BlockSpec((8, group, 128), lambda i: (0, chunk, 0))
+    return pl.pallas_call(
+        kernel,
+        grid=(1,),
         out_shape=[
             jax.ShapeDtypeStruct((rows, width), bf16),
             jax.ShapeDtypeStruct((8, rows), f32),
         ],
-        in_specs=[SMEM] + [VMEM] * 13,
-        out_specs=[VMEM, VMEM],
+        in_specs=[SMEM, pl.BlockSpec((rows, onehot.shape[1]), lambda i: (chunk, 0))]
+        + [whole(t) for t in tables]
+        + [at_col, at_col, mid, mid, whole(decay), whole(gain)],
+        out_specs=[
+            pl.BlockSpec((rows, width), lambda i: (0, 0)),
+            pl.BlockSpec((8, rows), lambda i: (0, 0)),
+        ],
         scratch_shapes=[pltpu.VMEM((rows, 128), f32)],
         compiler_params=params(),
         name="first_layer",
         cost_estimate=pl.CostEstimate(flops=2000000000, bytes_accessed=4000000, transcendentals=0),
-    )(where, sl(onehot, rows), *tables, *lc, mid(out_factors), mid(in_factors), decay, gain)
-
-
-def product(where, rel, lifted, lifted_peer, weights, weights_peer, out_dtype):
-    rows, width = lifted.shape
-    blocks = 4
-    piece = width // blocks
-
-    def kernel(where_ref, a_ref, b_ref, wa_ref, wb_ref, out_ref):
-        out_ref[...] = (
-            jnp.dot(a_ref[...], wa_ref[0], preferred_element_type=f32)
-            + jnp.dot(b_ref[...], wb_ref[0], preferred_element_type=f32)
-        ).astype(out_dtype)
-
+    )(where, onehot, *tables, *lows, out_factors, in_factors, decay, gain)
+
+
+def product(where, rel, first, count, lifted, weights, weights_peer, out_dtype):
+    rows, width = lifted[0].shape
+    piece = width // 4
+    chunks = len(lifted)
+
+    def kernel(where_ref, *refs):
+        wa_ref, wb_ref, out_ref = refs[chunks:]
+        for k in range(chunks // 2):
+            out_ref[k * rows : (k + 1) * rows, :] = (
+                jnp.dot(refs[k][...], wa_ref[0], preferred_element_type=f32)
+                + jnp.dot(refs[chunks // 2 + k][...], wb_ref[...], preferred_element_type=f32)
+            ).astype(out_dtype)
+
+    total = rows * chunks // 2
     return pl.pallas_call(
         kernel,
         grid_spec=pltpu.PrefetchScalarGridSpec(
             num_scalar_prefetch=1,
-            grid=(blocks,),
-            in_specs=[
-                pl.BlockSpec((rows, width), lambda n, s: (0, 0)),
-                pl.BlockSpec((rows, width), lambda n, s: (0, 0)),
+            grid=(count,),
+            in_specs=[pl.BlockSpec((rows, width), lambda n, s: (0, 0))] * chunks
+            + [
                 pl.BlockSpec(
                     (1, width, piece),
-                    lambda n, s: (1, 0, ((s[1] ^ rel) * 2 + s[2]) * blocks + n),
+                    lambda n, s: (1, 0, ((s[1] ^ rel) * 2 + s[2]) * 4 + first + n),
                 ),
-                pl.BlockSpec((1, width, piece), lambda n, s: (rel, 0, n)),
+                pl.BlockSpec((width, piece), lambda n, s: (0, first + n)),
             ],
-            out_specs=pl.BlockSpec((rows, piece), lambda n, s: (0, n)),
+            out_specs=pl.BlockSpec((total, piece), lambda n, s: (0, n)),
         ),
-        out_shape=jax.ShapeDtypeStruct((rows, width), out_dtype),
+        out_shape=jax.ShapeDtypeStruct((total, piece * count), out_dtype),
         compiler_params=params(),
         name="product",
         cost_estimate=pl.CostEstimate(
-            flops=4 * rows * width * width, bytes_accessed=6 * width * width, transcendentals=0
+            flops=4 * total * width * piece * count,
+            bytes_accessed=6 * width * piece * count,
+            transcendentals=0,
         ),
-    )(where, lifted, lifted_peer, weights, weights_peer)
-
-
-def second_layer(chunk, where, coef, full_width, onehot, embedding, tables, lows, stats, lifted,
-                 own, other, out_factors, decay, gain, reward):
-    rows = lifted.shape[0]
+    )(where, *lifted, weights, weights_peer)
+
+
+def second_layer(n, where, coef, full_width, onehot, embedding, table, lows, stats, lifted,
+                 own, other, out_factors, decay, gain, reward, before):
+    rows = onehot.shape[0] // CHUNKS
     group = out_factors.shape[1] // CHUNKS
-    width = decay.shape[1]
     steps = 16
     per = rows // steps
 
-    def kernel(where_ref, o_ref, e_ref, t0, t1, t2, t3, l0, l1, l2, l3, s0, s1, s2, s3, lifted_ref,
-               own_ref, other_ref, b_ref, d_ref, g_ref, r_ref,
+    def kernel(where_ref, o_ref, e_ref, t_ref, l0, l1, s0, s1, up0, up1, up2,
+               own_ref, other_ref, b_ref, d_ref, g_ref, r_ref, before_ref,
                stats_ref, hidden_ref, last_ref, square, lr, xr):
-        z = where_ref[0]
-        from_hidden = l0[...] + l1[...] + l2[...] + l3[...]
-        so_far = s0[...] + s1[...] + s2[...] + s3[...]
-        norm = lax.rsqrt(so_far[0:1] / full_width + norm_eps)
-        low = (from_hidden + norm * so_far) * coef
-        spread_low = spread(low, 1, group)
-        norm_col = jnp.transpose(jnp.broadcast_to(norm, (8, rows)))[:, 0:1]
-        square[...] = jnp.zeros_like(square)
-        lr[...] = jnp.zeros_like(lr)
-        xr[...] = jnp.zeros_like(xr)
-        for k, table in enumerate((t0, t1, t2, t3)):
-            blk = (z - k + 4) % 4
-            cols = pl.ds(pl.multiple_of(blk * 256, 256), 256)
-            factor = jnp.concatenate([b_ref[2 * blk], b_ref[2 * blk + 1]], axis=1)
-            both = own_ref[:, cols] + other_ref[:, cols].astype(f32)
+        y = where_ref[3]
+        table = t_ref[(y - n + 4) % 4]
+        factor = jnp.concatenate([b_ref[0], b_ref[1]], axis=1)
+        e = e_ref[...]
+        d = d_ref[...]
+        g = g_ref[...]
+        r = r_ref[...]
+        rest = 1.0 - d
+        gr = g * r
+        for k, up in enumerate((up0, up1, up2)):
+            span_k = slice(k * rows, (k + 1) * rows)
+            so_far = s0[:, span_k] + s1[:, span_k]
+            norm = lax.rsqrt(so_far[0:1] / full_width + norm_eps)
+            low = (l0[:, span_k] + l1[:, span_k] + norm * so_far) * coef
+            spread_low = spread(low, 1, group)
+            norm_col = jnp.transpose(jnp.broadcast_to(norm, (8, rows)))[:, 0:1]
+            both = own_ref[span_k] + other_ref[span_k].astype(f32)
+            o = o_ref[span_k]
             u = (
-                jnp.dot(o_ref[...], table[...], preferred_element_type=f32)
-                + dot(spread_low, factor, 0, 0)
+                jnp.dot(o, table, preferred_element_type=f32)
+                + dot(spread_low, factor[k * group : (k + 1) * group], 0, 0)
                 + norm_col * both
             )
-            x = jnp.dot(o_ref[...], e_ref[:, cols], preferred_element_type=f32)
-            x = (x + norm_col * lifted_ref[:, cols].astype(f32)).astype(bf16)
-            d = d_ref[:, cols]
-            g = g_ref[:, cols]
-            r = r_ref[:, cols]
-            rest = 1.0 - d
+            x = jnp.dot(o, e, preferred_element_type=f32)
+            x = (x + norm_col * up[...].astype(f32)).astype(bf16)
             h = jnp.zeros((per, 256), f32)
             xrr = x.astype(f32) * r
-            xr[...] += xrr[:, :128] + xrr[:, 128:]
-            gr = g * r
+            xr[...] = xrr[:, :128] + xrr[:, 128:]
             for t in range(steps):
                 span = slice(t * per, (t + 1) * per)
                 h = d * h + rest * u[span]
                 hr = h * gr
                 hh = h * h
-                square[span] += hh[:, :128] + hh[:, 128:]
-                lr[span] += hr[:, :128] + hr[:, 128:]
-            hidden_ref[:, cols] = x[(steps - 1) * per :].astype(f32)
-            last_ref[:, cols] = h * g
-        ones = jnp.ones((8, 128), f32)
-        sums = [dot(ones, a[...], 1, 1, lax.Precision.HIGHEST) for a in (square, lr, xr)]
-        row = lax.broadcasted_iota(jnp.int32, (8, rows), 0)
-        stats_ref[...] = jnp.where(row == 0, sums[0], jnp.where(row == 1, sums[1], sums[2]))
-
-    sl = lambda a, n: lax.slice_in_dim(a, chunk * n, (chunk + 1) * n, axis=0)
-    lc = [lax.slice_in_dim(a, chunk * rows, (chunk + 1) * rows, axis=1) for a in lows]
-    mid = lambda a: lax.slice_in_dim(a, chunk * group, (chunk + 1) * group, axis=1)
-    return pl.pallas_call(
-        kernel,
+                square[span] = hh[:, :128] + hh[:, 128:]
+                lr[span] = hr[:, :128] + hr[:, 128:]
+            tail = slice(k * per, (k + 1) * per)
+            hidden_ref[tail] = x[(steps - 1) * per :].astype(f32)
+            last_ref[tail] = h * g
+            ones = jnp.ones((8, 128), f32)
+            sums = [dot(ones, a[...], 1, 1, lax.Precision.HIGHEST) for a in (square, lr, xr)]
+            row = lax.broadcasted_iota(jnp.int32, (8, rows), 0)
+            stats_ref[:, span_k] = before_ref[:, span_k] + jnp.where(
+                row == 0, sums[0], jnp.where(row == 1, sums[1], sums[2])
+            )
+
+    whole = lambda a: pl.BlockSpec(a.shape, lambda i, m=a.ndim: (0,) * m)
+    col = lambda a: pl.BlockSpec((a.shape[0], 256), lambda i: (0, n))
+    total = rows * CHUNKS
+    return pl.pallas_call(
+        kernel,
+        grid=(1,),
         out_shape=[
-            jax.ShapeDtypeStruct((8, rows), f32),
-            jax.ShapeDtypeStruct((per, width), f32),
-            jax.ShapeDtypeStruct((per, width), f32),
+            jax.ShapeDtypeStruct((8, total), f32),
+            jax.ShapeDtypeStruct((per * CHUNKS, 256), f32),
+            jax.ShapeDtypeStruct((per * CHUNKS, 256), f32),
         ],
-        in_specs=[SMEM] + [VMEM] * 21,
-        out_specs=[VMEM] * 3,
+        in_specs=[SMEM, whole(onehot), col(embedding), whole(table)]
+        + [whole(a) for a in (*lows, *stats)]
+        + [col(a) for a in lifted]
+        + [col(own), whole(other)]
+        + [pl.BlockSpec((2, group * CHUNKS, 128), lambda i: (n, 0, 0))]
+        + [col(a) for a in (decay, gain, reward)]
+        + [whole(before)],
+        out_specs=[
+            pl.BlockSpec((8, total), lambda i: (0, 0)),
+            pl.BlockSpec((per * CHUNKS, 256), lambda i: (0, 0)),
+            pl.BlockSpec((per * CHUNKS, 256), lambda i: (0, 0)),
+        ],
         scratch_shapes=[pltpu.VMEM((rows, 128), f32)] * 3,
         compiler_params=params(),
         name="second_layer",
         cost_estimate=pl.CostEstimate(flops=2000000000, bytes_accessed=4000000, transcendentals=0),
-    )(where, sl(onehot, rows), embedding, *tables, *lc, *stats, lifted, own, other,
-      mid(out_factors), decay, gain, reward)
+    )(where, onehot, embedding, table, *lows, *stats, *lifted, own, other,
+      out_factors, decay, gain, reward, before)
 
 
 def step_kernel(where, ins, outs, width):
@@ -393,46 +417,62 @@
     xh, c = (lax.axis_index(a) for a in MP)
     where = jnp.stack([z, xh, c, y, xl]).astype(jnp.int32)
     rows_all = members * seq_count * step_count
-    rows = rows_all // CHUNKS
-
-    tables = []
-    for layer in range(2):
-        peer, own = table_partial(layer, where, embedding, mix_weights)
-        pair = own.astype(f32) + swap(peer, "c").astype(f32)
-        crossing = swap(pair[1].astype(bf16), "xh")
-        table = (pair[0] + crossing.astype(f32)).astype(bf16)
-        tables.append(ring_copies(table, "z"))
 
     order = token_ids.reshape(CHUNKS, -1, step_count).transpose(0, 2, 1).reshape(-1)
     onehot = (order[:, None] == jnp.arange(vocab, dtype=jnp.int32)[None, :]).astype(bf16)
-    a_blocks = regroup(factors_in, "regroup_in", 0)
-    b_blocks = regroup(factors_out, "regroup_out", 0)
+
+    def own_sum(own, peer):
+        pair = own.astype(f32) + swap(peer, "c").astype(f32)
+        return pair[0], pair[1].astype(bf16)
+
+    peer, own = table_partial(0, 0, where, embedding, mix_weights)
+    onehot = after(onehot, peer)
+    a_blocks = regroup(after(factors_in, peer), "regroup_in", 0)
+    keep, cross = own_sum(own, peer)
+    lows = mp_parts(low_kernel(onehot, embedding, a_blocks))
+    table = (keep + swap(cross, "xh").astype(f32)).astype(bf16)
+    first_tables = ring_copies(table, "z")
+
+    peer, own = table_partial(1, 3, after(where, cross), embedding, mix_weights)
+    keep, cross = own_sum(own, peer)
+    table_next = (keep + swap(after(cross, table), "xh").astype(f32)).astype(bf16)
+    table_next = after(table_next, table)
+    second_tables = jnp.stack(ring_copies(table_next, "y"))
+
+    b_blocks = regroup(after(factors_out, lows[0]), "regroup_out", 0)
     b_own = lax.dynamic_slice_in_dim(b_blocks, (xh * 2 + c) * 8, 8, 0)
-    lows = mp_parts(low_kernel(onehot, embedding, a_blocks))
-
-    peer_cols = [
-        lax.dynamic_slice(mix_weights, (1, 0, ((xh ^ rel) * 2 + (1 - c)) * width), (1, width, width))
+
+    late_weights = after(mix_weights, table)
+    weights_peer = [
+        swap(
+            lax.dynamic_slice(
+                late_weights, (1, 0, ((xh ^ rel) * 2 + (1 - c)) * width), (1, width, width)
+            )[0],
+            "c",
+        )
         for rel in range(2)
     ]
-    weights_peer = swap(jnp.concatenate(peer_cols, axis=0), "c")
 
     decay = [decay_rates[l : l + 1] for l in range(2)]
     gain = [norm_gain[l : l + 1] for l in range(2)]
-    lifted, stats, sent, own_half, peers = [], [], [], [], []
+    lifted, stats, peers = [], [], []
     for k in range(CHUNKS):
         up, st = first_layer(
-            k, where, coef, onehot, tables_of(tables, 0), lows, b_own, a_blocks, decay[0], gain[0]
+            k, where, coef, onehot, first_tables, lows, b_own, a_blocks, decay[0], gain[0]
         )
         lifted.append(up)
         peers.append(swap(up, "c"))
-        stats.append(mp_parts(st))
-    for k in range(CHUNKS):
-        half = product(where, 1, lifted[k], peers[k], mix_weights, weights_peer, bf16)
+        stats.append(st)
+    stats = mp_parts(jnp.concatenate(stats, axis=1))
+    both = lifted + peers
+    sent = []
+    for n in range(4):
+        half = product(where, 1, n, 1, both, mix_weights, weights_peer[1], bf16)
         sent.append(swap(half, "xh"))
-    for k in range(CHUNKS):
-        own_half.append(product(where, 0, lifted[k], peers[k], mix_weights, weights_peer, f32))
+    own_half = product(after(where, half), 0, 0, 4, both, mix_weights, weights_peer[0], f32)
 
     pair_in = jnp.stack([a_blocks, swap(a_blocks, "xl")])
+    pair_in = after(pair_in, lifted[0])
     first, second = pair_in[:, :4], pair_in[:, 4:]
     first_z = jnp.stack(ring_copies(first, "z"))
     second_y = jnp.stack(ring_copies(second, "y"))
@@ -440,13 +480,19 @@
     second_yz = ring_copies(second_y, "z")
     half_rows = b_blocks.shape[1] // 2
     my_rows = lax.dynamic_slice_in_dim(b_blocks, c * half_rows, half_rows, 1)
-    mine = lax.all_to_all(my_rows, POP, 0, 0, tiled=True)
+    digits = jnp.stack([fitness_ranks // 32, fitness_ranks % 32]).astype(bf16)
+    digits = jnp.pad(digits, ((0, 6), (0, 128 - members)))
+    digits = jnp.broadcast_to(digits[None], (pop_count, 8, 128))
+    packed = after(jnp.concatenate([my_rows, digits], axis=1), half)
+    arrived = lax.all_to_all(packed, POP, 0, 0, tiled=True)
+    mine = arrived[:, :half_rows]
+    digits_all = arrived[:, half_rows : half_rows + 2, :members].astype(f32)
+    ranks_every = (digits_all[:, 0] * 32.0 + digits_all[:, 1]).reshape(-1)
     theirs = swap(mine, "c")
     outs = jnp.where(
         c == 0, jnp.concatenate([mine, theirs], axis=1), jnp.concatenate([theirs, mine], axis=1)
     )
-    ranks_every = lax.all_gather(fitness_ranks, POP, tiled=True)
-    shares_all = ranks_every.astype(f32) / members_all
+    shares_all = ranks_every / members_all
     rank_mean = jnp.mean(shares_all)
     rank_spread = jnp.mean((shares_all - rank_mean) * (shares_all - rank_mean)) + spread_eps
     shaped = (shares_all - rank_mean) * lax.rsqrt(rank_spread)
@@ -455,25 +501,23 @@
     outs = (outs.astype(f32) * shaped_rows[:, :, None]).astype(bf16)
     weight_step = step_kernel(where, [first_zy, second_yz], outs, width)
 
-    finals, terms = [], []
-    for k in range(CHUNKS):
+    st = jnp.zeros((8, rows_all), f32)
+    hiddens, lasts = [], []
+    for n in range(4):
         st, hidden, last = second_layer(
-            k, where, coef, full_width, onehot, embedding, tables_of(tables, 1), lows, stats[k],
-            lifted[k], own_half[k], sent[k], b_own, decay[1], gain[1], reward_dir[None],
+            n, where, coef, full_width, onehot, embedding, second_tables, lows, stats,
+            lifted, own_half, sent[n], b_own, decay[1], gain[1], reward_dir[None], st,
         )
-        so_far = sum(mp_parts(st))
-        norm = lax.rsqrt(so_far[0] / full_width + norm_eps)
-        terms.append(so_far[2] + norm * so_far[1])
-        tail = norm[-last.shape[0] :]
-        finals.append((hidden + last * tail[:, None]).astype(bf16))
-    final_features = jnp.concatenate(finals, axis=0).reshape(members, seq_count, width)
-    scores = jnp.mean(jnp.stack(terms).reshape(CHUNKS, step_count, -1), axis=1)
-    scores = scores.reshape(members, seq_count) * full_width ** (-0.5)
+        hiddens.append(hidden)
+        lasts.append(last)
+    so_far = sum(mp_parts(st))
+    norm = lax.rsqrt(so_far[0] / full_width + norm_eps)
+    terms = (so_far[2] + norm * so_far[1]).reshape(CHUNKS, step_count, -1)
+    tail = norm.reshape(CHUNKS, step_count, -1)[:, -1].reshape(-1)
+    finals = jnp.concatenate(hiddens, axis=1) + jnp.concatenate(lasts, axis=1) * tail[:, None]
+    final_features = finals.astype(bf16).reshape(members, seq_count, width)
+    scores = jnp.mean(terms, axis=1).reshape(members, seq_count) * full_width ** (-0.5)
     return (final_features, scores, weight_step)
-
-
-def tables_of(tables, layer):
-    return tables[layer]
 
 
 def solution(mesh):

time: 217 us -> 202 us (0.931)
  waiting for transfers between devices: 32.1 us -> 66.8 us
  starting transfers between devices: 90.5 us -> 59.4 us
  blocking collectives: 14.9 us -> 0 us
  Pallas kernels: 52.6 us -> 50.2 us
    all_to_all x1, waiting for transfers between devices: 0.01 us -> 29.1 us  [shards(): arrived = lax.all_to_all(packed, POP, 0, 0, tiled=True)]
    ppermute x27 -> x21, starting transfers between devices: 50.9 us -> 32.8 us  [swap(): return lax.ppermute(value, axis, [(0, 1), (1, 0)])]
    unnamed x1 -> x0, blocking collectives: 14.9 us -> none
    ppermute x7 -> x0, starting transfers between devices: 10.4 us -> none  [mp_parts(): both = lax.ppermute(value, MP, [(i, 3 - i) for i in range(4)])]
    pallas_call x6 -> x5, Pallas kernels: 26.7 us -> 17.7 us  [product(): pl.pallas_call(kernel, grid_spec=pltpu.PrefetchScalarGridSpec(num_scalar_...]
    pallas_call x6 -> x7, Pallas kernels: 11.2 us -> 17.6 us  [the longest x4 12.3 us: second_layer(): pl.pallas_call(kernel, grid=(1,), out_shape=[jax.ShapeDtypeStruct((8, tot...]
    ppermute x18, waiting for transfers between devices: 26.5 us -> 32.2 us  [shift(): return lax.ppermute(value, axis, [(i, (i + by) % n) for i in range(n)])]
    squeeze x0 -> x3, local copies, waits for them, and re-layouts: none -> 4.79 us  [the longest x1 4.64 us: shards(): lax.dynamic_slice(late_weights, (1, 0, ((xh ^ rel) * 2 + (1 - c)) * width...]
  transfers between devices with their start and end apart: 53 -> 40, of which waited for: 11 -> 8; matrix products, arithmetic and copies ran while one was open for 8% -> 9% of each run, Pallas kernels for 24% -> 20%
where the time goes in v1:
time: 202 us; the launch traced here: 200 us
  waiting for transfers between devices  66.8 us (33%)
  starting transfers between devices  59.4 us (29%)
  Pallas kernels  50.2 us (25%)
  local copies, waits for them, and re-layouts  12.1 us (6%)
  other arithmetic  9.28 us (5%)
  between operations  2.63 us (1%)
    ppermute x21, starting transfers between devices, swap(): return lax.ppermute(value, axis, [(0, 1), (1, 0)])  32.8 us
    ppermute x18, waiting for transfers between devices, shift(): return lax.ppermute(value, axis, [(i, (i + by) % n) for i in range(n)])  32.2 us
    all_to_all x1, waiting for transfers between devices, shards(): arrived = lax.all_to_all(packed, POP, 0, 0, tiled=True)  29.1 us
    ppermute x18, starting transfers between devices, shift(): return lax.ppermute(value, axis, [(i, (i + by) % n) for i in range(n)])  22.7 us
    pallas_call x5, Pallas kernels, product(): pl.pallas_call(kernel, grid_spec=pltpu.PrefetchScalarGridSpec(num_scalar_...  17.7 us
    pallas_call x4, Pallas kernels, second_layer(): pl.pallas_call(kernel, grid=(1,), out_shape=[jax.ShapeDtypeStruct((8, tot...  12.3 us
    pallas_call x1, Pallas kernels, step_kernel(): pl.pallas_call(kernel, out_shape=jax.ShapeDtypeStruct((2, width, cols), f...  8.06 us
    ppermute x21, waiting for transfers between devices, swap(): return lax.ppermute(value, axis, [(0, 1), (1, 0)])  5.54 us
  transfers between devices with their start and end apart: 40, of which 8 were waited for; matrix products, arithmetic and copies ran while one was open for 9% of the time, Pallas kernels for 20%

profile of v1, /device:TPU:1, one launch (start us, length us, event | category | flops | bytes accessed | tf_op | source)
XLA Modules:
  0.0 200.4 jit_solution(4366541911487224996)
XLA Ops:
  1.8 2.7 %table.2 = (bf16[2,256,256]{2,1,0:T(8,128)(2,1)S(1)}, bf16[2,256,256]{2,1,0:T(8,128)(2,1)S(1)}) custom-call(s32[5]{0:T(128)S(1)} %stack.89.where_ref, bf16[256,1024]{1,0:T(8,128)(2,1)S(1)} %copy-done.2, bf16[2,1024,4096]{2,1,0:T(8,128)(2,1)} %refs_6_.9, bf16[2,1024,4096]{2,1,0:T(8,128)(2,1)} %refs_6_.9), custom_call_target="tpu_custom_call" | custom-call | flops 536870912 | bytes 2097152 | tf_op jit(solution)/shard_map/table/pallas_call | solution.py:86
  9.6 2.9 %collective-permute-start.8 = (f32[8,768]{1,0:T(8,128)S(1)}, f32[8,768]{1,0:T(8,128)S(1)}, u32[]{:S(2)}, u32[]{:S(2)}) collective-permute-start(f32[8,768]{1,0:T(8,128)S(1)} %add.94.l0), channel_id=1, source_target_pairs={{0,2},{2,0},{1,3},{3,1},{4,6},{6,4},{5,7},{7,5},{8,10},{10,8},{9,1... | collective-permute-start | bytes 73736 | tf_op jit(solution)/shard_map/ppermute | solution.py:27
  14.1 2.7 %table.3 = (bf16[2,256,256]{2,1,0:T(8,128)(2,1)S(1)}, bf16[2,256,256]{2,1,0:T(8,128)(2,1)S(1)}) custom-call(s32[5]{0:T(128)S(1)} %stack.89.where_ref, bf16[256,1024]{1,0:T(8,128)(2,1)S(1)} %copy-done.3, bf16[2,1024,4096]{2,1,0:T(8,128)(2,1)} %refs_6_.9, bf16[2,1024,4096]{2,1,0:T(8,128)(2,1)} %refs_6_.9), custom_call_target="tpu_custom_call" | custom-call | flops 536870912 | bytes 2097152 | tf_op jit(solution)/shard_map/table/pallas_call | solution.py:86
  21.5 3.3 %collective-permute-start.10 = (bf16[256,256]{1,0:T(8,128)(2,1)S(1)}, bf16[256,256]{1,0:T(8,128)(2,1)S(1)}, u32[]{:S(2)}, u32[]{:S(2)}) collective-permute-start(bf16[256,256]{1,0:T(8,128)(2,1)S(1)} %fusion.2.t0), channel_id=1, source_target_pairs={{0,8},{4,12},{8,0},{12,4},{1,9},{5,13},{9,1},{13,5},{2,10},{6,14},... | collective-permute-start | bytes 393224 | tf_op jit(solution)/shard_map/ppermute | solution.py:32
  25.6 4.6 %dynamic-slice_bitcast_fusion = (bf16[1024,1024]{1,0:T(8,128)(2,1)}, bf16[1024,1024]{1,0:T(8,128)(2,1)}) fusion(bf16[2,1024,4096]{2,1,0:T(8,128)(2,1)} %refs_6_.9, s32[]{:T(128)S(6)} %select_n.34, s32[]{:T(128)S(6)} %select_n.33), kind=kLoop, calls=%fused_computation | loop fusion | bytes 8388616 | tf_op jit(solution)/shard_map/squeeze | solution.py:448
  43.5 2.7 %collective-permute-start.6 = (bf16[256,256]{1,0:T(8,128)(2,1)}, bf16[256,256]{1,0:T(8,128)(2,1)}, u32[]{:S(2)}, u32[]{:S(2)}) collective-permute-start(bf16[256,256]{1,0:T(8,128)(2,1)} %fusion.4), channel_id=1, source_target_pairs={{0,96},{32,0},{64,32},{96,64},{1,97},{33,1},{65,33},{97,65},{2,98}... | collective-permute-start | bytes 393224 | tf_op jit(solution)/shard_map/ppermute | solution.py:32
  49.7 3.4 %collective-permute-start.14 = (bf16[256,1024]{1,0:T(8,128)(2,1)S(1)}, bf16[256,1024]{1,0:T(8,128)(2,1)S(1)}, u32[]{:S(2)}, u32[]{:S(2)}) collective-permute-start(bf16[256,1024]{1,0:T(8,128)(2,1)S(1)} %get-tuple-element.48.refs_0_.up0), channel_id=1, source_target_pairs={{0,1},{1,0},{2,3},{3,2},{4,5},{5,4},{6,7},{7,6},{8,9},{9,8},{10,11... | collective-permute-start | bytes 1572872 | tf_op jit(solution)/shard_map/ppermute | solution.py:27
  53.1 3.0 %collective-permute-start.15 = (bf16[256,1024]{1,0:T(8,128)(2,1)S(1)}, bf16[256,1024]{1,0:T(8,128)(2,1)S(1)}, u32[]{:S(2)}, u32[]{:S(2)}) collective-permute-start(bf16[256,1024]{1,0:T(8,128)(2,1)S(1)} %get-tuple-element.49.refs_1_.up1), channel_id=1, source_target_pairs={{0,1},{1,0},{2,3},{3,2},{4,5},{5,4},{6,7},{7,6},{8,9},{9,8},{10,11... | collective-permute-start | bytes 1572872 | tf_op jit(solution)/shard_map/ppermute | solution.py:27
  62.2 2.6 %product.7 = bf16[768,256]{1,0:T(8,128)(2,1)S(1)} custom-call(s32[5]{0:T(128)S(1)} %stack.89.where_ref, bf16[256,1024]{1,0:T(8,128)(2,1)S(1)} %get-tuple-element.48.refs_0_.up0, bf16[256,1024]{1,0:T(8,128)(2,1)S(1)} %get-tuple-element.49.refs_1_.up1, bf16[256,1024]{1,0:T(8,128)(2,1)S(1)} %copy-done.1, bf16[256,1024]{1,0:T(8,128)(2,1)S(1)} %collective-permute-done.14.refs_3_, ...), custom_call_target="tpu_custom_call" | custom-call | flops 805306368 | bytes 1572864 | tf_op jit(solution)/shard_map/product/pallas_call | solution.py:234
  66.6 2.6 %product.5 = bf16[768,256]{1,0:T(8,128)(2,1)S(1)} custom-call(s32[5]{0:T(128)S(1)} %stack.89.where_ref, bf16[256,1024]{1,0:T(8,128)(2,1)S(1)} %get-tuple-element.48.refs_0_.up0, bf16[256,1024]{1,0:T(8,128)(2,1)S(1)} %get-tuple-element.49.refs_1_.up1, bf16[256,1024]{1,0:T(8,128)(2,1)S(1)} %copy-done.1, bf16[256,1024]{1,0:T(8,128)(2,1)S(1)} %collective-permute-done.14.refs_3_, ...), custom_call_target="tpu_custom_call" | custom-call | flops 805306368 | bytes 1572864 | tf_op jit(solution)/shard_map/product/pallas_call | solution.py:234
  69.2 2.6 %product.9 = bf16[768,256]{1,0:T(8,128)(2,1)S(1)} custom-call(s32[5]{0:T(128)S(1)} %stack.89.where_ref, bf16[256,1024]{1,0:T(8,128)(2,1)S(1)} %get-tuple-element.48.refs_0_.up0, bf16[256,1024]{1,0:T(8,128)(2,1)S(1)} %get-tuple-element.49.refs_1_.up1, bf16[256,1024]{1,0:T(8,128)(2,1)S(1)} %copy-done.1, bf16[256,1024]{1,0:T(8,128)(2,1)S(1)} %collective-permute-done.14.refs_3_, ...), custom_call_target="tpu_custom_call" | custom-call | flops 805306368 | bytes 1572864 | tf_op jit(solution)/shard_map/product/pallas_call | solution.py:234
  73.1 2.6 %product.8 = bf16[768,256]{1,0:T(8,128)(2,1)S(1)} custom-call(s32[5]{0:T(128)S(1)} %stack.89.where_ref, bf16[256,1024]{1,0:T(8,128)(2,1)S(1)} %get-tuple-element.48.refs_0_.up0, bf16[256,1024]{1,0:T(8,128)(2,1)S(1)} %get-tuple-element.49.refs_1_.up1, bf16[256,1024]{1,0:T(8,128)(2,1)S(1)} %copy-done.1, bf16[256,1024]{1,0:T(8,128)(2,1)S(1)} %collective-permute-done.14.refs_3_, ...), custom_call_target="tpu_custom_call" | custom-call | flops 805306368 | bytes 1572864 | tf_op jit(solution)/shard_map/product/pallas_call | solution.py:234
  77.6 7.3 %product.6.own_ref = f32[768,1024]{1,0:T(8,128)} custom-call(s32[5]{0:T(128)S(1)} %stack.89.where_ref, bf16[256,1024]{1,0:T(8,128)(2,1)S(1)} %get-tuple-element.48.refs_0_.up0, bf16[256,1024]{1,0:T(8,128)(2,1)S(1)} %get-tuple-element.49.refs_1_.up1, bf16[256,1024]{1,0:T(8,128)(2,1)S(1)} %copy-done.1, bf16[256,1024]{1,0:T(8,128)(2,1)S(1)} %collective-permute-done.14.refs_3_, ...), custom_call_target="tpu_custom_call" | custom-call | flops 3221225472 | bytes 6291456 | tf_op jit(solution)/shard_map/product/pallas_call | solution.py:234
  88.4 3.1 %second_layer.4 = (f32[8,768]{1,0:T(8,128)S(1)}, f32[48,256]{1,0:T(8,128)S(1)}, f32[48,256]{1,0:T(8,128)S(1)}) custom-call(s32[5]{0:T(128)S(1)} %stack.89.where_ref, bf16[768,256]{1,0:T(8,128)(2,1)S(1)} %copy-done.8, bf16[256,1024]{1,0:T(8,128)(2,1)S(1)} %copy-done.4, bf16[4,256,256]{2,1,0:T(8,128)(2,1)S(1)} %pad_maximum_fusion.2.t_ref, ...), custom_call_target="tpu_custom_call" | custom-call | flops 2000000000 | bytes 4000000 | tf_op jit(solution)/shard_map/second_layer/pallas_call | solution.py:318
  94.5 3.1 %second_layer.5 = (f32[8,768]{1,0:T(8,128)S(1)}, f32[48,256]{1,0:T(8,128)S(1)}, f32[48,256]{1,0:T(8,128)S(1)}) custom-call(s32[5]{0:T(128)S(1)} %stack.89.where_ref, bf16[768,256]{1,0:T(8,128)(2,1)S(1)} %copy-done.8, bf16[256,1024]{1,0:T(8,128)(2,1)S(1)} %copy-done.4, bf16[4,256,256]{2,1,0:T(8,128)(2,1)S(1)} %pad_maximum_fusion.2.t_ref, ...), custom_call_target="tpu_custom_call" | custom-call | flops 2000000000 | bytes 4000000 | tf_op jit(solution)/shard_map/second_layer/pallas_call | solution.py:318
  97.9 3.1 %second_layer.6 = (f32[8,768]{1,0:T(8,128)S(1)}, f32[48,256]{1,0:T(8,128)S(1)}, f32[48,256]{1,0:T(8,128)S(1)}) custom-call(s32[5]{0:T(128)S(1)} %stack.89.where_ref, bf16[768,256]{1,0:T(8,128)(2,1)S(1)} %copy-done.8, bf16[256,1024]{1,0:T(8,128)(2,1)S(1)} %copy-done.4, bf16[4,256,256]{2,1,0:T(8,128)(2,1)S(1)} %pad_maximum_fusion.2.t_ref, ...), custom_call_target="tpu_custom_call" | custom-call | flops 2000000000 | bytes 4000000 | tf_op jit(solution)/shard_map/second_layer/pallas_call | solution.py:318
  102.5 3.1 %second_layer.7 = (f32[8,768]{1,0:T(8,128)S(1)}, f32[48,256]{1,0:T(8,128)S(1)}, f32[48,256]{1,0:T(8,128)S(1)}) custom-call(s32[5]{0:T(128)S(1)} %stack.89.where_ref, bf16[768,256]{1,0:T(8,128)(2,1)S(1)} %copy-done.8, bf16[256,1024]{1,0:T(8,128)(2,1)S(1)} %copy-done.4, bf16[4,256,256]{2,1,0:T(8,128)(2,1)S(1)} %pad_maximum_fusion.2.t_ref, ...), custom_call_target="tpu_custom_call" | custom-call | flops 2000000000 | bytes 4000000 | tf_op jit(solution)/shard_map/second_layer/pallas_call | solution.py:318
  105.6 3.3 %collective-permute-start.23 = (f32[8,768]{1,0:T(8,128)S(1)}, f32[8,768]{1,0:T(8,128)S(1)}, u32[]{:S(2)}, u32[]{:S(2)}) collective-permute-start(f32[8,768]{1,0:T(8,128)S(1)} %get-tuple-element.64), channel_id=1, source_target_pairs={{0,1},{1,0},{2,3},{3,2},{4,5},{5,4},{6,7},{7,6},{8,9},{9,8},{10,11... | collective-permute-start | bytes 73736 | tf_op jit(solution)/shard_map/ppermute | solution.py:27
  110.5 2.8 %collective-permute-start.31 = (bf16[4,2,4,96,128]{4,3,2,1,0:T(8,128)(2,1)S(1)}, bf16[4,2,4,96,128]{4,3,2,1,0:T(8,128)(2,1)}, u32[]{:S(2)}, u32[]{:S(2)}) collective-permute-start(bf16[4,2,4,96,128]{4,3,2,1,0:T(8,128)(2,1)S(1)} %pad_maximum_fusion.refs_0_), channel_id=1, source_target_pairs={{0,64},{32,96},{64,0},{96,32},{1,65},{33,97},{65,1},{97,33},{2,66}... | collective-permute-start | bytes 2359304 | tf_op jit(solution)/shard_map/ppermute | solution.py:32
  117.5 3.9 %all-to-all-start = ((bf16[32,56,128]{2,1,0:T(8,128)(2,1)}), bf16[32,56,128]{2,1,0:T(8,128)(2,1)S(1)}, u32[]{:S(2)}, u32[]{:S(2)}) async-start(bf16[32,56,128]{2,1,0:T(8,128)(2,1)} %pad_maximum_fusion.3), calls=%async_computation | async-start | bytes 917504 | tf_op jit(solution)/shard_map/all_to_all | solution.py:487
  123.5 29.1 %all-to-all-done = bf16[32,56,128]{2,1,0:T(8,128)(2,1)S(1)} async-done(((bf16[32,56,128]{2,1,0:T(8,128)(2,1)}), bf16[32,56,128]{2,1,0:T(8,128)(2,1)S(1)}, u32[]{:S(2)}, u32[]{:S(2)}) %all-to-all-start) | async-done | bytes 458784 | tf_op jit(solution)/shard_map/all_to_all | solution.py:487
  160.5 15.6 %collective-permute-done.37.refs_6_ = bf16[4,2,4,96,128]{4,3,2,1,0:T(8,128)(2,1)S(1)} collective-permute-done((bf16[4,2,4,96,128]{4,3,2,1,0:T(8,128)(2,1)S(1)}, bf16[4,2,4,96,128]{4,3,2,1,0:T(8,128)(2,1)S(1)}, u32[]{:S(2)}, u32[]{:S(2)}) %collective-permute-start.37) | collective-permute-done | bytes 786464 | tf_op jit(solution)/shard_map/ppermute | solution.py:32
  176.1 16.2 %collective-permute-done.38.refs_7_ = bf16[4,2,4,96,128]{4,3,2,1,0:T(8,128)(2,1)} collective-permute-done((bf16[4,2,4,96,128]{4,3,2,1,0:T(8,128)(2,1)S(1)}, bf16[4,2,4,96,128]{4,3,2,1,0:T(8,128)(2,1)}, u32[]{:S(2)}, u32[]{:S(2)}) %collective-permute-start.38) | collective-permute-done | bytes 786464 | tf_op jit(solution)/shard_map/ppermute | solution.py:32
  192.3 8.1 %weight_step.1 = f32[2,1024,128]{2,1,0:T(8,128)} custom-call(s32[5]{0:T(128)} %copy-done.11, bf16[32,96,128]{2,1,0:T(8,128)(2,1)} %multiply_convert_fusion.outs_ref, bf16[4,2,4,96,128]{4,3,2,1,0:T(8,128)(2,1)} %copy-done.18, bf16[4,2,4,96,128]{4,3,2,1,0:T(8,128)(2,1)} %collective-permute-done.30.refs_1_, ...), custom_call_target="tpu_custom_call" | custom-call | flops 2000000000 | bytes 8000000 | tf_op jit(solution)/shard_map/weight_step/pallas_call | solution.py:382
  (198 shorter events, 63.4 us)
Async XLA Ops:
  9.6 23.2 %collective-permute-start.8 = (f32[8,768]{1,0:T(8,128)S(1)}, f32[8,768]{1,0:T(8,128)S(1)}, u32[]{:S(2)}, u32[]{:S(2)}) collective-permute-start(f32[8,768]{1,0:T(8,128)S(1)} %add.94.l0), channel_id=1, source_target_pairs={{0,2},{2,0},{1,3},{3,1},{4,6},{6,4},{5,7},{7,5},{8,10},{10,8},{9,1... | collective-permute-start | bytes 73736 | tf_op jit(solution)/shard_map/ppermute | solution.py:27
  16.9 13.3 %collective-permute-start.1 = (bf16[2,256,256]{2,1,0:T(8,128)(2,1)S(1)}, bf16[2,256,256]{2,1,0:T(8,128)(2,1)S(1)}, u32[]{:S(2)}, u32[]{:S(2)}) collective-permute-start(bf16[2,256,256]{2,1,0:T(8,128)(2,1)S(1)} %get-tuple-element.40), channel_id=1, source_target_pairs={{0,1},{1,0},{2,3},{3,2},{4,5},{5,4},{6,7},{7,6},{8,9},{9,8},{10,11... | collective-permute-start | bytes 786440 | tf_op jit(solution)/shard_map/ppermute | solution.py:27
  19.8 13.4 %collective-permute-start.9 = (bf16[256,256]{1,0:T(8,128)(2,1)S(1)}, bf16[256,256]{1,0:T(8,128)(2,1)S(1)}, u32[]{:S(2)}, u32[]{:S(2)}) collective-permute-start(bf16[256,256]{1,0:T(8,128)(2,1)S(1)} %fusion.2.t0), channel_id=1, source_target_pairs={{0,4},{4,8},{8,12},{12,0},{1,5},{5,9},{9,13},{13,1},{2,6},{6,10},{... | collective-permute-start | bytes 393224 | tf_op jit(solution)/shard_map/ppermute | solution.py:32
  30.2 32.0 %collective-permute-start.17 = (bf16[1024,1024]{1,0:T(8,128)(2,1)}, bf16[1024,1024]{1,0:T(8,128)(2,1)S(1)}, u32[]{:S(2)}, u32[]{:S(2)}) collective-permute-start(bf16[1024,1024]{1,0:T(8,128)(2,1)} %get-tuple-element.79), channel_id=1, source_target_pairs={{0,1},{1,0},{2,3},{3,2},{4,5},{5,4},{6,7},{7,6},{8,9},{9,8},{10,11... | collective-permute-start | bytes 6291464 | tf_op jit(solution)/shard_map/ppermute | solution.py:27
  32.8 13.4 %collective-permute-start.26 = (bf16[8,96,128]{2,1,0:T(8,128)(2,1)S(1)}, bf16[8,96,128]{2,1,0:T(8,128)(2,1)S(1)}, u32[]{:S(2)}, u32[]{:S(2)}) collective-permute-start(bf16[8,96,128]{2,1,0:T(8,128)(2,1)S(1)} %regroup_in.1.a_ref), channel_id=1, source_target_pairs={{0,16},{16,0},{1,17},{17,1},{2,18},{18,2},{3,19},{19,3},{4,20},{20... | collective-permute-start | bytes 589832 | tf_op jit(solution)/shard_map/ppermute | solution.py:27
  33.2 42.6 %collective-permute-start.18 = (bf16[1024,1024]{1,0:T(8,128)(2,1)}, bf16[1024,1024]{1,0:T(8,128)(2,1)}, u32[]{:S(2)}, u32[]{:S(2)}) collective-permute-start(bf16[1024,1024]{1,0:T(8,128)(2,1)} %get-tuple-element.78), channel_id=1, source_target_pairs={{0,1},{1,0},{2,3},{3,2},{4,5},{5,4},{6,7},{7,6},{8,9},{9,8},{10,11... | collective-permute-start | bytes 6291464 | tf_op jit(solution)/shard_map/ppermute | solution.py:27
  60.6 40.4 %collective-permute-start.29 = (bf16[2,4,96,128]{3,2,1,0:T(8,128)(2,1)S(1)}, bf16[2,4,96,128]{3,2,1,0:T(8,128)(2,1)S(1)}, u32[]{:S(2)}, u32[]{:S(2)}) collective-permute-start(bf16[2,4,96,128]{3,2,1,0:T(8,128)(2,1)S(1)} %get-tuple-element.83), channel_id=1, source_target_pairs={{0,12},{4,0},{8,4},{12,8},{1,13},{5,1},{9,5},{13,9},{2,14},{6,2},{... | collective-permute-start | bytes 589832 | tf_op jit(solution)/shard_map/ppermute | solution.py:32
  60.7 24.2 %collective-permute-start.13 = (f32[8,768]{1,0:T(8,128)S(1)}, f32[8,768]{1,0:T(8,128)S(1)}, u32[]{:S(2)}, u32[]{:S(2)}) collective-permute-start(f32[8,768]{1,0:T(8,128)S(1)} %add.97.s0), channel_id=1, source_target_pairs={{0,2},{2,0},{1,3},{3,1},{4,6},{6,4},{5,7},{7,5},{8,10},{10,8},{9,1... | collective-permute-start | bytes 73736 | tf_op jit(solution)/shard_map/ppermute | solution.py:27
  64.8 22.4 %collective-permute-start.19 = (bf16[768,256]{1,0:T(8,128)(2,1)S(1)}, bf16[768,256]{1,0:T(8,128)(2,1)S(1)}, u32[]{:S(2)}, u32[]{:S(2)}) collective-permute-start(bf16[768,256]{1,0:T(8,128)(2,1)S(1)} %product.7), channel_id=1, source_target_pairs={{0,2},{2,0},{1,3},{3,1},{4,6},{6,4},{5,7},{7,5},{8,10},{10,8},{9,1... | collective-permute-start | bytes 1179656 | tf_op jit(solution)/shard_map/ppermute | solution.py:27
  71.8 25.8 %collective-permute-start.21 = (bf16[768,256]{1,0:T(8,128)(2,1)S(1)}, bf16[768,256]{1,0:T(8,128)(2,1)S(1)}, u32[]{:S(2)}, u32[]{:S(2)}) collective-permute-start(bf16[768,256]{1,0:T(8,128)(2,1)S(1)} %product.9), channel_id=1, source_target_pairs={{0,2},{2,0},{1,3},{3,1},{4,6},{6,4},{5,7},{7,5},{8,10},{10,8},{9,1... | collective-permute-start | bytes 1179656 | tf_op jit(solution)/shard_map/ppermute | solution.py:27
  75.8 17.8 %collective-permute-start.20 = (bf16[768,256]{1,0:T(8,128)(2,1)S(1)}, bf16[768,256]{1,0:T(8,128)(2,1)S(1)}, u32[]{:S(2)}, u32[]{:S(2)}) collective-permute-start(bf16[768,256]{1,0:T(8,128)(2,1)S(1)} %product.8), channel_id=1, source_target_pairs={{0,2},{2,0},{1,3},{3,1},{4,6},{6,4},{5,7},{7,5},{8,10},{10,8},{9,1... | collective-permute-start | bytes 1179656 | tf_op jit(solution)/shard_map/ppermute | solution.py:27
  84.9 20.7 %collective-permute-start.28 = (bf16[2,4,96,128]{3,2,1,0:T(8,128)(2,1)S(1)}, bf16[2,4,96,128]{3,2,1,0:T(8,128)(2,1)S(1)}, u32[]{:S(2)}, u32[]{:S(2)}) collective-permute-start(bf16[2,4,96,128]{3,2,1,0:T(8,128)(2,1)S(1)} %get-tuple-element.83), channel_id=1, source_target_pairs={{0,8},{4,12},{8,0},{12,4},{1,9},{5,13},{9,1},{13,5},{2,10},{6,14},... | collective-permute-start | bytes 589832 | tf_op jit(solution)/shard_map/ppermute | solution.py:32
  87.2 14.9 %collective-permute-start.22 = (bf16[768,256]{1,0:T(8,128)(2,1)S(1)}, bf16[768,256]{1,0:T(8,128)(2,1)S(1)}, u32[]{:S(2)}, u32[]{:S(2)}) collective-permute-start(bf16[768,256]{1,0:T(8,128)(2,1)S(1)} %product.5), channel_id=1, source_target_pairs={{0,2},{2,0},{1,3},{3,1},{4,6},{6,4},{5,7},{7,5},{8,10},{10,8},{9,1... | collective-permute-start | bytes 1179656 | tf_op jit(solution)/shard_map/ppermute | solution.py:27
  93.6 15.3 %collective-permute-start.27 = (bf16[2,4,96,128]{3,2,1,0:T(8,128)(2,1)S(1)}, bf16[2,4,96,128]{3,2,1,0:T(8,128)(2,1)S(1)}, u32[]{:S(2)}, u32[]{:S(2)}) collective-permute-start(bf16[2,4,96,128]{3,2,1,0:T(8,128)(2,1)S(1)} %get-tuple-element.83), channel_id=1, source_target_pairs={{0,4},{4,8},{8,12},{12,0},{1,5},{5,9},{9,13},{13,1},{2,6},{6,10},{... | collective-permute-start | bytes 589832 | tf_op jit(solution)/shard_map/ppermute | solution.py:32
  97.6 15.7 %collective-permute-start.35 = (bf16[2,4,96,128]{3,2,1,0:T(8,128)(2,1)S(1)}, bf16[2,4,96,128]{3,2,1,0:T(8,128)(2,1)S(1)}, u32[]{:S(2)}, u32[]{:S(2)}) collective-permute-start(bf16[2,4,96,128]{3,2,1,0:T(8,128)(2,1)S(1)} %get-tuple-element.82), channel_id=1, source_target_pairs={{0,96},{32,0},{64,32},{96,64},{1,97},{33,1},{65,33},{97,65},{2,98}... | collective-permute-start | bytes 589832 | tf_op jit(solution)/shard_map/ppermute | solution.py:32
  101.0 13.8 %collective-permute-start.34 = (bf16[2,4,96,128]{3,2,1,0:T(8,128)(2,1)S(1)}, bf16[2,4,96,128]{3,2,1,0:T(8,128)(2,1)S(1)}, u32[]{:S(2)}, u32[]{:S(2)}) collective-permute-start(bf16[2,4,96,128]{3,2,1,0:T(8,128)(2,1)S(1)} %get-tuple-element.82), channel_id=1, source_target_pairs={{0,64},{32,96},{64,0},{96,32},{1,65},{33,97},{65,1},{97,33},{2,66}... | collective-permute-start | bytes 589832 | tf_op jit(solution)/shard_map/ppermute | solution.py:32
  102.1 14.5 %collective-permute-start.33 = (bf16[2,4,96,128]{3,2,1,0:T(8,128)(2,1)S(1)}, bf16[2,4,96,128]{3,2,1,0:T(8,128)(2,1)S(1)}, u32[]{:S(2)}, u32[]{:S(2)}) collective-permute-start(bf16[2,4,96,128]{3,2,1,0:T(8,128)(2,1)S(1)} %get-tuple-element.82), channel_id=1, source_target_pairs={{0,32},{32,64},{64,96},{96,0},{1,33},{33,65},{65,97},{97,1},{2,34}... | collective-permute-start | bytes 589832 | tf_op jit(solution)/shard_map/ppermute | solution.py:32
  109.0 46.3 %collective-permute-start.30 = (bf16[4,2,4,96,128]{4,3,2,1,0:T(8,128)(2,1)S(1)}, bf16[4,2,4,96,128]{4,3,2,1,0:T(8,128)(2,1)}, u32[]{:S(2)}, u32[]{:S(2)}) collective-permute-start(bf16[4,2,4,96,128]{4,3,2,1,0:T(8,128)(2,1)S(1)} %pad_maximum_fusion.refs_0_), channel_id=1, source_target_pairs={{0,32},{32,64},{64,96},{96,0},{1,33},{33,65},{65,97},{97,1},{2,34}... | collective-permute-start | bytes 2359304 | tf_op jit(solution)/shard_map/ppermute | solution.py:32
  110.5 49.9 %collective-permute-start.31 = (bf16[4,2,4,96,128]{4,3,2,1,0:T(8,128)(2,1)S(1)}, bf16[4,2,4,96,128]{4,3,2,1,0:T(8,128)(2,1)}, u32[]{:S(2)}, u32[]{:S(2)}) collective-permute-start(bf16[4,2,4,96,128]{4,3,2,1,0:T(8,128)(2,1)S(1)} %pad_maximum_fusion.refs_0_), channel_id=1, source_target_pairs={{0,64},{32,96},{64,0},{96,32},{1,65},{33,97},{65,1},{97,33},{2,66}... | collective-permute-start | bytes 2359304 | tf_op jit(solution)/shard_map/ppermute | solution.py:32
  113.3 47.1 %collective-permute-start.32 = (bf16[4,2,4,96,128]{4,3,2,1,0:T(8,128)(2,1)S(1)}, bf16[4,2,4,96,128]{4,3,2,1,0:T(8,128)(2,1)}, u32[]{:S(2)}, u32[]{:S(2)}) collective-permute-start(bf16[4,2,4,96,128]{4,3,2,1,0:T(8,128)(2,1)S(1)} %pad_maximum_fusion.refs_0_), channel_id=1, source_target_pairs={{0,96},{32,0},{64,32},{96,64},{1,97},{33,1},{65,33},{97,65},{2,98}... | collective-permute-start | bytes 2359304 | tf_op jit(solution)/shard_map/ppermute | solution.py:32
  116.7 43.8 %collective-permute-start.36 = (bf16[4,2,4,96,128]{4,3,2,1,0:T(8,128)(2,1)S(1)}, bf16[4,2,4,96,128]{4,3,2,1,0:T(8,128)(2,1)}, u32[]{:S(2)}, u32[]{:S(2)}) collective-permute-start(bf16[4,2,4,96,128]{4,3,2,1,0:T(8,128)(2,1)S(1)} %pad_maximum_fusion.1.refs_4_), channel_id=1, source_target_pairs={{0,4},{4,8},{8,12},{12,0},{1,5},{5,9},{9,13},{13,1},{2,6},{6,10},{... | collective-permute-start | bytes 2359304 | tf_op jit(solution)/shard_map/ppermute | solution.py:32
  117.5 35.1 %all-to-all-start = ((bf16[32,56,128]{2,1,0:T(8,128)(2,1)}), bf16[32,56,128]{2,1,0:T(8,128)(2,1)S(1)}, u32[]{:S(2)}, u32[]{:S(2)}) async-start(bf16[32,56,128]{2,1,0:T(8,128)(2,1)} %pad_maximum_fusion.3), calls=%async_computation | async-start | bytes 917504 | tf_op jit(solution)/shard_map/all_to_all | solution.py:487
  155.4 20.7 %collective-permute-start.37 = (bf16[4,2,4,96,128]{4,3,2,1,0:T(8,128)(2,1)S(1)}, bf16[4,2,4,96,128]{4,3,2,1,0:T(8,128)(2,1)S(1)}, u32[]{:S(2)}, u32[]{:S(2)}) collective-permute-start(bf16[4,2,4,96,128]{4,3,2,1,0:T(8,128)(2,1)S(1)} %pad_maximum_fusion.1.refs_4_), channel_id=1, source_target_pairs={{0,8},{4,12},{8,0},{12,4},{1,9},{5,13},{9,1},{13,5},{2,10},{6,14},... | collective-permute-start | bytes 2359304 | tf_op jit(solution)/shard_map/ppermute | solution.py:32
  156.9 35.4 %collective-permute-start.38 = (bf16[4,2,4,96,128]{4,3,2,1,0:T(8,128)(2,1)S(1)}, bf16[4,2,4,96,128]{4,3,2,1,0:T(8,128)(2,1)}, u32[]{:S(2)}, u32[]{:S(2)}) collective-permute-start(bf16[4,2,4,96,128]{4,3,2,1,0:T(8,128)(2,1)S(1)} %pad_maximum_fusion.1.refs_4_), channel_id=1, source_target_pairs={{0,12},{4,0},{8,4},{12,8},{1,13},{5,1},{9,5},{13,9},{2,14},{6,2},{... | collective-permute-start | bytes 2359304 | tf_op jit(solution)/shard_map/ppermute | solution.py:32
  (48 other events, 557.6 us)

commit v2 on v1

v2 whole, which is shorter than its diff:
```python
import jax
import jax.numpy as jnp
from jax import lax
from jax.experimental import pallas as pl
from jax.experimental.pallas import tpu as pltpu
from jax.sharding import Mesh
from jax.sharding import PartitionSpec as P

noise_scale = 0.25
norm_eps = 1e-06
spread_eps = 1e-05

POP = ("y", "xl", "z")
MP = ("xh", "c")
CHUNKS = 3
f32 = jnp.float32
bf16 = jnp.bfloat16
SMEM = pl.BlockSpec(memory_space=pltpu.SMEM)
VMEM = pl.BlockSpec(memory_space=pltpu.VMEM)
small_cost = pl.CostEstimate(flops=1000, bytes_accessed=1000, transcendentals=0)


def params(mib=24):
    return pltpu.CompilerParams(vmem_limit_bytes=mib * 1024 * 1024)


def swap(value, axis):
    return lax.ppermute(value, axis, [(0, 1), (1, 0)])


def after(value, *earlier):
    return lax.optimization_barrier((value, *earlier))[0]


def mp_parts(value):
    pair = value + swap(value, "c")
    return pair, swap(pair, "xh")


def dot(a, b, ca, cb, precision=None):
    return lax.dot_general(
        a, b, (((ca,), (cb,)), ((), ())), preferred_element_type=f32, precision=precision
    )


def regroup(factors, first, second):
    layers, members, ranks, width = factors.shape
    blocks = width // 128

    def kernel(in_ref, out_ref):
        for m in range(members):
            rows = jnp.concatenate(
                [in_ref[l, m].astype(f32) for l in range(layers)], axis=0
            ).astype(bf16)
            lo = m * layers * ranks
            for b in range(blocks):
                out_ref[b, lo : lo + layers * ranks, :] = rows[:, b * 128 : (b + 1) * 128]

    return pl.pallas_call(
        kernel,
        out_shape=jax.ShapeDtypeStruct((blocks, members * layers * ranks, 128), bf16),
        in_specs=[VMEM],
        out_specs=VMEM,
        compiler_params=params(),
        name=first,
        cost_estimate=small_cost,
    )(factors)


def product(layer, rel, flip, where, lefts, weights, first=0, count=4):
    rows, width = lefts[0].shape
    total = rows * len(lefts)
    flips = len(flip)

    def kernel(where_ref, w_ref, *refs):
        left_refs = refs[: len(lefts)]
        out_refs = refs[len(lefts) : len(lefts) + flips]
        block, sems = refs[len(lefts) + flips :]

        def fetch(n, f):
            owner = (where_ref[1] ^ rel) * 2 + (where_ref[2] ^ flip[f])
            at = pl.multiple_of(owner * width + (first + n) * 256, 256)
            return pltpu.make_async_copy(
                w_ref.at[layer, :, pl.ds(at, 256)], block.at[n * flips + f], sems.at[n * flips + f]
            )

        for n in range(count):
            for f in range(flips):
                fetch(n, f).start()

        def one(n, carry):
            for f in range(flips):
                fetch(n, f).wait()
                w = block[n * flips + f]
                for k, left in enumerate(left_refs):
                    out_refs[f][n, k * rows : (k + 1) * rows, :] = jnp.dot(
                        left[...], w, preferred_element_type=f32
                    ).astype(bf16)
            return carry

        lax.fori_loop(0, count, one, 0)

    return pl.pallas_call(
        kernel,
        out_shape=[jax.ShapeDtypeStruct((count, total, 256), bf16)] * len(flip),
        in_specs=[SMEM, pl.BlockSpec(memory_space=pltpu.HBM)] + [VMEM] * len(lefts),
        out_specs=[VMEM] * len(flip),
        scratch_shapes=[
            pltpu.VMEM((count * flips, width, 256), bf16),
            pltpu.SemaphoreType.DMA((count * flips,)),
        ],
        compiler_params=params(16),
        name="product",
        cost_estimate=small_cost,
    )(where, weights, *lefts)


def member_of(shape, per, dim):
    return lax.broadcasted_iota(jnp.int32, shape, dim) // per


def low_kernel(onehot, embedding, factors):
    rows = onehot.shape[0]
    per_chunk = rows // CHUNKS
    group = factors.shape[1] // CHUNKS

    def kernel(o_ref, e_ref, a_ref, out_ref):
        for k in range(CHUNKS):
            x = jnp.dot(
                o_ref[k * per_chunk : (k + 1) * per_chunk, :], e_ref[...], preferred_element_type=f32
            ).astype(bf16)
            total = jnp.zeros((group, per_chunk), f32)
            for b in range(factors.shape[0]):
                total += dot(
                    a_ref[b, k * group : (k + 1) * group, :], x[:, b * 128 : (b + 1) * 128], 1, 1
                )
            out_ref[:, k * per_chunk : (k + 1) * per_chunk] = diagonal(total)

    return pl.pallas_call(
        kernel,
        out_shape=jax.ShapeDtypeStruct((8, rows), f32),
        in_specs=[VMEM] * 3,
        out_specs=VMEM,
        compiler_params=params(),
        name="low",
        cost_estimate=small_cost,
    )(onehot, embedding, factors)


def diagonal(total):
    group, cols = total.shape
    row_member = member_of((group, cols), 8, 0)
    col_member = (lax.broadcasted_iota(jnp.int32, (group, cols), 1) % 16) // 4
    kept = jnp.where(row_member == col_member, total, 0.0)
    out = kept[0:8]
    for m in range(1, group // 8):
        out = out + kept[m * 8 : (m + 1) * 8]
    return out


def spread(low, layer, group):
    cols = low.shape[1]
    row = lax.broadcasted_iota(jnp.int32, (group, cols), 0)
    col_member = (lax.broadcasted_iota(jnp.int32, (group, cols), 1) % 16) // 4
    keep = (row // 8 == col_member) & ((row % 8) // 4 == layer)
    tiled = jnp.concatenate([low] * (group // 8), axis=0)
    return jnp.where(keep, tiled, 0.0).astype(bf16)


def first_layer(chunk, where, coef, onehot, table_parts, lows, out_factors, in_factors, decay, gain):
    rows = onehot.shape[0] // CHUNKS
    group = out_factors.shape[1] // CHUNKS
    width = decay.shape[1]
    steps = 16
    per = rows // steps

    def kernel(o_ref, t0, t1, t2, l0, l1, b_ref, a_ref, d_ref, g_ref, lifted_ref, stats_ref, square):
        at = slice(chunk * rows, (chunk + 1) * rows)
        mine = slice(chunk * group, (chunk + 1) * group)
        low = (l0[:, at] + l1[:, at]) * coef
        spread_low = spread(low, 0, group)
        total = jnp.zeros((group, rows), f32)
        for n in range(width // 256):
            cols = slice(n * 256, (n + 1) * 256)
            table = (t0[n].astype(f32) + t1[n].astype(f32) + t2[n].astype(f32)).astype(bf16)
            factor = jnp.concatenate([b_ref[2 * n, mine], b_ref[2 * n + 1, mine]], axis=1)
            u = jnp.dot(o_ref[at], table, preferred_element_type=f32) + dot(
                spread_low, factor, 0, 0
            )
            d = d_ref[:, cols]
            g = g_ref[:, cols]
            rest = 1.0 - d
            h = jnp.zeros((per, 256), f32)
            for t in range(steps):
                span = slice(t * per, (t + 1) * per)
                h = d * h + rest * u[span]
                lifted_ref[span, cols] = (h * g).astype(bf16)
                hh = h * h
                hh = hh[:, :128] + hh[:, 128:]
                if n == 0:
                    square[span] = hh
                else:
                    square[span] += hh
            factor_in = jnp.concatenate([a_ref[2 * n, mine], a_ref[2 * n + 1, mine]], axis=1)
            total += dot(factor_in, lifted_ref[:, cols], 1, 1)
        sums = dot(jnp.ones((8, 128), f32), square[...], 1, 1, lax.Precision.HIGHEST)
        low_next = diagonal(total)
        row = lax.broadcasted_iota(jnp.int32, (8, rows), 0)
        stats_ref[...] = jnp.where(row < 4, sums, low_next)

    return pl.pallas_call(
        kernel,
        out_shape=[
            jax.ShapeDtypeStruct((rows, width), bf16),
            jax.ShapeDtypeStruct((8, rows), f32),
        ],
        in_specs=[VMEM] * 10,
        out_specs=[VMEM, VMEM],
        scratch_shapes=[pltpu.VMEM((rows, 128), f32)],
        compiler_params=params(16),
        name="first_layer",
        cost_estimate=small_cost,
    )(onehot, *table_parts, *lows, out_factors, in_factors, decay, gain)


def next_hidden(full_width, onehot, embedding, stats, lifted):
    rows = lifted[0].shape[0]
    total, width = rows * CHUNKS, embedding.shape[1]

    def kernel(o_ref, e_ref, s0, s1, up0, up1, up2, out_ref):
        for k, up in enumerate((up0, up1, up2)):
            span = slice(k * rows, (k + 1) * rows)
            so_far = s0[:, span] + s1[:, span]
            norm = lax.rsqrt(so_far / full_width + norm_eps)
            norm_col = jnp.transpose(norm)[:, 0:1]
            x = jnp.dot(o_ref[span], e_ref[...], preferred_element_type=f32)
            out_ref[span] = (x + norm_col * up[...].astype(f32)).astype(bf16)

    return pl.pallas_call(
        kernel,
        out_shape=jax.ShapeDtypeStruct((total, width), bf16),
        in_specs=[VMEM] * 7,
        out_specs=VMEM,
        compiler_params=params(16),
        name="next_hidden",
        cost_estimate=small_cost,
    )(onehot, embedding, *stats, *lifted)


def second_layer(n, coef, full_width, hidden, lows, stats, halves, crossed, out_factors,
                 decay, gain, reward, before):
    rows = hidden.shape[0] // CHUNKS
    group = out_factors.shape[1] // CHUNKS
    steps = 16
    per = rows // steps
    cols = slice(n * 256, (n + 1) * 256)

    def kernel(x_ref, l0, l1, s0, s1, own_ref, peer_ref, other_ref, b_ref, d_ref, g_ref, r_ref,
               before_ref, stats_ref, last_ref, square, lr, xr):
        factor = jnp.concatenate([b_ref[2 * n], b_ref[2 * n + 1]], axis=1)
        d = d_ref[:, cols]
        g = g_ref[:, cols]
        r = r_ref[:, cols]
        rest = 1.0 - d
        gr = g * r
        for k in range(CHUNKS):
            span_k = slice(k * rows, (k + 1) * rows)
            so_far = s0[:, span_k] + s1[:, span_k]
            norm = lax.rsqrt(so_far[0:1] / full_width + norm_eps)
            low = (l0[:, span_k] + l1[:, span_k] + norm * so_far) * coef
            spread_low = spread(low, 1, group)
            u = dot(spread_low, factor[k * group : (k + 1) * group], 0, 0) + (
                own_ref[n, span_k].astype(f32)
                + peer_ref[n, span_k].astype(f32)
                + other_ref[0, span_k].astype(f32)
            )
            h = jnp.zeros((per, 256), f32)
            xrr = x_ref[span_k, cols].astype(f32) * r
            xr[span_k] = xrr[:, :128] + xrr[:, 128:]
            for t in range(steps):
                span = slice(k * rows + t * per, k * rows + (t + 1) * per)
                h = d * h + rest * u[t * per : (t + 1) * per]
                hr = h * gr
                hh = h * h
                square[span] = hh[:, :128] + hh[:, 128:]
                lr[span] = hr[:, :128] + hr[:, 128:]
            last_ref[k * per : (k + 1) * per] = h * g
        ones = jnp.ones((8, 128), f32)
        sums = [dot(ones, a[...], 1, 1, lax.Precision.HIGHEST) for a in (square, lr, xr)]
        row = lax.broadcasted_iota(jnp.int32, (8, rows * CHUNKS), 0)
        stats_ref[...] = before_ref[...] + jnp.where(
            row == 0, sums[0], jnp.where(row == 1, sums[1], sums[2])
        )

    total = rows * CHUNKS
    return pl.pallas_call(
        kernel,
        out_shape=[
            jax.ShapeDtypeStruct((8, total), f32),
            jax.ShapeDtypeStruct((per * CHUNKS, 256), f32),
        ],
        in_specs=[VMEM] * 13,
        out_specs=[VMEM] * 2,
        scratch_shapes=[pltpu.VMEM((total, 128), f32)] * 3,
        compiler_params=params(16),
        name="second_layer",
        cost_estimate=small_cost,
    )(hidden, *lows, *stats, *halves, crossed, out_factors, decay, gain, reward, before)


def step_kernel(where, ins, outs):
    pops, blocks, k, lanes = ins.shape
    width = blocks * lanes

    def kernel(where_ref, ins_ref, outs_ref, mine_ref, theirs_ref, paired):
        xl = where_ref[4]
        layer = (lax.broadcasted_iota(jnp.int32, (k, lanes), 0) % 8) // 4
        for p in range(pops):
            at = slice(p * k, (p + 1) * k)
            for rel in range(2):
                o = outs_ref[p, xl ^ rel]
                zero = jnp.zeros_like(o)
                for l in range(2):
                    lo = (rel * 2 + l) * lanes
                    paired[at, lo : lo + lanes] = jnp.where(layer == l, o, zero)
        right = paired[...]
        for b in range(0, blocks, 2):
            left = jnp.concatenate(
                [
                    jnp.concatenate([ins_ref[p, b], ins_ref[p, b + 1]], axis=1)
                    for p in range(pops)
                ],
                axis=0,
            )
            out = dot(left, right, 0, 0)
            rows = slice(b * lanes, (b + 2) * lanes)
            for l in range(2):
                mine_ref[l, rows, :] = out[:, l * lanes : (l + 1) * lanes]
                theirs_ref[l, rows, :] = out[:, (2 + l) * lanes : (3 + l) * lanes].astype(bf16)

    return pl.pallas_call(
        kernel,
        out_shape=[
            jax.ShapeDtypeStruct((2, width, lanes), f32),
            jax.ShapeDtypeStruct((2, width, lanes), bf16),
        ],
        in_specs=[SMEM, VMEM, VMEM],
        out_specs=[VMEM, VMEM],
        scratch_shapes=[pltpu.VMEM((pops * k, 4 * lanes), bf16)],
        compiler_params=params(24),
        name="weight_step",
        cost_estimate=small_cost,
    )(where, ins, outs)


def shards(
    token_ids,
    fitness_ranks,
    embedding,
    mix_weights,
    factors_in,
    factors_out,
    decay_rates,
    norm_gain,
    reward_dir,
):
    members, seq_count, step_count = token_ids.shape
    vocab, width = embedding.shape
    full_width = mix_weights.shape[2]
    rank_count = factors_in.shape[2]
    pop_count = lax.axis_size(POP)
    members_all = members * pop_count
    coef = noise_scale * (full_width * rank_count) ** (-0.5)
    y, xl, z = (lax.axis_index(a) for a in POP)
    xh, c = (lax.axis_index(a) for a in MP)
    where = jnp.stack([z, xh, c, y, xl]).astype(jnp.int32)
    rows_all = members * seq_count * step_count

    order = token_ids.reshape(CHUNKS, -1, step_count).transpose(0, 2, 1).reshape(-1)
    onehot = (order[:, None] == jnp.arange(vocab, dtype=jnp.int32)[None, :]).astype(bf16)

    a_blocks = regroup(factors_in, "regroup_in", 0)
    ins_all = lax.all_gather(a_blocks, ("y", "z"))

    def added(a, b):
        return (a.astype(f32) + b.astype(f32)).astype(bf16)

    def sums_to_send(layer, lefts, first=0, count=4, dep=()):
        at = after(where, *dep) if dep else where
        peer, own = product(layer, 1, (1, 0), at, lefts, mix_weights, first, count)
        return added(own, swap(peer, "c"))

    def sums_to_keep(layer, lefts, dep):
        peer, own = product(layer, 0, (1, 0), after(where, *dep), lefts, mix_weights)
        return own, swap(peer, "c")

    lows = mp_parts(low_kernel(onehot, embedding, a_blocks))
    cross = sums_to_send(0, [embedding], dep=(lows[0],))
    table_cross = swap(cross, "xh")
    peer, own = product(0, 0, (1, 0), after(where, cross), [embedding], mix_weights)
    keep = jnp.concatenate([swap(peer[:2], "c"), swap(peer[2:], "c")])
    first_table = [own, keep, table_cross]

    b_blocks = regroup(after(factors_out, cross), "regroup_out", 0)
    b_own = lax.dynamic_slice_in_dim(b_blocks, (xh * 2 + c) * 8, 8, 0)

    decay = [decay_rates[l : l + 1] for l in range(2)]
    gain = [norm_gain[l : l + 1] for l in range(2)]
    lifted, stats = [], []
    for k in range(CHUNKS):
        up, st = first_layer(
            k, where, coef, onehot, first_table, lows, b_own, a_blocks, decay[0], gain[0]
        )
        lifted.append(up)
        stats.append(st)
    stats = mp_parts(jnp.concatenate(stats, axis=1))
    hidden = next_hidden(full_width, onehot, embedding, stats, lifted)
    sent, parts = [], []
    for n in range(4):
        part = sums_to_send(1, [hidden], n, 1, parts[n - 2 : n - 1] if n > 1 else ())
        parts.append(part)
        sent.append(swap(part, "xh"))
    halves = sums_to_keep(1, [hidden], (part,))

    half_rows = b_blocks.shape[1] // 2
    my_rows = lax.dynamic_slice_in_dim(b_blocks, c * half_rows, half_rows, 1)
    digits = jnp.stack([fitness_ranks // 32, fitness_ranks % 32]).astype(bf16)
    digits = jnp.pad(digits, ((0, 6), (0, 128 - members)))
    digits = jnp.broadcast_to(digits[None], (pop_count, 8, 128))
    packed = jnp.concatenate([my_rows, digits], axis=1)
    packed = packed.reshape(4, 2, 4, -1, 128).transpose(0, 2, 1, 3, 4).reshape(16, 2, -1, 128)
    arrived = lax.all_to_all(after(packed, part), ("y", "z"), 0, 0, tiled=True)
    mine = arrived[:, :, :half_rows]
    digits_all = arrived[:, 0, half_rows : half_rows + 2, :members].astype(f32)
    ranks_here = digits_all[:, 0] * 32.0 + digits_all[:, 1]
    ranks_there = swap(ranks_here, "xl")
    theirs = swap(mine, "c")
    outs = jnp.where(
        c == 0, jnp.concatenate([mine, theirs], axis=2), jnp.concatenate([theirs, mine], axis=2)
    )
    shares = ranks_here / members_all
    shares_there = ranks_there / members_all
    rank_mean = (jnp.sum(shares) + jnp.sum(shares_there)) / members_all
    spread_sum = jnp.sum((shares - rank_mean) ** 2) + jnp.sum((shares_there - rank_mean) ** 2)
    shaped = (shares - rank_mean) * lax.rsqrt(spread_sum / members_all + spread_eps)
    shaped = shaped * (members_all * rank_count) ** (-0.5)
    shaped_rows = jnp.repeat(shaped, 2 * rank_count, axis=1)
    outs = (outs.astype(f32) * shaped_rows[:, None, :, None]).astype(bf16)
    step_mine, step_theirs = step_kernel(where, ins_all, outs)

    st = jnp.zeros((8, rows_all), f32)
    lasts = []
    for n in range(4):
        st, last = second_layer(
            n, coef, full_width, hidden, lows, stats, halves, sent[n], b_own,
            decay[1], gain[1], reward_dir[None], st,
        )
        lasts.append(last)
    weight_step = step_mine + swap(after(step_theirs, sent[3]), "xl").astype(f32)
    so_far = sum(mp_parts(st))
    norm = lax.rsqrt(so_far[0] / full_width + norm_eps)
    terms = (so_far[2] + norm * so_far[1]).reshape(CHUNKS, step_count, -1)
    tail = norm.reshape(CHUNKS, step_count, -1)[:, -1].reshape(-1)
    last_hidden = hidden.reshape(CHUNKS, step_count, -1, width)[:, -1].reshape(-1, width)
    finals = last_hidden.astype(f32) + jnp.concatenate(lasts, axis=1) * tail[:, None]
    final_features = finals.astype(bf16).reshape(members, seq_count, width)
    scores = jnp.mean(terms, axis=1).reshape(members, seq_count) * full_width ** (-0.5)
    return (final_features, scores, weight_step)


def solution(mesh):
    fine = Mesh(mesh.devices.reshape(4, 2, 4, 2, 2), POP + MP)
    return jax.shard_map(
        shards,
        mesh=fine,
        in_specs=(
            P(POP, None, None),
            P(POP),
            P(None, MP),
            P(None, MP, None),
            P(None, POP, None, MP),
            P(None, POP, None, None),
            P(None, MP),
            P(None, MP),
            P(MP),
        ),
        out_specs=(P(POP, None, MP), P(POP, None), P(None, MP, POP)),
        check_vma=False,
    )
```

time: 202 us -> 190 us (0.941)
  starting transfers between devices: 59.4 us -> 31.8 us
  waiting for transfers between devices: 66.8 us -> 41.2 us
  local copies, waits for them, and re-layouts: 12.1 us -> 29.9 us
  between operations: 2.63 us -> 17.1 us
  other arithmetic: 9.28 us -> 13.9 us
  Pallas kernels: 50.2 us -> 54.2 us
    ppermute x21 -> x22, waiting for transfers between devices: 5.54 us -> 41.2 us  [swap(): return lax.ppermute(value, axis, [(0, 1), (1, 0)])]
    ppermute x18 -> x0, waiting for transfers between devices: 32.2 us -> none  [shift(): return lax.ppermute(value, axis, [(i, (i + by) % n) for i in range(n)])]
    all_to_all x1, waiting for transfers between devices: 29.1 us -> 0.01 us  [shards(): arrived = lax.all_to_all(after(packed, part), ('y', 'z'), 0, 0, tiled=True)]
    ppermute x18 -> x0, starting transfers between devices: 22.7 us -> none  [shift(): return lax.ppermute(value, axis, [(i, (i + by) % n) for i in range(n)])]
    unnamed x68 -> x47, local copies, waits for them, and re-layouts: 4.72 us -> 22.6 us
    ppermute x21 -> x22, starting transfers between devices: 32.8 us -> 23.8 us  [swap(): return lax.ppermute(value, axis, [(0, 1), (1, 0)])]
    convert_element_type x4 -> x8, other arithmetic: 2.05 us -> 8.59 us  [the longest x5 5.45 us: added(): return (a.astype(f32) + b.astype(f32)).astype(bf16)]
    squeeze x1 -> x0, local copies, waits for them, and re-layouts: 4.64 us -> none  [shards(): lax.dynamic_slice(late_weights, (1, 0, ((xh ^ rel) * 2 + (1 - c)) * width...]
  transfers between devices with their start and end apart: 40 -> 24, of which waited for: 8 -> 11; matrix products, arithmetic and copies ran while one was open for 9% -> 11% of each run, Pallas kernels for 20% -> 27%
where the time goes in v2:
time: 190 us; the launch traced here: 188 us
  Pallas kernels  54.2 us (29%)
  waiting for transfers between devices  41.2 us (22%)
  starting transfers between devices  31.8 us (17%)
  local copies, waits for them, and re-layouts  29.9 us (16%)
  between operations  17.1 us (9%)
  other arithmetic  13.9 us (7%)
    ppermute x22, waiting for transfers between devices, swap(): return lax.ppermute(value, axis, [(0, 1), (1, 0)])  41.2 us
    pallas_call x7, Pallas kernels, product(): pl.pallas_call(kernel, out_shape=[jax.ShapeDtypeStruct((count, total, 256...  29.4 us
    ppermute x22, starting transfers between devices, swap(): return lax.ppermute(value, axis, [(0, 1), (1, 0)])  23.8 us
    unnamed x47, local copies, waits for them, and re-layouts  22.6 us
    pallas_call x4, Pallas kernels, second_layer(): pl.pallas_call(kernel, out_shape=[jax.ShapeDtypeStruct((8, total), f32),...  12.3 us
    all_to_all x1, starting transfers between devices, shards(): arrived = lax.all_to_all(after(packed, part), ('y', 'z'), 0, 0, tiled=True)  7.91 us
    pallas_call x3, Pallas kernels, first_layer(): pl.pallas_call(kernel, out_shape=[jax.ShapeDtypeStruct((rows, width), bf1...  6.37 us
    convert_element_type x5, other arithmetic, added(): return (a.astype(f32) + b.astype(f32)).astype(bf16)  5.45 us
  transfers between devices with their start and end apart: 24, of which 11 were waited for; matrix products, arithmetic and copies ran while one was open for 11% of the time, Pallas kernels for 27%

profile of v2, /device:TPU:1, one launch (start us, length us, event | category | flops | bytes accessed | tf_op | source)
XLA Modules:
  0.0 188.0 jit_solution(17460023706929624806)
XLA Ops:
  15.4 5.8 %copy-done = bf16[2,1024,4096]{2,1,0:T(8,128)(2,1)S(1)} copy-done((bf16[2,1024,4096]{2,1,0:T(8,128)(2,1)S(1)}, bf16[2,1024,4096]{2,1,0:T(8,128)(2,1)}, u32[]{:S(2)}) %copy-start) | copy-done | bytes 16777240
  21.2 4.6 %product.7 = (bf16[4,256,256]{2,1,0:T(8,128)(2,1)S(1)}, bf16[4,256,256]{2,1,0:T(8,128)(2,1)S(1)}) custom-call(s32[5]{0:T(128)S(1)} %stack.35.where_ref, bf16[2,1024,4096]{2,1,0:T(8,128)(2,1)S(1)} %copy-done, bf16[256,1024]{1,0:T(8,128)(2,1)S(1)} %copy-done.4), custom_call_target="tpu_custom_call" | custom-call | flops 1000 | bytes 1000 | tf_op jit(solution)/shard_map/product/pallas_call | solution.py:103
  28.7 2.8 %collective-permute-start.4 = (bf16[4,256,256]{2,1,0:T(8,128)(2,1)}, bf16[4,256,256]{2,1,0:T(8,128)(2,1)S(1)}, u32[]{:S(2)}, u32[]{:S(2)}) collective-permute-start(bf16[4,256,256]{2,1,0:T(8,128)(2,1)} %add_convert_fusion), channel_id=1, source_target_pairs={{0,2},{2,0},{1,3},{3,1},{4,6},{6,4},{5,7},{7,5},{8,10},{10,8},{9,1... | collective-permute-start | bytes 1572872 | tf_op jit(solution)/shard_map/ppermute | solution.py:28
  31.6 4.6 %product.8 = (bf16[4,256,256]{2,1,0:T(8,128)(2,1)S(1)}, bf16[4,256,256]{2,1,0:T(8,128)(2,1)S(1)}) custom-call(s32[5]{0:T(128)S(1)} %stack.35.where_ref, bf16[2,1024,4096]{2,1,0:T(8,128)(2,1)S(1)} %copy-done, bf16[256,1024]{1,0:T(8,128)(2,1)S(1)} %copy-done.4), custom_call_target="tpu_custom_call" | custom-call | flops 1000 | bytes 1000 | tf_op jit(solution)/shard_map/product/pallas_call | solution.py:103
  39.4 4.7 %collective-permute-done.5.l1 = f32[8,768]{1,0:T(8,128)S(1)} collective-permute-done((f32[8,768]{1,0:T(8,128)S(1)}, f32[8,768]{1,0:T(8,128)S(1)}, u32[]{:S(2)}, u32[]{:S(2)}) %collective-permute-start.5) | collective-permute-done | bytes 24608 | tf_op jit(solution)/shard_map/ppermute | solution.py:28
  46.2 2.2 %first_layer.4 = (bf16[256,1024]{1,0:T(8,128)(2,1)S(1)}, f32[8,256]{1,0:T(8,128)S(1)}) custom-call(bf16[768,256]{1,0:T(8,128)(2,1)S(1)} %fusion.o_ref, bf16[4,256,256]{2,1,0:T(8,128)(2,1)S(1)} %get-tuple-element.45.t0, bf16[4,256,256]{2,1,0:T(8,128)(2,1)S(1)} %constant_dynamic-update-slice_fusion.t1, bf16[4,256,256]{2,1,0:T(8,128)(2,1)S(1)} %collective-permute-done.4.t2, ...), custom_call_target="tpu_custom_call" | custom-call | flops 1000 | bytes 1000 | tf_op jit(solution)/shard_map/first_layer/pallas_call | solution.py:211
  52.7 2.8 %collective-permute-start.7 = (f32[8,768]{1,0:T(8,128)S(1)}, f32[8,768]{1,0:T(8,128)S(1)}, u32[]{:S(2)}, u32[]{:S(2)}) collective-permute-start(f32[8,768]{1,0:T(8,128)S(1)} %add.92.s0), channel_id=1, source_target_pairs={{0,2},{2,0},{1,3},{3,1},{4,6},{6,4},{5,7},{7,5},{8,10},{10,8},{9,1... | collective-permute-start | bytes 73736 | tf_op jit(solution)/shard_map/ppermute | solution.py:28
  57.6 5.8 %copy-done.1 = bf16[2,1024,4096]{2,1,0:T(8,128)(2,1)S(1)} copy-done((bf16[2,1024,4096]{2,1,0:T(8,128)(2,1)S(1)}, bf16[2,1024,4096]{2,1,0:T(8,128)(2,1)}, u32[]{:S(2)}) %copy-start.1) | copy-done | bytes 16777240
  63.4 2.6 %product.9 = (bf16[1,768,256]{2,1,0:T(8,128)(2,1)S(1)}, bf16[1,768,256]{2,1,0:T(8,128)(2,1)S(1)}) custom-call(s32[5]{0:T(128)S(1)} %stack.35.where_ref, bf16[2,1024,4096]{2,1,0:T(8,128)(2,1)S(1)} %copy-done.1, bf16[768,1024]{1,0:T(8,128)(2,1)S(1)} %next_hidden.1.refs_0_.x_ref), custom_call_target="tpu_custom_call" | custom-call | flops 1000 | bytes 1000 | tf_op jit(solution)/shard_map/product/pallas_call | solution.py:103
  67.6 5.8 %copy-done.2 = bf16[2,1024,4096]{2,1,0:T(8,128)(2,1)S(1)} copy-done((bf16[2,1024,4096]{2,1,0:T(8,128)(2,1)S(1)}, bf16[2,1024,4096]{2,1,0:T(8,128)(2,1)}, u32[]{:S(2)}) %copy-start.2) | copy-done | bytes 16777240
  73.4 2.6 %product.12 = (bf16[1,768,256]{2,1,0:T(8,128)(2,1)S(1)}, bf16[1,768,256]{2,1,0:T(8,128)(2,1)S(1)}) custom-call(s32[5]{0:T(128)S(1)} %stack.35.where_ref, bf16[2,1024,4096]{2,1,0:T(8,128)(2,1)S(1)} %copy-done.2, bf16[768,1024]{1,0:T(8,128)(2,1)S(1)} %next_hidden.1.refs_0_.x_ref), custom_call_target="tpu_custom_call" | custom-call | flops 1000 | bytes 1000 | tf_op jit(solution)/shard_map/product/pallas_call | solution.py:103
  77.2 2.6 %product.10 = (bf16[1,768,256]{2,1,0:T(8,128)(2,1)S(1)}, bf16[1,768,256]{2,1,0:T(8,128)(2,1)S(1)}) custom-call(s32[5]{0:T(128)S(1)} %stack.35.where_ref, bf16[2,1024,4096]{2,1,0:T(8,128)(2,1)S(1)} %copy-done.2, bf16[768,1024]{1,0:T(8,128)(2,1)S(1)} %next_hidden.1.refs_0_.x_ref), custom_call_target="tpu_custom_call" | custom-call | flops 1000 | bytes 1000 | tf_op jit(solution)/shard_map/product/pallas_call | solution.py:103
  82.1 2.6 %product.13 = (bf16[1,768,256]{2,1,0:T(8,128)(2,1)}, bf16[1,768,256]{2,1,0:T(8,128)(2,1)S(1)}) custom-call(s32[5]{0:T(128)S(1)} %stack.35.where_ref, bf16[2,1024,4096]{2,1,0:T(8,128)(2,1)S(1)} %copy-done.2, bf16[768,1024]{1,0:T(8,128)(2,1)S(1)} %next_hidden.1.refs_0_.x_ref), custom_call_target="tpu_custom_call" | custom-call | flops 1000 | bytes 1000 | tf_op jit(solution)/shard_map/product/pallas_call | solution.py:103
  85.8 9.6 %product.11 = (bf16[4,768,256]{2,1,0:T(8,128)(2,1)}, bf16[4,768,256]{2,1,0:T(8,128)(2,1)S(1)}) custom-call(s32[5]{0:T(128)S(1)} %stack.35.where_ref, bf16[2,1024,4096]{2,1,0:T(8,128)(2,1)S(1)} %copy-done.2, bf16[768,1024]{1,0:T(8,128)(2,1)S(1)} %next_hidden.1.refs_0_.x_ref), custom_call_target="tpu_custom_call" | custom-call | flops 1000 | bytes 1000 | tf_op jit(solution)/shard_map/product/pallas_call | solution.py:103
  96.0 7.9 %all-to-all-start = ((bf16[16,2,56,128]{3,2,1,0:T(8,128)(2,1)}), bf16[16,2,56,128]{3,2,1,0:T(8,128)(2,1)}, u32[]{:S(2)}, u32[]{:S(2)}) async-start(bf16[16,2,56,128]{3,2,1,0:T(8,128)(2,1)} %bitcast.36), calls=%async_computation | async-start | bytes 917504 | tf_op jit(solution)/shard_map/all_to_all | solution.py:432
  106.3 2.7 %collective-permute-start.13 = (bf16[1,768,256]{2,1,0:T(8,128)(2,1)}, bf16[1,768,256]{2,1,0:T(8,128)(2,1)}, u32[]{:S(2)}, u32[]{:S(2)}) collective-permute-start(bf16[1,768,256]{2,1,0:T(8,128)(2,1)} %add_convert_fusion.4), channel_id=1, source_target_pairs={{0,2},{2,0},{1,3},{3,1},{4,6},{6,4},{5,7},{7,5},{8,10},{10,8},{9,1... | collective-permute-start | bytes 1179656 | tf_op jit(solution)/shard_map/ppermute | solution.py:28
  109.3 2.7 %collective-permute-start.16 = (bf16[1,768,256]{2,1,0:T(8,128)(2,1)}, bf16[1,768,256]{2,1,0:T(8,128)(2,1)}, u32[]{:S(2)}, u32[]{:S(2)}) collective-permute-start(bf16[1,768,256]{2,1,0:T(8,128)(2,1)} %add_convert_fusion.3), channel_id=1, source_target_pairs={{0,2},{2,0},{1,3},{3,1},{4,6},{6,4},{5,7},{7,5},{8,10},{10,8},{9,1... | collective-permute-start | bytes 1179656 | tf_op jit(solution)/shard_map/ppermute | solution.py:28
  118.0 17.6 %collective-permute-done.20 = f32[16,12]{1,0:T(8,128)S(1)} collective-permute-done((f32[16,12]{1,0:T(8,128)S(1)}, f32[16,12]{1,0:T(8,128)S(1)}, u32[]{:S(2)}, u32[]{:S(2)}) %collective-permute-start.20) | collective-permute-done | bytes 800 | tf_op jit(solution)/shard_map/ppermute | solution.py:28
  143.9 2.9 %second_layer.4 = (f32[8,768]{1,0:T(8,128)S(1)}, f32[48,256]{1,0:T(8,128)S(1)}) custom-call(bf16[768,1024]{1,0:T(8,128)(2,1)S(1)} %next_hidden.1.refs_0_.x_ref, f32[8,768]{1,0:T(8,128)S(1)} %add.88.l0, f32[8,768]{1,0:T(8,128)S(1)} %collective-permute-done.5.l1, f32[8,768]{1,0:T(8,128)S(1)} %add.92.s0, f32[8,768]{1,0:T(8,128)S(1)} %collective-permute-done.7.s1, ...), custom_call_target="tpu_custom_call" | custom-call | flops 1000 | bytes 1000 | tf_op jit(solution)/shard_map/second_layer/pallas_call | solution.py:296
  146.8 2.9 %second_layer.5 = (f32[8,768]{1,0:T(8,128)S(1)}, f32[48,256]{1,0:T(8,128)S(1)}) custom-call(bf16[768,1024]{1,0:T(8,128)(2,1)S(1)} %next_hidden.1.refs_0_.x_ref, f32[8,768]{1,0:T(8,128)S(1)} %add.88.l0, f32[8,768]{1,0:T(8,128)S(1)} %collective-permute-done.5.l1, f32[8,768]{1,0:T(8,128)S(1)} %add.92.s0, f32[8,768]{1,0:T(8,128)S(1)} %collective-permute-done.7.s1, ...), custom_call_target="tpu_custom_call" | custom-call | flops 1000 | bytes 1000 | tf_op jit(solution)/shard_map/second_layer/pallas_call | solution.py:296
  149.7 2.9 %second_layer.6 = (f32[8,768]{1,0:T(8,128)S(1)}, f32[48,256]{1,0:T(8,128)S(1)}) custom-call(bf16[768,1024]{1,0:T(8,128)(2,1)S(1)} %next_hidden.1.refs_0_.x_ref, f32[8,768]{1,0:T(8,128)S(1)} %add.88.l0, f32[8,768]{1,0:T(8,128)S(1)} %collective-permute-done.5.l1, f32[8,768]{1,0:T(8,128)S(1)} %add.92.s0, f32[8,768]{1,0:T(8,128)S(1)} %collective-permute-done.7.s1, ...), custom_call_target="tpu_custom_call" | custom-call | flops 1000 | bytes 1000 | tf_op jit(solution)/shard_map/second_layer/pallas_call | solution.py:296
  152.7 3.5 %second_layer.7 = (f32[8,768]{1,0:T(8,128)}, f32[48,256]{1,0:T(8,128)S(1)}) custom-call(bf16[768,1024]{1,0:T(8,128)(2,1)S(1)} %next_hidden.1.refs_0_.x_ref, f32[8,768]{1,0:T(8,128)S(1)} %add.88.l0, f32[8,768]{1,0:T(8,128)S(1)} %collective-permute-done.5.l1, f32[8,768]{1,0:T(8,128)S(1)} %add.92.s0, f32[8,768]{1,0:T(8,128)S(1)} %collective-permute-done.7.s1, ...), custom_call_target="tpu_custom_call" | custom-call | flops 1000 | bytes 1000 | tf_op jit(solution)/shard_map/second_layer/pallas_call | solution.py:296
  165.4 2.5 %weight_step.1 = (f32[2,1024,128]{2,1,0:T(8,128)S(1)}, bf16[2,1024,128]{2,1,0:T(8,128)(2,1)S(1)}) custom-call(s32[5]{0:T(128)S(1)} %stack.35.where_ref, bf16[16,8,96,128]{3,2,1,0:T(8,128)(2,1)S(1)} %bitcast.31, bf16[16,2,96,128]{3,2,1,0:T(8,128)(2,1)S(1)} %multiply_convert_fusion.outs_ref), custom_call_target="tpu_custom_call" | custom-call | flops 1000 | bytes 1000 | tf_op jit(solution)/shard_map/weight_step/pallas_call | solution.py:341
  169.6 10.5 %collective-permute-done.21 = bf16[2,1024,128]{2,1,0:T(8,128)(2,1)S(1)} collective-permute-done((bf16[2,1024,128]{2,1,0:T(8,128)(2,1)S(1)}, bf16[2,1024,128]{2,1,0:T(8,128)(2,1)S(1)}, u32[]{:S(2)}, u32[]{:S(2)}) %collective-permute-start.21) | collective-permute-done | bytes 524320 | tf_op jit(solution)/shard_map/ppermute | solution.py:28
  (145 shorter events, 55.4 us)
Async XLA Ops:
  7.2 156.4 %all-gather.3.cloned.1.call-start = ((), (), s32[]{:S(2)}) async-start(), calls=%async_computation.1 | async-start | bytes 3342336 | tf_op jit(solution)/shard_map/all_gather | solution.py:383
  13.1 2.3 %collective-permute-start = (f32[8,768]{1,0:T(8,128)S(1)}, f32[8,768]{1,0:T(8,128)S(1)}, u32[]{:S(2)}, u32[]{:S(2)}) collective-permute-start(f32[8,768]{1,0:T(8,128)S(1)} %low.1), channel_id=1, source_target_pairs={{0,1},{1,0},{2,3},{3,2},{4,5},{5,4},{6,7},{7,6},{8,9},{9,8},{10,11... | collective-permute-start | bytes 73736 | tf_op jit(solution)/shard_map/ppermute | solution.py:28
  25.8 2.0 %collective-permute-start.1 = (bf16[4,256,256]{2,1,0:T(8,128)(2,1)S(1)}, bf16[4,256,256]{2,1,0:T(8,128)(2,1)S(1)}, u32[]{:S(2)}, u32[]{:S(2)}) collective-permute-start(bf16[4,256,256]{2,1,0:T(8,128)(2,1)S(1)} %get-tuple-element.43), channel_id=1, source_target_pairs={{0,1},{1,0},{2,3},{3,2},{4,5},{5,4},{6,7},{7,6},{8,9},{9,8},{10,11... | collective-permute-start | bytes 1572872 | tf_op jit(solution)/shard_map/ppermute | solution.py:28
  28.7 15.4 %collective-permute-start.4 = (bf16[4,256,256]{2,1,0:T(8,128)(2,1)}, bf16[4,256,256]{2,1,0:T(8,128)(2,1)S(1)}, u32[]{:S(2)}, u32[]{:S(2)}) collective-permute-start(bf16[4,256,256]{2,1,0:T(8,128)(2,1)} %add_convert_fusion), channel_id=1, source_target_pairs={{0,2},{2,0},{1,3},{3,1},{4,6},{6,4},{5,7},{7,5},{8,10},{10,8},{9,1... | collective-permute-start | bytes 1572872 | tf_op jit(solution)/shard_map/ppermute | solution.py:28
  37.0 2.0 %collective-permute-start.2 = (bf16[2,256,256]{2,1,0:T(8,128)(2,1)}, bf16[2,256,256]{2,1,0:T(8,128)(2,1)S(1)}, u32[]{:S(2)}, u32[]{:S(2)}) collective-permute-start(bf16[2,256,256]{2,1,0:T(8,128)(2,1)} %get-tuple-element.92), channel_id=1, source_target_pairs={{0,1},{1,0},{2,3},{3,2},{4,5},{5,4},{6,7},{7,6},{8,9},{9,8},{10,11... | collective-permute-start | bytes 786440 | tf_op jit(solution)/shard_map/ppermute | solution.py:28
  37.6 1.7 collective-permute-start.3
  37.7 6.4 %collective-permute-start.5 = (f32[8,768]{1,0:T(8,128)S(1)}, f32[8,768]{1,0:T(8,128)S(1)}, u32[]{:S(2)}, u32[]{:S(2)}) collective-permute-start(f32[8,768]{1,0:T(8,128)S(1)} %add.88.l0), channel_id=1, source_target_pairs={{0,2},{2,0},{1,3},{3,1},{4,6},{6,4},{5,7},{7,5},{8,10},{10,8},{9,1... | collective-permute-start | bytes 73736 | tf_op jit(solution)/shard_map/ppermute | solution.py:28
  50.5 2.1 %collective-permute-start.6 = (f32[8,768]{1,0:T(8,128)S(1)}, f32[8,768]{1,0:T(8,128)S(1)}, u32[]{:S(2)}, u32[]{:S(2)}) collective-permute-start(f32[8,768]{1,0:T(8,128)S(1)} %constant_dynamic-update-slice_fusion.2), channel_id=1, source_target_pairs={{0,1},{1,0},{2,3},{3,2},{4,5},{5,4},{6,7},{7,6},{8,9},{9,8},{10,11... | collective-permute-start | bytes 73736 | tf_op jit(solution)/shard_map/ppermute | solution.py:28
  52.7 4.2 %collective-permute-start.7 = (f32[8,768]{1,0:T(8,128)S(1)}, f32[8,768]{1,0:T(8,128)S(1)}, u32[]{:S(2)}, u32[]{:S(2)}) collective-permute-start(f32[8,768]{1,0:T(8,128)S(1)} %add.92.s0), channel_id=1, source_target_pairs={{0,2},{2,0},{1,3},{3,1},{4,6},{6,4},{5,7},{7,5},{8,10},{10,8},{9,1... | collective-permute-start | bytes 73736 | tf_op jit(solution)/shard_map/ppermute | solution.py:28
  66.0 10.3 %collective-permute-start.8 = (bf16[1,768,256]{2,1,0:T(8,128)(2,1)S(1)}, bf16[1,768,256]{2,1,0:T(8,128)(2,1)S(1)}, u32[]{:S(2)}, u32[]{:S(2)}) collective-permute-start(bf16[1,768,256]{2,1,0:T(8,128)(2,1)S(1)} %get-tuple-element.55), channel_id=1, source_target_pairs={{0,1},{1,0},{2,3},{3,2},{4,5},{5,4},{6,7},{7,6},{8,9},{9,8},{10,11... | collective-permute-start | bytes 1179656 | tf_op jit(solution)/shard_map/ppermute | solution.py:28
  76.0 5.3 %collective-permute-start.11 = (bf16[1,768,256]{2,1,0:T(8,128)(2,1)S(1)}, bf16[1,768,256]{2,1,0:T(8,128)(2,1)S(1)}, u32[]{:S(2)}, u32[]{:S(2)}) collective-permute-start(bf16[1,768,256]{2,1,0:T(8,128)(2,1)S(1)} %get-tuple-element.63), channel_id=1, source_target_pairs={{0,1},{1,0},{2,3},{3,2},{4,5},{5,4},{6,7},{7,6},{8,9},{9,8},{10,11... | collective-permute-start | bytes 1179656 | tf_op jit(solution)/shard_map/ppermute | solution.py:28
  79.8 5.1 %collective-permute-start.9 = (bf16[1,768,256]{2,1,0:T(8,128)(2,1)S(1)}, bf16[1,768,256]{2,1,0:T(8,128)(2,1)S(1)}, u32[]{:S(2)}, u32[]{:S(2)}) collective-permute-start(bf16[1,768,256]{2,1,0:T(8,128)(2,1)S(1)} %get-tuple-element.58), channel_id=1, source_target_pairs={{0,1},{1,0},{2,3},{3,2},{4,5},{5,4},{6,7},{7,6},{8,9},{9,8},{10,11... | collective-permute-start | bytes 1179656 | tf_op jit(solution)/shard_map/ppermute | solution.py:28
  84.8 27.2 %collective-permute-start.14 = (bf16[1,768,256]{2,1,0:T(8,128)(2,1)}, bf16[1,768,256]{2,1,0:T(8,128)(2,1)}, u32[]{:S(2)}, u32[]{:S(2)}) collective-permute-start(bf16[1,768,256]{2,1,0:T(8,128)(2,1)} %get-tuple-element.69), channel_id=1, source_target_pairs={{0,1},{1,0},{2,3},{3,2},{4,5},{5,4},{6,7},{7,6},{8,9},{9,8},{10,11... | collective-permute-start | bytes 1179656 | tf_op jit(solution)/shard_map/ppermute | solution.py:28
  95.4 48.5 %collective-permute-start.10 = (bf16[4,768,256]{2,1,0:T(8,128)(2,1)}, bf16[4,768,256]{2,1,0:T(8,128)(2,1)}, u32[]{:S(2)}, u32[]{:S(2)}) collective-permute-start(bf16[4,768,256]{2,1,0:T(8,128)(2,1)} %get-tuple-element.61), channel_id=1, source_target_pairs={{0,1},{1,0},{2,3},{3,2},{4,5},{5,4},{6,7},{7,6},{8,9},{9,8},{10,11... | collective-permute-start | bytes 4718600 | tf_op jit(solution)/shard_map/ppermute | solution.py:28
  96.0 18.0 %all-to-all-start = ((bf16[16,2,56,128]{3,2,1,0:T(8,128)(2,1)}), bf16[16,2,56,128]{3,2,1,0:T(8,128)(2,1)}, u32[]{:S(2)}, u32[]{:S(2)}) async-start(bf16[16,2,56,128]{3,2,1,0:T(8,128)(2,1)} %bitcast.36), calls=%async_computation | async-start | bytes 917504 | tf_op jit(solution)/shard_map/all_to_all | solution.py:432
  106.3 40.5 %collective-permute-start.13 = (bf16[1,768,256]{2,1,0:T(8,128)(2,1)}, bf16[1,768,256]{2,1,0:T(8,128)(2,1)}, u32[]{:S(2)}, u32[]{:S(2)}) collective-permute-start(bf16[1,768,256]{2,1,0:T(8,128)(2,1)} %add_convert_fusion.4), channel_id=1, source_target_pairs={{0,2},{2,0},{1,3},{3,1},{4,6},{6,4},{5,7},{7,5},{8,10},{10,8},{9,1... | collective-permute-start | bytes 1179656 | tf_op jit(solution)/shard_map/ppermute | solution.py:28
  109.0 32.8 %collective-permute-start.12 = (bf16[1,768,256]{2,1,0:T(8,128)(2,1)}, bf16[1,768,256]{2,1,0:T(8,128)(2,1)}, u32[]{:S(2)}, u32[]{:S(2)}) collective-permute-start(bf16[1,768,256]{2,1,0:T(8,128)(2,1)} %add_convert_fusion.2), channel_id=1, source_target_pairs={{0,2},{2,0},{1,3},{3,1},{4,6},{6,4},{5,7},{7,5},{8,10},{10,8},{9,1... | collective-permute-start | bytes 1179656 | tf_op jit(solution)/shard_map/ppermute | solution.py:28
  109.3 43.4 %collective-permute-start.16 = (bf16[1,768,256]{2,1,0:T(8,128)(2,1)}, bf16[1,768,256]{2,1,0:T(8,128)(2,1)}, u32[]{:S(2)}, u32[]{:S(2)}) collective-permute-start(bf16[1,768,256]{2,1,0:T(8,128)(2,1)} %add_convert_fusion.3), channel_id=1, source_target_pairs={{0,2},{2,0},{1,3},{3,1},{4,6},{6,4},{5,7},{7,5},{8,10},{10,8},{9,1... | collective-permute-start | bytes 1179656 | tf_op jit(solution)/shard_map/ppermute | solution.py:28
  114.7 20.9 %collective-permute-start.20 = (f32[16,12]{1,0:T(8,128)S(1)}, f32[16,12]{1,0:T(8,128)S(1)}, u32[]{:S(2)}, u32[]{:S(2)}) collective-permute-start(f32[16,12]{1,0:T(8,128)S(1)} %bitcast.38), channel_id=1, source_target_pairs={{0,16},{16,0},{1,17},{17,1},{2,18},{18,2},{3,19},{19,3},{4,20},{20... | collective-permute-start | bytes 2312 | tf_op jit(solution)/shard_map/ppermute | solution.py:28
  135.6 14.1 %collective-permute-start.15 = (bf16[1,768,256]{2,1,0:T(8,128)(2,1)}, bf16[1,768,256]{2,1,0:T(8,128)(2,1)}, u32[]{:S(2)}, u32[]{:S(2)}) collective-permute-start(bf16[1,768,256]{2,1,0:T(8,128)(2,1)} %add_convert_fusion.1), channel_id=1, source_target_pairs={{0,2},{2,0},{1,3},{3,1},{4,6},{6,4},{5,7},{7,5},{8,10},{10,8},{9,1... | collective-permute-start | bytes 1179656 | tf_op jit(solution)/shard_map/ppermute | solution.py:28
  141.8 18.4 %collective-permute-start.19 = (bf16[16,2,48,128]{3,2,1,0:T(8,128)(2,1)}, bf16[16,2,48,128]{3,2,1,0:T(8,128)(2,1)}, u32[]{:S(2)}, u32[]{:S(2)}) collective-permute-start(bf16[16,2,48,128]{3,2,1,0:T(8,128)(2,1)} %slice.65), channel_id=1, source_target_pairs={{0,1},{1,0},{2,3},{3,2},{4,5},{5,4},{6,7},{7,6},{8,9},{9,8},{10,11... | collective-permute-start | bytes 1179656 | tf_op jit(solution)/shard_map/ppermute | solution.py:28
  156.9 1.4 collective-permute-start.17
  159.0 4.2 %collective-permute-start.18 = (f32[8,768]{1,0:T(8,128)S(1)}, f32[8,768]{1,0:T(8,128)S(1)}, u32[]{:S(2)}, u32[]{:S(2)}) collective-permute-start(f32[8,768]{1,0:T(8,128)S(1)} %add.97), channel_id=1, source_target_pairs={{0,2},{2,0},{1,3},{3,1},{4,6},{6,4},{5,7},{7,5},{8,10},{10,8},{9,1... | collective-permute-start | bytes 73736 | tf_op jit(solution)/shard_map/ppermute | solution.py:28
  167.9 12.2 %collective-permute-start.21 = (bf16[2,1024,128]{2,1,0:T(8,128)(2,1)S(1)}, bf16[2,1024,128]{2,1,0:T(8,128)(2,1)S(1)}, u32[]{:S(2)}, u32[]{:S(2)}) collective-permute-start(bf16[2,1024,128]{2,1,0:T(8,128)(2,1)S(1)} %get-tuple-element.78), channel_id=1, source_target_pairs={{0,16},{16,0},{1,17},{17,1},{2,18},{18,2},{3,19},{19,3},{4,20},{20... | collective-permute-start | bytes 1572872 | tf_op jit(solution)/shard_map/ppermute | solution.py:28
  (21 other events, 137.1 us)
Sparse Core Ops, SparseCore 0:
  10.2 51.0 all-gather.2

commit v3 on v2

--- a/solution.py
+++ b/solution.py
@@ -43,76 +43,87 @@
     )
 
 
-def regroup(factors, first, second):
-    layers, members, ranks, width = factors.shape
+def pack(where, digits, factors_in, factors_out, pops):
+    layers, members, ranks, width = factors_in.shape
+    k = members * layers * ranks
+    half = members // 2
     blocks = width // 128
-
-    def kernel(in_ref, out_ref):
+    part = k // 2 + 8
+    rows = blocks * k + 2 * part
+
+    def kernel(where_ref, digits_ref, in_ref, out_ref, a_ref, b_ref, packed_ref):
+        own = pl.multiple_of((where_ref[1] * 2 + where_ref[2]) * width, width)
+        c = where_ref[2]
+
+        def member(ref, m, cols):
+            return jnp.concatenate(
+                [ref[l, m, :, cols].astype(f32) for l in range(layers)], axis=0
+            ).astype(bf16)
+
         for m in range(members):
-            rows = jnp.concatenate(
-                [in_ref[l, m].astype(f32) for l in range(layers)], axis=0
+            a = member(in_ref, m, slice(None))
+            b = member(out_ref, m, pl.ds(own, width))
+            at = slice(m * 8, m * 8 + 8)
+            for n in range(blocks):
+                a_ref[n, at, :] = a[:, n * 128 : (n + 1) * 128]
+                b_ref[n, at, :] = b[:, n * 128 : (n + 1) * 128]
+        for m in range(half):
+            b = member(out_ref, c * half + m, slice(None))
+            for o in range(2 * pops):
+                y, x, z = o // 8, (o // 4) % 2, o % 4
+                lo = blocks * k + x * part + m * 8
+                packed_ref[y * 4 + z, lo : lo + 8, :] = b[:, o * 128 : (o + 1) * 128]
+        for p in range(pops):
+            for n in range(blocks):
+                packed_ref[p, n * k : (n + 1) * k, :] = a_ref[n]
+            for x in range(2):
+                lo = blocks * k + x * part + k // 2
+                packed_ref[p, lo : lo + 8, :] = digits_ref[...]
+
+    return pl.pallas_call(
+        kernel,
+        out_shape=[
+            jax.ShapeDtypeStruct((blocks, k, 128), bf16),
+            jax.ShapeDtypeStruct((blocks, k, 128), bf16),
+            jax.ShapeDtypeStruct((pops, rows, 128), bf16),
+        ],
+        in_specs=[SMEM] + [VMEM] * 3,
+        out_specs=[VMEM] * 3,
+        compiler_params=params(16),
+        name="pack",
+        cost_estimate=small_cost,
+    )(where, digits, factors_in, factors_out)
+
+
+def product(layer, rel, where, left, weights, piece, first=0, count=1):
+    rows, width = left.shape
+    per_owner = width // piece
+
+    def kernel(where_ref, left_ref, w0_ref, w1_ref, out0_ref, out1_ref):
+        for w_ref, out_ref in ((w0_ref, out0_ref), (w1_ref, out1_ref)):
+            out_ref[0] = jnp.dot(
+                left_ref[...], w_ref[0], preferred_element_type=f32
             ).astype(bf16)
-            lo = m * layers * ranks
-            for b in range(blocks):
-                out_ref[b, lo : lo + layers * ranks, :] = rows[:, b * 128 : (b + 1) * 128]
-
-    return pl.pallas_call(
-        kernel,
-        out_shape=jax.ShapeDtypeStruct((blocks, members * layers * ranks, 128), bf16),
-        in_specs=[VMEM],
-        out_specs=VMEM,
-        compiler_params=params(),
-        name=first,
-        cost_estimate=small_cost,
-    )(factors)
-
-
-def product(layer, rel, flip, where, lefts, weights, first=0, count=4):
-    rows, width = lefts[0].shape
-    total = rows * len(lefts)
-    flips = len(flip)
-
-    def kernel(where_ref, w_ref, *refs):
-        left_refs = refs[: len(lefts)]
-        out_refs = refs[len(lefts) : len(lefts) + flips]
-        block, sems = refs[len(lefts) + flips :]
-
-        def fetch(n, f):
-            owner = (where_ref[1] ^ rel) * 2 + (where_ref[2] ^ flip[f])
-            at = pl.multiple_of(owner * width + (first + n) * 256, 256)
-            return pltpu.make_async_copy(
-                w_ref.at[layer, :, pl.ds(at, 256)], block.at[n * flips + f], sems.at[n * flips + f]
-            )
-
-        for n in range(count):
-            for f in range(flips):
-                fetch(n, f).start()
-
-        def one(n, carry):
-            for f in range(flips):
-                fetch(n, f).wait()
-                w = block[n * flips + f]
-                for k, left in enumerate(left_refs):
-                    out_refs[f][n, k * rows : (k + 1) * rows, :] = jnp.dot(
-                        left[...], w, preferred_element_type=f32
-                    ).astype(bf16)
-            return carry
-
-        lax.fori_loop(0, count, one, 0)
-
-    return pl.pallas_call(
-        kernel,
-        out_shape=[jax.ShapeDtypeStruct((count, total, 256), bf16)] * len(flip),
-        in_specs=[SMEM, pl.BlockSpec(memory_space=pltpu.HBM)] + [VMEM] * len(lefts),
-        out_specs=[VMEM] * len(flip),
-        scratch_shapes=[
-            pltpu.VMEM((count * flips, width, 256), bf16),
-            pltpu.SemaphoreType.DMA((count * flips,)),
-        ],
-        compiler_params=params(16),
+
+    def block(flip):
+        def at(n, s):
+            return (layer, 0, ((s[1] ^ rel) * 2 + (s[2] ^ flip)) * per_owner + first + n)
+
+        return pl.BlockSpec((1, width, piece), at)
+
+    return pl.pallas_call(
+        kernel,
+        grid_spec=pltpu.PrefetchScalarGridSpec(
+            num_scalar_prefetch=1,
+            grid=(count,),
+            in_specs=[VMEM, block(1), block(0)],
+            out_specs=[pl.BlockSpec((1, rows, piece), lambda n, s: (n, 0, 0))] * 2,
+        ),
+        out_shape=[jax.ShapeDtypeStruct((count, rows, piece), bf16)] * 2,
+        compiler_params=params(48),
         name="product",
         cost_estimate=small_cost,
-    )(where, weights, *lefts)
+    )(where, left, weights, weights)
 
 
 def member_of(shape, per, dim):
@@ -182,7 +193,8 @@
         total = jnp.zeros((group, rows), f32)
         for n in range(width // 256):
             cols = slice(n * 256, (n + 1) * 256)
-            table = (t0[n].astype(f32) + t1[n].astype(f32) + t2[n].astype(f32)).astype(bf16)
+            in_half = slice(n % 2 * 256, n % 2 * 256 + 256)
+            table = sum(t[n // 2, :, in_half].astype(f32) for t in (t0, t1, t2)).astype(bf16)
             factor = jnp.concatenate([b_ref[2 * n, mine], b_ref[2 * n + 1, mine]], axis=1)
             u = jnp.dot(o_ref[at], table, preferred_element_type=f32) + dot(
                 spread_low, factor, 0, 0
@@ -227,20 +239,26 @@
     rows = lifted[0].shape[0]
     total, width = rows * CHUNKS, embedding.shape[1]
 
-    def kernel(o_ref, e_ref, s0, s1, up0, up1, up2, out_ref):
+    def kernel(o_ref, e_ref, s0, s1, up0, up1, up2, out_ref, last_ref):
         for k, up in enumerate((up0, up1, up2)):
             span = slice(k * rows, (k + 1) * rows)
             so_far = s0[:, span] + s1[:, span]
             norm = lax.rsqrt(so_far / full_width + norm_eps)
             norm_col = jnp.transpose(norm)[:, 0:1]
             x = jnp.dot(o_ref[span], e_ref[...], preferred_element_type=f32)
-            out_ref[span] = (x + norm_col * up[...].astype(f32)).astype(bf16)
-
-    return pl.pallas_call(
-        kernel,
-        out_shape=jax.ShapeDtypeStruct((total, width), bf16),
+            x = (x + norm_col * up[...].astype(f32)).astype(bf16)
+            out_ref[span] = x
+            per = rows // 16
+            last_ref[k * per : (k + 1) * per] = x[rows - per :].astype(f32)
+
+    return pl.pallas_call(
+        kernel,
+        out_shape=[
+            jax.ShapeDtypeStruct((total, width), bf16),
+            jax.ShapeDtypeStruct((total // 16, width), f32),
+        ],
         in_specs=[VMEM] * 7,
-        out_specs=VMEM,
+        out_specs=[VMEM] * 2,
         compiler_params=params(16),
         name="next_hidden",
         cost_estimate=small_cost,
@@ -270,8 +288,8 @@
             low = (l0[:, span_k] + l1[:, span_k] + norm * so_far) * coef
             spread_low = spread(low, 1, group)
             u = dot(spread_low, factor[k * group : (k + 1) * group], 0, 0) + (
-                own_ref[n, span_k].astype(f32)
-                + peer_ref[n, span_k].astype(f32)
+                own_ref[0, span_k].astype(f32)
+                + peer_ref[0, span_k].astype(f32)
                 + other_ref[0, span_k].astype(f32)
             )
             h = jnp.zeros((per, 256), f32)
@@ -308,35 +326,69 @@
     )(hidden, *lows, *stats, *halves, crossed, out_factors, decay, gain, reward, before)
 
 
-def step_kernel(where, ins, outs):
-    pops, blocks, k, lanes = ins.shape
+def step_kernel(where, arrived, arrived_peer, members, members_all, scale):
+    pops, rows, lanes = arrived.shape
+    k = members * 8
+    part = k // 2 + 8
+    blocks = (rows - 2 * part) // k
     width = blocks * lanes
 
-    def kernel(where_ref, ins_ref, outs_ref, mine_ref, theirs_ref, paired):
-        xl = where_ref[4]
+    def kernel(where_ref, in_ref, peer_ref, mine_ref, theirs_ref, paired, digit_rows):
+        xl, c = where_ref[4], where_ref[2]
+        head = blocks * k
+        for p in range(pops):
+            digits = in_ref[p, head + k // 2 : head + k // 2 + 8, :].astype(f32)
+            for i in range(4):
+                digit_rows[i, p : p + 1, :] = digits[i : i + 1, :]
+        lane = lax.broadcasted_iota(jnp.int32, (pops, lanes), 1)
+        real = lane < members
+        here = (digit_rows[0] * 32.0 + digit_rows[1]) / members_all
+        there = (digit_rows[2] * 32.0 + digit_rows[3]) / members_all
+        mean = (
+            jnp.sum(jnp.where(real, here, 0.0), keepdims=True)
+            + jnp.sum(jnp.where(real, there, 0.0), keepdims=True)
+        ) / members_all
+        here = jnp.where(real, here - mean, 0.0)
+        there = jnp.where(real, there - mean, 0.0)
+        var = (
+            jnp.sum(here * here, keepdims=True) + jnp.sum(there * there, keepdims=True)
+        ) / members_all
+        shaped = here * (lax.rsqrt(var + spread_eps) * scale)
+        pick = lax.broadcasted_iota(jnp.int32, (k, lanes), 0) // 8 == lax.broadcasted_iota(
+            jnp.int32, (k, lanes), 1
+        )
+        by_row = dot(pick.astype(f32), shaped, 1, 1, lax.Precision.HIGHEST)
         layer = (lax.broadcasted_iota(jnp.int32, (k, lanes), 0) % 8) // 4
         for p in range(pops):
             at = slice(p * k, (p + 1) * k)
             for rel in range(2):
-                o = outs_ref[p, xl ^ rel]
-                zero = jnp.zeros_like(o)
+                lo = pl.multiple_of((xl ^ rel) * part, 8)
+                mine = in_ref[p, pl.ds(head + lo, k // 2), :].astype(f32)
+                theirs = peer_ref[p, pl.ds(lo, k // 2), :].astype(f32)
+                o = jnp.concatenate(
+                    [jnp.where(c == 0, mine, theirs), jnp.where(c == 0, theirs, mine)], axis=0
+                )
+                o = o * by_row[:, p : p + 1]
                 for l in range(2):
-                    lo = (rel * 2 + l) * lanes
-                    paired[at, lo : lo + lanes] = jnp.where(layer == l, o, zero)
+                    col = (rel * 2 + l) * lanes
+                    paired[at, col : col + lanes] = jnp.where(layer == l, o, 0.0).astype(bf16)
         right = paired[...]
         for b in range(0, blocks, 2):
             left = jnp.concatenate(
                 [
-                    jnp.concatenate([ins_ref[p, b], ins_ref[p, b + 1]], axis=1)
+                    jnp.concatenate(
+                        [in_ref[p, b * k : (b + 1) * k, :], in_ref[p, (b + 1) * k : (b + 2) * k, :]],
+                        axis=1,
+                    )
                     for p in range(pops)
                 ],
                 axis=0,
             )
             out = dot(left, right, 0, 0)
-            rows = slice(b * lanes, (b + 2) * lanes)
+            span = slice(b * lanes, (b + 2) * lanes)
             for l in range(2):
-                mine_ref[l, rows, :] = out[:, l * lanes : (l + 1) * lanes]
-                theirs_ref[l, rows, :] = out[:, (2 + l) * lanes : (3 + l) * lanes].astype(bf16)
+                mine_ref[l, span, :] = out[:, l * lanes : (l + 1) * lanes]
+                theirs_ref[l, span, :] = out[:, (2 + l) * lanes : (3 + l) * lanes].astype(bf16)
 
     return pl.pallas_call(
         kernel,
@@ -346,11 +398,14 @@
         ],
         in_specs=[SMEM, VMEM, VMEM],
         out_specs=[VMEM, VMEM],
-        scratch_shapes=[pltpu.VMEM((pops * k, 4 * lanes), bf16)],
+        scratch_shapes=[
+            pltpu.VMEM((pops * k, 4 * lanes), bf16),
+            pltpu.VMEM((4, pops, lanes), f32),
+        ],
         compiler_params=params(24),
         name="weight_step",
         cost_estimate=small_cost,
-    )(where, ins, outs)
+    )(where, arrived, arrived_peer)
 
 
 def shards(
@@ -379,30 +434,24 @@
     order = token_ids.reshape(CHUNKS, -1, step_count).transpose(0, 2, 1).reshape(-1)
     onehot = (order[:, None] == jnp.arange(vocab, dtype=jnp.int32)[None, :]).astype(bf16)
 
-    a_blocks = regroup(factors_in, "regroup_in", 0)
-    ins_all = lax.all_gather(a_blocks, ("y", "z"))
-
     def added(a, b):
         return (a.astype(f32) + b.astype(f32)).astype(bf16)
 
-    def sums_to_send(layer, lefts, first=0, count=4, dep=()):
-        at = after(where, *dep) if dep else where
-        peer, own = product(layer, 1, (1, 0), at, lefts, mix_weights, first, count)
-        return added(own, swap(peer, "c"))
-
-    def sums_to_keep(layer, lefts, dep):
-        peer, own = product(layer, 0, (1, 0), after(where, *dep), lefts, mix_weights)
-        return own, swap(peer, "c")
-
-    lows = mp_parts(low_kernel(onehot, embedding, a_blocks))
-    cross = sums_to_send(0, [embedding], dep=(lows[0],))
+    peer, own = product(0, 1, where, embedding, mix_weights, 512, 0, 2)
+    cross = added(own, swap(peer, "c"))
     table_cross = swap(cross, "xh")
-    peer, own = product(0, 0, (1, 0), after(where, cross), [embedding], mix_weights)
-    keep = jnp.concatenate([swap(peer[:2], "c"), swap(peer[2:], "c")])
+    both = jnp.stack([fitness_ranks, swap(fitness_ranks, "xl")])
+    digits = jnp.stack([both[0] // 32, both[0] % 32, both[1] // 32, both[1] % 32]).astype(bf16)
+    digits = jnp.pad(digits, ((0, 4), (0, 128 - members)))
+    pops = lax.axis_size("y") * lax.axis_size("z")
+    a_blocks, b_own, packed = pack(
+        after(where, peer), digits, factors_in, factors_out, pops
+    )
+    lows = mp_parts(low_kernel(after(onehot, peer), embedding, a_blocks))
+    peer, own = product(0, 0, after(where, cross, lows[0]), embedding, mix_weights, 512, 0, 2)
+    keep = jnp.concatenate([swap(peer[:1], "c"), swap(peer[1:], "c")])
     first_table = [own, keep, table_cross]
-
-    b_blocks = regroup(after(factors_out, cross), "regroup_out", 0)
-    b_own = lax.dynamic_slice_in_dim(b_blocks, (xh * 2 + c) * 8, 8, 0)
+    arrived = lax.all_to_all(after(packed, own), ("y", "z"), 0, 0, tiled=True)
 
     decay = [decay_rates[l : l + 1] for l in range(2)]
     gain = [norm_gain[l : l + 1] for l in range(2)]
@@ -414,45 +463,32 @@
         lifted.append(up)
         stats.append(st)
     stats = mp_parts(jnp.concatenate(stats, axis=1))
-    hidden = next_hidden(full_width, onehot, embedding, stats, lifted)
-    sent, parts = [], []
+    hidden, last_hidden = next_hidden(full_width, onehot, embedding, stats, lifted)
+    sent, parts, halves = [], [], []
     for n in range(4):
-        part = sums_to_send(1, [hidden], n, 1, parts[n - 2 : n - 1] if n > 1 else ())
-        parts.append(part)
-        sent.append(swap(part, "xh"))
-    halves = sums_to_keep(1, [hidden], (part,))
-
-    half_rows = b_blocks.shape[1] // 2
-    my_rows = lax.dynamic_slice_in_dim(b_blocks, c * half_rows, half_rows, 1)
-    digits = jnp.stack([fitness_ranks // 32, fitness_ranks % 32]).astype(bf16)
-    digits = jnp.pad(digits, ((0, 6), (0, 128 - members)))
-    digits = jnp.broadcast_to(digits[None], (pop_count, 8, 128))
-    packed = jnp.concatenate([my_rows, digits], axis=1)
-    packed = packed.reshape(4, 2, 4, -1, 128).transpose(0, 2, 1, 3, 4).reshape(16, 2, -1, 128)
-    arrived = lax.all_to_all(after(packed, part), ("y", "z"), 0, 0, tiled=True)
-    mine = arrived[:, :, :half_rows]
-    digits_all = arrived[:, 0, half_rows : half_rows + 2, :members].astype(f32)
-    ranks_here = digits_all[:, 0] * 32.0 + digits_all[:, 1]
-    ranks_there = swap(ranks_here, "xl")
-    theirs = swap(mine, "c")
-    outs = jnp.where(
-        c == 0, jnp.concatenate([mine, theirs], axis=2), jnp.concatenate([theirs, mine], axis=2)
+        at = after(where, parts[n - 2]) if n > 1 else where
+        peer, own = product(1, 1, at, hidden, mix_weights, 256, n)
+        parts.append(added(own, swap(peer, "c")))
+        sent.append(swap(parts[n], "xh"))
+    for n in range(4):
+        at = after(where, sent[n - 1]) if n > 0 else after(where, parts[3])
+        peer, own = product(1, 0, at, hidden, mix_weights, 256, n)
+        halves.append((own, swap(peer, "c")))
+
+    outs_rows = 2 * (members * rank_count + 8)
+    arrived = after(arrived, sent[2])
+    arrived_peer = swap(arrived[:, -outs_rows:], "c")
+    step_mine, step_theirs = step_kernel(
+        where, arrived, arrived_peer, members, members_all, (members_all * rank_count) ** (-0.5)
     )
-    shares = ranks_here / members_all
-    shares_there = ranks_there / members_all
-    rank_mean = (jnp.sum(shares) + jnp.sum(shares_there)) / members_all
-    spread_sum = jnp.sum((shares - rank_mean) ** 2) + jnp.sum((shares_there - rank_mean) ** 2)
-    shaped = (shares - rank_mean) * lax.rsqrt(spread_sum / members_all + spread_eps)
-    shaped = shaped * (members_all * rank_count) ** (-0.5)
-    shaped_rows = jnp.repeat(shaped, 2 * rank_count, axis=1)
-    outs = (outs.astype(f32) * shaped_rows[:, None, :, None]).astype(bf16)
-    step_mine, step_theirs = step_kernel(where, ins_all, outs)
 
     st = jnp.zeros((8, rows_all), f32)
     lasts = []
     for n in range(4):
+        if n == 3:
+            st = after(st, step_theirs)
         st, last = second_layer(
-            n, coef, full_width, hidden, lows, stats, halves, sent[n], b_own,
+            n, coef, full_width, hidden, lows, stats, halves[n], sent[n], b_own,
             decay[1], gain[1], reward_dir[None], st,
         )
         lasts.append(last)
@@ -461,8 +497,7 @@
     norm = lax.rsqrt(so_far[0] / full_width + norm_eps)
     terms = (so_far[2] + norm * so_far[1]).reshape(CHUNKS, step_count, -1)
     tail = norm.reshape(CHUNKS, step_count, -1)[:, -1].reshape(-1)
-    last_hidden = hidden.reshape(CHUNKS, step_count, -1, width)[:, -1].reshape(-1, width)
-    finals = last_hidden.astype(f32) + jnp.concatenate(lasts, axis=1) * tail[:, None]
+    finals = last_hidden + jnp.concatenate(lasts, axis=1) * tail[:, None]
     final_features = finals.astype(bf16).reshape(members, seq_count, width)
     scores = jnp.mean(terms, axis=1).reshape(members, seq_count) * full_width ** (-0.5)
     return (final_features, scores, weight_step)

time: 190 us -> 141 us (0.74)
  local copies, waits for them, and re-layouts: 29.9 us -> 6.82 us
  between operations: 17.1 us -> 1.02 us
  other arithmetic: 13.9 us -> 6.09 us
  Pallas kernels: 54.2 us -> 48.4 us
  waiting for transfers between devices: 41.2 us -> 44.4 us
  starting transfers between devices: 31.8 us -> 33.8 us
    unnamed x47 -> x34, local copies, waits for them, and re-layouts: 22.6 us -> 4.38 us
    pallas_call x4, Pallas kernels: 12.3 us -> 6.75 us  [second_layer(): pl.pallas_call(kernel, out_shape=[jax.ShapeDtypeStruct((8, total), f32),...]
    ppermute x22 -> x25, waiting for transfers between devices: 41.2 us -> 44.4 us  [swap(): return lax.ppermute(value, axis, [(0, 1), (1, 0)])]
    convert_element_type x3 -> x0, other arithmetic: 3.15 us -> none  [the longest x1 1.64 us: shards(): outs = (outs.astype(f32) * shaped_rows[:, None, :, None]).astype(bf16)]
    pallas_call x1, Pallas kernels: 2.46 us -> 5.42 us  [step_kernel(): pl.pallas_call(kernel, out_shape=[jax.ShapeDtypeStruct((2, width, lanes),...]
    pallas_call x3, Pallas kernels: 6.37 us -> 3.59 us  [first_layer(): pl.pallas_call(kernel, out_shape=[jax.ShapeDtypeStruct((rows, width), bf1...]
    reduce_sum x4 -> x0, other arithmetic: 2.41 us -> none  [the longest x2 1.2 us: shards(): rank_mean = (jnp.sum(shares) + jnp.sum(shares_there)) / members_all]
    ppermute x22 -> x25, starting transfers between devices: 23.8 us -> 26 us  [swap(): return lax.ppermute(value, axis, [(0, 1), (1, 0)])]
  transfers between devices with their start and end apart: 24 -> 26, of which waited for: 11 -> 10; matrix products, arithmetic and copies ran while one was open for 11% -> 4% of each run, Pallas kernels for 27% -> 31%
where the time goes in v3:
time: 141 us
  Pallas kernels  48.4 us (34%)
  waiting for transfers between devices  44.4 us (31%)
  starting transfers between devices  33.8 us (24%)
  local copies, waits for them, and re-layouts  6.82 us (5%)
  other arithmetic  6.09 us (4%)
    ppermute x25, waiting for transfers between devices, swap(): return lax.ppermute(value, axis, [(0, 1), (1, 0)])  44.4 us
    pallas_call x10, Pallas kernels, product(): pl.pallas_call(kernel, grid_spec=pltpu.PrefetchScalarGridSpec(num_scalar_...  29.8 us
    ppermute x25, starting transfers between devices, swap(): return lax.ppermute(value, axis, [(0, 1), (1, 0)])  26 us
    all_to_all x1, starting transfers between devices, shards(): arrived = lax.all_to_all(after(packed, own), ('y', 'z'), 0, 0, tiled=True)  7.83 us
    pallas_call x4, Pallas kernels, second_layer(): pl.pallas_call(kernel, out_shape=[jax.ShapeDtypeStruct((8, total), f32),...  6.75 us
    pallas_call x1, Pallas kernels, step_kernel(): pl.pallas_call(kernel, out_shape=[jax.ShapeDtypeStruct((2, width, lanes),...  5.42 us
    convert_element_type x5, other arithmetic, added(): return (a.astype(f32) + b.astype(f32)).astype(bf16)  4.64 us
    unnamed x34, local copies, waits for them, and re-layouts  4.38 us
  transfers between devices with their start and end apart: 26, of which 10 were waited for; matrix products, arithmetic and copies ran while one was open for 4% of the time, Pallas kernels for 31%

profile of v3, /device:TPU:1, one launch (start us, length us, event | category | flops | bytes accessed | tf_op | source)
XLA Modules:
  0.0 140.6 jit_solution(14196156644299286809)
XLA Ops:
  0.6 2.1 %collective-permute-start.1 = (s32[12]{0:T(128)}, s32[12]{0:T(128)S(1)}, u32[]{:S(2)}, u32[]{:S(2)}) collective-permute-start(s32[12]{0:T(128)} %param.10), channel_id=1, source_target_pairs={{0,16},{16,0},{1,17},{17,1},{2,18},{18,2},{3,19},{19,3},{4,20},{20... | collective-permute-start | bytes 152 | tf_op jit(solution)/shard_map/ppermute | solution.py:28
  3.9 3.6 %product.10 = (bf16[2,256,512]{2,1,0:T(8,128)(2,1)S(1)}, bf16[2,256,512]{2,1,0:T(8,128)(2,1)S(1)}) custom-call(s32[5]{0:T(128)S(1)} %stack.43.where_ref, bf16[256,1024]{1,0:T(8,128)(2,1)S(1)} %copy-done, bf16[2,1024,4096]{2,1,0:T(8,128)(2,1)} %w1_ref.19, bf16[2,1024,4096]{2,1,0:T(8,128)(2,1)} %w1_ref.19), custom_call_target="tpu_custom_call" | custom-call | flops 1000 | bytes 1000 | tf_op jit(solution)/shard_map/product/pallas_call | solution.py:114
  16.2 3.6 %product.11 = (bf16[2,256,512]{2,1,0:T(8,128)(2,1)S(1)}, bf16[2,256,512]{2,1,0:T(8,128)(2,1)S(1)}) custom-call(s32[5]{0:T(128)S(1)} %stack.43.where_ref, bf16[256,1024]{1,0:T(8,128)(2,1)S(1)} %copy-done.1, bf16[2,1024,4096]{2,1,0:T(8,128)(2,1)} %w1_ref.19, bf16[2,1024,4096]{2,1,0:T(8,128)(2,1)} %w1_ref.19), custom_call_target="tpu_custom_call" | custom-call | flops 1000 | bytes 1000 | tf_op jit(solution)/shard_map/product/pallas_call | solution.py:114
  19.8 7.8 %all-to-all-start = ((bf16[16,880,128]{2,1,0:T(8,128)(2,1)}), bf16[16,880,128]{2,1,0:T(8,128)(2,1)}, u32[]{:S(2)}, u32[]{:S(2)}) async-start(bf16[16,880,128]{2,1,0:T(8,128)(2,1)} %copy-done.2), calls=%async_computation | async-start | bytes 7208960 | tf_op jit(solution)/shard_map/all_to_all | solution.py:454
  27.6 2.5 %collective-permute-start.5 = (bf16[2,256,512]{2,1,0:T(8,128)(2,1)}, bf16[2,256,512]{2,1,0:T(8,128)(2,1)S(1)}, u32[]{:S(2)}, u32[]{:S(2)}) collective-permute-start(bf16[2,256,512]{2,1,0:T(8,128)(2,1)} %add_convert_fusion), channel_id=1, source_target_pairs={{0,2},{2,0},{1,3},{3,1},{4,6},{6,4},{5,7},{7,5},{8,10},{10,8},{9,1... | collective-permute-start | bytes 1572872 | tf_op jit(solution)/shard_map/ppermute | solution.py:28
  32.5 10.6 %collective-permute-done.6.l1 = f32[8,768]{1,0:T(8,128)S(1)} collective-permute-done((f32[8,768]{1,0:T(8,128)S(1)}, f32[8,768]{1,0:T(8,128)S(1)}, u32[]{:S(2)}, u32[]{:S(2)}) %collective-permute-start.6) | collective-permute-done | bytes 24608 | tf_op jit(solution)/shard_map/ppermute | solution.py:28
  48.8 2.4 %collective-permute-start.8 = (f32[8,768]{1,0:T(8,128)S(1)}, f32[8,768]{1,0:T(8,128)S(1)}, u32[]{:S(2)}, u32[]{:S(2)}) collective-permute-start(f32[8,768]{1,0:T(8,128)S(1)} %add.72.s0), channel_id=1, source_target_pairs={{0,2},{2,0},{1,3},{3,1},{4,6},{6,4},{5,7},{7,5},{8,10},{10,8},{9,1... | collective-permute-start | bytes 73736 | tf_op jit(solution)/shard_map/ppermute | solution.py:28
  51.3 2.1 %collective-permute-done.8.s1 = f32[8,768]{1,0:T(8,128)S(1)} collective-permute-done((f32[8,768]{1,0:T(8,128)S(1)}, f32[8,768]{1,0:T(8,128)S(1)}, u32[]{:S(2)}, u32[]{:S(2)}) %collective-permute-start.8) | collective-permute-done | bytes 24608 | tf_op jit(solution)/shard_map/ppermute | solution.py:28
  54.1 2.7 %product.15 = (bf16[1,768,256]{2,1,0:T(8,128)(2,1)S(1)}, bf16[1,768,256]{2,1,0:T(8,128)(2,1)S(1)}) custom-call(s32[5]{0:T(128)S(1)} %stack.43.where_ref, bf16[768,1024]{1,0:T(8,128)(2,1)S(1)} %get-tuple-element.73.left_ref.x_ref, bf16[2,1024,4096]{2,1,0:T(8,128)(2,1)} %w1_ref.19, bf16[2,1024,4096]{2,1,0:T(8,128)(2,1)} %w1_ref.19), custom_call_target="tpu_custom_call" | custom-call | flops 1000 | bytes 1000 | tf_op jit(solution)/shard_map/product/pallas_call | solution.py:114
  58.0 2.7 %product.12 = (bf16[1,768,256]{2,1,0:T(8,128)(2,1)S(1)}, bf16[1,768,256]{2,1,0:T(8,128)(2,1)S(1)}) custom-call(s32[5]{0:T(128)S(1)} %stack.43.where_ref, bf16[768,1024]{1,0:T(8,128)(2,1)S(1)} %get-tuple-element.73.left_ref.x_ref, bf16[2,1024,4096]{2,1,0:T(8,128)(2,1)} %w1_ref.19, bf16[2,1024,4096]{2,1,0:T(8,128)(2,1)} %w1_ref.19), custom_call_target="tpu_custom_call" | custom-call | flops 1000 | bytes 1000 | tf_op jit(solution)/shard_map/product/pallas_call | solution.py:114
  61.7 2.7 %product.18 = (bf16[1,768,256]{2,1,0:T(8,128)(2,1)S(1)}, bf16[1,768,256]{2,1,0:T(8,128)(2,1)S(1)}) custom-call(s32[5]{0:T(128)S(1)} %stack.43.where_ref, bf16[768,1024]{1,0:T(8,128)(2,1)S(1)} %get-tuple-element.73.left_ref.x_ref, bf16[2,1024,4096]{2,1,0:T(8,128)(2,1)} %w1_ref.19, bf16[2,1024,4096]{2,1,0:T(8,128)(2,1)} %w1_ref.19), custom_call_target="tpu_custom_call" | custom-call | flops 1000 | bytes 1000 | tf_op jit(solution)/shard_map/product/pallas_call | solution.py:114
  66.1 2.7 %product.13 = (bf16[1,768,256]{2,1,0:T(8,128)(2,1)S(1)}, bf16[1,768,256]{2,1,0:T(8,128)(2,1)S(1)}) custom-call(s32[5]{0:T(128)S(1)} %stack.43.where_ref, bf16[768,1024]{1,0:T(8,128)(2,1)S(1)} %get-tuple-element.73.left_ref.x_ref, bf16[2,1024,4096]{2,1,0:T(8,128)(2,1)} %w1_ref.19, bf16[2,1024,4096]{2,1,0:T(8,128)(2,1)} %w1_ref.19), custom_call_target="tpu_custom_call" | custom-call | flops 1000 | bytes 1000 | tf_op jit(solution)/shard_map/product/pallas_call | solution.py:114
  68.9 2.5 %collective-permute-start.13 = (bf16[1,768,256]{2,1,0:T(8,128)(2,1)}, bf16[1,768,256]{2,1,0:T(8,128)(2,1)S(1)}, u32[]{:S(2)}, u32[]{:S(2)}) collective-permute-start(bf16[1,768,256]{2,1,0:T(8,128)(2,1)} %add_convert_fusion.2), channel_id=1, source_target_pairs={{0,2},{2,0},{1,3},{3,1},{4,6},{6,4},{5,7},{7,5},{8,10},{10,8},{9,1... | collective-permute-start | bytes 1179656 | tf_op jit(solution)/shard_map/ppermute | solution.py:28
  72.1 2.5 %collective-permute-start.18 = (bf16[1,768,256]{2,1,0:T(8,128)(2,1)S(1)}, bf16[1,768,256]{2,1,0:T(8,128)(2,1)S(1)}, u32[]{:S(2)}, u32[]{:S(2)}) collective-permute-start(bf16[1,768,256]{2,1,0:T(8,128)(2,1)S(1)} %add_convert_fusion.1), channel_id=1, source_target_pairs={{0,2},{2,0},{1,3},{3,1},{4,6},{6,4},{5,7},{7,5},{8,10},{10,8},{9,1... | collective-permute-start | bytes 1179656 | tf_op jit(solution)/shard_map/ppermute | solution.py:28
  75.4 3.5 %product.14 = (bf16[1,768,256]{2,1,0:T(8,128)(2,1)}, bf16[1,768,256]{2,1,0:T(8,128)(2,1)S(1)}) custom-call(s32[5]{0:T(128)S(1)} %stack.43.where_ref, bf16[768,1024]{1,0:T(8,128)(2,1)S(1)} %get-tuple-element.73.left_ref.x_ref, bf16[2,1024,4096]{2,1,0:T(8,128)(2,1)} %w1_ref.19, bf16[2,1024,4096]{2,1,0:T(8,128)(2,1)} %w1_ref.19), custom_call_target="tpu_custom_call" | custom-call | flops 1000 | bytes 1000 | tf_op jit(solution)/shard_map/product/pallas_call | solution.py:114
  81.0 16.8 %collective-permute-done.18.other_ref = bf16[1,768,256]{2,1,0:T(8,128)(2,1)S(1)} collective-permute-done((bf16[1,768,256]{2,1,0:T(8,128)(2,1)S(1)}, bf16[1,768,256]{2,1,0:T(8,128)(2,1)S(1)}, u32[]{:S(2)}, u32[]{:S(2)}) %collective-permute-start.18) | collective-permute-done | bytes 393248 | tf_op jit(solution)/shard_map/ppermute | solution.py:28
  100.2 2.7 %product.16 = (bf16[1,768,256]{2,1,0:T(8,128)(2,1)S(1)}, bf16[1,768,256]{2,1,0:T(8,128)(2,1)S(1)}) custom-call(s32[5]{0:T(128)S(1)} %stack.43.where_ref, bf16[768,1024]{1,0:T(8,128)(2,1)S(1)} %get-tuple-element.73.left_ref.x_ref, bf16[2,1024,4096]{2,1,0:T(8,128)(2,1)} %w1_ref.19, bf16[2,1024,4096]{2,1,0:T(8,128)(2,1)} %w1_ref.19), custom_call_target="tpu_custom_call" | custom-call | flops 1000 | bytes 1000 | tf_op jit(solution)/shard_map/product/pallas_call | solution.py:114
  103.1 2.7 %product.17 = (bf16[1,768,256]{2,1,0:T(8,128)(2,1)S(1)}, bf16[1,768,256]{2,1,0:T(8,128)(2,1)S(1)}) custom-call(s32[5]{0:T(128)S(1)} %stack.43.where_ref, bf16[768,1024]{1,0:T(8,128)(2,1)S(1)} %get-tuple-element.73.left_ref.x_ref, bf16[2,1024,4096]{2,1,0:T(8,128)(2,1)} %w1_ref.19, bf16[2,1024,4096]{2,1,0:T(8,128)(2,1)} %w1_ref.19), custom_call_target="tpu_custom_call" | custom-call | flops 1000 | bytes 1000 | tf_op jit(solution)/shard_map/product/pallas_call | solution.py:114
  106.4 2.5 %collective-permute-start.20 = (bf16[1,768,256]{2,1,0:T(8,128)(2,1)S(1)}, bf16[1,768,256]{2,1,0:T(8,128)(2,1)S(1)}, u32[]{:S(2)}, u32[]{:S(2)}) collective-permute-start(bf16[1,768,256]{2,1,0:T(8,128)(2,1)S(1)} %copy-done.10), channel_id=1, source_target_pairs={{0,2},{2,0},{1,3},{3,1},{4,6},{6,4},{5,7},{7,5},{8,10},{10,8},{9,1... | collective-permute-start | bytes 1179656 | tf_op jit(solution)/shard_map/ppermute | solution.py:28
  108.9 2.7 %product.19 = (bf16[1,768,256]{2,1,0:T(8,128)(2,1)S(1)}, bf16[1,768,256]{2,1,0:T(8,128)(2,1)S(1)}) custom-call(s32[5]{0:T(128)S(1)} %stack.43.where_ref, bf16[768,1024]{1,0:T(8,128)(2,1)S(1)} %get-tuple-element.73.left_ref.x_ref, bf16[2,1024,4096]{2,1,0:T(8,128)(2,1)} %w1_ref.19, bf16[2,1024,4096]{2,1,0:T(8,128)(2,1)} %w1_ref.19), custom_call_target="tpu_custom_call" | custom-call | flops 1000 | bytes 1000 | tf_op jit(solution)/shard_map/product/pallas_call | solution.py:114
  112.3 2.4 %second_layer.4 = (f32[8,768]{1,0:T(8,128)S(1)}, f32[48,256]{1,0:T(8,128)S(1)}) custom-call(bf16[768,1024]{1,0:T(8,128)(2,1)S(1)} %get-tuple-element.73.left_ref.x_ref, f32[8,768]{1,0:T(8,128)S(1)} %add.71.l0, f32[8,768]{1,0:T(8,128)S(1)} %collective-permute-done.6.l1, f32[8,768]{1,0:T(8,128)S(1)} %add.72.s0, f32[8,768]{1,0:T(8,128)S(1)} %collective-permute-done.8.s1, ...), custom_call_target="tpu_custom_call" | custom-call | flops 1000 | bytes 1000 | tf_op jit(solution)/shard_map/second_layer/pallas_call | solution.py:314
  117.7 5.4 %weight_step.1 = (f32[2,1024,128]{2,1,0:T(8,128)S(1)}, bf16[2,1024,128]{2,1,0:T(8,128)(2,1)}) custom-call(s32[5]{0:T(128)S(1)} %stack.43.where_ref, bf16[16,880,128]{2,1,0:T(8,128)(2,1)} %all-to-all-done.in_ref, bf16[16,112,128]{2,1,0:T(8,128)(2,1)S(1)} %collective-permute-done.21.peer_ref), custom_call_target="tpu_custom_call" | custom-call | flops 1000 | bytes 1000 | tf_op jit(solution)/shard_map/weight_step/pallas_call | solution.py:393
  126.5 3.4 %collective-permute-done.23 = f32[8,768]{1,0:T(8,128)S(1)} collective-permute-done((f32[8,768]{1,0:T(8,128)S(1)}, f32[8,768]{1,0:T(8,128)S(1)}, u32[]{:S(2)}, u32[]{:S(2)}) %collective-permute-start.23) | collective-permute-done | bytes 24608 | tf_op jit(solution)/shard_map/ppermute | solution.py:28
  131.9 7.7 %collective-permute-done.24 = bf16[2,1024,128]{2,1,0:T(8,128)(2,1)S(1)} collective-permute-done((bf16[2,1024,128]{2,1,0:T(8,128)(2,1)}, bf16[2,1024,128]{2,1,0:T(8,128)(2,1)S(1)}, u32[]{:S(2)}, u32[]{:S(2)}) %collective-permute-start.24) | collective-permute-done | bytes 524320 | tf_op jit(solution)/shard_map/ppermute | solution.py:28
  (117 shorter events, 39.0 us)
Async XLA Ops:
  0.6 8.2 %collective-permute-start.1 = (s32[12]{0:T(128)}, s32[12]{0:T(128)S(1)}, u32[]{:S(2)}, u32[]{:S(2)}) collective-permute-start(s32[12]{0:T(128)} %param.10), channel_id=1, source_target_pairs={{0,16},{16,0},{1,17},{17,1},{2,18},{18,2},{3,19},{19,3},{4,20},{20... | collective-permute-start | bytes 152 | tf_op jit(solution)/shard_map/ppermute | solution.py:28
  7.5 6.7 %collective-permute-start = (bf16[2,256,512]{2,1,0:T(8,128)(2,1)S(1)}, bf16[2,256,512]{2,1,0:T(8,128)(2,1)}, u32[]{:S(2)}, u32[]{:S(2)}) collective-permute-start(bf16[2,256,512]{2,1,0:T(8,128)(2,1)S(1)} %get-tuple-element.58), channel_id=1, source_target_pairs={{0,1},{1,0},{2,3},{3,2},{4,5},{5,4},{6,7},{7,6},{8,9},{9,8},{10,11... | collective-permute-start | bytes 1572872 | tf_op jit(solution)/shard_map/ppermute | solution.py:28
  19.8 78.1 %all-to-all-start = ((bf16[16,880,128]{2,1,0:T(8,128)(2,1)}), bf16[16,880,128]{2,1,0:T(8,128)(2,1)}, u32[]{:S(2)}, u32[]{:S(2)}) async-start(bf16[16,880,128]{2,1,0:T(8,128)(2,1)} %copy-done.2), calls=%async_computation | async-start | bytes 7208960 | tf_op jit(solution)/shard_map/all_to_all | solution.py:454
  27.6 15.5 %collective-permute-start.5 = (bf16[2,256,512]{2,1,0:T(8,128)(2,1)}, bf16[2,256,512]{2,1,0:T(8,128)(2,1)S(1)}, u32[]{:S(2)}, u32[]{:S(2)}) collective-permute-start(bf16[2,256,512]{2,1,0:T(8,128)(2,1)} %add_convert_fusion), channel_id=1, source_target_pairs={{0,2},{2,0},{1,3},{3,1},{4,6},{6,4},{5,7},{7,5},{8,10},{10,8},{9,1... | collective-permute-start | bytes 1572872 | tf_op jit(solution)/shard_map/ppermute | solution.py:28
  30.2 2.0 %collective-permute-start.3 = (bf16[1,256,512]{2,1,0:T(8,128)(2,1)S(1)}, bf16[1,256,512]{2,1,0:T(8,128)(2,1)S(1)}, u32[]{:S(2)}, u32[]{:S(2)}) collective-permute-start(bf16[1,256,512]{2,1,0:T(8,128)(2,1)S(1)} %get-tuple-element.121), channel_id=1, source_target_pairs={{0,1},{1,0},{2,3},{3,2},{4,5},{5,4},{6,7},{7,6},{8,9},{9,8},{10,11... | collective-permute-start | bytes 786440 | tf_op jit(solution)/shard_map/ppermute | solution.py:28
  31.0 1.5 %collective-permute-start.4 = (bf16[1,256,512]{2,1,0:T(8,128)(2,1)S(1)}, bf16[1,256,512]{2,1,0:T(8,128)(2,1)S(1)}, u32[]{:S(2)}, u32[]{:S(2)}) collective-permute-start(bf16[1,256,512]{2,1,0:T(8,128)(2,1)S(1)} %get-tuple-element.120), channel_id=1, source_target_pairs={{0,1},{1,0},{2,3},{3,2},{4,5},{5,4},{6,7},{7,6},{8,9},{9,8},{10,11... | collective-permute-start | bytes 786440 | tf_op jit(solution)/shard_map/ppermute | solution.py:28
  31.1 12.0 %collective-permute-start.6 = (f32[8,768]{1,0:T(8,128)S(1)}, f32[8,768]{1,0:T(8,128)S(1)}, u32[]{:S(2)}, u32[]{:S(2)}) collective-permute-start(f32[8,768]{1,0:T(8,128)S(1)} %add.71.l0), channel_id=1, source_target_pairs={{0,2},{2,0},{1,3},{3,1},{4,6},{6,4},{5,7},{7,5},{8,10},{10,8},{9,1... | collective-permute-start | bytes 73736 | tf_op jit(solution)/shard_map/ppermute | solution.py:28
  46.7 2.1 %collective-permute-start.7 = (f32[8,768]{1,0:T(8,128)S(1)}, f32[8,768]{1,0:T(8,128)S(1)}, u32[]{:S(2)}, u32[]{:S(2)}) collective-permute-start(f32[8,768]{1,0:T(8,128)S(1)} %constant_dynamic-update-slice_fusion.2), channel_id=1, source_target_pairs={{0,1},{1,0},{2,3},{3,2},{4,5},{5,4},{6,7},{7,6},{8,9},{9,8},{10,11... | collective-permute-start | bytes 73736 | tf_op jit(solution)/shard_map/ppermute | solution.py:28
  48.8 4.6 %collective-permute-start.8 = (f32[8,768]{1,0:T(8,128)S(1)}, f32[8,768]{1,0:T(8,128)S(1)}, u32[]{:S(2)}, u32[]{:S(2)}) collective-permute-start(f32[8,768]{1,0:T(8,128)S(1)} %add.72.s0), channel_id=1, source_target_pairs={{0,2},{2,0},{1,3},{3,1},{4,6},{6,4},{5,7},{7,5},{8,10},{10,8},{9,1... | collective-permute-start | bytes 73736 | tf_op jit(solution)/shard_map/ppermute | solution.py:28
  56.8 4.0 %collective-permute-start.12 = (bf16[1,768,256]{2,1,0:T(8,128)(2,1)S(1)}, bf16[1,768,256]{2,1,0:T(8,128)(2,1)S(1)}, u32[]{:S(2)}, u32[]{:S(2)}) collective-permute-start(bf16[1,768,256]{2,1,0:T(8,128)(2,1)S(1)} %get-tuple-element.83), channel_id=1, source_target_pairs={{0,1},{1,0},{2,3},{3,2},{4,5},{5,4},{6,7},{7,6},{8,9},{9,8},{10,11... | collective-permute-start | bytes 1179656 | tf_op jit(solution)/shard_map/ppermute | solution.py:28
  60.8 4.4 %collective-permute-start.9 = (bf16[1,768,256]{2,1,0:T(8,128)(2,1)S(1)}, bf16[1,768,256]{2,1,0:T(8,128)(2,1)S(1)}, u32[]{:S(2)}, u32[]{:S(2)}) collective-permute-start(bf16[1,768,256]{2,1,0:T(8,128)(2,1)S(1)} %get-tuple-element.75), channel_id=1, source_target_pairs={{0,1},{1,0},{2,3},{3,2},{4,5},{5,4},{6,7},{7,6},{8,9},{9,8},{10,11... | collective-permute-start | bytes 1179656 | tf_op jit(solution)/shard_map/ppermute | solution.py:28
  64.4 7.5 %collective-permute-start.17 = (bf16[1,768,256]{2,1,0:T(8,128)(2,1)S(1)}, bf16[1,768,256]{2,1,0:T(8,128)(2,1)S(1)}, u32[]{:S(2)}, u32[]{:S(2)}) collective-permute-start(bf16[1,768,256]{2,1,0:T(8,128)(2,1)S(1)} %get-tuple-element.95), channel_id=1, source_target_pairs={{0,1},{1,0},{2,3},{3,2},{4,5},{5,4},{6,7},{7,6},{8,9},{9,8},{10,11... | collective-permute-start | bytes 1179656 | tf_op jit(solution)/shard_map/ppermute | solution.py:28
  68.8 5.8 %collective-permute-start.10 = (bf16[1,768,256]{2,1,0:T(8,128)(2,1)S(1)}, bf16[1,768,256]{2,1,0:T(8,128)(2,1)S(1)}, u32[]{:S(2)}, u32[]{:S(2)}) collective-permute-start(bf16[1,768,256]{2,1,0:T(8,128)(2,1)S(1)} %get-tuple-element.78), channel_id=1, source_target_pairs={{0,1},{1,0},{2,3},{3,2},{4,5},{5,4},{6,7},{7,6},{8,9},{9,8},{10,11... | collective-permute-start | bytes 1179656 | tf_op jit(solution)/shard_map/ppermute | solution.py:28
  68.9 31.3 %collective-permute-start.13 = (bf16[1,768,256]{2,1,0:T(8,128)(2,1)}, bf16[1,768,256]{2,1,0:T(8,128)(2,1)S(1)}, u32[]{:S(2)}, u32[]{:S(2)}) collective-permute-start(bf16[1,768,256]{2,1,0:T(8,128)(2,1)} %add_convert_fusion.2), channel_id=1, source_target_pairs={{0,2},{2,0},{1,3},{3,1},{4,6},{6,4},{5,7},{7,5},{8,10},{10,8},{9,1... | collective-permute-start | bytes 1179656 | tf_op jit(solution)/shard_map/ppermute | solution.py:28
  71.4 31.6 %collective-permute-start.15 = (bf16[1,768,256]{2,1,0:T(8,128)(2,1)}, bf16[1,768,256]{2,1,0:T(8,128)(2,1)S(1)}, u32[]{:S(2)}, u32[]{:S(2)}) collective-permute-start(bf16[1,768,256]{2,1,0:T(8,128)(2,1)} %add_convert_fusion.4), channel_id=1, source_target_pairs={{0,2},{2,0},{1,3},{3,1},{4,6},{6,4},{5,7},{7,5},{8,10},{10,8},{9,1... | collective-permute-start | bytes 1179656 | tf_op jit(solution)/shard_map/ppermute | solution.py:28
  72.1 25.8 %collective-permute-start.18 = (bf16[1,768,256]{2,1,0:T(8,128)(2,1)S(1)}, bf16[1,768,256]{2,1,0:T(8,128)(2,1)S(1)}, u32[]{:S(2)}, u32[]{:S(2)}) collective-permute-start(bf16[1,768,256]{2,1,0:T(8,128)(2,1)S(1)} %add_convert_fusion.1), channel_id=1, source_target_pairs={{0,2},{2,0},{1,3},{3,1},{4,6},{6,4},{5,7},{7,5},{8,10},{10,8},{9,1... | collective-permute-start | bytes 1179656 | tf_op jit(solution)/shard_map/ppermute | solution.py:28
  79.8 31.8 %collective-permute-start.11 = (bf16[1,768,256]{2,1,0:T(8,128)(2,1)}, bf16[1,768,256]{2,1,0:T(8,128)(2,1)}, u32[]{:S(2)}, u32[]{:S(2)}) collective-permute-start(bf16[1,768,256]{2,1,0:T(8,128)(2,1)} %get-tuple-element.81), channel_id=1, source_target_pairs={{0,1},{1,0},{2,3},{3,2},{4,5},{5,4},{6,7},{7,6},{8,9},{9,8},{10,11... | collective-permute-start | bytes 1179656 | tf_op jit(solution)/shard_map/ppermute | solution.py:28
  98.9 18.8 %collective-permute-start.21 = (bf16[16,112,128]{2,1,0:T(8,128)(2,1)S(1)}, bf16[16,112,128]{2,1,0:T(8,128)(2,1)S(1)}, u32[]{:S(2)}, u32[]{:S(2)}) collective-permute-start(bf16[16,112,128]{2,1,0:T(8,128)(2,1)S(1)} %slice.39), channel_id=1, source_target_pairs={{0,1},{1,0},{2,3},{3,2},{4,5},{5,4},{6,7},{7,6},{8,9},{9,8},{10,11... | collective-permute-start | bytes 1376264 | tf_op jit(solution)/shard_map/ppermute | solution.py:28
  103.0 11.8 %collective-permute-start.14 = (bf16[1,768,256]{2,1,0:T(8,128)(2,1)S(1)}, bf16[1,768,256]{2,1,0:T(8,128)(2,1)S(1)}, u32[]{:S(2)}, u32[]{:S(2)}) collective-permute-start(bf16[1,768,256]{2,1,0:T(8,128)(2,1)S(1)} %get-tuple-element.87), channel_id=1, source_target_pairs={{0,1},{1,0},{2,3},{3,2},{4,5},{5,4},{6,7},{7,6},{8,9},{9,8},{10,11... | collective-permute-start | bytes 1179656 | tf_op jit(solution)/shard_map/ppermute | solution.py:28
  105.8 10.3 %collective-permute-start.16 = (bf16[1,768,256]{2,1,0:T(8,128)(2,1)S(1)}, bf16[1,768,256]{2,1,0:T(8,128)(2,1)S(1)}, u32[]{:S(2)}, u32[]{:S(2)}) collective-permute-start(bf16[1,768,256]{2,1,0:T(8,128)(2,1)S(1)} %get-tuple-element.92), channel_id=1, source_target_pairs={{0,1},{1,0},{2,3},{3,2},{4,5},{5,4},{6,7},{7,6},{8,9},{9,8},{10,11... | collective-permute-start | bytes 1179656 | tf_op jit(solution)/shard_map/ppermute | solution.py:28
  106.4 16.7 %collective-permute-start.20 = (bf16[1,768,256]{2,1,0:T(8,128)(2,1)S(1)}, bf16[1,768,256]{2,1,0:T(8,128)(2,1)S(1)}, u32[]{:S(2)}, u32[]{:S(2)}) collective-permute-start(bf16[1,768,256]{2,1,0:T(8,128)(2,1)S(1)} %copy-done.10), channel_id=1, source_target_pairs={{0,2},{2,0},{1,3},{3,1},{4,6},{6,4},{5,7},{7,5},{8,10},{10,8},{9,1... | collective-permute-start | bytes 1179656 | tf_op jit(solution)/shard_map/ppermute | solution.py:28
  111.6 11.5 %collective-permute-start.19 = (bf16[1,768,256]{2,1,0:T(8,128)(2,1)S(1)}, bf16[1,768,256]{2,1,0:T(8,128)(2,1)S(1)}, u32[]{:S(2)}, u32[]{:S(2)}) collective-permute-start(bf16[1,768,256]{2,1,0:T(8,128)(2,1)S(1)} %get-tuple-element.100), channel_id=1, source_target_pairs={{0,1},{1,0},{2,3},{3,2},{4,5},{5,4},{6,7},{7,6},{8,9},{9,8},{10,11... | collective-permute-start | bytes 1179656 | tf_op jit(solution)/shard_map/ppermute | solution.py:28
  125.8 4.2 %collective-permute-start.23 = (f32[8,768]{1,0:T(8,128)S(1)}, f32[8,768]{1,0:T(8,128)S(1)}, u32[]{:S(2)}, u32[]{:S(2)}) collective-permute-start(f32[8,768]{1,0:T(8,128)S(1)} %add.77), channel_id=1, source_target_pairs={{0,2},{2,0},{1,3},{3,1},{4,6},{6,4},{5,7},{7,5},{8,10},{10,8},{9,1... | collective-permute-start | bytes 73736 | tf_op jit(solution)/shard_map/ppermute | solution.py:28
  126.3 13.3 %collective-permute-start.24 = (bf16[2,1024,128]{2,1,0:T(8,128)(2,1)}, bf16[2,1024,128]{2,1,0:T(8,128)(2,1)S(1)}, u32[]{:S(2)}, u32[]{:S(2)}) collective-permute-start(bf16[2,1024,128]{2,1,0:T(8,128)(2,1)} %get-tuple-element.110), channel_id=1, source_target_pairs={{0,16},{16,0},{1,17},{17,1},{2,18},{18,2},{3,19},{19,3},{4,20},{20... | collective-permute-start | bytes 1572872 | tf_op jit(solution)/shard_map/ppermute | solution.py:28
  (17 other events, 88.3 us)

commit v4 on v3

--- a/solution.py
+++ b/solution.py
@@ -95,7 +95,7 @@
     )(where, digits, factors_in, factors_out)
 
 
-def product(layer, rel, where, left, weights, piece, first=0, count=1):
+def product(layer, where, left, weights, piece):
     rows, width = left.shape
     per_owner = width // piece
 
@@ -106,24 +106,77 @@
             ).astype(bf16)
 
     def block(flip):
-        def at(n, s):
-            return (layer, 0, ((s[1] ^ rel) * 2 + (s[2] ^ flip)) * per_owner + first + n)
+        def at(i, s):
+            half = s[1] ^ (1 - i // per_owner)
+            return (layer, 0, (half * 2 + (s[2] ^ flip)) * per_owner + i % per_owner)
 
         return pl.BlockSpec((1, width, piece), at)
 
+    count = 2 * per_owner
     return pl.pallas_call(
         kernel,
         grid_spec=pltpu.PrefetchScalarGridSpec(
             num_scalar_prefetch=1,
             grid=(count,),
             in_specs=[VMEM, block(1), block(0)],
-            out_specs=[pl.BlockSpec((1, rows, piece), lambda n, s: (n, 0, 0))] * 2,
+            out_specs=[pl.BlockSpec((1, rows, piece), lambda i, s: (i, 0, 0))] * 2,
         ),
         out_shape=[jax.ShapeDtypeStruct((count, rows, piece), bf16)] * 2,
         compiler_params=params(48),
         name="product",
         cost_estimate=small_cost,
     )(where, left, weights, weights)
+
+
+def stay(layer, weights):
+    _, width, full = weights.shape
+    cuts = 8
+    rows = width // cuts
+
+    def kernel(w_ref, out_ref, sems):
+        def part(i):
+            span = slice(i * rows, (i + 1) * rows)
+            return pltpu.make_async_copy(w_ref.at[layer, span], out_ref.at[span], sems.at[i])
+
+        for i in range(cuts):
+            part(i).start()
+        for i in range(cuts):
+            part(i).wait()
+
+    return pl.pallas_call(
+        kernel,
+        out_shape=jax.ShapeDtypeStruct((width, full), bf16),
+        in_specs=[pl.BlockSpec(memory_space=pltpu.HBM)],
+        out_specs=VMEM,
+        scratch_shapes=[pltpu.SemaphoreType.DMA((cuts,))],
+        compiler_params=params(40),
+        name="stay",
+        cost_estimate=small_cost,
+    )(weights)
+
+
+def dense(rel, where, left, weights, piece, first=0, count=1, earlier=()):
+    rows, width = left.shape
+
+    def kernel(where_ref, left_ref, w_ref, *refs):
+        out0_ref, out1_ref = refs[len(earlier) :]
+        for flip, out_ref in ((1, out0_ref), (0, out1_ref)):
+            owner = (where_ref[1] ^ rel) * 2 + (where_ref[2] ^ flip)
+            for n in range(count):
+                at = pl.multiple_of(owner * width + (first + n) * piece, piece)
+                out_ref[n] = jnp.dot(
+                    left_ref[...], w_ref[:, pl.ds(at, piece)], preferred_element_type=f32
+                ).astype(bf16)
+
+    return pl.pallas_call(
+        kernel,
+        out_shape=[jax.ShapeDtypeStruct((count, rows, piece), bf16)] * 2,
+        in_specs=[SMEM, VMEM, VMEM] + [pl.BlockSpec(memory_space=pl.ANY)] * len(earlier),
+        out_specs=[VMEM] * 2,
+        compiler_params=params(16),
+        name="dense",
+        cost_estimate=small_cost,
+    )(where, left, weights, *earlier)
 
 
 def member_of(shape, per, dim):
@@ -194,7 +247,8 @@
         for n in range(width // 256):
             cols = slice(n * 256, (n + 1) * 256)
             in_half = slice(n % 2 * 256, n % 2 * 256 + 256)
-            table = sum(t[n // 2, :, in_half].astype(f32) for t in (t0, t1, t2)).astype(bf16)
+            parts = (t0[2 + n // 2, :, in_half], t1[2 + n // 2, :, in_half], t2[n // 2, :, in_half])
+            table = sum(p.astype(f32) for p in parts).astype(bf16)
             factor = jnp.concatenate([b_ref[2 * n, mine], b_ref[2 * n + 1, mine]], axis=1)
             u = jnp.dot(o_ref[at], table, preferred_element_type=f32) + dot(
                 spread_low, factor, 0, 0
@@ -326,14 +380,14 @@
     )(hidden, *lows, *stats, *halves, crossed, out_factors, decay, gain, reward, before)
 
 
-def step_kernel(where, arrived, arrived_peer, members, members_all, scale):
+def step_kernel(where, arrived, arrived_peer, members, members_all, scale, earlier):
     pops, rows, lanes = arrived.shape
     k = members * 8
     part = k // 2 + 8
     blocks = (rows - 2 * part) // k
     width = blocks * lanes
 
-    def kernel(where_ref, in_ref, peer_ref, mine_ref, theirs_ref, paired, digit_rows):
+    def kernel(where_ref, in_ref, peer_ref, _, mine_ref, theirs_ref, paired, digit_rows):
         xl, c = where_ref[4], where_ref[2]
         head = blocks * k
         for p in range(pops):
@@ -396,7 +450,7 @@
             jax.ShapeDtypeStruct((2, width, lanes), f32),
             jax.ShapeDtypeStruct((2, width, lanes), bf16),
         ],
-        in_specs=[SMEM, VMEM, VMEM],
+        in_specs=[SMEM, VMEM, VMEM, pl.BlockSpec(memory_space=pl.ANY)],
         out_specs=[VMEM, VMEM],
         scratch_shapes=[
             pltpu.VMEM((pops * k, 4 * lanes), bf16),
@@ -405,7 +459,7 @@
         compiler_params=params(24),
         name="weight_step",
         cost_estimate=small_cost,
-    )(where, arrived, arrived_peer)
+    )(where, arrived, arrived_peer, earlier)
 
 
 def shards(
@@ -437,10 +491,11 @@
     def added(a, b):
         return (a.astype(f32) + b.astype(f32)).astype(bf16)
 
-    peer, own = product(0, 1, where, embedding, mix_weights, 512, 0, 2)
-    cross = added(own, swap(peer, "c"))
-    table_cross = swap(cross, "xh")
-    both = jnp.stack([fitness_ranks, swap(fitness_ranks, "xl")])
+    peer, own = product(0, where, embedding, mix_weights, 512)
+    theirs = swap(peer, "c")
+    cross = added(own[:2], theirs[:2])
+    first_table = [own, theirs, swap(cross, "xh")]
+    both = jnp.stack([fitness_ranks, swap(after(fitness_ranks, peer), "xl")])
     digits = jnp.stack([both[0] // 32, both[0] % 32, both[1] // 32, both[1] % 32]).astype(bf16)
     digits = jnp.pad(digits, ((0, 4), (0, 128 - members)))
     pops = lax.axis_size("y") * lax.axis_size("z")
@@ -448,10 +503,7 @@
         after(where, peer), digits, factors_in, factors_out, pops
     )
     lows = mp_parts(low_kernel(after(onehot, peer), embedding, a_blocks))
-    peer, own = product(0, 0, after(where, cross, lows[0]), embedding, mix_weights, 512, 0, 2)
-    keep = jnp.concatenate([swap(peer[:1], "c"), swap(peer[1:], "c")])
-    first_table = [own, keep, table_cross]
-    arrived = lax.all_to_all(after(packed, own), ("y", "z"), 0, 0, tiled=True)
+    arrived = lax.all_to_all(after(packed, cross, lows[0]), ("y", "z"), 0, 0, tiled=True)
 
     decay = [decay_rates[l : l + 1] for l in range(2)]
     gain = [norm_gain[l : l + 1] for l in range(2)]
@@ -463,29 +515,30 @@
         lifted.append(up)
         stats.append(st)
     stats = mp_parts(jnp.concatenate(stats, axis=1))
+    late_weights = stay(1, after(mix_weights, stats[0]))
     hidden, last_hidden = next_hidden(full_width, onehot, embedding, stats, lifted)
-    sent, parts, halves = [], [], []
+    sent, parts = [], []
     for n in range(4):
-        at = after(where, parts[n - 2]) if n > 1 else where
-        peer, own = product(1, 1, at, hidden, mix_weights, 256, n)
+        earlier = parts[n - 2 : n - 1] if n > 1 else ()
+        peer, own = dense(1, where, hidden, late_weights, 256, n, 1, earlier)
         parts.append(added(own, swap(peer, "c")))
         sent.append(swap(parts[n], "xh"))
+    halves = []
     for n in range(4):
-        at = after(where, sent[n - 1]) if n > 0 else after(where, parts[3])
-        peer, own = product(1, 0, at, hidden, mix_weights, 256, n)
+        peer, own = dense(0, where, hidden, late_weights, 256, n, 1, (sent[max(n - 1, 0)],))
         halves.append((own, swap(peer, "c")))
-
-    outs_rows = 2 * (members * rank_count + 8)
-    arrived = after(arrived, sent[2])
-    arrived_peer = swap(arrived[:, -outs_rows:], "c")
-    step_mine, step_theirs = step_kernel(
-        where, arrived, arrived_peer, members, members_all, (members_all * rank_count) ** (-0.5)
-    )
 
     st = jnp.zeros((8, rows_all), f32)
     lasts = []
     for n in range(4):
-        if n == 3:
+        if n == 1:
+            outs_rows = 2 * (members * rank_count + 8)
+            arrived_peer = swap(after(arrived, st)[:, -outs_rows:], "c")
+        if n == 2:
+            step_mine, step_theirs = step_kernel(
+                where, arrived, arrived_peer, members, members_all,
+                (members_all * rank_count) ** (-0.5), st,
+            )
             st = after(st, step_theirs)
         st, last = second_layer(
             n, coef, full_width, hidden, lows, stats, halves[n], sent[n], b_own,

time: 141 us -> 129 us (0.915)
  waiting for transfers between devices: 44.4 us -> 32.3 us
  Pallas kernels: 48.4 us -> 43.1 us
  local copies, waits for them, and re-layouts: 6.82 us -> 11.7 us
    pallas_call x10 -> x1, Pallas kernels: 29.8 us -> 6.45 us  [product(): pl.pallas_call(kernel, grid_spec=pltpu.PrefetchScalarGridSpec(num_scalar_...]
    pallas_call x0 -> x9, Pallas kernels: none -> 18 us  [the longest x8 14.6 us: dense(): pl.pallas_call(kernel, out_shape=[jax.ShapeDtypeStruct((count, rows, piec...]
    ppermute x25 -> x23, waiting for transfers between devices: 44.4 us -> 32.3 us  [swap(): return lax.ppermute(value, axis, [(0, 1), (1, 0)])]
    unnamed x34 -> x43, local copies, waits for them, and re-layouts: 4.38 us -> 9.25 us
    ppermute x25 -> x23, starting transfers between devices: 26 us -> 25.2 us  [swap(): return lax.ppermute(value, axis, [(0, 1), (1, 0)])]
  transfers between devices with their start and end apart: 26 -> 24, of which waited for: 10 -> 8; matrix products, arithmetic and copies ran while one was open for 4% -> 5% of each run, Pallas kernels for 31% -> 28%
where the time goes in v4:
time: 129 us; the launch traced here: 128 us
  Pallas kernels  43.1 us (33%)
  starting transfers between devices  33.2 us (26%)
  waiting for transfers between devices  32.3 us (25%)
  local copies, waits for them, and re-layouts  11.7 us (9%)
  other arithmetic  6.78 us (5%)
    ppermute x23, waiting for transfers between devices, swap(): return lax.ppermute(value, axis, [(0, 1), (1, 0)])  32.3 us
    ppermute x23, starting transfers between devices, swap(): return lax.ppermute(value, axis, [(0, 1), (1, 0)])  25.2 us
    pallas_call x8, Pallas kernels, dense(): pl.pallas_call(kernel, out_shape=[jax.ShapeDtypeStruct((count, rows, piec...  14.6 us
    unnamed x43, local copies, waits for them, and re-layouts  9.25 us
    all_to_all x1, starting transfers between devices, shards(): lax.all_to_all(after(packed, cross, lows[0]), ('y', 'z'), 0, 0, tiled=True)  8.03 us
    pallas_call x4, Pallas kernels, second_layer(): pl.pallas_call(kernel, out_shape=[jax.ShapeDtypeStruct((8, total), f32),...  6.73 us
    pallas_call x1, Pallas kernels, product(): pl.pallas_call(kernel, grid_spec=pltpu.PrefetchScalarGridSpec(num_scalar_...  6.45 us
    pallas_call x1, Pallas kernels, step_kernel(): pl.pallas_call(kernel, out_shape=[jax.ShapeDtypeStruct((2, width, lanes),...  5.42 us
  transfers between devices with their start and end apart: 24, of which 8 were waited for; matrix products, arithmetic and copies ran while one was open for 5% of the time, Pallas kernels for 28%

profile of v4, /device:TPU:1, one launch (start us, length us, event | category | flops | bytes accessed | tf_op | source)
XLA Modules:
  0.0 128.0 jit_solution(14656702028670655884)
XLA Ops:
  1.8 6.4 %product.1 = (bf16[4,256,512]{2,1,0:T(8,128)(2,1)}, bf16[4,256,512]{2,1,0:T(8,128)(2,1)S(1)}) custom-call(s32[5]{0:T(128)S(1)} %stack.43.where_ref, bf16[256,1024]{1,0:T(8,128)(2,1)S(1)} %copy-done.2, bf16[2,1024,4096]{2,1,0:T(8,128)(2,1)} %w_ref, bf16[2,1024,4096]{2,1,0:T(8,128)(2,1)} %w_ref), custom_call_target="tpu_custom_call" | custom-call | flops 1000 | bytes 1000 | tf_op jit(solution)/shard_map/product/pallas_call | solution.py:116
  15.3 1.8 %copy-done.5 = bf16[16,880,128]{2,1,0:T(8,128)(2,1)} copy-done((bf16[16,880,128]{2,1,0:T(8,128)(2,1)}, bf16[16,880,128]{2,1,0:T(8,128)(2,1)S(1)}, u32[]{:S(2)}) %copy-start.5) | copy-done | bytes 3604504
  21.2 8.0 %all-to-all-start = ((bf16[16,880,128]{2,1,0:T(8,128)(2,1)}), bf16[16,880,128]{2,1,0:T(8,128)(2,1)}, u32[]{:S(2)}, u32[]{:S(2)}) async-start(bf16[16,880,128]{2,1,0:T(8,128)(2,1)} %copy-done.5), calls=%async_computation | async-start | bytes 7208960 | tf_op jit(solution)/shard_map/all_to_all | solution.py:506
  29.2 2.8 %collective-permute-start.1 = (bf16[2,256,512]{2,1,0:T(8,128)(2,1)}, bf16[2,256,512]{2,1,0:T(8,128)(2,1)S(1)}, u32[]{:S(2)}, u32[]{:S(2)}) collective-permute-start(bf16[2,256,512]{2,1,0:T(8,128)(2,1)} %add_convert_fusion), channel_id=1, source_target_pairs={{0,2},{2,0},{1,3},{3,1},{4,6},{6,4},{5,7},{7,5},{8,10},{10,8},{9,1... | collective-permute-start | bytes 1572872 | tf_op jit(solution)/shard_map/ppermute | solution.py:28
  32.3 12.2 %collective-permute-done.4.l1 = f32[8,768]{1,0:T(8,128)S(1)} collective-permute-done((f32[8,768]{1,0:T(8,128)S(1)}, f32[8,768]{1,0:T(8,128)S(1)}, u32[]{:S(2)}, u32[]{:S(2)}) %collective-permute-start.4) | collective-permute-done | bytes 24608 | tf_op jit(solution)/shard_map/ppermute | solution.py:28
  50.5 2.7 %collective-permute-start.6 = (f32[8,768]{1,0:T(8,128)S(1)}, f32[8,768]{1,0:T(8,128)S(1)}, u32[]{:S(2)}, u32[]{:S(2)}) collective-permute-start(f32[8,768]{1,0:T(8,128)S(1)} %add.72.s0), channel_id=1, source_target_pairs={{0,2},{2,0},{1,3},{3,1},{4,6},{6,4},{5,7},{7,5},{8,10},{10,8},{9,1... | collective-permute-start | bytes 73736 | tf_op jit(solution)/shard_map/ppermute | solution.py:28
  53.2 3.5 %stay.1.w_ref = bf16[1024,4096]{1,0:T(8,128)(2,1)S(1)} custom-call(bf16[2,1024,4096]{2,1,0:T(8,128)(2,1)} %w_ref), custom_call_target="tpu_custom_call" | custom-call | flops 1000 | bytes 1000 | tf_op jit(solution)/shard_map/stay/pallas_call | solution.py:146
  57.4 1.5 %dense.8 = (bf16[1,768,256]{2,1,0:T(8,128)(2,1)S(1)}, bf16[1,768,256]{2,1,0:T(8,128)(2,1)S(1)}) custom-call(s32[5]{0:T(128)S(1)} %stack.43.where_ref, bf16[768,1024]{1,0:T(8,128)(2,1)S(1)} %get-tuple-element.64.left_ref.x_ref, bf16[1024,4096]{1,0:T(8,128)(2,1)S(1)} %stay.1.w_ref), custom_call_target="tpu_custom_call" | custom-call | flops 1000 | bytes 1000 | tf_op jit(solution)/shard_map/dense/pallas_call | solution.py:171
  59.9 1.5 %dense.11 = (bf16[1,768,256]{2,1,0:T(8,128)(2,1)S(1)}, bf16[1,768,256]{2,1,0:T(8,128)(2,1)S(1)}) custom-call(s32[5]{0:T(128)S(1)} %stack.43.where_ref, bf16[768,1024]{1,0:T(8,128)(2,1)S(1)} %get-tuple-element.64.left_ref.x_ref, bf16[1024,4096]{1,0:T(8,128)(2,1)S(1)} %stay.1.w_ref), custom_call_target="tpu_custom_call" | custom-call | flops 1000 | bytes 1000 | tf_op jit(solution)/shard_map/dense/pallas_call | solution.py:171
  63.1 1.5 %dense.13 = (bf16[1,768,256]{2,1,0:T(8,128)(2,1)S(1)}, bf16[1,768,256]{2,1,0:T(8,128)(2,1)S(1)}) custom-call(s32[5]{0:T(128)S(1)} %stack.43.where_ref, bf16[768,1024]{1,0:T(8,128)(2,1)S(1)} %get-tuple-element.64.left_ref.x_ref, bf16[1024,4096]{1,0:T(8,128)(2,1)S(1)} %stay.1.w_ref, bf16[1,768,256]{2,1,0:T(8,128)(2,1)S(1)} %add_convert_fusion.4.refs_0_), custom_call_target="tpu_custom_call" | custom-call | flops 1000 | bytes 1000 | tf_op jit(solution)/shard_map/dense/pallas_call | solution.py:171
  65.6 1.7 %collective-permute-start.12 = (bf16[1,768,256]{2,1,0:T(8,128)(2,1)S(1)}, bf16[1,768,256]{2,1,0:T(8,128)(2,1)S(1)}, u32[]{:S(2)}, u32[]{:S(2)}) collective-permute-start(bf16[1,768,256]{2,1,0:T(8,128)(2,1)S(1)} %add_convert_fusion.3.refs_0_), channel_id=1, source_target_pairs={{0,2},{2,0},{1,3},{3,1},{4,6},{6,4},{5,7},{7,5},{8,10},{10,8},{9,1... | collective-permute-start | bytes 1179656 | tf_op jit(solution)/shard_map/ppermute | solution.py:28
  67.3 6.3 %collective-permute-done.8.refs_0_.other_ref = bf16[1,768,256]{2,1,0:T(8,128)(2,1)S(1)} collective-permute-done((bf16[1,768,256]{2,1,0:T(8,128)(2,1)S(1)}, bf16[1,768,256]{2,1,0:T(8,128)(2,1)S(1)}, u32[]{:S(2)}, u32[]{:S(2)}) %collective-permute-start.8) | collective-permute-done | bytes 393248 | tf_op jit(solution)/shard_map/ppermute | solution.py:28
  73.6 1.5 %dense.9 = (bf16[1,768,256]{2,1,0:T(8,128)(2,1)S(1)}, bf16[1,768,256]{2,1,0:T(8,128)(2,1)S(1)}) custom-call(s32[5]{0:T(128)S(1)} %stack.43.where_ref, bf16[768,1024]{1,0:T(8,128)(2,1)S(1)} %get-tuple-element.64.left_ref.x_ref, bf16[1024,4096]{1,0:T(8,128)(2,1)S(1)} %stay.1.w_ref, bf16[1,768,256]{2,1,0:T(8,128)(2,1)S(1)} %collective-permute-done.8.refs_0_.other_ref), custom_call_target="tpu_custom_call" | custom-call | flops 1000 | bytes 1000 | tf_op jit(solution)/shard_map/dense/pallas_call | solution.py:171
  75.1 2.4 %collective-permute-start.9 = (bf16[1,768,256]{2,1,0:T(8,128)(2,1)S(1)}, bf16[1,768,256]{2,1,0:T(8,128)(2,1)S(1)}, u32[]{:S(2)}, u32[]{:S(2)}) collective-permute-start(bf16[1,768,256]{2,1,0:T(8,128)(2,1)S(1)} %get-tuple-element.69), channel_id=1, source_target_pairs={{0,1},{1,0},{2,3},{3,2},{4,5},{5,4},{6,7},{7,6},{8,9},{9,8},{10,11... | collective-permute-start | bytes 1179656 | tf_op jit(solution)/shard_map/ppermute | solution.py:28
  77.5 2.3 %dense.15 = (bf16[1,768,256]{2,1,0:T(8,128)(2,1)}, bf16[1,768,256]{2,1,0:T(8,128)(2,1)S(1)}) custom-call(s32[5]{0:T(128)S(1)} %stack.43.where_ref, bf16[768,1024]{1,0:T(8,128)(2,1)S(1)} %get-tuple-element.64.left_ref.x_ref, bf16[1024,4096]{1,0:T(8,128)(2,1)S(1)} %stay.1.w_ref, bf16[1,768,256]{2,1,0:T(8,128)(2,1)S(1)} %add_convert_fusion.3.refs_0_), custom_call_target="tpu_custom_call" | custom-call | flops 1000 | bytes 1000 | tf_op jit(solution)/shard_map/dense/pallas_call | solution.py:171
  82.1 2.3 %dense.10 = (bf16[1,768,256]{2,1,0:T(8,128)(2,1)}, bf16[1,768,256]{2,1,0:T(8,128)(2,1)S(1)}) custom-call(s32[5]{0:T(128)S(1)} %stack.43.where_ref, bf16[768,1024]{1,0:T(8,128)(2,1)S(1)} %get-tuple-element.64.left_ref.x_ref, bf16[1024,4096]{1,0:T(8,128)(2,1)S(1)} %stay.1.w_ref, bf16[1,768,256]{2,1,0:T(8,128)(2,1)S(1)} %collective-permute-done.8.refs_0_.other_ref), custom_call_target="tpu_custom_call" | custom-call | flops 1000 | bytes 1000 | tf_op jit(solution)/shard_map/dense/pallas_call | solution.py:171
  85.2 2.3 %dense.12 = (bf16[1,768,256]{2,1,0:T(8,128)(2,1)}, bf16[1,768,256]{2,1,0:T(8,128)(2,1)S(1)}) custom-call(s32[5]{0:T(128)S(1)} %stack.43.where_ref, bf16[768,1024]{1,0:T(8,128)(2,1)S(1)} %get-tuple-element.64.left_ref.x_ref, bf16[1024,4096]{1,0:T(8,128)(2,1)S(1)} %stay.1.w_ref, bf16[1,768,256]{2,1,0:T(8,128)(2,1)S(1)} %collective-permute-done.12.other_ref.refs_0_), custom_call_target="tpu_custom_call" | custom-call | flops 1000 | bytes 1000 | tf_op jit(solution)/shard_map/dense/pallas_call | solution.py:171
  91.8 1.7 %collective-permute-start.19 = (bf16[1,768,256]{2,1,0:T(8,128)(2,1)S(1)}, bf16[1,768,256]{2,1,0:T(8,128)(2,1)S(1)}, u32[]{:S(2)}, u32[]{:S(2)}) collective-permute-start(bf16[1,768,256]{2,1,0:T(8,128)(2,1)S(1)} %add_convert_fusion.1), channel_id=1, source_target_pairs={{0,2},{2,0},{1,3},{3,1},{4,6},{6,4},{5,7},{7,5},{8,10},{10,8},{9,1... | collective-permute-start | bytes 1179656 | tf_op jit(solution)/shard_map/ppermute | solution.py:28
  93.5 3.4 %copy-done.1 = bf16[1024,4096]{1,0:T(8,128)(2,1)S(1)} copy-done((bf16[1024,4096]{1,0:T(8,128)(2,1)S(1)}, bf16[1024,4096]{1,0:T(8,128)(2,1)}, u32[]{:S(2)}) %copy-start.1) | copy-done | bytes 8388632
  99.0 2.4 %second_layer.5 = (f32[8,768]{1,0:T(8,128)S(1)}, f32[48,256]{1,0:T(8,128)S(1)}) custom-call(bf16[768,1024]{1,0:T(8,128)(2,1)S(1)} %get-tuple-element.64.left_ref.x_ref, f32[8,768]{1,0:T(8,128)S(1)} %add.71.l0, f32[8,768]{1,0:T(8,128)S(1)} %collective-permute-done.4.l1, f32[8,768]{1,0:T(8,128)S(1)} %add.72.s0, f32[8,768]{1,0:T(8,128)S(1)} %collective-permute-done.6.s1, ...), custom_call_target="tpu_custom_call" | custom-call | flops 1000 | bytes 1000 | tf_op jit(solution)/shard_map/second_layer/pallas_call | solution.py:368
  101.4 5.4 %weight_step.1 = (f32[2,1024,128]{2,1,0:T(8,128)S(1)}, bf16[2,1024,128]{2,1,0:T(8,128)(2,1)}) custom-call(s32[5]{0:T(128)S(1)} %stack.43.where_ref, bf16[16,880,128]{2,1,0:T(8,128)(2,1)} %all-to-all-done.in_ref, bf16[16,112,128]{2,1,0:T(8,128)(2,1)S(1)} %collective-permute-done.16.peer_ref, f32[8,768]{1,0:T(8,128)S(1)} %get-tuple-element.86._.before_ref), custom_call_target="tpu_custom_call" | custom-call | flops 1000 | bytes 1000 | tf_op jit(solution)/shard_map/weight_step/pallas_call | solution.py:447
  112.8 2.5 %collective-permute-done.21 = f32[8,768]{1,0:T(8,128)S(1)} collective-permute-done((f32[8,768]{1,0:T(8,128)S(1)}, f32[8,768]{1,0:T(8,128)S(1)}, u32[]{:S(2)}, u32[]{:S(2)}) %collective-permute-start.21) | collective-permute-done | bytes 24608 | tf_op jit(solution)/shard_map/ppermute | solution.py:28
  118.0 7.7 %collective-permute-done.22 = bf16[2,1024,128]{2,1,0:T(8,128)(2,1)S(1)} collective-permute-done((bf16[2,1024,128]{2,1,0:T(8,128)(2,1)}, bf16[2,1024,128]{2,1,0:T(8,128)(2,1)S(1)}, u32[]{:S(2)}, u32[]{:S(2)}) %collective-permute-start.22) | collective-permute-done | bytes 524320 | tf_op jit(solution)/shard_map/ppermute | solution.py:28
  125.7 2.3 %convert_add_fusion = f32[2,1024,128]{2,1,0:T(8,128)} fusion(f32[2,1024,128]{2,1,0:T(8,128)} %copy-done.6, bf16[2,1024,128]{2,1,0:T(8,128)(2,1)S(1)} %collective-permute-done.22), kind=kLoop, calls=%fused_computation | loop fusion | flops 524288 | bytes 2621440 | tf_op jit(solution)/shard_map/add | solution.py:548
  (120 shorter events, 40.8 us)
Async XLA Ops:
  8.2 12.0 %collective-permute-start = (bf16[4,256,512]{2,1,0:T(8,128)(2,1)}, bf16[4,256,512]{2,1,0:T(8,128)(2,1)S(1)}, u32[]{:S(2)}, u32[]{:S(2)}) collective-permute-start(bf16[4,256,512]{2,1,0:T(8,128)(2,1)} %get-tuple-element.51), channel_id=1, source_target_pairs={{0,1},{1,0},{2,3},{3,2},{4,5},{5,4},{6,7},{7,6},{8,9},{9,8},{10,11... | collective-permute-start | bytes 3145736 | tf_op jit(solution)/shard_map/ppermute | solution.py:28
  9.6 2.4 %collective-permute-start.2 = (s32[12]{0:T(128)S(1)}, s32[12]{0:T(128)S(1)}, u32[]{:S(2)}, u32[]{:S(2)}) collective-permute-start(s32[12]{0:T(128)S(1)} %copy-done.19), channel_id=1, source_target_pairs={{0,16},{16,0},{1,17},{17,1},{2,18},{18,2},{3,19},{19,3},{4,20},{20... | collective-permute-start | bytes 152 | tf_op jit(solution)/shard_map/ppermute | solution.py:28
  18.1 2.1 %collective-permute-start.3 = (f32[8,768]{1,0:T(8,128)S(1)}, f32[8,768]{1,0:T(8,128)S(1)}, u32[]{:S(2)}, u32[]{:S(2)}) collective-permute-start(f32[8,768]{1,0:T(8,128)S(1)} %low.1), channel_id=1, source_target_pairs={{0,1},{1,0},{2,3},{3,2},{4,5},{5,4},{6,7},{7,6},{8,9},{9,8},{10,11... | collective-permute-start | bytes 73736 | tf_op jit(solution)/shard_map/ppermute | solution.py:28
  21.2 67.7 %all-to-all-start = ((bf16[16,880,128]{2,1,0:T(8,128)(2,1)}), bf16[16,880,128]{2,1,0:T(8,128)(2,1)}, u32[]{:S(2)}, u32[]{:S(2)}) async-start(bf16[16,880,128]{2,1,0:T(8,128)(2,1)} %copy-done.5), calls=%async_computation | async-start | bytes 7208960 | tf_op jit(solution)/shard_map/all_to_all | solution.py:506
  29.2 15.3 %collective-permute-start.1 = (bf16[2,256,512]{2,1,0:T(8,128)(2,1)}, bf16[2,256,512]{2,1,0:T(8,128)(2,1)S(1)}, u32[]{:S(2)}, u32[]{:S(2)}) collective-permute-start(bf16[2,256,512]{2,1,0:T(8,128)(2,1)} %add_convert_fusion), channel_id=1, source_target_pairs={{0,2},{2,0},{1,3},{3,1},{4,6},{6,4},{5,7},{7,5},{8,10},{10,8},{9,1... | collective-permute-start | bytes 1572872 | tf_op jit(solution)/shard_map/ppermute | solution.py:28
  32.1 12.4 %collective-permute-start.4 = (f32[8,768]{1,0:T(8,128)S(1)}, f32[8,768]{1,0:T(8,128)S(1)}, u32[]{:S(2)}, u32[]{:S(2)}) collective-permute-start(f32[8,768]{1,0:T(8,128)S(1)} %add.71.l0), channel_id=1, source_target_pairs={{0,2},{2,0},{1,3},{3,1},{4,6},{6,4},{5,7},{7,5},{8,10},{10,8},{9,1... | collective-permute-start | bytes 73736 | tf_op jit(solution)/shard_map/ppermute | solution.py:28
  48.1 2.3 %collective-permute-start.5 = (f32[8,768]{1,0:T(8,128)S(1)}, f32[8,768]{1,0:T(8,128)S(1)}, u32[]{:S(2)}, u32[]{:S(2)}) collective-permute-start(f32[8,768]{1,0:T(8,128)S(1)} %constant_dynamic-update-slice_fusion), channel_id=1, source_target_pairs={{0,1},{1,0},{2,3},{3,2},{4,5},{5,4},{6,7},{7,6},{8,9},{9,8},{10,11... | collective-permute-start | bytes 73736 | tf_op jit(solution)/shard_map/ppermute | solution.py:28
  50.5 6.2 %collective-permute-start.6 = (f32[8,768]{1,0:T(8,128)S(1)}, f32[8,768]{1,0:T(8,128)S(1)}, u32[]{:S(2)}, u32[]{:S(2)}) collective-permute-start(f32[8,768]{1,0:T(8,128)S(1)} %add.72.s0), channel_id=1, source_target_pairs={{0,2},{2,0},{1,3},{3,1},{4,6},{6,4},{5,7},{7,5},{8,10},{10,8},{9,1... | collective-permute-start | bytes 73736 | tf_op jit(solution)/shard_map/ppermute | solution.py:28
  59.3 2.3 %collective-permute-start.7 = (bf16[1,768,256]{2,1,0:T(8,128)(2,1)S(1)}, bf16[1,768,256]{2,1,0:T(8,128)(2,1)S(1)}, u32[]{:S(2)}, u32[]{:S(2)}) collective-permute-start(bf16[1,768,256]{2,1,0:T(8,128)(2,1)S(1)} %get-tuple-element.67), channel_id=1, source_target_pairs={{0,1},{1,0},{2,3},{3,2},{4,5},{5,4},{6,7},{7,6},{8,9},{9,8},{10,11... | collective-permute-start | bytes 1179656 | tf_op jit(solution)/shard_map/ppermute | solution.py:28
  61.5 4.1 %collective-permute-start.11 = (bf16[1,768,256]{2,1,0:T(8,128)(2,1)S(1)}, bf16[1,768,256]{2,1,0:T(8,128)(2,1)S(1)}, u32[]{:S(2)}, u32[]{:S(2)}) collective-permute-start(bf16[1,768,256]{2,1,0:T(8,128)(2,1)S(1)} %get-tuple-element.74), channel_id=1, source_target_pairs={{0,1},{1,0},{2,3},{3,2},{4,5},{5,4},{6,7},{7,6},{8,9},{9,8},{10,11... | collective-permute-start | bytes 1179656 | tf_op jit(solution)/shard_map/ppermute | solution.py:28
  61.7 11.9 %collective-permute-start.8 = (bf16[1,768,256]{2,1,0:T(8,128)(2,1)S(1)}, bf16[1,768,256]{2,1,0:T(8,128)(2,1)S(1)}, u32[]{:S(2)}, u32[]{:S(2)}) collective-permute-start(bf16[1,768,256]{2,1,0:T(8,128)(2,1)S(1)} %add_convert_fusion.4.refs_0_), channel_id=1, source_target_pairs={{0,2},{2,0},{1,3},{3,1},{4,6},{6,4},{5,7},{7,5},{8,10},{10,8},{9,1... | collective-permute-start | bytes 1179656 | tf_op jit(solution)/shard_map/ppermute | solution.py:28
  64.7 15.2 %collective-permute-start.14 = (bf16[1,768,256]{2,1,0:T(8,128)(2,1)S(1)}, bf16[1,768,256]{2,1,0:T(8,128)(2,1)S(1)}, u32[]{:S(2)}, u32[]{:S(2)}) collective-permute-start(bf16[1,768,256]{2,1,0:T(8,128)(2,1)S(1)} %get-tuple-element.80), channel_id=1, source_target_pairs={{0,1},{1,0},{2,3},{3,2},{4,5},{5,4},{6,7},{7,6},{8,9},{9,8},{10,11... | collective-permute-start | bytes 1179656 | tf_op jit(solution)/shard_map/ppermute | solution.py:28
  65.6 19.5 %collective-permute-start.12 = (bf16[1,768,256]{2,1,0:T(8,128)(2,1)S(1)}, bf16[1,768,256]{2,1,0:T(8,128)(2,1)S(1)}, u32[]{:S(2)}, u32[]{:S(2)}) collective-permute-start(bf16[1,768,256]{2,1,0:T(8,128)(2,1)S(1)} %add_convert_fusion.3.refs_0_), channel_id=1, source_target_pairs={{0,2},{2,0},{1,3},{3,1},{4,6},{6,4},{5,7},{7,5},{8,10},{10,8},{9,1... | collective-permute-start | bytes 1179656 | tf_op jit(solution)/shard_map/ppermute | solution.py:28
  75.1 12.4 %collective-permute-start.9 = (bf16[1,768,256]{2,1,0:T(8,128)(2,1)S(1)}, bf16[1,768,256]{2,1,0:T(8,128)(2,1)S(1)}, u32[]{:S(2)}, u32[]{:S(2)}) collective-permute-start(bf16[1,768,256]{2,1,0:T(8,128)(2,1)S(1)} %get-tuple-element.69), channel_id=1, source_target_pairs={{0,1},{1,0},{2,3},{3,2},{4,5},{5,4},{6,7},{7,6},{8,9},{9,8},{10,11... | collective-permute-start | bytes 1179656 | tf_op jit(solution)/shard_map/ppermute | solution.py:28
  79.8 10.8 %collective-permute-start.18 = (bf16[1,768,256]{2,1,0:T(8,128)(2,1)}, bf16[1,768,256]{2,1,0:T(8,128)(2,1)}, u32[]{:S(2)}, u32[]{:S(2)}) collective-permute-start(bf16[1,768,256]{2,1,0:T(8,128)(2,1)} %get-tuple-element.91), channel_id=1, source_target_pairs={{0,1},{1,0},{2,3},{3,2},{4,5},{5,4},{6,7},{7,6},{8,9},{9,8},{10,11... | collective-permute-start | bytes 1179656 | tf_op jit(solution)/shard_map/ppermute | solution.py:28
  80.7 12.8 %collective-permute-start.15 = (bf16[1,768,256]{2,1,0:T(8,128)(2,1)}, bf16[1,768,256]{2,1,0:T(8,128)(2,1)S(1)}, u32[]{:S(2)}, u32[]{:S(2)}) collective-permute-start(bf16[1,768,256]{2,1,0:T(8,128)(2,1)} %add_convert_fusion.2), channel_id=1, source_target_pairs={{0,2},{2,0},{1,3},{3,1},{4,6},{6,4},{5,7},{7,5},{8,10},{10,8},{9,1... | collective-permute-start | bytes 1179656 | tf_op jit(solution)/shard_map/ppermute | solution.py:28
  84.4 14.6 %collective-permute-start.10 = (bf16[1,768,256]{2,1,0:T(8,128)(2,1)}, bf16[1,768,256]{2,1,0:T(8,128)(2,1)}, u32[]{:S(2)}, u32[]{:S(2)}) collective-permute-start(bf16[1,768,256]{2,1,0:T(8,128)(2,1)} %get-tuple-element.72), channel_id=1, source_target_pairs={{0,1},{1,0},{2,3},{3,2},{4,5},{5,4},{6,7},{7,6},{8,9},{9,8},{10,11... | collective-permute-start | bytes 1179656 | tf_op jit(solution)/shard_map/ppermute | solution.py:28
  87.5 19.4 %collective-permute-start.13 = (bf16[1,768,256]{2,1,0:T(8,128)(2,1)}, bf16[1,768,256]{2,1,0:T(8,128)(2,1)S(1)}, u32[]{:S(2)}, u32[]{:S(2)}) collective-permute-start(bf16[1,768,256]{2,1,0:T(8,128)(2,1)} %get-tuple-element.78), channel_id=1, source_target_pairs={{0,1},{1,0},{2,3},{3,2},{4,5},{5,4},{6,7},{7,6},{8,9},{9,8},{10,11... | collective-permute-start | bytes 1179656 | tf_op jit(solution)/shard_map/ppermute | solution.py:28
  90.0 11.4 %collective-permute-start.16 = (bf16[16,112,128]{2,1,0:T(8,128)(2,1)S(1)}, bf16[16,112,128]{2,1,0:T(8,128)(2,1)S(1)}, u32[]{:S(2)}, u32[]{:S(2)}) collective-permute-start(bf16[16,112,128]{2,1,0:T(8,128)(2,1)S(1)} %slice.39), channel_id=1, source_target_pairs={{0,1},{1,0},{2,3},{3,2},{4,5},{5,4},{6,7},{7,6},{8,9},{9,8},{10,11... | collective-permute-start | bytes 1376264 | tf_op jit(solution)/shard_map/ppermute | solution.py:28
  91.8 16.5 %collective-permute-start.19 = (bf16[1,768,256]{2,1,0:T(8,128)(2,1)S(1)}, bf16[1,768,256]{2,1,0:T(8,128)(2,1)S(1)}, u32[]{:S(2)}, u32[]{:S(2)}) collective-permute-start(bf16[1,768,256]{2,1,0:T(8,128)(2,1)S(1)} %add_convert_fusion.1), channel_id=1, source_target_pairs={{0,2},{2,0},{1,3},{3,1},{4,6},{6,4},{5,7},{7,5},{8,10},{10,8},{9,1... | collective-permute-start | bytes 1179656 | tf_op jit(solution)/shard_map/ppermute | solution.py:28
  98.4 9.9 %collective-permute-start.17 = (bf16[1,768,256]{2,1,0:T(8,128)(2,1)S(1)}, bf16[1,768,256]{2,1,0:T(8,128)(2,1)S(1)}, u32[]{:S(2)}, u32[]{:S(2)}) collective-permute-start(bf16[1,768,256]{2,1,0:T(8,128)(2,1)S(1)} %get-tuple-element.89), channel_id=1, source_target_pairs={{0,1},{1,0},{2,3},{3,2},{4,5},{5,4},{6,7},{7,6},{8,9},{9,8},{10,11... | collective-permute-start | bytes 1179656 | tf_op jit(solution)/shard_map/ppermute | solution.py:28
  109.8 1.3 collective-permute-start.20
  111.1 4.2 %collective-permute-start.21 = (f32[8,768]{1,0:T(8,128)S(1)}, f32[8,768]{1,0:T(8,128)S(1)}, u32[]{:S(2)}, u32[]{:S(2)}) collective-permute-start(f32[8,768]{1,0:T(8,128)S(1)} %add.77), channel_id=1, source_target_pairs={{0,2},{2,0},{1,3},{3,1},{4,6},{6,4},{5,7},{7,5},{8,10},{10,8},{9,1... | collective-permute-start | bytes 73736 | tf_op jit(solution)/shard_map/ppermute | solution.py:28
  112.4 13.3 %collective-permute-start.22 = (bf16[2,1024,128]{2,1,0:T(8,128)(2,1)}, bf16[2,1024,128]{2,1,0:T(8,128)(2,1)S(1)}, u32[]{:S(2)}, u32[]{:S(2)}) collective-permute-start(bf16[2,1024,128]{2,1,0:T(8,128)(2,1)} %get-tuple-element.96), channel_id=1, source_target_pairs={{0,16},{16,0},{1,17},{17,1},{2,18},{18,2},{3,19},{19,3},{4,20},{20... | collective-permute-start | bytes 1572872 | tf_op jit(solution)/shard_map/ppermute | solution.py:28
  (20 other events, 135.6 us)

commit v5 on v4

--- a/solution.py
+++ b/solution.py
@@ -43,32 +43,43 @@
     )
 
 
-def pack(where, digits, factors_in, factors_out, pops):
-    layers, members, ranks, width = factors_in.shape
-    k = members * layers * ranks
+def regroup(factors, start):
+    layers, members, ranks, _ = factors.shape
+    blocks, k = 8, members * layers * ranks
+
+    def kernel(start_ref, in_ref, out_ref):
+        cols = pl.ds(pl.multiple_of(start_ref[0], 1024), 1024)
+        for m in range(members):
+            rows = jnp.concatenate(
+                [in_ref[l, m, :, cols].astype(f32) for l in range(layers)], axis=0
+            ).astype(bf16)
+            for n in range(blocks):
+                out_ref[n, m * 8 : m * 8 + 8, :] = rows[:, n * 128 : (n + 1) * 128]
+
+    return pl.pallas_call(
+        kernel,
+        out_shape=jax.ShapeDtypeStruct((blocks, k, 128), bf16),
+        in_specs=[SMEM, VMEM],
+        out_specs=VMEM,
+        compiler_params=params(16),
+        name="regroup",
+        cost_estimate=small_cost,
+    )(start, factors)
+
+
+def pack(where, digits, a_blocks, factors_out, pops):
+    layers, members, ranks, full = factors_out.shape
+    blocks, k, _ = a_blocks.shape
     half = members // 2
-    blocks = width // 128
     part = k // 2 + 8
     rows = blocks * k + 2 * part
 
-    def kernel(where_ref, digits_ref, in_ref, out_ref, a_ref, b_ref, packed_ref):
-        own = pl.multiple_of((where_ref[1] * 2 + where_ref[2]) * width, width)
+    def kernel(where_ref, digits_ref, a_ref, out_ref, packed_ref):
         c = where_ref[2]
-
-        def member(ref, m, cols):
-            return jnp.concatenate(
-                [ref[l, m, :, cols].astype(f32) for l in range(layers)], axis=0
+        for m in range(half):
+            b = jnp.concatenate(
+                [out_ref[l, c * half + m].astype(f32) for l in range(layers)], axis=0
             ).astype(bf16)
-
-        for m in range(members):
-            a = member(in_ref, m, slice(None))
-            b = member(out_ref, m, pl.ds(own, width))
-            at = slice(m * 8, m * 8 + 8)
-            for n in range(blocks):
-                a_ref[n, at, :] = a[:, n * 128 : (n + 1) * 128]
-                b_ref[n, at, :] = b[:, n * 128 : (n + 1) * 128]
-        for m in range(half):
-            b = member(out_ref, c * half + m, slice(None))
             for o in range(2 * pops):
                 y, x, z = o // 8, (o // 4) % 2, o % 4
                 lo = blocks * k + x * part + m * 8
@@ -82,50 +93,63 @@
 
     return pl.pallas_call(
         kernel,
-        out_shape=[
-            jax.ShapeDtypeStruct((blocks, k, 128), bf16),
-            jax.ShapeDtypeStruct((blocks, k, 128), bf16),
-            jax.ShapeDtypeStruct((pops, rows, 128), bf16),
-        ],
+        out_shape=jax.ShapeDtypeStruct((pops, rows, 128), bf16),
         in_specs=[SMEM] + [VMEM] * 3,
-        out_specs=[VMEM] * 3,
+        out_specs=VMEM,
         compiler_params=params(16),
         name="pack",
         cost_estimate=small_cost,
-    )(where, digits, factors_in, factors_out)
+    )(where, digits, a_blocks, factors_out)
 
 
 def product(layer, where, left, weights, piece):
     rows, width = left.shape
+    full = weights.shape[2]
     per_owner = width // piece
-
-    def kernel(where_ref, left_ref, w0_ref, w1_ref, out0_ref, out1_ref):
-        for w_ref, out_ref in ((w0_ref, out0_ref), (w1_ref, out1_ref)):
-            out_ref[0] = jnp.dot(
-                left_ref[...], w_ref[0], preferred_element_type=f32
-            ).astype(bf16)
-
-    def block(flip):
-        def at(i, s):
-            half = s[1] ^ (1 - i // per_owner)
-            return (layer, 0, (half * 2 + (s[2] ^ flip)) * per_owner + i % per_owner)
-
-        return pl.BlockSpec((1, width, piece), at)
-
+    cuts = 4
+    depth = width // cuts
     count = 2 * per_owner
-    return pl.pallas_call(
-        kernel,
-        grid_spec=pltpu.PrefetchScalarGridSpec(
-            num_scalar_prefetch=1,
-            grid=(count,),
-            in_specs=[VMEM, block(1), block(0)],
-            out_specs=[pl.BlockSpec((1, rows, piece), lambda i, s: (i, 0, 0))] * 2,
-        ),
+
+    def kernel(where_ref, left_ref, w_ref, out0_ref, out1_ref, total):
+        k = pl.program_id(0)
+        part = left_ref[:, pl.ds(pl.multiple_of(k * depth, depth), depth)]
+
+        @pl.when(k == 0)
+        def _():
+            for n in range(full // piece):
+                cols = slice(n * piece, (n + 1) * piece)
+                total[:, cols] = jnp.dot(part, w_ref[0, :, cols], preferred_element_type=f32)
+
+        @pl.when(k > 0)
+        def _():
+            for n in range(full // piece):
+                cols = slice(n * piece, (n + 1) * piece)
+                total[:, cols] += jnp.dot(part, w_ref[0, :, cols], preferred_element_type=f32)
+
+        @pl.when(k == cuts - 1)
+        def _():
+            for flip, out_ref in ((1, out0_ref), (0, out1_ref)):
+                for i in range(count):
+                    half = where_ref[1] ^ (1 - i // per_owner)
+                    owner = half * 2 + (where_ref[2] ^ flip)
+                    at = pl.multiple_of(owner * width + i % per_owner * piece, piece)
+                    out_ref[i] = total[:, pl.ds(at, piece)].astype(bf16)
+
+    return pl.pallas_call(
+        kernel,
+        grid=(cuts,),
+        in_specs=[
+            SMEM,
+            pl.BlockSpec((rows, width), lambda k: (0, 0)),
+            pl.BlockSpec((1, depth, full), lambda k: (layer, k, 0)),
+        ],
+        out_specs=[pl.BlockSpec((count, rows, piece), lambda k: (0, 0, 0))] * 2,
         out_shape=[jax.ShapeDtypeStruct((count, rows, piece), bf16)] * 2,
+        scratch_shapes=[pltpu.VMEM((rows, full), f32)],
         compiler_params=params(48),
         name="product",
         cost_estimate=small_cost,
-    )(where, left, weights, weights)
+    )(where, left, weights)
 
 
 def stay(layer, weights):
@@ -319,7 +343,7 @@
     )(onehot, embedding, *stats, *lifted)
 
 
-def second_layer(n, coef, full_width, hidden, lows, stats, halves, crossed, out_factors,
+def second_layer(n, coef, full_width, hidden, lows, stats, halves, crossed, slot, out_factors,
                  decay, gain, reward, before):
     rows = hidden.shape[0] // CHUNKS
     group = out_factors.shape[1] // CHUNKS
@@ -344,7 +368,7 @@
             u = dot(spread_low, factor[k * group : (k + 1) * group], 0, 0) + (
                 own_ref[0, span_k].astype(f32)
                 + peer_ref[0, span_k].astype(f32)
-                + other_ref[0, span_k].astype(f32)
+                + other_ref[slot, span_k].astype(f32)
             )
             h = jnp.zeros((per, 256), f32)
             xrr = x_ref[span_k, cols].astype(f32) * r
@@ -380,20 +404,22 @@
     )(hidden, *lows, *stats, *halves, crossed, out_factors, decay, gain, reward, before)
 
 
-def step_kernel(where, arrived, arrived_peer, members, members_all, scale, earlier):
+def step_kernel(where, arrived, arrived_peer, digits_there, members, members_all, scale, earlier):
     pops, rows, lanes = arrived.shape
     k = members * 8
     part = k // 2 + 8
     blocks = (rows - 2 * part) // k
     width = blocks * lanes
 
-    def kernel(where_ref, in_ref, peer_ref, _, mine_ref, theirs_ref, paired, digit_rows):
+    def kernel(where_ref, in_ref, peer_ref, there_ref, _, mine_ref, theirs_ref, paired, digit_rows):
         xl, c = where_ref[4], where_ref[2]
         head = blocks * k
         for p in range(pops):
-            digits = in_ref[p, head + k // 2 : head + k // 2 + 8, :].astype(f32)
-            for i in range(4):
-                digit_rows[i, p : p + 1, :] = digits[i : i + 1, :]
+            here = in_ref[p, head + k // 2 : head + k // 2 + 8, :].astype(f32)
+            there = there_ref[p].astype(f32)
+            for i in range(2):
+                digit_rows[i, p : p + 1, :] = here[i : i + 1, :]
+                digit_rows[2 + i, p : p + 1, :] = there[i : i + 1, :]
         lane = lax.broadcasted_iota(jnp.int32, (pops, lanes), 1)
         real = lane < members
         here = (digit_rows[0] * 32.0 + digit_rows[1]) / members_all
@@ -450,7 +476,7 @@
             jax.ShapeDtypeStruct((2, width, lanes), f32),
             jax.ShapeDtypeStruct((2, width, lanes), bf16),
         ],
-        in_specs=[SMEM, VMEM, VMEM, pl.BlockSpec(memory_space=pl.ANY)],
+        in_specs=[SMEM, VMEM, VMEM, VMEM, pl.BlockSpec(memory_space=pl.ANY)],
         out_specs=[VMEM, VMEM],
         scratch_shapes=[
             pltpu.VMEM((pops * k, 4 * lanes), bf16),
@@ -459,7 +485,7 @@
         compiler_params=params(24),
         name="weight_step",
         cost_estimate=small_cost,
-    )(where, arrived, arrived_peer, earlier)
+    )(where, arrived, arrived_peer, digits_there, earlier)
 
 
 def shards(
@@ -495,15 +521,15 @@
     theirs = swap(peer, "c")
     cross = added(own[:2], theirs[:2])
     first_table = [own, theirs, swap(cross, "xh")]
-    both = jnp.stack([fitness_ranks, swap(after(fitness_ranks, peer), "xl")])
-    digits = jnp.stack([both[0] // 32, both[0] % 32, both[1] // 32, both[1] % 32]).astype(bf16)
-    digits = jnp.pad(digits, ((0, 4), (0, 128 - members)))
+    a_blocks = regroup(after(factors_in, peer), jnp.zeros((1,), jnp.int32))
+    lows = mp_parts(low_kernel(after(onehot, peer), embedding, a_blocks))
+    digits = jnp.stack([fitness_ranks // 32, fitness_ranks % 32]).astype(bf16)
+    digits = jnp.pad(digits, ((0, 6), (0, 128 - members)))
     pops = lax.axis_size("y") * lax.axis_size("z")
-    a_blocks, b_own, packed = pack(
-        after(where, peer), digits, factors_in, factors_out, pops
-    )
-    lows = mp_parts(low_kernel(after(onehot, peer), embedding, a_blocks))
-    arrived = lax.all_to_all(after(packed, cross, lows[0]), ("y", "z"), 0, 0, tiled=True)
+    late_out = after(factors_out, cross)
+    b_own = regroup(late_out, ((xh * 2 + c) * width).reshape(1).astype(jnp.int32))
+    packed = pack(where, digits, a_blocks, late_out, pops)
+    arrived = lax.all_to_all(after(packed, lows[0]), ("y", "z"), 0, 0, tiled=True)
 
     decay = [decay_rates[l : l + 1] for l in range(2)]
     gain = [norm_gain[l : l + 1] for l in range(2)]
@@ -517,35 +543,35 @@
     stats = mp_parts(jnp.concatenate(stats, axis=1))
     late_weights = stay(1, after(mix_weights, stats[0]))
     hidden, last_hidden = next_hidden(full_width, onehot, embedding, stats, lifted)
-    sent, parts = [], []
-    for n in range(4):
-        earlier = parts[n - 2 : n - 1] if n > 1 else ()
-        peer, own = dense(1, where, hidden, late_weights, 256, n, 1, earlier)
-        parts.append(added(own, swap(peer, "c")))
-        sent.append(swap(parts[n], "xh"))
+    sent, parts, place = [], [], []
+    for first, count in ((0, 3), (3, 1)):
+        peer, own = dense(1, where, hidden, late_weights, 256, first, count, ())
+        part = added(own, swap(peer, "c"))
+        parts.append(part)
+        sent.append(swap(part, "xh"))
+        place += [(len(sent) - 1, n) for n in range(count)]
     halves = []
     for n in range(4):
-        peer, own = dense(0, where, hidden, late_weights, 256, n, 1, (sent[max(n - 1, 0)],))
+        peer, own = dense(0, where, hidden, late_weights, 256, n, 1, (*parts, *(h[1] for h in halves)))
         halves.append((own, swap(peer, "c")))
 
-    st = jnp.zeros((8, rows_all), f32)
+    outs_rows = 2 * (members * rank_count + 8)
+    tail_rows = after(arrived, halves[3][0])[:, -outs_rows:]
+    arrived_peer = swap(tail_rows, "c")
+    digits_there = swap(tail_rows[:, -8:], "xl")
+    step_mine, step_theirs = step_kernel(
+        where, arrived, arrived_peer, digits_there, members, members_all,
+        (members_all * rank_count) ** (-0.5), halves[3][0],
+    )
+    st = after(jnp.zeros((8, rows_all), f32), step_theirs)
     lasts = []
     for n in range(4):
-        if n == 1:
-            outs_rows = 2 * (members * rank_count + 8)
-            arrived_peer = swap(after(arrived, st)[:, -outs_rows:], "c")
-        if n == 2:
-            step_mine, step_theirs = step_kernel(
-                where, arrived, arrived_peer, members, members_all,
-                (members_all * rank_count) ** (-0.5), st,
-            )
-            st = after(st, step_theirs)
         st, last = second_layer(
-            n, coef, full_width, hidden, lows, stats, halves[n], sent[n], b_own,
+            n, coef, full_width, hidden, lows, stats, halves[n], sent[place[n][0]], place[n][1], b_own,
             decay[1], gain[1], reward_dir[None], st,
         )
         lasts.append(last)
-    weight_step = step_mine + swap(after(step_theirs, sent[3]), "xl").astype(f32)
+    weight_step = step_mine + swap(after(step_theirs, sent[-1]), "xl").astype(f32)
     so_far = sum(mp_parts(st))
     norm = lax.rsqrt(so_far[0] / full_width + norm_eps)
     terms = (so_far[2] + norm * so_far[1]).reshape(CHUNKS, step_count, -1)

time: 129 us -> 135 us (1.047)
  waiting for transfers between devices: 32.3 us -> 41.2 us
  starting transfers between devices: 33.2 us -> 27.4 us
  other arithmetic: 6.78 us -> 2.76 us
  local copies, waits for them, and re-layouts: 11.7 us -> 15.7 us
  Pallas kernels: 43.1 us -> 46.3 us
    ppermute x23 -> x19, waiting for transfers between devices: 32.3 us -> 39.6 us  [swap(): return lax.ppermute(value, axis, [(0, 1), (1, 0)])]
    ppermute x23 -> x19, starting transfers between devices: 25.2 us -> 19.4 us  [swap(): return lax.ppermute(value, axis, [(0, 1), (1, 0)])]
    pallas_call x8 -> x6, Pallas kernels: 14.6 us -> 10.8 us  [dense(): pl.pallas_call(kernel, out_shape=[jax.ShapeDtypeStruct((count, rows, piec...]
    pallas_call x4, Pallas kernels: 6.73 us -> 9.98 us  [second_layer(): pl.pallas_call(kernel, out_shape=[jax.ShapeDtypeStruct((8, total), f32),...]
    unnamed x43 -> x73, local copies, waits for them, and re-layouts: 9.25 us -> 12.5 us
    pallas_call x3, Pallas kernels: 3.59 us -> 6.73 us  [first_layer(): pl.pallas_call(kernel, out_shape=[jax.ShapeDtypeStruct((rows, width), bf1...]
    convert_element_type x5 -> x3, other arithmetic: 3.3 us -> 1.3 us  [added(): return (a.astype(f32) + b.astype(f32)).astype(bf16)]
    all_to_all x1, waiting for transfers between devices: 0.01 us -> 1.59 us  [shards(): lax.all_to_all(after(packed, lows[0]), ('y', 'z'), 0, 0, tiled=True)]
  transfers between devices with their start and end apart: 24 -> 20, of which waited for: 8 -> 12; matrix products, arithmetic and copies ran while one was open for 5% -> 4% of each run, Pallas kernels for 28% -> 28%
where the time goes in v5:
time: 135 us; the launch traced here: 134 us
  Pallas kernels  46.3 us (34%)
  waiting for transfers between devices  41.2 us (31%)
  starting transfers between devices  27.4 us (20%)
  local copies, waits for them, and re-layouts  15.7 us (12%)
  other arithmetic  2.76 us (2%)
    ppermute x19, waiting for transfers between devices, swap(): return lax.ppermute(value, axis, [(0, 1), (1, 0)])  39.6 us
    ppermute x19, starting transfers between devices, swap(): return lax.ppermute(value, axis, [(0, 1), (1, 0)])  19.4 us
    unnamed x73, local copies, waits for them, and re-layouts  12.5 us
    pallas_call x6, Pallas kernels, dense(): pl.pallas_call(kernel, out_shape=[jax.ShapeDtypeStruct((count, rows, piec...  10.8 us
    pallas_call x4, Pallas kernels, second_layer(): pl.pallas_call(kernel, out_shape=[jax.ShapeDtypeStruct((8, total), f32),...  9.98 us
    all_to_all x1, starting transfers between devices, shards(): lax.all_to_all(after(packed, lows[0]), ('y', 'z'), 0, 0, tiled=True)  7.94 us
    pallas_call x1, Pallas kernels, product(): pl.pallas_call(kernel, grid=(cuts,), in_specs=[SMEM, pl.BlockSpec((rows,...  6.83 us
    pallas_call x3, Pallas kernels, first_layer(): pl.pallas_call(kernel, out_shape=[jax.ShapeDtypeStruct((rows, width), bf1...  6.73 us
  transfers between devices with their start and end apart: 20, of which 12 were waited for; matrix products, arithmetic and copies ran while one was open for 4% of the time, Pallas kernels for 28%

profile of v5, /device:TPU:1, one launch (start us, length us, event | category | flops | bytes accessed | tf_op | source)
XLA Modules:
  0.0 134.4 jit_solution(10492632229552817293)
XLA Ops:
  1.8 6.8 %product.1 = (bf16[4,256,512]{2,1,0:T(8,128)(2,1)}, bf16[4,256,512]{2,1,0:T(8,128)(2,1)S(1)}) custom-call(s32[5]{0:T(128)S(1)} %stack.35.where_ref, bf16[256,1024]{1,0:T(8,128)(2,1)S(1)} %copy-done.3, bf16[2,1024,4096]{2,1,0:T(8,128)(2,1)} %w_ref.2), custom_call_target="tpu_custom_call" | custom-call | flops 1000 | bytes 1000 | tf_op jit(solution)/shard_map/product/pallas_call | solution.py:138
  13.6 2.8 %collective-permute-start.1 = (bf16[2,256,512]{2,1,0:T(8,128)(2,1)}, bf16[2,256,512]{2,1,0:T(8,128)(2,1)}, u32[]{:S(2)}, u32[]{:S(2)}) collective-permute-start(bf16[2,256,512]{2,1,0:T(8,128)(2,1)} %add_convert_fusion.1), channel_id=1, source_target_pairs={{0,2},{2,0},{1,3},{3,1},{4,6},{6,4},{5,7},{7,5},{8,10},{10,8},{9,1... | collective-permute-start | bytes 1572872 | tf_op jit(solution)/shard_map/ppermute | solution.py:28
  17.5 1.8 %copy-done = bf16[16,880,128]{2,1,0:T(8,128)(2,1)} copy-done((bf16[16,880,128]{2,1,0:T(8,128)(2,1)}, bf16[16,880,128]{2,1,0:T(8,128)(2,1)S(1)}, u32[]{:S(2)}) %copy-start) | copy-done | bytes 3604504
  19.2 7.9 %all-to-all-start = ((bf16[16,880,128]{2,1,0:T(8,128)(2,1)}), bf16[16,880,128]{2,1,0:T(8,128)(2,1)}, u32[]{:S(2)}, u32[]{:S(2)}) async-start(bf16[16,880,128]{2,1,0:T(8,128)(2,1)} %copy-done), calls=%async_computation | async-start | bytes 7208960 | tf_op jit(solution)/shard_map/all_to_all | solution.py:532
  28.7 2.7 %collective-permute-done.3.l1 = f32[8,768]{1,0:T(8,128)S(1)} collective-permute-done((f32[8,768]{1,0:T(8,128)S(1)}, f32[8,768]{1,0:T(8,128)S(1)}, u32[]{:S(2)}, u32[]{:S(2)}) %collective-permute-start.3) | collective-permute-done | bytes 24608 | tf_op jit(solution)/shard_map/ppermute | solution.py:28
  31.5 2.2 %first_layer.3 = (bf16[256,1024]{1,0:T(8,128)(2,1)S(1)}, f32[8,256]{1,0:T(8,128)S(1)}) custom-call(bf16[768,256]{1,0:T(8,128)(2,1)S(1)} %fusion.o_ref, bf16[4,256,512]{2,1,0:T(8,128)(2,1)S(1)} %get-tuple-element.43.t0, bf16[4,256,512]{2,1,0:T(8,128)(2,1)S(1)} %collective-permute-done.t1, bf16[2,256,512]{2,1,0:T(8,128)(2,1)} %collective-permute-done.1.t2, ...), custom_call_target="tpu_custom_call" | custom-call | flops 1000 | bytes 1000 | tf_op jit(solution)/shard_map/first_layer/pallas_call | solution.py:301
  33.7 2.3 %first_layer.4 = (bf16[256,1024]{1,0:T(8,128)(2,1)S(1)}, f32[8,256]{1,0:T(8,128)S(1)}) custom-call(bf16[768,256]{1,0:T(8,128)(2,1)S(1)} %fusion.o_ref, bf16[4,256,512]{2,1,0:T(8,128)(2,1)S(1)} %get-tuple-element.43.t0, bf16[4,256,512]{2,1,0:T(8,128)(2,1)S(1)} %collective-permute-done.t1, bf16[2,256,512]{2,1,0:T(8,128)(2,1)} %collective-permute-done.1.t2, ...), custom_call_target="tpu_custom_call" | custom-call | flops 1000 | bytes 1000 | tf_op jit(solution)/shard_map/first_layer/pallas_call | solution.py:301
  35.9 2.3 %first_layer.5 = (bf16[256,1024]{1,0:T(8,128)(2,1)S(1)}, f32[8,256]{1,0:T(8,128)S(1)}) custom-call(bf16[768,256]{1,0:T(8,128)(2,1)S(1)} %fusion.o_ref, bf16[4,256,512]{2,1,0:T(8,128)(2,1)S(1)} %get-tuple-element.43.t0, bf16[4,256,512]{2,1,0:T(8,128)(2,1)S(1)} %collective-permute-done.t1, bf16[2,256,512]{2,1,0:T(8,128)(2,1)} %collective-permute-done.1.t2, ...), custom_call_target="tpu_custom_call" | custom-call | flops 1000 | bytes 1000 | tf_op jit(solution)/shard_map/first_layer/pallas_call | solution.py:301
  38.2 2.3 %collective-permute-start.4 = (f32[8,768]{1,0:T(8,128)S(1)}, f32[8,768]{1,0:T(8,128)S(1)}, u32[]{:S(2)}, u32[]{:S(2)}) collective-permute-start(f32[8,768]{1,0:T(8,128)S(1)} %constant_dynamic-update-slice_fusion), channel_id=1, source_target_pairs={{0,1},{1,0},{2,3},{3,2},{4,5},{5,4},{6,7},{7,6},{8,9},{9,8},{10,11... | collective-permute-start | bytes 73736 | tf_op jit(solution)/shard_map/ppermute | solution.py:28
  41.6 3.5 %stay.1.w_ref = bf16[1024,4096]{1,0:T(8,128)(2,1)S(1)} custom-call(bf16[2,1024,4096]{2,1,0:T(8,128)(2,1)} %w_ref.2), custom_call_target="tpu_custom_call" | custom-call | flops 1000 | bytes 1000 | tf_op jit(solution)/shard_map/stay/pallas_call | solution.py:170
  46.7 3.2 %dense.6 = (bf16[3,768,256]{2,1,0:T(8,128)(2,1)S(1)}, bf16[3,768,256]{2,1,0:T(8,128)(2,1)S(1)}) custom-call(s32[5]{0:T(128)S(1)} %stack.35.where_ref, bf16[768,1024]{1,0:T(8,128)(2,1)S(1)} %get-tuple-element.55.left_ref.x_ref, bf16[1024,4096]{1,0:T(8,128)(2,1)S(1)} %stay.1.w_ref), custom_call_target="tpu_custom_call" | custom-call | flops 1000 | bytes 1000 | tf_op jit(solution)/shard_map/dense/pallas_call | solution.py:195
  53.0 1.7 %collective-permute-done.7 = bf16[1,768,256]{2,1,0:T(8,128)(2,1)S(1)} collective-permute-done((bf16[1,768,256]{2,1,0:T(8,128)(2,1)S(1)}, bf16[1,768,256]{2,1,0:T(8,128)(2,1)S(1)}, u32[]{:S(2)}, u32[]{:S(2)}) %collective-permute-start.7) | collective-permute-done | bytes 393248 | tf_op jit(solution)/shard_map/ppermute | solution.py:28
  55.1 1.5 %dense.8 = (bf16[1,768,256]{2,1,0:T(8,128)(2,1)S(1)}, bf16[1,768,256]{2,1,0:T(8,128)(2,1)S(1)}) custom-call(s32[5]{0:T(128)S(1)} %stack.35.where_ref, bf16[768,1024]{1,0:T(8,128)(2,1)S(1)} %get-tuple-element.55.left_ref.x_ref, bf16[1024,4096]{1,0:T(8,128)(2,1)S(1)} %stay.1.w_ref, bf16[3,768,256]{2,1,0:T(8,128)(2,1)S(1)} %add_convert_fusion.refs_0_, ...), custom_call_target="tpu_custom_call" | custom-call | flops 1000 | bytes 1000 | tf_op jit(solution)/shard_map/dense/pallas_call | solution.py:195
  57.5 1.6 %collective-permute-done.8.refs_2_.peer_ref = bf16[1,768,256]{2,1,0:T(8,128)(2,1)S(1)} collective-permute-done((bf16[1,768,256]{2,1,0:T(8,128)(2,1)S(1)}, bf16[1,768,256]{2,1,0:T(8,128)(2,1)S(1)}, u32[]{:S(2)}, u32[]{:S(2)}) %collective-permute-start.8) | collective-permute-done | bytes 393248 | tf_op jit(solution)/shard_map/ppermute | solution.py:28
  71.1 1.6 %all-to-all-done.in_ref = bf16[16,880,128]{2,1,0:T(8,128)(2,1)} async-done(((bf16[16,880,128]{2,1,0:T(8,128)(2,1)}), bf16[16,880,128]{2,1,0:T(8,128)(2,1)}, u32[]{:S(2)}, u32[]{:S(2)}) %all-to-all-start) | async-done | bytes 3604512 | tf_op jit(solution)/shard_map/all_to_all | solution.py:532
  73.7 3.4 %collective-permute-start.12 = (bf16[16,112,128]{2,1,0:T(8,128)(2,1)S(1)}, bf16[16,112,128]{2,1,0:T(8,128)(2,1)S(1)}, u32[]{:S(2)}, u32[]{:S(2)}) collective-permute-start(bf16[16,112,128]{2,1,0:T(8,128)(2,1)S(1)} %slice.43), channel_id=1, source_target_pairs={{0,1},{1,0},{2,3},{3,2},{4,5},{5,4},{6,7},{7,6},{8,9},{9,8},{10,11... | collective-permute-start | bytes 1376264 | tf_op jit(solution)/shard_map/ppermute | solution.py:28
  79.7 18.4 %collective-permute-done.13.there_ref = bf16[16,8,128]{2,1,0:T(8,128)(2,1)S(1)} collective-permute-done((bf16[16,8,128]{2,1,0:T(8,128)(2,1)S(1)}, bf16[16,8,128]{2,1,0:T(8,128)(2,1)S(1)}, u32[]{:S(2)}, u32[]{:S(2)}) %collective-permute-start.13) | collective-permute-done | bytes 32800 | tf_op jit(solution)/shard_map/ppermute | solution.py:28
  99.1 5.5 %weight_step.1 = (f32[2,1024,128]{2,1,0:T(8,128)S(1)}, bf16[2,1024,128]{2,1,0:T(8,128)(2,1)}) custom-call(s32[5]{0:T(128)S(1)} %stack.35.where_ref, bf16[16,880,128]{2,1,0:T(8,128)(2,1)} %all-to-all-done.in_ref, bf16[16,112,128]{2,1,0:T(8,128)(2,1)S(1)} %collective-permute-done.12.peer_ref, bf16[16,8,128]{2,1,0:T(8,128)(2,1)S(1)} %collective-permute-done.13.there_ref, ...), custom_call_target="tpu_custom_call" | custom-call | flops 1000 | bytes 1000 | tf_op jit(solution)/shard_map/weight_step/pallas_call | solution.py:473
  104.6 3.1 %second_layer.4 = (f32[8,768]{1,0:T(8,128)S(1)}, f32[48,256]{1,0:T(8,128)S(1)}) custom-call(bf16[768,1024]{1,0:T(8,128)(2,1)S(1)} %get-tuple-element.55.left_ref.x_ref, f32[8,768]{1,0:T(8,128)S(1)} %add.61.l0, f32[8,768]{1,0:T(8,128)S(1)} %collective-permute-done.3.l1, f32[8,768]{1,0:T(8,128)S(1)} %add.63.s0, f32[8,768]{1,0:T(8,128)S(1)} %collective-permute-done.5.s1, ...), custom_call_target="tpu_custom_call" | custom-call | flops 1000 | bytes 1000 | tf_op jit(solution)/shard_map/second_layer/pallas_call | solution.py:392
  107.8 2.8 %second_layer.5 = (f32[8,768]{1,0:T(8,128)S(1)}, f32[48,256]{1,0:T(8,128)S(1)}) custom-call(bf16[768,1024]{1,0:T(8,128)(2,1)S(1)} %get-tuple-element.55.left_ref.x_ref, f32[8,768]{1,0:T(8,128)S(1)} %add.61.l0, f32[8,768]{1,0:T(8,128)S(1)} %collective-permute-done.3.l1, f32[8,768]{1,0:T(8,128)S(1)} %add.63.s0, f32[8,768]{1,0:T(8,128)S(1)} %collective-permute-done.5.s1, ...), custom_call_target="tpu_custom_call" | custom-call | flops 1000 | bytes 1000 | tf_op jit(solution)/shard_map/second_layer/pallas_call | solution.py:392
  111.2 2.7 %second_layer.6 = (f32[8,768]{1,0:T(8,128)S(1)}, f32[48,256]{1,0:T(8,128)S(1)}) custom-call(bf16[768,1024]{1,0:T(8,128)(2,1)S(1)} %get-tuple-element.55.left_ref.x_ref, f32[8,768]{1,0:T(8,128)S(1)} %add.61.l0, f32[8,768]{1,0:T(8,128)S(1)} %collective-permute-done.3.l1, f32[8,768]{1,0:T(8,128)S(1)} %add.63.s0, f32[8,768]{1,0:T(8,128)S(1)} %collective-permute-done.5.s1, ...), custom_call_target="tpu_custom_call" | custom-call | flops 1000 | bytes 1000 | tf_op jit(solution)/shard_map/second_layer/pallas_call | solution.py:392
  118.1 2.2 %collective-permute-start.17 = (f32[8,768]{1,0:T(8,128)S(1)}, f32[8,768]{1,0:T(8,128)S(1)}, u32[]{:S(2)}, u32[]{:S(2)}) collective-permute-start(f32[8,768]{1,0:T(8,128)S(1)} %add.67), channel_id=1, source_target_pairs={{0,2},{2,0},{1,3},{3,1},{4,6},{6,4},{5,7},{7,5},{8,10},{10,8},{9,1... | collective-permute-start | bytes 73736 | tf_op jit(solution)/shard_map/ppermute | solution.py:28
  120.3 2.0 %collective-permute-done.17 = f32[8,768]{1,0:T(8,128)S(1)} collective-permute-done((f32[8,768]{1,0:T(8,128)S(1)}, f32[8,768]{1,0:T(8,128)S(1)}, u32[]{:S(2)}, u32[]{:S(2)}) %collective-permute-start.17) | collective-permute-done | bytes 24608 | tf_op jit(solution)/shard_map/ppermute | solution.py:28
  124.2 9.1 %collective-permute-done.18 = bf16[2,1024,128]{2,1,0:T(8,128)(2,1)S(1)} collective-permute-done((bf16[2,1024,128]{2,1,0:T(8,128)(2,1)}, bf16[2,1024,128]{2,1,0:T(8,128)(2,1)S(1)}, u32[]{:S(2)}, u32[]{:S(2)}) %collective-permute-start.18) | collective-permute-done | bytes 524320 | tf_op jit(solution)/shard_map/ppermute | solution.py:28
  (140 shorter events, 40.1 us)
Async XLA Ops:
  1.8 8.3 %copy-start.31 = (s32[12,4,16]{2,1,0:T(4,128)S(1)}, s32[12,4,16]{2,1,0:T(4,128)}, u32[]{:S(2)}) copy-start(s32[12,4,16]{2,1,0:T(4,128)} %param.9) | copy-start | bytes 9220
  8.6 4.0 %collective-permute-start = (bf16[4,256,512]{2,1,0:T(8,128)(2,1)}, bf16[4,256,512]{2,1,0:T(8,128)(2,1)S(1)}, u32[]{:S(2)}, u32[]{:S(2)}) collective-permute-start(bf16[4,256,512]{2,1,0:T(8,128)(2,1)} %get-tuple-element.44), channel_id=1, source_target_pairs={{0,1},{1,0},{2,3},{3,2},{4,5},{5,4},{6,7},{7,6},{8,9},{9,8},{10,11... | collective-permute-start | bytes 3145736 | tf_op jit(solution)/shard_map/ppermute | solution.py:28
  12.6 3.8 %collective-permute-start.2 = (f32[8,768]{1,0:T(8,128)S(1)}, f32[8,768]{1,0:T(8,128)S(1)}, u32[]{:S(2)}, u32[]{:S(2)}) collective-permute-start(f32[8,768]{1,0:T(8,128)S(1)} %low.1), channel_id=1, source_target_pairs={{0,1},{1,0},{2,3},{3,2},{4,5},{5,4},{6,7},{7,6},{8,9},{9,8},{10,11... | collective-permute-start | bytes 73736 | tf_op jit(solution)/shard_map/ppermute | solution.py:28
  13.6 17.9 %collective-permute-start.1 = (bf16[2,256,512]{2,1,0:T(8,128)(2,1)}, bf16[2,256,512]{2,1,0:T(8,128)(2,1)}, u32[]{:S(2)}, u32[]{:S(2)}) collective-permute-start(bf16[2,256,512]{2,1,0:T(8,128)(2,1)} %add_convert_fusion.1), channel_id=1, source_target_pairs={{0,2},{2,0},{1,3},{3,1},{4,6},{6,4},{5,7},{7,5},{8,10},{10,8},{9,1... | collective-permute-start | bytes 1572872 | tf_op jit(solution)/shard_map/ppermute | solution.py:28
  19.2 53.4 %all-to-all-start = ((bf16[16,880,128]{2,1,0:T(8,128)(2,1)}), bf16[16,880,128]{2,1,0:T(8,128)(2,1)}, u32[]{:S(2)}, u32[]{:S(2)}) async-start(bf16[16,880,128]{2,1,0:T(8,128)(2,1)} %copy-done), calls=%async_computation | async-start | bytes 7208960 | tf_op jit(solution)/shard_map/all_to_all | solution.py:532
  27.2 4.3 %collective-permute-start.3 = (f32[8,768]{1,0:T(8,128)S(1)}, f32[8,768]{1,0:T(8,128)S(1)}, u32[]{:S(2)}, u32[]{:S(2)}) collective-permute-start(f32[8,768]{1,0:T(8,128)S(1)} %add.61.l0), channel_id=1, source_target_pairs={{0,2},{2,0},{1,3},{3,1},{4,6},{6,4},{5,7},{7,5},{8,10},{10,8},{9,1... | collective-permute-start | bytes 73736 | tf_op jit(solution)/shard_map/ppermute | solution.py:28
  38.2 3.1 %collective-permute-start.4 = (f32[8,768]{1,0:T(8,128)S(1)}, f32[8,768]{1,0:T(8,128)S(1)}, u32[]{:S(2)}, u32[]{:S(2)}) collective-permute-start(f32[8,768]{1,0:T(8,128)S(1)} %constant_dynamic-update-slice_fusion), channel_id=1, source_target_pairs={{0,1},{1,0},{2,3},{3,2},{4,5},{5,4},{6,7},{7,6},{8,9},{9,8},{10,11... | collective-permute-start | bytes 73736 | tf_op jit(solution)/shard_map/ppermute | solution.py:28
  41.4 4.6 %collective-permute-start.5 = (f32[8,768]{1,0:T(8,128)S(1)}, f32[8,768]{1,0:T(8,128)S(1)}, u32[]{:S(2)}, u32[]{:S(2)}) collective-permute-start(f32[8,768]{1,0:T(8,128)S(1)} %add.63.s0), channel_id=1, source_target_pairs={{0,2},{2,0},{1,3},{3,1},{4,6},{6,4},{5,7},{7,5},{8,10},{10,8},{9,1... | collective-permute-start | bytes 73736 | tf_op jit(solution)/shard_map/ppermute | solution.py:28
  49.9 4.9 %collective-permute-start.6 = (bf16[3,768,256]{2,1,0:T(8,128)(2,1)S(1)}, bf16[3,768,256]{2,1,0:T(8,128)(2,1)S(1)}, u32[]{:S(2)}, u32[]{:S(2)}) collective-permute-start(bf16[3,768,256]{2,1,0:T(8,128)(2,1)S(1)} %get-tuple-element.58), channel_id=1, source_target_pairs={{0,1},{1,0},{2,3},{3,2},{4,5},{5,4},{6,7},{7,6},{8,9},{9,8},{10,11... | collective-permute-start | bytes 3538952 | tf_op jit(solution)/shard_map/ppermute | solution.py:28
  52.7 2.0 %collective-permute-start.7 = (bf16[1,768,256]{2,1,0:T(8,128)(2,1)S(1)}, bf16[1,768,256]{2,1,0:T(8,128)(2,1)S(1)}, u32[]{:S(2)}, u32[]{:S(2)}) collective-permute-start(bf16[1,768,256]{2,1,0:T(8,128)(2,1)S(1)} %get-tuple-element.60), channel_id=1, source_target_pairs={{0,1},{1,0},{2,3},{3,2},{4,5},{5,4},{6,7},{7,6},{8,9},{9,8},{10,11... | collective-permute-start | bytes 1179656 | tf_op jit(solution)/shard_map/ppermute | solution.py:28
  57.4 1.7 %collective-permute-start.8 = (bf16[1,768,256]{2,1,0:T(8,128)(2,1)S(1)}, bf16[1,768,256]{2,1,0:T(8,128)(2,1)S(1)}, u32[]{:S(2)}, u32[]{:S(2)}) collective-permute-start(bf16[1,768,256]{2,1,0:T(8,128)(2,1)S(1)} %get-tuple-element.62), channel_id=1, source_target_pairs={{0,1},{1,0},{2,3},{3,2},{4,5},{5,4},{6,7},{7,6},{8,9},{9,8},{10,11... | collective-permute-start | bytes 1179656 | tf_op jit(solution)/shard_map/ppermute | solution.py:28
  61.4 1.7 %collective-permute-start.10 = (bf16[1,768,256]{2,1,0:T(8,128)(2,1)S(1)}, bf16[1,768,256]{2,1,0:T(8,128)(2,1)S(1)}, u32[]{:S(2)}, u32[]{:S(2)}) collective-permute-start(bf16[1,768,256]{2,1,0:T(8,128)(2,1)S(1)} %get-tuple-element.64), channel_id=1, source_target_pairs={{0,1},{1,0},{2,3},{3,2},{4,5},{5,4},{6,7},{7,6},{8,9},{9,8},{10,11... | collective-permute-start | bytes 1179656 | tf_op jit(solution)/shard_map/ppermute | solution.py:28
  61.5 43.0 %collective-permute-start.9 = (bf16[3,768,256]{2,1,0:T(8,128)(2,1)S(1)}, bf16[3,768,256]{2,1,0:T(8,128)(2,1)}, u32[]{:S(2)}, u32[]{:S(2)}) collective-permute-start(bf16[3,768,256]{2,1,0:T(8,128)(2,1)S(1)} %add_convert_fusion.refs_0_), channel_id=1, source_target_pairs={{0,2},{2,0},{1,3},{3,1},{4,6},{6,4},{5,7},{7,5},{8,10},{10,8},{9,1... | collective-permute-start | bytes 3538952 | tf_op jit(solution)/shard_map/ppermute | solution.py:28
  65.4 1.8 %collective-permute-start.11 = (bf16[1,768,256]{2,1,0:T(8,128)(2,1)S(1)}, bf16[1,768,256]{2,1,0:T(8,128)(2,1)S(1)}, u32[]{:S(2)}, u32[]{:S(2)}) collective-permute-start(bf16[1,768,256]{2,1,0:T(8,128)(2,1)S(1)} %get-tuple-element.65), channel_id=1, source_target_pairs={{0,1},{1,0},{2,3},{3,2},{4,5},{5,4},{6,7},{7,6},{8,9},{9,8},{10,11... | collective-permute-start | bytes 1179656 | tf_op jit(solution)/shard_map/ppermute | solution.py:28
  73.7 24.4 %collective-permute-start.12 = (bf16[16,112,128]{2,1,0:T(8,128)(2,1)S(1)}, bf16[16,112,128]{2,1,0:T(8,128)(2,1)S(1)}, u32[]{:S(2)}, u32[]{:S(2)}) collective-permute-start(bf16[16,112,128]{2,1,0:T(8,128)(2,1)S(1)} %slice.43), channel_id=1, source_target_pairs={{0,1},{1,0},{2,3},{3,2},{4,5},{5,4},{6,7},{7,6},{8,9},{9,8},{10,11... | collective-permute-start | bytes 1376264 | tf_op jit(solution)/shard_map/ppermute | solution.py:28
  77.1 37.4 %collective-permute-start.15 = (bf16[1,768,256]{2,1,0:T(8,128)(2,1)S(1)}, bf16[1,768,256]{2,1,0:T(8,128)(2,1)S(1)}, u32[]{:S(2)}, u32[]{:S(2)}) collective-permute-start(bf16[1,768,256]{2,1,0:T(8,128)(2,1)S(1)} %add_convert_fusion.2.refs_1_), channel_id=1, source_target_pairs={{0,2},{2,0},{1,3},{3,1},{4,6},{6,4},{5,7},{7,5},{8,10},{10,8},{9,1... | collective-permute-start | bytes 1179656 | tf_op jit(solution)/shard_map/ppermute | solution.py:28
  77.4 37.1 %collective-permute-start.14 = (bf16[1,768,256]{2,1,0:T(8,128)(2,1)}, bf16[1,768,256]{2,1,0:T(8,128)(2,1)S(1)}, u32[]{:S(2)}, u32[]{:S(2)}) collective-permute-start(bf16[1,768,256]{2,1,0:T(8,128)(2,1)} %copy-done.30), channel_id=1, source_target_pairs={{0,1},{1,0},{2,3},{3,2},{4,5},{5,4},{6,7},{7,6},{8,9},{9,8},{10,11... | collective-permute-start | bytes 1179656 | tf_op jit(solution)/shard_map/ppermute | solution.py:28
  77.7 26.8 %copy-start.25 = (f32[1024]{0:T(1024)S(1)}, f32[1024]{0:T(1024)}, u32[]{:S(2)}) copy-start(f32[1024]{0:T(1024)} %param.17) | copy-start | bytes 12292
  78.5 26.1 %copy-start.2 = (bf16[1,768,256]{2,1,0:T(8,128)(2,1)S(1)}, bf16[1,768,256]{2,1,0:T(8,128)(2,1)}, u32[]{:S(2)}) copy-start(bf16[1,768,256]{2,1,0:T(8,128)(2,1)} %copy-done.1) | copy-start | bytes 1179652
  78.5 19.6 %collective-permute-start.13 = (bf16[16,8,128]{2,1,0:T(8,128)(2,1)S(1)}, bf16[16,8,128]{2,1,0:T(8,128)(2,1)S(1)}, u32[]{:S(2)}, u32[]{:S(2)}) collective-permute-start(bf16[16,8,128]{2,1,0:T(8,128)(2,1)S(1)} %slice.44), channel_id=1, source_target_pairs={{0,16},{16,0},{1,17},{17,1},{2,18},{18,2},{3,19},{19,3},{4,20},{20... | collective-permute-start | bytes 98312 | tf_op jit(solution)/shard_map/ppermute | solution.py:28
  114.6 18.7 %copy-start.15 = (f32[2,1024,128]{2,1,0:T(8,128)S(1)}, f32[2,1024,128]{2,1,0:T(8,128)}, u32[]{:S(2)}) copy-start(f32[2,1024,128]{2,1,0:T(8,128)} %copy-done.14) | copy-start | bytes 3145732
  116.0 2.1 %collective-permute-start.16 = (f32[8,768]{1,0:T(8,128)S(1)}, f32[8,768]{1,0:T(8,128)S(1)}, u32[]{:S(2)}, u32[]{:S(2)}) collective-permute-start(f32[8,768]{1,0:T(8,128)S(1)} %get-tuple-element.80), channel_id=1, source_target_pairs={{0,1},{1,0},{2,3},{3,2},{4,5},{5,4},{6,7},{7,6},{8,9},{9,8},{10,11... | collective-permute-start | bytes 73736 | tf_op jit(solution)/shard_map/ppermute | solution.py:28
  118.1 4.2 %collective-permute-start.17 = (f32[8,768]{1,0:T(8,128)S(1)}, f32[8,768]{1,0:T(8,128)S(1)}, u32[]{:S(2)}, u32[]{:S(2)}) collective-permute-start(f32[8,768]{1,0:T(8,128)S(1)} %add.67), channel_id=1, source_target_pairs={{0,2},{2,0},{1,3},{3,1},{4,6},{6,4},{5,7},{7,5},{8,10},{10,8},{9,1... | collective-permute-start | bytes 73736 | tf_op jit(solution)/shard_map/ppermute | solution.py:28
  120.2 13.1 %collective-permute-start.18 = (bf16[2,1024,128]{2,1,0:T(8,128)(2,1)}, bf16[2,1024,128]{2,1,0:T(8,128)(2,1)S(1)}, u32[]{:S(2)}, u32[]{:S(2)}) collective-permute-start(bf16[2,1024,128]{2,1,0:T(8,128)(2,1)} %get-tuple-element.82), channel_id=1, source_target_pairs={{0,16},{16,0},{1,17},{17,1},{2,18},{18,2},{3,19},{19,3},{4,20},{20... | collective-permute-start | bytes 1572872 | tf_op jit(solution)/shard_map/ppermute | solution.py:28
  (31 other events, 113.5 us)

commit v6 on v5

--- a/solution.py
+++ b/solution.py
@@ -404,22 +404,20 @@
     )(hidden, *lows, *stats, *halves, crossed, out_factors, decay, gain, reward, before)
 
 
-def step_kernel(where, arrived, arrived_peer, digits_there, members, members_all, scale, earlier):
+def step_kernel(where, arrived, arrived_peer, members, members_all, scale, earlier):
     pops, rows, lanes = arrived.shape
     k = members * 8
     part = k // 2 + 8
     blocks = (rows - 2 * part) // k
     width = blocks * lanes
 
-    def kernel(where_ref, in_ref, peer_ref, there_ref, _, mine_ref, theirs_ref, paired, digit_rows):
+    def kernel(where_ref, in_ref, peer_ref, _, mine_ref, theirs_ref, paired, digit_rows):
         xl, c = where_ref[4], where_ref[2]
         head = blocks * k
         for p in range(pops):
-            here = in_ref[p, head + k // 2 : head + k // 2 + 8, :].astype(f32)
-            there = there_ref[p].astype(f32)
-            for i in range(2):
-                digit_rows[i, p : p + 1, :] = here[i : i + 1, :]
-                digit_rows[2 + i, p : p + 1, :] = there[i : i + 1, :]
+            digits = in_ref[p, head + k // 2 : head + k // 2 + 8, :].astype(f32)
+            for i in range(4):
+                digit_rows[i, p : p + 1, :] = digits[i : i + 1, :]
         lane = lax.broadcasted_iota(jnp.int32, (pops, lanes), 1)
         real = lane < members
         here = (digit_rows[0] * 32.0 + digit_rows[1]) / members_all
@@ -476,7 +474,7 @@
             jax.ShapeDtypeStruct((2, width, lanes), f32),
             jax.ShapeDtypeStruct((2, width, lanes), bf16),
         ],
-        in_specs=[SMEM, VMEM, VMEM, VMEM, pl.BlockSpec(memory_space=pl.ANY)],
+        in_specs=[SMEM, VMEM, VMEM, pl.BlockSpec(memory_space=pl.ANY)],
         out_specs=[VMEM, VMEM],
         scratch_shapes=[
             pltpu.VMEM((pops * k, 4 * lanes), bf16),
@@ -485,7 +483,7 @@
         compiler_params=params(24),
         name="weight_step",
         cost_estimate=small_cost,
-    )(where, arrived, arrived_peer, digits_there, earlier)
+    )(where, arrived, arrived_peer, earlier)
 
 
 def shards(
@@ -523,8 +521,9 @@
     first_table = [own, theirs, swap(cross, "xh")]
     a_blocks = regroup(after(factors_in, peer), jnp.zeros((1,), jnp.int32))
     lows = mp_parts(low_kernel(after(onehot, peer), embedding, a_blocks))
-    digits = jnp.stack([fitness_ranks // 32, fitness_ranks % 32]).astype(bf16)
-    digits = jnp.pad(digits, ((0, 6), (0, 128 - members)))
+    both = jnp.stack([fitness_ranks, swap(after(fitness_ranks, peer), "xl")])
+    digits = jnp.stack([both[0] // 32, both[0] % 32, both[1] // 32, both[1] % 32]).astype(bf16)
+    digits = jnp.pad(digits, ((0, 4), (0, 128 - members)))
     pops = lax.axis_size("y") * lax.axis_size("z")
     late_out = after(factors_out, cross)
     b_own = regroup(late_out, ((xh * 2 + c) * width).reshape(1).astype(jnp.int32))
@@ -558,9 +557,8 @@
     outs_rows = 2 * (members * rank_count + 8)
     tail_rows = after(arrived, halves[3][0])[:, -outs_rows:]
     arrived_peer = swap(tail_rows, "c")
-    digits_there = swap(tail_rows[:, -8:], "xl")
     step_mine, step_theirs = step_kernel(
-        where, arrived, arrived_peer, digits_there, members, members_all,
+        where, arrived, arrived_peer, members, members_all,
         (members_all * rank_count) ** (-0.5), halves[3][0],
     )
     st = after(jnp.zeros((8, rows_all), f32), step_theirs)

time: 135 us -> 122 us (0.904)
  waiting for transfers between devices: 41.2 us -> 26.5 us
  starting transfers between devices: 27.4 us -> 29.9 us
    ppermute x19, waiting for transfers between devices: 39.6 us -> 25.4 us  [swap(): return lax.ppermute(value, axis, [(0, 1), (1, 0)])]
    ppermute x19, starting transfers between devices: 19.4 us -> 22 us  [swap(): return lax.ppermute(value, axis, [(0, 1), (1, 0)])]
  transfers between devices with their start and end apart: 20 -> 20, of which waited for: 12 -> 11; matrix products, arithmetic and copies ran while one was open for 4% -> 4% of each run, Pallas kernels for 28% -> 31%
where the time goes in v6:
time: 122 us; the launch traced here: 121 us
  Pallas kernels  46.1 us (38%)
  starting transfers between devices  29.9 us (25%)
  waiting for transfers between devices  26.5 us (22%)
  local copies, waits for them, and re-layouts  14.9 us (12%)
  other arithmetic  2.84 us (2%)
    ppermute x19, waiting for transfers between devices, swap(): return lax.ppermute(value, axis, [(0, 1), (1, 0)])  25.4 us
    ppermute x19, starting transfers between devices, swap(): return lax.ppermute(value, axis, [(0, 1), (1, 0)])  22 us
    unnamed x73, local copies, waits for them, and re-layouts  12.5 us
    pallas_call x6, Pallas kernels, dense(): pl.pallas_call(kernel, out_shape=[jax.ShapeDtypeStruct((count, rows, piec...  10.8 us
    pallas_call x4, Pallas kernels, second_layer(): pl.pallas_call(kernel, out_shape=[jax.ShapeDtypeStruct((8, total), f32),...  9.7 us
    all_to_all x1, starting transfers between devices, shards(): lax.all_to_all(after(packed, lows[0]), ('y', 'z'), 0, 0, tiled=True)  7.94 us
    pallas_call x1, Pallas kernels, product(): pl.pallas_call(kernel, grid=(cuts,), in_specs=[SMEM, pl.BlockSpec((rows,...  6.82 us
    pallas_call x3, Pallas kernels, first_layer(): pl.pallas_call(kernel, out_shape=[jax.ShapeDtypeStruct((rows, width), bf1...  6.82 us
  transfers between devices with their start and end apart: 20, of which 11 were waited for; matrix products, arithmetic and copies ran while one was open for 4% of the time, Pallas kernels for 31%

profile of v6, /device:TPU:1, one launch (start us, length us, event | category | flops | bytes accessed | tf_op | source)
XLA Modules:
  0.0 121.3 jit_solution(13267282333566651135)
XLA Ops:
  1.8 6.8 %product.1 = (bf16[4,256,512]{2,1,0:T(8,128)(2,1)}, bf16[4,256,512]{2,1,0:T(8,128)(2,1)S(1)}) custom-call(s32[5]{0:T(128)S(1)} %stack.43.where_ref, bf16[256,1024]{1,0:T(8,128)(2,1)S(1)} %copy-done.3, bf16[2,1024,4096]{2,1,0:T(8,128)(2,1)} %w_ref.2), custom_call_target="tpu_custom_call" | custom-call | flops 1000 | bytes 1000 | tf_op jit(solution)/shard_map/product/pallas_call | solution.py:138
  15.0 2.5 %collective-permute-start.1 = (bf16[2,256,512]{2,1,0:T(8,128)(2,1)}, bf16[2,256,512]{2,1,0:T(8,128)(2,1)}, u32[]{:S(2)}, u32[]{:S(2)}) collective-permute-start(bf16[2,256,512]{2,1,0:T(8,128)(2,1)} %add_convert_fusion.1), channel_id=1, source_target_pairs={{0,2},{2,0},{1,3},{3,1},{4,6},{6,4},{5,7},{7,5},{8,10},{10,8},{9,1... | collective-permute-start | bytes 1572872 | tf_op jit(solution)/shard_map/ppermute | solution.py:28
  18.5 1.8 %copy-done = bf16[16,880,128]{2,1,0:T(8,128)(2,1)} copy-done((bf16[16,880,128]{2,1,0:T(8,128)(2,1)}, bf16[16,880,128]{2,1,0:T(8,128)(2,1)S(1)}, u32[]{:S(2)}) %copy-start) | copy-done | bytes 3604504
  20.3 7.9 %all-to-all-start = ((bf16[16,880,128]{2,1,0:T(8,128)(2,1)}), bf16[16,880,128]{2,1,0:T(8,128)(2,1)}, u32[]{:S(2)}, u32[]{:S(2)}) async-start(bf16[16,880,128]{2,1,0:T(8,128)(2,1)} %copy-done), calls=%async_computation | async-start | bytes 7208960 | tf_op jit(solution)/shard_map/all_to_all | solution.py:531
  30.1 2.4 %collective-permute-done.3.l1 = f32[8,768]{1,0:T(8,128)S(1)} collective-permute-done((f32[8,768]{1,0:T(8,128)S(1)}, f32[8,768]{1,0:T(8,128)S(1)}, u32[]{:S(2)}, u32[]{:S(2)}) %collective-permute-start.3) | collective-permute-done | bytes 24608 | tf_op jit(solution)/shard_map/ppermute | solution.py:28
  32.5 2.3 %first_layer.3 = (bf16[256,1024]{1,0:T(8,128)(2,1)S(1)}, f32[8,256]{1,0:T(8,128)S(1)}) custom-call(bf16[768,256]{1,0:T(8,128)(2,1)S(1)} %fusion.o_ref, bf16[4,256,512]{2,1,0:T(8,128)(2,1)S(1)} %get-tuple-element.44.t0, bf16[4,256,512]{2,1,0:T(8,128)(2,1)S(1)} %collective-permute-done.t1, bf16[2,256,512]{2,1,0:T(8,128)(2,1)} %collective-permute-done.1.t2, ...), custom_call_target="tpu_custom_call" | custom-call | flops 1000 | bytes 1000 | tf_op jit(solution)/shard_map/first_layer/pallas_call | solution.py:301
  34.7 2.3 %first_layer.4 = (bf16[256,1024]{1,0:T(8,128)(2,1)S(1)}, f32[8,256]{1,0:T(8,128)S(1)}) custom-call(bf16[768,256]{1,0:T(8,128)(2,1)S(1)} %fusion.o_ref, bf16[4,256,512]{2,1,0:T(8,128)(2,1)S(1)} %get-tuple-element.44.t0, bf16[4,256,512]{2,1,0:T(8,128)(2,1)S(1)} %collective-permute-done.t1, bf16[2,256,512]{2,1,0:T(8,128)(2,1)} %collective-permute-done.1.t2, ...), custom_call_target="tpu_custom_call" | custom-call | flops 1000 | bytes 1000 | tf_op jit(solution)/shard_map/first_layer/pallas_call | solution.py:301
  37.0 2.3 %first_layer.5 = (bf16[256,1024]{1,0:T(8,128)(2,1)S(1)}, f32[8,256]{1,0:T(8,128)S(1)}) custom-call(bf16[768,256]{1,0:T(8,128)(2,1)S(1)} %fusion.o_ref, bf16[4,256,512]{2,1,0:T(8,128)(2,1)S(1)} %get-tuple-element.44.t0, bf16[4,256,512]{2,1,0:T(8,128)(2,1)S(1)} %collective-permute-done.t1, bf16[2,256,512]{2,1,0:T(8,128)(2,1)} %collective-permute-done.1.t2, ...), custom_call_target="tpu_custom_call" | custom-call | flops 1000 | bytes 1000 | tf_op jit(solution)/shard_map/first_layer/pallas_call | solution.py:301
  39.4 2.5 %collective-permute-start.4 = (f32[8,768]{1,0:T(8,128)S(1)}, f32[8,768]{1,0:T(8,128)S(1)}, u32[]{:S(2)}, u32[]{:S(2)}) collective-permute-start(f32[8,768]{1,0:T(8,128)S(1)} %constant_dynamic-update-slice_fusion), channel_id=1, source_target_pairs={{0,1},{1,0},{2,3},{3,2},{4,5},{5,4},{6,7},{7,6},{8,9},{9,8},{10,11... | collective-permute-start | bytes 73736 | tf_op jit(solution)/shard_map/ppermute | solution.py:28
  43.8 3.5 %stay.1.w_ref = bf16[1024,4096]{1,0:T(8,128)(2,1)S(1)} custom-call(bf16[2,1024,4096]{2,1,0:T(8,128)(2,1)} %w_ref.2), custom_call_target="tpu_custom_call" | custom-call | flops 1000 | bytes 1000 | tf_op jit(solution)/shard_map/stay/pallas_call | solution.py:170
  48.1 3.2 %dense.6 = (bf16[3,768,256]{2,1,0:T(8,128)(2,1)S(1)}, bf16[3,768,256]{2,1,0:T(8,128)(2,1)S(1)}) custom-call(s32[5]{0:T(128)S(1)} %stack.43.where_ref, bf16[768,1024]{1,0:T(8,128)(2,1)S(1)} %get-tuple-element.56.left_ref.x_ref, bf16[1024,4096]{1,0:T(8,128)(2,1)S(1)} %stay.1.w_ref), custom_call_target="tpu_custom_call" | custom-call | flops 1000 | bytes 1000 | tf_op jit(solution)/shard_map/dense/pallas_call | solution.py:195
  54.3 1.7 %collective-permute-done.7 = bf16[1,768,256]{2,1,0:T(8,128)(2,1)S(1)} collective-permute-done((bf16[1,768,256]{2,1,0:T(8,128)(2,1)S(1)}, bf16[1,768,256]{2,1,0:T(8,128)(2,1)S(1)}, u32[]{:S(2)}, u32[]{:S(2)}) %collective-permute-start.7) | collective-permute-done | bytes 393248 | tf_op jit(solution)/shard_map/ppermute | solution.py:28
  56.4 1.5 %dense.8 = (bf16[1,768,256]{2,1,0:T(8,128)(2,1)S(1)}, bf16[1,768,256]{2,1,0:T(8,128)(2,1)S(1)}) custom-call(s32[5]{0:T(128)S(1)} %stack.43.where_ref, bf16[768,1024]{1,0:T(8,128)(2,1)S(1)} %get-tuple-element.56.left_ref.x_ref, bf16[1024,4096]{1,0:T(8,128)(2,1)S(1)} %stay.1.w_ref, bf16[3,768,256]{2,1,0:T(8,128)(2,1)S(1)} %add_convert_fusion.refs_0_, ...), custom_call_target="tpu_custom_call" | custom-call | flops 1000 | bytes 1000 | tf_op jit(solution)/shard_map/dense/pallas_call | solution.py:195
  58.9 1.6 %collective-permute-done.8.refs_2_.peer_ref = bf16[1,768,256]{2,1,0:T(8,128)(2,1)S(1)} collective-permute-done((bf16[1,768,256]{2,1,0:T(8,128)(2,1)S(1)}, bf16[1,768,256]{2,1,0:T(8,128)(2,1)S(1)}, u32[]{:S(2)}, u32[]{:S(2)}) %collective-permute-start.8) | collective-permute-done | bytes 393248 | tf_op jit(solution)/shard_map/ppermute | solution.py:28
  68.6 1.5 %dense.11 = (bf16[1,768,256]{2,1,0:T(8,128)(2,1)S(1)}, bf16[1,768,256]{2,1,0:T(8,128)(2,1)S(1)}) custom-call(s32[5]{0:T(128)S(1)} %stack.43.where_ref, bf16[768,1024]{1,0:T(8,128)(2,1)S(1)} %get-tuple-element.56.left_ref.x_ref, bf16[1024,4096]{1,0:T(8,128)(2,1)S(1)} %stay.1.w_ref, bf16[3,768,256]{2,1,0:T(8,128)(2,1)S(1)} %add_convert_fusion.refs_0_, ...), custom_call_target="tpu_custom_call" | custom-call | flops 1000 | bytes 1000 | tf_op jit(solution)/shard_map/dense/pallas_call | solution.py:195
  74.6 3.7 %collective-permute-start.13 = (bf16[16,112,128]{2,1,0:T(8,128)(2,1)S(1)}, bf16[16,112,128]{2,1,0:T(8,128)(2,1)S(1)}, u32[]{:S(2)}, u32[]{:S(2)}) collective-permute-start(bf16[16,112,128]{2,1,0:T(8,128)(2,1)S(1)} %slice.39), channel_id=1, source_target_pairs={{0,1},{1,0},{2,3},{3,2},{4,5},{5,4},{6,7},{7,6},{8,9},{9,8},{10,11... | collective-permute-start | bytes 1376264 | tf_op jit(solution)/shard_map/ppermute | solution.py:28
  80.9 5.5 %weight_step.1 = (f32[2,1024,128]{2,1,0:T(8,128)S(1)}, bf16[2,1024,128]{2,1,0:T(8,128)(2,1)}) custom-call(s32[5]{0:T(128)S(1)} %stack.43.where_ref, bf16[16,880,128]{2,1,0:T(8,128)(2,1)} %all-to-all-done.in_ref, bf16[16,112,128]{2,1,0:T(8,128)(2,1)S(1)} %collective-permute-done.13.peer_ref, bf16[1,768,256]{2,1,0:T(8,128)(2,1)S(1)} %copy-done.13), custom_call_target="tpu_custom_call" | custom-call | flops 1000 | bytes 1000 | tf_op jit(solution)/shard_map/weight_step/pallas_call | solution.py:471
  86.4 5.3 %collective-permute-done.9.other_ref = bf16[3,768,256]{2,1,0:T(8,128)(2,1)} collective-permute-done((bf16[3,768,256]{2,1,0:T(8,128)(2,1)S(1)}, bf16[3,768,256]{2,1,0:T(8,128)(2,1)}, u32[]{:S(2)}, u32[]{:S(2)}) %collective-permute-start.9) | collective-permute-done | bytes 1179680 | tf_op jit(solution)/shard_map/ppermute | solution.py:28
  91.7 2.8 %second_layer.4 = (f32[8,768]{1,0:T(8,128)S(1)}, f32[48,256]{1,0:T(8,128)S(1)}) custom-call(bf16[768,1024]{1,0:T(8,128)(2,1)S(1)} %get-tuple-element.56.left_ref.x_ref, f32[8,768]{1,0:T(8,128)S(1)} %add.66.l0, f32[8,768]{1,0:T(8,128)S(1)} %collective-permute-done.3.l1, f32[8,768]{1,0:T(8,128)S(1)} %add.68.s0, f32[8,768]{1,0:T(8,128)S(1)} %collective-permute-done.5.s1, ...), custom_call_target="tpu_custom_call" | custom-call | flops 1000 | bytes 1000 | tf_op jit(solution)/shard_map/second_layer/pallas_call | solution.py:392
  94.6 2.8 %second_layer.5 = (f32[8,768]{1,0:T(8,128)S(1)}, f32[48,256]{1,0:T(8,128)S(1)}) custom-call(bf16[768,1024]{1,0:T(8,128)(2,1)S(1)} %get-tuple-element.56.left_ref.x_ref, f32[8,768]{1,0:T(8,128)S(1)} %add.66.l0, f32[8,768]{1,0:T(8,128)S(1)} %collective-permute-done.3.l1, f32[8,768]{1,0:T(8,128)S(1)} %add.68.s0, f32[8,768]{1,0:T(8,128)S(1)} %collective-permute-done.5.s1, ...), custom_call_target="tpu_custom_call" | custom-call | flops 1000 | bytes 1000 | tf_op jit(solution)/shard_map/second_layer/pallas_call | solution.py:392
  98.0 2.7 %second_layer.6 = (f32[8,768]{1,0:T(8,128)S(1)}, f32[48,256]{1,0:T(8,128)S(1)}) custom-call(bf16[768,1024]{1,0:T(8,128)(2,1)S(1)} %get-tuple-element.56.left_ref.x_ref, f32[8,768]{1,0:T(8,128)S(1)} %add.66.l0, f32[8,768]{1,0:T(8,128)S(1)} %collective-permute-done.3.l1, f32[8,768]{1,0:T(8,128)S(1)} %add.68.s0, f32[8,768]{1,0:T(8,128)S(1)} %collective-permute-done.5.s1, ...), custom_call_target="tpu_custom_call" | custom-call | flops 1000 | bytes 1000 | tf_op jit(solution)/shard_map/second_layer/pallas_call | solution.py:392
  102.8 2.0 %collective-permute-start.16 = (f32[8,768]{1,0:T(8,128)S(1)}, f32[8,768]{1,0:T(8,128)S(1)}, u32[]{:S(2)}, u32[]{:S(2)}) collective-permute-start(f32[8,768]{1,0:T(8,128)S(1)} %get-tuple-element.82), channel_id=1, source_target_pairs={{0,1},{1,0},{2,3},{3,2},{4,5},{5,4},{6,7},{7,6},{8,9},{9,8},{10,11... | collective-permute-start | bytes 73736 | tf_op jit(solution)/shard_map/ppermute | solution.py:28
  107.1 2.8 %collective-permute-done.17 = f32[8,768]{1,0:T(8,128)S(1)} collective-permute-done((f32[8,768]{1,0:T(8,128)S(1)}, f32[8,768]{1,0:T(8,128)S(1)}, u32[]{:S(2)}, u32[]{:S(2)}) %collective-permute-start.17) | collective-permute-done | bytes 24608 | tf_op jit(solution)/shard_map/ppermute | solution.py:28
  111.8 8.3 %collective-permute-done.18 = bf16[2,1024,128]{2,1,0:T(8,128)(2,1)S(1)} collective-permute-done((bf16[2,1024,128]{2,1,0:T(8,128)(2,1)}, bf16[2,1024,128]{2,1,0:T(8,128)(2,1)S(1)}, u32[]{:S(2)}, u32[]{:S(2)}) %collective-permute-start.18) | collective-permute-done | bytes 524320 | tf_op jit(solution)/shard_map/ppermute | solution.py:28
  (140 shorter events, 40.6 us)
Async XLA Ops:
  8.6 5.4 %collective-permute-start = (bf16[4,256,512]{2,1,0:T(8,128)(2,1)}, bf16[4,256,512]{2,1,0:T(8,128)(2,1)S(1)}, u32[]{:S(2)}, u32[]{:S(2)}) collective-permute-start(bf16[4,256,512]{2,1,0:T(8,128)(2,1)} %get-tuple-element.45), channel_id=1, source_target_pairs={{0,1},{1,0},{2,3},{3,2},{4,5},{5,4},{6,7},{7,6},{8,9},{9,8},{10,11... | collective-permute-start | bytes 3145736 | tf_op jit(solution)/shard_map/ppermute | solution.py:28
  12.6 4.9 %collective-permute-start.2 = (f32[8,768]{1,0:T(8,128)S(1)}, f32[8,768]{1,0:T(8,128)S(1)}, u32[]{:S(2)}, u32[]{:S(2)}) collective-permute-start(f32[8,768]{1,0:T(8,128)S(1)} %low.1), channel_id=1, source_target_pairs={{0,1},{1,0},{2,3},{3,2},{4,5},{5,4},{6,7},{7,6},{8,9},{9,8},{10,11... | collective-permute-start | bytes 73736 | tf_op jit(solution)/shard_map/ppermute | solution.py:28
  12.6 4.8 %collective-permute-start.10 = (s32[12]{0:T(128)S(1)}, s32[12]{0:T(128)S(1)}, u32[]{:S(2)}, u32[]{:S(2)}) collective-permute-start(s32[12]{0:T(128)S(1)} %copy-done.34), channel_id=1, source_target_pairs={{0,16},{16,0},{1,17},{17,1},{2,18},{18,2},{3,19},{19,3},{4,20},{20... | collective-permute-start | bytes 152 | tf_op jit(solution)/shard_map/ppermute | solution.py:28
  15.0 17.5 %collective-permute-start.1 = (bf16[2,256,512]{2,1,0:T(8,128)(2,1)}, bf16[2,256,512]{2,1,0:T(8,128)(2,1)}, u32[]{:S(2)}, u32[]{:S(2)}) collective-permute-start(bf16[2,256,512]{2,1,0:T(8,128)(2,1)} %add_convert_fusion.1), channel_id=1, source_target_pairs={{0,2},{2,0},{1,3},{3,1},{4,6},{6,4},{5,7},{7,5},{8,10},{10,8},{9,1... | collective-permute-start | bytes 1572872 | tf_op jit(solution)/shard_map/ppermute | solution.py:28
  20.3 53.3 %all-to-all-start = ((bf16[16,880,128]{2,1,0:T(8,128)(2,1)}), bf16[16,880,128]{2,1,0:T(8,128)(2,1)}, u32[]{:S(2)}, u32[]{:S(2)}) async-start(bf16[16,880,128]{2,1,0:T(8,128)(2,1)} %copy-done), calls=%async_computation | async-start | bytes 7208960 | tf_op jit(solution)/shard_map/all_to_all | solution.py:531
  28.2 4.3 %collective-permute-start.3 = (f32[8,768]{1,0:T(8,128)S(1)}, f32[8,768]{1,0:T(8,128)S(1)}, u32[]{:S(2)}, u32[]{:S(2)}) collective-permute-start(f32[8,768]{1,0:T(8,128)S(1)} %add.66.l0), channel_id=1, source_target_pairs={{0,2},{2,0},{1,3},{3,1},{4,6},{6,4},{5,7},{7,5},{8,10},{10,8},{9,1... | collective-permute-start | bytes 73736 | tf_op jit(solution)/shard_map/ppermute | solution.py:28
  39.4 3.3 %collective-permute-start.4 = (f32[8,768]{1,0:T(8,128)S(1)}, f32[8,768]{1,0:T(8,128)S(1)}, u32[]{:S(2)}, u32[]{:S(2)}) collective-permute-start(f32[8,768]{1,0:T(8,128)S(1)} %constant_dynamic-update-slice_fusion), channel_id=1, source_target_pairs={{0,1},{1,0},{2,3},{3,2},{4,5},{5,4},{6,7},{7,6},{8,9},{9,8},{10,11... | collective-permute-start | bytes 73736 | tf_op jit(solution)/shard_map/ppermute | solution.py:28
  42.7 4.6 %collective-permute-start.5 = (f32[8,768]{1,0:T(8,128)S(1)}, f32[8,768]{1,0:T(8,128)S(1)}, u32[]{:S(2)}, u32[]{:S(2)}) collective-permute-start(f32[8,768]{1,0:T(8,128)S(1)} %add.68.s0), channel_id=1, source_target_pairs={{0,2},{2,0},{1,3},{3,1},{4,6},{6,4},{5,7},{7,5},{8,10},{10,8},{9,1... | collective-permute-start | bytes 73736 | tf_op jit(solution)/shard_map/ppermute | solution.py:28
  51.2 4.9 %collective-permute-start.6 = (bf16[3,768,256]{2,1,0:T(8,128)(2,1)S(1)}, bf16[3,768,256]{2,1,0:T(8,128)(2,1)S(1)}, u32[]{:S(2)}, u32[]{:S(2)}) collective-permute-start(bf16[3,768,256]{2,1,0:T(8,128)(2,1)S(1)} %get-tuple-element.59), channel_id=1, source_target_pairs={{0,1},{1,0},{2,3},{3,2},{4,5},{5,4},{6,7},{7,6},{8,9},{9,8},{10,11... | collective-permute-start | bytes 3538952 | tf_op jit(solution)/shard_map/ppermute | solution.py:28
  54.0 2.0 %collective-permute-start.7 = (bf16[1,768,256]{2,1,0:T(8,128)(2,1)S(1)}, bf16[1,768,256]{2,1,0:T(8,128)(2,1)S(1)}, u32[]{:S(2)}, u32[]{:S(2)}) collective-permute-start(bf16[1,768,256]{2,1,0:T(8,128)(2,1)S(1)} %get-tuple-element.61), channel_id=1, source_target_pairs={{0,1},{1,0},{2,3},{3,2},{4,5},{5,4},{6,7},{7,6},{8,9},{9,8},{10,11... | collective-permute-start | bytes 1179656 | tf_op jit(solution)/shard_map/ppermute | solution.py:28
  58.8 1.7 %collective-permute-start.8 = (bf16[1,768,256]{2,1,0:T(8,128)(2,1)S(1)}, bf16[1,768,256]{2,1,0:T(8,128)(2,1)S(1)}, u32[]{:S(2)}, u32[]{:S(2)}) collective-permute-start(bf16[1,768,256]{2,1,0:T(8,128)(2,1)S(1)} %get-tuple-element.63), channel_id=1, source_target_pairs={{0,1},{1,0},{2,3},{3,2},{4,5},{5,4},{6,7},{7,6},{8,9},{9,8},{10,11... | collective-permute-start | bytes 1179656 | tf_op jit(solution)/shard_map/ppermute | solution.py:28
  62.8 1.7 %collective-permute-start.11 = (bf16[1,768,256]{2,1,0:T(8,128)(2,1)S(1)}, bf16[1,768,256]{2,1,0:T(8,128)(2,1)S(1)}, u32[]{:S(2)}, u32[]{:S(2)}) collective-permute-start(bf16[1,768,256]{2,1,0:T(8,128)(2,1)S(1)} %get-tuple-element.66), channel_id=1, source_target_pairs={{0,1},{1,0},{2,3},{3,2},{4,5},{5,4},{6,7},{7,6},{8,9},{9,8},{10,11... | collective-permute-start | bytes 1179656 | tf_op jit(solution)/shard_map/ppermute | solution.py:28
  62.9 28.8 %collective-permute-start.9 = (bf16[3,768,256]{2,1,0:T(8,128)(2,1)S(1)}, bf16[3,768,256]{2,1,0:T(8,128)(2,1)}, u32[]{:S(2)}, u32[]{:S(2)}) collective-permute-start(bf16[3,768,256]{2,1,0:T(8,128)(2,1)S(1)} %add_convert_fusion.refs_0_), channel_id=1, source_target_pairs={{0,2},{2,0},{1,3},{3,1},{4,6},{6,4},{5,7},{7,5},{8,10},{10,8},{9,1... | collective-permute-start | bytes 3538952 | tf_op jit(solution)/shard_map/ppermute | solution.py:28
  66.8 1.8 %collective-permute-start.12 = (bf16[1,768,256]{2,1,0:T(8,128)(2,1)S(1)}, bf16[1,768,256]{2,1,0:T(8,128)(2,1)S(1)}, u32[]{:S(2)}, u32[]{:S(2)}) collective-permute-start(bf16[1,768,256]{2,1,0:T(8,128)(2,1)S(1)} %get-tuple-element.67), channel_id=1, source_target_pairs={{0,1},{1,0},{2,3},{3,2},{4,5},{5,4},{6,7},{7,6},{8,9},{9,8},{10,11... | collective-permute-start | bytes 1179656 | tf_op jit(solution)/shard_map/ppermute | solution.py:28
  74.6 5.3 %collective-permute-start.13 = (bf16[16,112,128]{2,1,0:T(8,128)(2,1)S(1)}, bf16[16,112,128]{2,1,0:T(8,128)(2,1)S(1)}, u32[]{:S(2)}, u32[]{:S(2)}) collective-permute-start(bf16[16,112,128]{2,1,0:T(8,128)(2,1)S(1)} %slice.39), channel_id=1, source_target_pairs={{0,1},{1,0},{2,3},{3,2},{4,5},{5,4},{6,7},{7,6},{8,9},{9,8},{10,11... | collective-permute-start | bytes 1376264 | tf_op jit(solution)/shard_map/ppermute | solution.py:28
  78.3 23.0 %collective-permute-start.15 = (bf16[1,768,256]{2,1,0:T(8,128)(2,1)S(1)}, bf16[1,768,256]{2,1,0:T(8,128)(2,1)S(1)}, u32[]{:S(2)}, u32[]{:S(2)}) collective-permute-start(bf16[1,768,256]{2,1,0:T(8,128)(2,1)S(1)} %add_convert_fusion.2.refs_1_), channel_id=1, source_target_pairs={{0,2},{2,0},{1,3},{3,1},{4,6},{6,4},{5,7},{7,5},{8,10},{10,8},{9,1... | collective-permute-start | bytes 1179656 | tf_op jit(solution)/shard_map/ppermute | solution.py:28
  79.6 12.1 %copy-start.2 = (bf16[1,768,256]{2,1,0:T(8,128)(2,1)S(1)}, bf16[1,768,256]{2,1,0:T(8,128)(2,1)}, u32[]{:S(2)}) copy-start(bf16[1,768,256]{2,1,0:T(8,128)(2,1)} %copy-done.1) | copy-start | bytes 1179652
  79.6 21.8 %collective-permute-start.14 = (bf16[1,768,256]{2,1,0:T(8,128)(2,1)}, bf16[1,768,256]{2,1,0:T(8,128)(2,1)S(1)}, u32[]{:S(2)}, u32[]{:S(2)}) collective-permute-start(bf16[1,768,256]{2,1,0:T(8,128)(2,1)} %copy-done.30), channel_id=1, source_target_pairs={{0,1},{1,0},{2,3},{3,2},{4,5},{5,4},{6,7},{7,6},{8,9},{9,8},{10,11... | collective-permute-start | bytes 1179656 | tf_op jit(solution)/shard_map/ppermute | solution.py:28
  80.9 10.8 %copy-start.17 = (bf16[1,768,256]{2,1,0:T(8,128)(2,1)S(1)}, bf16[1,768,256]{2,1,0:T(8,128)(2,1)}, u32[]{:S(2)}) copy-start(bf16[1,768,256]{2,1,0:T(8,128)(2,1)} %copy-done.16) | copy-start | bytes 1179652
  80.9 10.8 %copy-start.25 = (f32[1024]{0:T(1024)S(1)}, f32[1024]{0:T(1024)}, u32[]{:S(2)}) copy-start(f32[1024]{0:T(1024)} %param.17) | copy-start | bytes 12292
  101.4 18.8 %copy-start.15 = (f32[2,1024,128]{2,1,0:T(8,128)S(1)}, f32[2,1024,128]{2,1,0:T(8,128)}, u32[]{:S(2)}) copy-start(f32[2,1024,128]{2,1,0:T(8,128)} %copy-done.14) | copy-start | bytes 3145732
  102.8 2.9 %collective-permute-start.16 = (f32[8,768]{1,0:T(8,128)S(1)}, f32[8,768]{1,0:T(8,128)S(1)}, u32[]{:S(2)}, u32[]{:S(2)}) collective-permute-start(f32[8,768]{1,0:T(8,128)S(1)} %get-tuple-element.82), channel_id=1, source_target_pairs={{0,1},{1,0},{2,3},{3,2},{4,5},{5,4},{6,7},{7,6},{8,9},{9,8},{10,11... | collective-permute-start | bytes 73736 | tf_op jit(solution)/shard_map/ppermute | solution.py:28
  105.7 4.2 %collective-permute-start.17 = (f32[8,768]{1,0:T(8,128)S(1)}, f32[8,768]{1,0:T(8,128)S(1)}, u32[]{:S(2)}, u32[]{:S(2)}) collective-permute-start(f32[8,768]{1,0:T(8,128)S(1)} %add.73), channel_id=1, source_target_pairs={{0,2},{2,0},{1,3},{3,1},{4,6},{6,4},{5,7},{7,5},{8,10},{10,8},{9,1... | collective-permute-start | bytes 73736 | tf_op jit(solution)/shard_map/ppermute | solution.py:28
  107.1 13.1 %collective-permute-start.18 = (bf16[2,1024,128]{2,1,0:T(8,128)(2,1)}, bf16[2,1024,128]{2,1,0:T(8,128)(2,1)S(1)}, u32[]{:S(2)}, u32[]{:S(2)}) collective-permute-start(bf16[2,1024,128]{2,1,0:T(8,128)(2,1)} %get-tuple-element.84), channel_id=1, source_target_pairs={{0,16},{16,0},{1,17},{17,1},{2,18},{18,2},{3,19},{19,3},{4,20},{20... | collective-permute-start | bytes 1572872 | tf_op jit(solution)/shard_map/ppermute | solution.py:28
  (31 other events, 122.5 us)

commit v7 on v6

--- a/solution.py
+++ b/solution.py
@@ -255,14 +255,14 @@
     return jnp.where(keep, tiled, 0.0).astype(bf16)
 
 
-def first_layer(chunk, where, coef, onehot, table_parts, lows, out_factors, in_factors, decay, gain):
+def first_layer(chunk, where, coef, onehot, table, lows, out_factors, in_factors, decay, gain):
     rows = onehot.shape[0] // CHUNKS
     group = out_factors.shape[1] // CHUNKS
     width = decay.shape[1]
     steps = 16
     per = rows // steps
 
-    def kernel(o_ref, t0, t1, t2, l0, l1, b_ref, a_ref, d_ref, g_ref, lifted_ref, stats_ref, square):
+    def kernel(o_ref, t_ref, l0, l1, b_ref, a_ref, d_ref, g_ref, lifted_ref, stats_ref, square):
         at = slice(chunk * rows, (chunk + 1) * rows)
         mine = slice(chunk * group, (chunk + 1) * group)
         low = (l0[:, at] + l1[:, at]) * coef
@@ -271,8 +271,7 @@
         for n in range(width // 256):
             cols = slice(n * 256, (n + 1) * 256)
             in_half = slice(n % 2 * 256, n % 2 * 256 + 256)
-            parts = (t0[2 + n // 2, :, in_half], t1[2 + n // 2, :, in_half], t2[n // 2, :, in_half])
-            table = sum(p.astype(f32) for p in parts).astype(bf16)
+            table = t_ref[n // 2, :, in_half]
             factor = jnp.concatenate([b_ref[2 * n, mine], b_ref[2 * n + 1, mine]], axis=1)
             u = jnp.dot(o_ref[at], table, preferred_element_type=f32) + dot(
                 spread_low, factor, 0, 0
@@ -304,13 +303,13 @@
             jax.ShapeDtypeStruct((rows, width), bf16),
             jax.ShapeDtypeStruct((8, rows), f32),
         ],
-        in_specs=[VMEM] * 10,
+        in_specs=[VMEM] * 8,
         out_specs=[VMEM, VMEM],
         scratch_shapes=[pltpu.VMEM((rows, 128), f32)],
         compiler_params=params(16),
         name="first_layer",
         cost_estimate=small_cost,
-    )(onehot, *table_parts, *lows, out_factors, in_factors, decay, gain)
+    )(onehot, table, *lows, out_factors, in_factors, decay, gain)
 
 
 def next_hidden(full_width, onehot, embedding, stats, lifted):
@@ -352,13 +351,20 @@
     cols = slice(n * 256, (n + 1) * 256)
 
     def kernel(x_ref, l0, l1, s0, s1, own_ref, peer_ref, other_ref, b_ref, d_ref, g_ref, r_ref,
-               before_ref, stats_ref, last_ref, square, lr, xr):
+               before_ref, stats_ref, last_ref, square, lr, xr, other, sem):
+        fetch = pltpu.make_async_copy(other_ref.at[slot], other, sem)
+        fetch.start()
         factor = jnp.concatenate([b_ref[2 * n], b_ref[2 * n + 1]], axis=1)
         d = d_ref[:, cols]
         g = g_ref[:, cols]
         r = r_ref[:, cols]
         rest = 1.0 - d
         gr = g * r
+        for k in range(CHUNKS):
+            span_k = slice(k * rows, (k + 1) * rows)
+            xrr = x_ref[span_k, cols].astype(f32) * r
+            xr[span_k] = xrr[:, :128] + xrr[:, 128:]
+        fetch.wait()
         for k in range(CHUNKS):
             span_k = slice(k * rows, (k + 1) * rows)
             so_far = s0[:, span_k] + s1[:, span_k]
@@ -368,11 +374,9 @@
             u = dot(spread_low, factor[k * group : (k + 1) * group], 0, 0) + (
                 own_ref[0, span_k].astype(f32)
                 + peer_ref[0, span_k].astype(f32)
-                + other_ref[slot, span_k].astype(f32)
+                + other[span_k].astype(f32)
             )
             h = jnp.zeros((per, 256), f32)
-            xrr = x_ref[span_k, cols].astype(f32) * r
-            xr[span_k] = xrr[:, :128] + xrr[:, 128:]
             for t in range(steps):
                 span = slice(k * rows + t * per, k * rows + (t + 1) * per)
                 h = d * h + rest * u[t * per : (t + 1) * per]
@@ -395,9 +399,10 @@
             jax.ShapeDtypeStruct((8, total), f32),
             jax.ShapeDtypeStruct((per * CHUNKS, 256), f32),
         ],
-        in_specs=[VMEM] * 13,
+        in_specs=[VMEM] * 7 + [pl.BlockSpec(memory_space=pl.ANY)] + [VMEM] * 5,
         out_specs=[VMEM] * 2,
-        scratch_shapes=[pltpu.VMEM((total, 128), f32)] * 3,
+        scratch_shapes=[pltpu.VMEM((total, 128), f32)] * 3
+        + [pltpu.VMEM((total, 256), bf16), pltpu.SemaphoreType.DMA],
         compiler_params=params(16),
         name="second_layer",
         cost_estimate=small_cost,
@@ -518,7 +523,9 @@
     peer, own = product(0, where, embedding, mix_weights, 512)
     theirs = swap(peer, "c")
     cross = added(own[:2], theirs[:2])
-    first_table = [own, theirs, swap(cross, "xh")]
+    first_table = (
+        own[2:].astype(f32) + theirs[2:].astype(f32) + swap(cross, "xh").astype(f32)
+    ).astype(bf16)
     a_blocks = regroup(after(factors_in, peer), jnp.zeros((1,), jnp.int32))
     lows = mp_parts(low_kernel(after(onehot, peer), embedding, a_blocks))
     both = jnp.stack([fitness_ranks, swap(after(fitness_ranks, peer), "xl")])

time: 122 us -> 119 us (0.975)
  Pallas kernels: 46.1 us -> 42.4 us
  other arithmetic: 2.84 us -> 4.55 us
    pallas_call x3, Pallas kernels: 6.82 us -> 3.56 us  [first_layer(): pl.pallas_call(kernel, out_shape=[jax.ShapeDtypeStruct((rows, width), bf1...]
    all_to_all x1, waiting for transfers between devices: 1.09 us -> 3.53 us  [shards(): lax.all_to_all(after(packed, lows[0]), ('y', 'z'), 0, 0, tiled=True)]
    ppermute x19, waiting for transfers between devices: 25.4 us -> 23.8 us  [swap(): return lax.ppermute(value, axis, [(0, 1), (1, 0)])]
    convert_element_type x0 -> x1, other arithmetic: none -> 1.4 us  [shards(): first_table = (own[2:].astype(f32) + theirs[2:].astype(f32) + swap(cross,...]
    unnamed x73 -> x75, local copies, waits for them, and re-layouts: 12.5 us -> 11.6 us
  transfers between devices with their start and end apart: 20 -> 20, of which waited for: 11 -> 15; matrix products, arithmetic and copies ran while one was open for 4% -> 5% of each run, Pallas kernels for 31% -> 29%
where the time goes in v7:
time: 119 us; the launch traced here: 118 us
  Pallas kernels  42.4 us (36%)
  starting transfers between devices  28.9 us (24%)
  waiting for transfers between devices  27.4 us (23%)
  local copies, waits for them, and re-layouts  14 us (12%)
  other arithmetic  4.55 us (4%)
    ppermute x19, waiting for transfers between devices, swap(): return lax.ppermute(value, axis, [(0, 1), (1, 0)])  23.8 us
    ppermute x19, starting transfers between devices, swap(): return lax.ppermute(value, axis, [(0, 1), (1, 0)])  20.9 us
    unnamed x75, local copies, waits for them, and re-layouts  11.6 us
    pallas_call x6, Pallas kernels, dense(): pl.pallas_call(kernel, out_shape=[jax.ShapeDtypeStruct((count, rows, piec...  10.8 us
    pallas_call x4, Pallas kernels, second_layer(): pl.pallas_call(kernel, out_shape=[jax.ShapeDtypeStruct((8, total), f32),...  9.25 us
    all_to_all x1, starting transfers between devices, shards(): lax.all_to_all(after(packed, lows[0]), ('y', 'z'), 0, 0, tiled=True)  7.94 us
    pallas_call x1, Pallas kernels, product(): pl.pallas_call(kernel, grid=(cuts,), in_specs=[SMEM, pl.BlockSpec((rows,...  6.87 us
    pallas_call x1, Pallas kernels, step_kernel(): pl.pallas_call(kernel, out_shape=[jax.ShapeDtypeStruct((2, width, lanes),...  5.47 us
  transfers between devices with their start and end apart: 20, of which 15 were waited for; matrix products, arithmetic and copies ran while one was open for 5% of the time, Pallas kernels for 29%

profile of v7, /device:TPU:1, one launch (start us, length us, event | category | flops | bytes accessed | tf_op | source)
XLA Modules:
  0.0 118.3 jit_solution(12682065914816688309)
XLA Ops:
  1.8 6.9 %product.1 = (bf16[4,256,512]{2,1,0:T(8,128)(2,1)}, bf16[4,256,512]{2,1,0:T(8,128)(2,1)S(1)}) custom-call(s32[5]{0:T(128)S(1)} %stack.43.where_ref, bf16[256,1024]{1,0:T(8,128)(2,1)S(1)} %copy-done.3, bf16[2,1024,4096]{2,1,0:T(8,128)(2,1)} %w_ref.2), custom_call_target="tpu_custom_call" | custom-call | flops 1000 | bytes 1000 | tf_op jit(solution)/shard_map/product/pallas_call | solution.py:138
  15.3 2.6 %collective-permute-start.1 = (bf16[2,256,512]{2,1,0:T(8,128)(2,1)S(1)}, bf16[2,256,512]{2,1,0:T(8,128)(2,1)S(1)}, u32[]{:S(2)}, u32[]{:S(2)}) collective-permute-start(bf16[2,256,512]{2,1,0:T(8,128)(2,1)S(1)} %add_convert_fusion.2), channel_id=1, source_target_pairs={{0,2},{2,0},{1,3},{3,1},{4,6},{6,4},{5,7},{7,5},{8,10},{10,8},{9,1... | collective-permute-start | bytes 1572872 | tf_op jit(solution)/shard_map/ppermute | solution.py:28
  19.0 1.8 %copy-done = bf16[16,880,128]{2,1,0:T(8,128)(2,1)} copy-done((bf16[16,880,128]{2,1,0:T(8,128)(2,1)}, bf16[16,880,128]{2,1,0:T(8,128)(2,1)S(1)}, u32[]{:S(2)}) %copy-start) | copy-done | bytes 3604504
  20.8 7.9 %all-to-all-start = ((bf16[16,880,128]{2,1,0:T(8,128)(2,1)}), bf16[16,880,128]{2,1,0:T(8,128)(2,1)}, u32[]{:S(2)}, u32[]{:S(2)}) async-start(bf16[16,880,128]{2,1,0:T(8,128)(2,1)} %copy-done), calls=%async_computation | async-start | bytes 7208960 | tf_op jit(solution)/shard_map/all_to_all | solution.py:538
  31.1 2.0 %collective-permute-done.3.l1 = f32[8,768]{1,0:T(8,128)S(1)} collective-permute-done((f32[8,768]{1,0:T(8,128)S(1)}, f32[8,768]{1,0:T(8,128)S(1)}, u32[]{:S(2)}, u32[]{:S(2)}) %collective-permute-start.3) | collective-permute-done | bytes 24608 | tf_op jit(solution)/shard_map/ppermute | solution.py:28
  36.7 2.4 %collective-permute-start.4 = (f32[8,768]{1,0:T(8,128)S(1)}, f32[8,768]{1,0:T(8,128)S(1)}, u32[]{:S(2)}, u32[]{:S(2)}) collective-permute-start(f32[8,768]{1,0:T(8,128)S(1)} %constant_dynamic-update-slice_fusion), channel_id=1, source_target_pairs={{0,1},{1,0},{2,3},{3,2},{4,5},{5,4},{6,7},{7,6},{8,9},{9,8},{10,11... | collective-permute-start | bytes 73736 | tf_op jit(solution)/shard_map/ppermute | solution.py:28
  40.6 3.5 %stay.1.w_ref = bf16[1024,4096]{1,0:T(8,128)(2,1)S(1)} custom-call(bf16[2,1024,4096]{2,1,0:T(8,128)(2,1)} %w_ref.2), custom_call_target="tpu_custom_call" | custom-call | flops 1000 | bytes 1000 | tf_op jit(solution)/shard_map/stay/pallas_call | solution.py:170
  45.9 3.2 %dense.6 = (bf16[3,768,256]{2,1,0:T(8,128)(2,1)S(1)}, bf16[3,768,256]{2,1,0:T(8,128)(2,1)S(1)}) custom-call(s32[5]{0:T(128)S(1)} %stack.43.where_ref, bf16[768,1024]{1,0:T(8,128)(2,1)S(1)} %get-tuple-element.56.left_ref.x_ref, bf16[1024,4096]{1,0:T(8,128)(2,1)S(1)} %stay.1.w_ref), custom_call_target="tpu_custom_call" | custom-call | flops 1000 | bytes 1000 | tf_op jit(solution)/shard_map/dense/pallas_call | solution.py:195
  52.1 1.7 %collective-permute-done.7 = bf16[1,768,256]{2,1,0:T(8,128)(2,1)S(1)} collective-permute-done((bf16[1,768,256]{2,1,0:T(8,128)(2,1)S(1)}, bf16[1,768,256]{2,1,0:T(8,128)(2,1)S(1)}, u32[]{:S(2)}, u32[]{:S(2)}) %collective-permute-start.7) | collective-permute-done | bytes 393248 | tf_op jit(solution)/shard_map/ppermute | solution.py:28
  57.0 1.6 %collective-permute-done.8.refs_2_.peer_ref = bf16[1,768,256]{2,1,0:T(8,128)(2,1)S(1)} collective-permute-done((bf16[1,768,256]{2,1,0:T(8,128)(2,1)S(1)}, bf16[1,768,256]{2,1,0:T(8,128)(2,1)S(1)}, u32[]{:S(2)}, u32[]{:S(2)}) %collective-permute-start.8) | collective-permute-done | bytes 393248 | tf_op jit(solution)/shard_map/ppermute | solution.py:28
  58.6 1.5 %dense.9 = (bf16[1,768,256]{2,1,0:T(8,128)(2,1)S(1)}, bf16[1,768,256]{2,1,0:T(8,128)(2,1)S(1)}) custom-call(s32[5]{0:T(128)S(1)} %copy-done.28, bf16[768,1024]{1,0:T(8,128)(2,1)S(1)} %get-tuple-element.56.left_ref.x_ref, bf16[1024,4096]{1,0:T(8,128)(2,1)S(1)} %stay.1.w_ref, bf16[3,768,256]{2,1,0:T(8,128)(2,1)S(1)} %add_convert_fusion.refs_0_, ...), custom_call_target="tpu_custom_call" | custom-call | flops 1000 | bytes 1000 | tf_op jit(solution)/shard_map/dense/pallas_call | solution.py:195
  62.6 1.5 %dense.10 = (bf16[1,768,256]{2,1,0:T(8,128)(2,1)S(1)}, bf16[1,768,256]{2,1,0:T(8,128)(2,1)S(1)}) custom-call(s32[5]{0:T(128)S(1)} %copy-done.28, bf16[768,1024]{1,0:T(8,128)(2,1)S(1)} %get-tuple-element.56.left_ref.x_ref, bf16[1024,4096]{1,0:T(8,128)(2,1)S(1)} %stay.1.w_ref, bf16[3,768,256]{2,1,0:T(8,128)(2,1)S(1)} %add_convert_fusion.refs_0_, ...), custom_call_target="tpu_custom_call" | custom-call | flops 1000 | bytes 1000 | tf_op jit(solution)/shard_map/dense/pallas_call | solution.py:195
  66.8 1.5 %dense.11 = (bf16[1,768,256]{2,1,0:T(8,128)(2,1)S(1)}, bf16[1,768,256]{2,1,0:T(8,128)(2,1)S(1)}) custom-call(s32[5]{0:T(128)S(1)} %copy-done.28, bf16[768,1024]{1,0:T(8,128)(2,1)S(1)} %get-tuple-element.56.left_ref.x_ref, bf16[1024,4096]{1,0:T(8,128)(2,1)S(1)} %stay.1.w_ref, bf16[3,768,256]{2,1,0:T(8,128)(2,1)S(1)} %add_convert_fusion.refs_0_, ...), custom_call_target="tpu_custom_call" | custom-call | flops 1000 | bytes 1000 | tf_op jit(solution)/shard_map/dense/pallas_call | solution.py:195
  70.5 3.5 %all-to-all-done.in_ref = bf16[16,880,128]{2,1,0:T(8,128)(2,1)} async-done(((bf16[16,880,128]{2,1,0:T(8,128)(2,1)}), bf16[16,880,128]{2,1,0:T(8,128)(2,1)}, u32[]{:S(2)}, u32[]{:S(2)}) %all-to-all-start) | async-done | bytes 3604512 | tf_op jit(solution)/shard_map/all_to_all | solution.py:538
  75.1 3.7 %collective-permute-start.13 = (bf16[16,112,128]{2,1,0:T(8,128)(2,1)S(1)}, bf16[16,112,128]{2,1,0:T(8,128)(2,1)S(1)}, u32[]{:S(2)}, u32[]{:S(2)}) collective-permute-start(bf16[16,112,128]{2,1,0:T(8,128)(2,1)S(1)} %slice.47), channel_id=1, source_target_pairs={{0,1},{1,0},{2,3},{3,2},{4,5},{5,4},{6,7},{7,6},{8,9},{9,8},{10,11... | collective-permute-start | bytes 1376264 | tf_op jit(solution)/shard_map/ppermute | solution.py:28
  81.2 5.5 %weight_step.1 = (f32[2,1024,128]{2,1,0:T(8,128)S(1)}, bf16[2,1024,128]{2,1,0:T(8,128)(2,1)}) custom-call(s32[5]{0:T(128)S(1)} %copy-done.28, bf16[16,880,128]{2,1,0:T(8,128)(2,1)} %all-to-all-done.in_ref, bf16[16,112,128]{2,1,0:T(8,128)(2,1)S(1)} %collective-permute-done.13.peer_ref, bf16[1,768,256]{2,1,0:T(8,128)(2,1)S(1)} %copy-done.11), custom_call_target="tpu_custom_call" | custom-call | flops 1000 | bytes 1000 | tf_op jit(solution)/shard_map/weight_step/pallas_call | solution.py:476
  86.7 3.1 %collective-permute-done.9.other_ref = bf16[3,768,256]{2,1,0:T(8,128)(2,1)} collective-permute-done((bf16[3,768,256]{2,1,0:T(8,128)(2,1)S(1)}, bf16[3,768,256]{2,1,0:T(8,128)(2,1)}, u32[]{:S(2)}, u32[]{:S(2)}) %collective-permute-start.9) | collective-permute-done | bytes 1179680 | tf_op jit(solution)/shard_map/ppermute | solution.py:28
  89.8 2.5 %second_layer.4 = (f32[8,768]{1,0:T(8,128)S(1)}, f32[48,256]{1,0:T(8,128)S(1)}) custom-call(bf16[768,1024]{1,0:T(8,128)(2,1)S(1)} %get-tuple-element.56.left_ref.x_ref, f32[8,768]{1,0:T(8,128)S(1)} %add.74.l0, f32[8,768]{1,0:T(8,128)S(1)} %collective-permute-done.3.l1, f32[8,768]{1,0:T(8,128)S(1)} %add.76.s0, f32[8,768]{1,0:T(8,128)S(1)} %copy-done.16, ...), custom_call_target="tpu_custom_call" | custom-call | flops 1000 | bytes 1000 | tf_op jit(solution)/shard_map/second_layer/pallas_call | solution.py:396
  92.4 2.5 %second_layer.5 = (f32[8,768]{1,0:T(8,128)S(1)}, f32[48,256]{1,0:T(8,128)S(1)}) custom-call(bf16[768,1024]{1,0:T(8,128)(2,1)S(1)} %get-tuple-element.56.left_ref.x_ref, f32[8,768]{1,0:T(8,128)S(1)} %add.74.l0, f32[8,768]{1,0:T(8,128)S(1)} %collective-permute-done.3.l1, f32[8,768]{1,0:T(8,128)S(1)} %add.76.s0, f32[8,768]{1,0:T(8,128)S(1)} %copy-done.16, ...), custom_call_target="tpu_custom_call" | custom-call | flops 1000 | bytes 1000 | tf_op jit(solution)/shard_map/second_layer/pallas_call | solution.py:396
  95.0 2.5 %second_layer.6 = (f32[8,768]{1,0:T(8,128)S(1)}, f32[48,256]{1,0:T(8,128)S(1)}) custom-call(bf16[768,1024]{1,0:T(8,128)(2,1)S(1)} %get-tuple-element.56.left_ref.x_ref, f32[8,768]{1,0:T(8,128)S(1)} %add.74.l0, f32[8,768]{1,0:T(8,128)S(1)} %collective-permute-done.3.l1, f32[8,768]{1,0:T(8,128)S(1)} %add.76.s0, f32[8,768]{1,0:T(8,128)S(1)} %copy-done.16, ...), custom_call_target="tpu_custom_call" | custom-call | flops 1000 | bytes 1000 | tf_op jit(solution)/shard_map/second_layer/pallas_call | solution.py:396
  98.1 1.7 %second_layer.7 = (f32[8,768]{1,0:T(8,128)S(1)}, f32[48,256]{1,0:T(8,128)S(1)}) custom-call(bf16[768,1024]{1,0:T(8,128)(2,1)S(1)} %get-tuple-element.56.left_ref.x_ref, f32[8,768]{1,0:T(8,128)S(1)} %add.74.l0, f32[8,768]{1,0:T(8,128)S(1)} %collective-permute-done.3.l1, f32[8,768]{1,0:T(8,128)S(1)} %add.76.s0, f32[8,768]{1,0:T(8,128)S(1)} %copy-done.16, ...), custom_call_target="tpu_custom_call" | custom-call | flops 1000 | bytes 1000 | tf_op jit(solution)/shard_map/second_layer/pallas_call | solution.py:396
  99.9 2.0 %collective-permute-start.16 = (f32[8,768]{1,0:T(8,128)S(1)}, f32[8,768]{1,0:T(8,128)S(1)}, u32[]{:S(2)}, u32[]{:S(2)}) collective-permute-start(f32[8,768]{1,0:T(8,128)S(1)} %get-tuple-element.82), channel_id=1, source_target_pairs={{0,1},{1,0},{2,3},{3,2},{4,5},{5,4},{6,7},{7,6},{8,9},{9,8},{10,11... | collective-permute-start | bytes 73736 | tf_op jit(solution)/shard_map/ppermute | solution.py:28
  104.2 2.7 %collective-permute-done.17 = f32[8,768]{1,0:T(8,128)S(1)} collective-permute-done((f32[8,768]{1,0:T(8,128)S(1)}, f32[8,768]{1,0:T(8,128)S(1)}, u32[]{:S(2)}, u32[]{:S(2)}) %collective-permute-start.17) | collective-permute-done | bytes 24608 | tf_op jit(solution)/shard_map/ppermute | solution.py:28
  108.9 8.4 %collective-permute-done.18 = bf16[2,1024,128]{2,1,0:T(8,128)(2,1)S(1)} collective-permute-done((bf16[2,1024,128]{2,1,0:T(8,128)(2,1)}, bf16[2,1024,128]{2,1,0:T(8,128)(2,1)S(1)}, u32[]{:S(2)}, u32[]{:S(2)}) %collective-permute-start.18) | collective-permute-done | bytes 524320 | tf_op jit(solution)/shard_map/ppermute | solution.py:28
  (143 shorter events, 40.9 us)
Async XLA Ops:
  1.8 48.5 %copy-start.27 = (s32[5]{0:T(128)}, s32[5]{0:T(128)S(1)}, u32[]{:S(2)}) copy-start(s32[5]{0:T(128)S(1)} %stack.43.where_ref) | copy-start | bytes 64
  1.8 9.7 %copy-start.4 = (bf16[256,1024]{1,0:T(8,128)(2,1)S(1)}, bf16[256,1024]{1,0:T(8,128)(2,1)}, u32[]{:S(2)}) copy-start(bf16[256,1024]{1,0:T(8,128)(2,1)} %e_ref.3) | copy-start | bytes 1572868
  9.6 4.4 %collective-permute-start = (bf16[4,256,512]{2,1,0:T(8,128)(2,1)}, bf16[4,256,512]{2,1,0:T(8,128)(2,1)}, u32[]{:S(2)}, u32[]{:S(2)}) collective-permute-start(bf16[4,256,512]{2,1,0:T(8,128)(2,1)} %get-tuple-element.45), channel_id=1, source_target_pairs={{0,1},{1,0},{2,3},{3,2},{4,5},{5,4},{6,7},{7,6},{8,9},{9,8},{10,11... | collective-permute-start | bytes 3145736 | tf_op jit(solution)/shard_map/ppermute | solution.py:28
  12.5 5.4 %collective-permute-start.2 = (f32[8,768]{1,0:T(8,128)S(1)}, f32[8,768]{1,0:T(8,128)S(1)}, u32[]{:S(2)}, u32[]{:S(2)}) collective-permute-start(f32[8,768]{1,0:T(8,128)S(1)} %low.1), channel_id=1, source_target_pairs={{0,1},{1,0},{2,3},{3,2},{4,5},{5,4},{6,7},{7,6},{8,9},{9,8},{10,11... | collective-permute-start | bytes 73736 | tf_op jit(solution)/shard_map/ppermute | solution.py:28
  12.6 5.3 %collective-permute-start.10 = (s32[12]{0:T(128)S(1)}, s32[12]{0:T(128)S(1)}, u32[]{:S(2)}, u32[]{:S(2)}) collective-permute-start(s32[12]{0:T(128)S(1)} %copy-done.35), channel_id=1, source_target_pairs={{0,16},{16,0},{1,17},{17,1},{2,18},{18,2},{3,19},{19,3},{4,20},{20... | collective-permute-start | bytes 152 | tf_op jit(solution)/shard_map/ppermute | solution.py:28
  15.3 14.3 %collective-permute-start.1 = (bf16[2,256,512]{2,1,0:T(8,128)(2,1)S(1)}, bf16[2,256,512]{2,1,0:T(8,128)(2,1)S(1)}, u32[]{:S(2)}, u32[]{:S(2)}) collective-permute-start(bf16[2,256,512]{2,1,0:T(8,128)(2,1)S(1)} %add_convert_fusion.2), channel_id=1, source_target_pairs={{0,2},{2,0},{1,3},{3,1},{4,6},{6,4},{5,7},{7,5},{8,10},{10,8},{9,1... | collective-permute-start | bytes 1572872 | tf_op jit(solution)/shard_map/ppermute | solution.py:28
  20.8 53.3 %all-to-all-start = ((bf16[16,880,128]{2,1,0:T(8,128)(2,1)}), bf16[16,880,128]{2,1,0:T(8,128)(2,1)}, u32[]{:S(2)}, u32[]{:S(2)}) async-start(bf16[16,880,128]{2,1,0:T(8,128)(2,1)} %copy-done), calls=%async_computation | async-start | bytes 7208960 | tf_op jit(solution)/shard_map/all_to_all | solution.py:538
  28.8 4.3 %collective-permute-start.3 = (f32[8,768]{1,0:T(8,128)S(1)}, f32[8,768]{1,0:T(8,128)S(1)}, u32[]{:S(2)}, u32[]{:S(2)}) collective-permute-start(f32[8,768]{1,0:T(8,128)S(1)} %add.74.l0), channel_id=1, source_target_pairs={{0,2},{2,0},{1,3},{3,1},{4,6},{6,4},{5,7},{7,5},{8,10},{10,8},{9,1... | collective-permute-start | bytes 73736 | tf_op jit(solution)/shard_map/ppermute | solution.py:28
  36.7 3.3 %collective-permute-start.4 = (f32[8,768]{1,0:T(8,128)S(1)}, f32[8,768]{1,0:T(8,128)S(1)}, u32[]{:S(2)}, u32[]{:S(2)}) collective-permute-start(f32[8,768]{1,0:T(8,128)S(1)} %constant_dynamic-update-slice_fusion), channel_id=1, source_target_pairs={{0,1},{1,0},{2,3},{3,2},{4,5},{5,4},{6,7},{7,6},{8,9},{9,8},{10,11... | collective-permute-start | bytes 73736 | tf_op jit(solution)/shard_map/ppermute | solution.py:28
  39.9 4.6 %collective-permute-start.5 = (f32[8,768]{1,0:T(8,128)S(1)}, f32[8,768]{1,0:T(8,128)S(1)}, u32[]{:S(2)}, u32[]{:S(2)}) collective-permute-start(f32[8,768]{1,0:T(8,128)S(1)} %add.76.s0), channel_id=1, source_target_pairs={{0,2},{2,0},{1,3},{3,1},{4,6},{6,4},{5,7},{7,5},{8,10},{10,8},{9,1... | collective-permute-start | bytes 73736 | tf_op jit(solution)/shard_map/ppermute | solution.py:28
  49.1 4.8 %collective-permute-start.6 = (bf16[3,768,256]{2,1,0:T(8,128)(2,1)S(1)}, bf16[3,768,256]{2,1,0:T(8,128)(2,1)S(1)}, u32[]{:S(2)}, u32[]{:S(2)}) collective-permute-start(bf16[3,768,256]{2,1,0:T(8,128)(2,1)S(1)} %get-tuple-element.59), channel_id=1, source_target_pairs={{0,1},{1,0},{2,3},{3,2},{4,5},{5,4},{6,7},{7,6},{8,9},{9,8},{10,11... | collective-permute-start | bytes 3538952 | tf_op jit(solution)/shard_map/ppermute | solution.py:28
  51.8 2.0 %collective-permute-start.7 = (bf16[1,768,256]{2,1,0:T(8,128)(2,1)S(1)}, bf16[1,768,256]{2,1,0:T(8,128)(2,1)S(1)}, u32[]{:S(2)}, u32[]{:S(2)}) collective-permute-start(bf16[1,768,256]{2,1,0:T(8,128)(2,1)S(1)} %get-tuple-element.61), channel_id=1, source_target_pairs={{0,1},{1,0},{2,3},{3,2},{4,5},{5,4},{6,7},{7,6},{8,9},{9,8},{10,11... | collective-permute-start | bytes 1179656 | tf_op jit(solution)/shard_map/ppermute | solution.py:28
  56.8 1.7 %collective-permute-start.8 = (bf16[1,768,256]{2,1,0:T(8,128)(2,1)S(1)}, bf16[1,768,256]{2,1,0:T(8,128)(2,1)S(1)}, u32[]{:S(2)}, u32[]{:S(2)}) collective-permute-start(bf16[1,768,256]{2,1,0:T(8,128)(2,1)S(1)} %get-tuple-element.63), channel_id=1, source_target_pairs={{0,1},{1,0},{2,3},{3,2},{4,5},{5,4},{6,7},{7,6},{8,9},{9,8},{10,11... | collective-permute-start | bytes 1179656 | tf_op jit(solution)/shard_map/ppermute | solution.py:28
  60.9 1.7 %collective-permute-start.11 = (bf16[1,768,256]{2,1,0:T(8,128)(2,1)S(1)}, bf16[1,768,256]{2,1,0:T(8,128)(2,1)S(1)}, u32[]{:S(2)}, u32[]{:S(2)}) collective-permute-start(bf16[1,768,256]{2,1,0:T(8,128)(2,1)S(1)} %get-tuple-element.66), channel_id=1, source_target_pairs={{0,1},{1,0},{2,3},{3,2},{4,5},{5,4},{6,7},{7,6},{8,9},{9,8},{10,11... | collective-permute-start | bytes 1179656 | tf_op jit(solution)/shard_map/ppermute | solution.py:28
  61.0 28.8 %collective-permute-start.9 = (bf16[3,768,256]{2,1,0:T(8,128)(2,1)S(1)}, bf16[3,768,256]{2,1,0:T(8,128)(2,1)}, u32[]{:S(2)}, u32[]{:S(2)}) collective-permute-start(bf16[3,768,256]{2,1,0:T(8,128)(2,1)S(1)} %add_convert_fusion.refs_0_), channel_id=1, source_target_pairs={{0,2},{2,0},{1,3},{3,1},{4,6},{6,4},{5,7},{7,5},{8,10},{10,8},{9,1... | collective-permute-start | bytes 3538952 | tf_op jit(solution)/shard_map/ppermute | solution.py:28
  64.9 1.8 %collective-permute-start.12 = (bf16[1,768,256]{2,1,0:T(8,128)(2,1)S(1)}, bf16[1,768,256]{2,1,0:T(8,128)(2,1)S(1)}, u32[]{:S(2)}, u32[]{:S(2)}) collective-permute-start(bf16[1,768,256]{2,1,0:T(8,128)(2,1)S(1)} %get-tuple-element.67), channel_id=1, source_target_pairs={{0,1},{1,0},{2,3},{3,2},{4,5},{5,4},{6,7},{7,6},{8,9},{9,8},{10,11... | collective-permute-start | bytes 1179656 | tf_op jit(solution)/shard_map/ppermute | solution.py:28
  75.1 5.1 %collective-permute-start.13 = (bf16[16,112,128]{2,1,0:T(8,128)(2,1)S(1)}, bf16[16,112,128]{2,1,0:T(8,128)(2,1)S(1)}, u32[]{:S(2)}, u32[]{:S(2)}) collective-permute-start(bf16[16,112,128]{2,1,0:T(8,128)(2,1)S(1)} %slice.47), channel_id=1, source_target_pairs={{0,1},{1,0},{2,3},{3,2},{4,5},{5,4},{6,7},{7,6},{8,9},{9,8},{10,11... | collective-permute-start | bytes 1376264 | tf_op jit(solution)/shard_map/ppermute | solution.py:28
  78.8 19.3 %collective-permute-start.15 = (bf16[1,768,256]{2,1,0:T(8,128)(2,1)S(1)}, bf16[1,768,256]{2,1,0:T(8,128)(2,1)S(1)}, u32[]{:S(2)}, u32[]{:S(2)}) collective-permute-start(bf16[1,768,256]{2,1,0:T(8,128)(2,1)S(1)} %add_convert_fusion.3.refs_1_), channel_id=1, source_target_pairs={{0,2},{2,0},{1,3},{3,1},{4,6},{6,4},{5,7},{7,5},{8,10},{10,8},{9,1... | collective-permute-start | bytes 1179656 | tf_op jit(solution)/shard_map/ppermute | solution.py:28
  79.5 10.3 %copy-start.2 = (bf16[1,768,256]{2,1,0:T(8,128)(2,1)S(1)}, bf16[1,768,256]{2,1,0:T(8,128)(2,1)}, u32[]{:S(2)}) copy-start(bf16[1,768,256]{2,1,0:T(8,128)(2,1)} %copy-done.1) | copy-start | bytes 1179652
  79.5 18.6 %collective-permute-start.14 = (bf16[1,768,256]{2,1,0:T(8,128)(2,1)}, bf16[1,768,256]{2,1,0:T(8,128)(2,1)S(1)}, u32[]{:S(2)}, u32[]{:S(2)}) collective-permute-start(bf16[1,768,256]{2,1,0:T(8,128)(2,1)} %copy-done.31), channel_id=1, source_target_pairs={{0,1},{1,0},{2,3},{3,2},{4,5},{5,4},{6,7},{7,6},{8,9},{9,8},{10,11... | collective-permute-start | bytes 1179656 | tf_op jit(solution)/shard_map/ppermute | solution.py:28
  98.1 19.2 %copy-start.13 = (f32[2,1024,128]{2,1,0:T(8,128)S(1)}, f32[2,1024,128]{2,1,0:T(8,128)}, u32[]{:S(2)}) copy-start(f32[2,1024,128]{2,1,0:T(8,128)} %copy-done.12) | copy-start | bytes 3145732
  99.9 2.9 %collective-permute-start.16 = (f32[8,768]{1,0:T(8,128)S(1)}, f32[8,768]{1,0:T(8,128)S(1)}, u32[]{:S(2)}, u32[]{:S(2)}) collective-permute-start(f32[8,768]{1,0:T(8,128)S(1)} %get-tuple-element.82), channel_id=1, source_target_pairs={{0,1},{1,0},{2,3},{3,2},{4,5},{5,4},{6,7},{7,6},{8,9},{9,8},{10,11... | collective-permute-start | bytes 73736 | tf_op jit(solution)/shard_map/ppermute | solution.py:28
  102.8 4.2 %collective-permute-start.17 = (f32[8,768]{1,0:T(8,128)S(1)}, f32[8,768]{1,0:T(8,128)S(1)}, u32[]{:S(2)}, u32[]{:S(2)}) collective-permute-start(f32[8,768]{1,0:T(8,128)S(1)} %add.81), channel_id=1, source_target_pairs={{0,2},{2,0},{1,3},{3,1},{4,6},{6,4},{5,7},{7,5},{8,10},{10,8},{9,1... | collective-permute-start | bytes 73736 | tf_op jit(solution)/shard_map/ppermute | solution.py:28
  104.2 13.1 %collective-permute-start.18 = (bf16[2,1024,128]{2,1,0:T(8,128)(2,1)}, bf16[2,1024,128]{2,1,0:T(8,128)(2,1)S(1)}, u32[]{:S(2)}, u32[]{:S(2)}) collective-permute-start(bf16[2,1024,128]{2,1,0:T(8,128)(2,1)} %get-tuple-element.84), channel_id=1, source_target_pairs={{0,16},{16,0},{1,17},{17,1},{2,18},{18,2},{3,19},{19,3},{4,20},{20... | collective-permute-start | bytes 1572872 | tf_op jit(solution)/shard_map/ppermute | solution.py:28
  (32 other events, 128.3 us)

commit v8 on v7

--- a/solution.py
+++ b/solution.py
@@ -577,7 +577,8 @@
         )
         lasts.append(last)
     weight_step = step_mine + swap(after(step_theirs, sent[-1]), "xl").astype(f32)
-    so_far = sum(mp_parts(st))
+    pair, other_pair = mp_parts(st)
+    so_far = after(pair + other_pair, weight_step)
     norm = lax.rsqrt(so_far[0] / full_width + norm_eps)
     terms = (so_far[2] + norm * so_far[1]).reshape(CHUNKS, step_count, -1)
     tail = norm.reshape(CHUNKS, step_count, -1)[:, -1].reshape(-1)

time: 119 us -> 122 us (1.025)
  waiting for transfers between devices: 27.4 us -> 32.5 us
    ppermute x19, waiting for transfers between devices: 23.8 us -> 28.8 us  [swap(): return lax.ppermute(value, axis, [(0, 1), (1, 0)])]
    unnamed x75 -> x69, local copies, waits for them, and re-layouts: 11.6 us -> 10.9 us
  transfers between devices with their start and end apart: 20 -> 20, of which waited for: 15 -> 13; matrix products, arithmetic and copies ran while one was open for 5% -> 4% of each run, Pallas kernels for 29% -> 29%
where the time goes in v8:
time: 122 us; the launch traced here: 121 us
  Pallas kernels  41.6 us (34%)
  waiting for transfers between devices  32.5 us (27%)
  starting transfers between devices  28.3 us (23%)
  local copies, waits for them, and re-layouts  13.4 us (11%)
  other arithmetic  4.55 us (4%)
    ppermute x19, waiting for transfers between devices, swap(): return lax.ppermute(value, axis, [(0, 1), (1, 0)])  28.8 us
    ppermute x19, starting transfers between devices, swap(): return lax.ppermute(value, axis, [(0, 1), (1, 0)])  20.3 us
    unnamed x69, local copies, waits for them, and re-layouts  10.9 us
    pallas_call x6, Pallas kernels, dense(): pl.pallas_call(kernel, out_shape=[jax.ShapeDtypeStruct((count, rows, piec...  10.8 us
    pallas_call x4, Pallas kernels, second_layer(): pl.pallas_call(kernel, out_shape=[jax.ShapeDtypeStruct((8, total), f32),...  9.25 us
    all_to_all x1, starting transfers between devices, shards(): lax.all_to_all(after(packed, lows[0]), ('y', 'z'), 0, 0, tiled=True)  7.94 us
    pallas_call x1, Pallas kernels, product(): pl.pallas_call(kernel, grid=(cuts,), in_specs=[SMEM, pl.BlockSpec((rows,...  6.87 us
    pallas_call x1, Pallas kernels, step_kernel(): pl.pallas_call(kernel, out_shape=[jax.ShapeDtypeStruct((2, width, lanes),...  4.64 us
  transfers between devices with their start and end apart: 20, of which 13 were waited for; matrix products, arithmetic and copies ran while one was open for 4% of the time, Pallas kernels for 29%

profile of v8, /device:TPU:1, one launch (start us, length us, event | category | flops | bytes accessed | tf_op | source)
XLA Modules:
  0.0 121.5 jit_solution(17664244719381414957)
XLA Ops:
  1.8 6.9 %product.1 = (bf16[4,256,512]{2,1,0:T(8,128)(2,1)}, bf16[4,256,512]{2,1,0:T(8,128)(2,1)S(1)}) custom-call(s32[5]{0:T(128)S(1)} %stack.43.where_ref, bf16[256,1024]{1,0:T(8,128)(2,1)S(1)} %copy-done.3, bf16[2,1024,4096]{2,1,0:T(8,128)(2,1)} %w_ref.2), custom_call_target="tpu_custom_call" | custom-call | flops 1000 | bytes 1000 | tf_op jit(solution)/shard_map/product/pallas_call | solution.py:138
  15.3 2.6 %collective-permute-start.1 = (bf16[2,256,512]{2,1,0:T(8,128)(2,1)S(1)}, bf16[2,256,512]{2,1,0:T(8,128)(2,1)S(1)}, u32[]{:S(2)}, u32[]{:S(2)}) collective-permute-start(bf16[2,256,512]{2,1,0:T(8,128)(2,1)S(1)} %add_convert_fusion.2), channel_id=1, source_target_pairs={{0,2},{2,0},{1,3},{3,1},{4,6},{6,4},{5,7},{7,5},{8,10},{10,8},{9,1... | collective-permute-start | bytes 1572872 | tf_op jit(solution)/shard_map/ppermute | solution.py:28
  19.0 1.8 %copy-done = bf16[16,880,128]{2,1,0:T(8,128)(2,1)} copy-done((bf16[16,880,128]{2,1,0:T(8,128)(2,1)}, bf16[16,880,128]{2,1,0:T(8,128)(2,1)S(1)}, u32[]{:S(2)}) %copy-start) | copy-done | bytes 3604504
  20.8 7.9 %all-to-all-start = ((bf16[16,880,128]{2,1,0:T(8,128)(2,1)}), bf16[16,880,128]{2,1,0:T(8,128)(2,1)}, u32[]{:S(2)}, u32[]{:S(2)}) async-start(bf16[16,880,128]{2,1,0:T(8,128)(2,1)} %copy-done), calls=%async_computation | async-start | bytes 7208960 | tf_op jit(solution)/shard_map/all_to_all | solution.py:538
  31.1 2.0 %collective-permute-done.3.l1 = f32[8,768]{1,0:T(8,128)S(1)} collective-permute-done((f32[8,768]{1,0:T(8,128)S(1)}, f32[8,768]{1,0:T(8,128)S(1)}, u32[]{:S(2)}, u32[]{:S(2)}) %collective-permute-start.3) | collective-permute-done | bytes 24608 | tf_op jit(solution)/shard_map/ppermute | solution.py:28
  36.6 2.4 %collective-permute-start.4 = (f32[8,768]{1,0:T(8,128)S(1)}, f32[8,768]{1,0:T(8,128)S(1)}, u32[]{:S(2)}, u32[]{:S(2)}) collective-permute-start(f32[8,768]{1,0:T(8,128)S(1)} %constant_dynamic-update-slice_fusion), channel_id=1, source_target_pairs={{0,1},{1,0},{2,3},{3,2},{4,5},{5,4},{6,7},{7,6},{8,9},{9,8},{10,11... | collective-permute-start | bytes 73736 | tf_op jit(solution)/shard_map/ppermute | solution.py:28
  40.5 3.5 %stay.1.w_ref = bf16[1024,4096]{1,0:T(8,128)(2,1)S(1)} custom-call(bf16[2,1024,4096]{2,1,0:T(8,128)(2,1)} %w_ref.2), custom_call_target="tpu_custom_call" | custom-call | flops 1000 | bytes 1000 | tf_op jit(solution)/shard_map/stay/pallas_call | solution.py:170
  45.9 3.2 %dense.6 = (bf16[3,768,256]{2,1,0:T(8,128)(2,1)S(1)}, bf16[3,768,256]{2,1,0:T(8,128)(2,1)S(1)}) custom-call(s32[5]{0:T(128)S(1)} %stack.43.where_ref, bf16[768,1024]{1,0:T(8,128)(2,1)S(1)} %get-tuple-element.57.left_ref.x_ref, bf16[1024,4096]{1,0:T(8,128)(2,1)S(1)} %stay.1.w_ref), custom_call_target="tpu_custom_call" | custom-call | flops 1000 | bytes 1000 | tf_op jit(solution)/shard_map/dense/pallas_call | solution.py:195
  50.3 1.5 %dense.7 = (bf16[1,768,256]{2,1,0:T(8,128)(2,1)S(1)}, bf16[1,768,256]{2,1,0:T(8,128)(2,1)S(1)}) custom-call(s32[5]{0:T(128)S(1)} %stack.43.where_ref, bf16[768,1024]{1,0:T(8,128)(2,1)S(1)} %get-tuple-element.57.left_ref.x_ref, bf16[1024,4096]{1,0:T(8,128)(2,1)S(1)} %stay.1.w_ref), custom_call_target="tpu_custom_call" | custom-call | flops 1000 | bytes 1000 | tf_op jit(solution)/shard_map/dense/pallas_call | solution.py:195
  52.1 1.7 %collective-permute-done.7 = bf16[1,768,256]{2,1,0:T(8,128)(2,1)S(1)} collective-permute-done((bf16[1,768,256]{2,1,0:T(8,128)(2,1)S(1)}, bf16[1,768,256]{2,1,0:T(8,128)(2,1)S(1)}, u32[]{:S(2)}, u32[]{:S(2)}) %collective-permute-start.7) | collective-permute-done | bytes 393248 | tf_op jit(solution)/shard_map/ppermute | solution.py:28
  56.9 1.6 %collective-permute-done.8.refs_2_.peer_ref = bf16[1,768,256]{2,1,0:T(8,128)(2,1)S(1)} collective-permute-done((bf16[1,768,256]{2,1,0:T(8,128)(2,1)S(1)}, bf16[1,768,256]{2,1,0:T(8,128)(2,1)S(1)}, u32[]{:S(2)}, u32[]{:S(2)}) %collective-permute-start.8) | collective-permute-done | bytes 393248 | tf_op jit(solution)/shard_map/ppermute | solution.py:28
  58.5 1.5 %dense.9 = (bf16[1,768,256]{2,1,0:T(8,128)(2,1)S(1)}, bf16[1,768,256]{2,1,0:T(8,128)(2,1)S(1)}) custom-call(s32[5]{0:T(128)S(1)} %copy-done.26, bf16[768,1024]{1,0:T(8,128)(2,1)S(1)} %get-tuple-element.57.left_ref.x_ref, bf16[1024,4096]{1,0:T(8,128)(2,1)S(1)} %stay.1.w_ref, bf16[3,768,256]{2,1,0:T(8,128)(2,1)S(1)} %add_convert_fusion.refs_0_, ...), custom_call_target="tpu_custom_call" | custom-call | flops 1000 | bytes 1000 | tf_op jit(solution)/shard_map/dense/pallas_call | solution.py:195
  60.9 1.6 %collective-permute-done.11.refs_3_.peer_ref = bf16[1,768,256]{2,1,0:T(8,128)(2,1)S(1)} collective-permute-done((bf16[1,768,256]{2,1,0:T(8,128)(2,1)S(1)}, bf16[1,768,256]{2,1,0:T(8,128)(2,1)S(1)}, u32[]{:S(2)}, u32[]{:S(2)}) %collective-permute-start.11) | collective-permute-done | bytes 393248 | tf_op jit(solution)/shard_map/ppermute | solution.py:28
  62.5 1.5 %dense.10 = (bf16[1,768,256]{2,1,0:T(8,128)(2,1)S(1)}, bf16[1,768,256]{2,1,0:T(8,128)(2,1)S(1)}) custom-call(s32[5]{0:T(128)S(1)} %copy-done.26, bf16[768,1024]{1,0:T(8,128)(2,1)S(1)} %get-tuple-element.57.left_ref.x_ref, bf16[1024,4096]{1,0:T(8,128)(2,1)S(1)} %stay.1.w_ref, bf16[3,768,256]{2,1,0:T(8,128)(2,1)S(1)} %add_convert_fusion.refs_0_, ...), custom_call_target="tpu_custom_call" | custom-call | flops 1000 | bytes 1000 | tf_op jit(solution)/shard_map/dense/pallas_call | solution.py:195
  70.3 3.7 %all-to-all-done.in_ref = bf16[16,880,128]{2,1,0:T(8,128)(2,1)} async-done(((bf16[16,880,128]{2,1,0:T(8,128)(2,1)}), bf16[16,880,128]{2,1,0:T(8,128)(2,1)}, u32[]{:S(2)}, u32[]{:S(2)}) %all-to-all-start) | async-done | bytes 3604512 | tf_op jit(solution)/shard_map/all_to_all | solution.py:538
  75.2 3.7 %collective-permute-start.13 = (bf16[16,112,128]{2,1,0:T(8,128)(2,1)S(1)}, bf16[16,112,128]{2,1,0:T(8,128)(2,1)S(1)}, u32[]{:S(2)}, u32[]{:S(2)}) collective-permute-start(bf16[16,112,128]{2,1,0:T(8,128)(2,1)S(1)} %slice.47), channel_id=1, source_target_pairs={{0,1},{1,0},{2,3},{3,2},{4,5},{5,4},{6,7},{7,6},{8,9},{9,8},{10,11... | collective-permute-start | bytes 1376264 | tf_op jit(solution)/shard_map/ppermute | solution.py:28
  81.3 4.6 %weight_step.1 = (f32[2,1024,128]{2,1,0:T(8,128)S(1)}, bf16[2,1024,128]{2,1,0:T(8,128)(2,1)S(1)}) custom-call(s32[5]{0:T(128)S(1)} %copy-done.26, bf16[16,880,128]{2,1,0:T(8,128)(2,1)} %all-to-all-done.in_ref, bf16[16,112,128]{2,1,0:T(8,128)(2,1)S(1)} %collective-permute-done.13.peer_ref, bf16[1,768,256]{2,1,0:T(8,128)(2,1)S(1)} %copy-done.11), custom_call_target="tpu_custom_call" | custom-call | flops 1000 | bytes 1000 | tf_op jit(solution)/shard_map/weight_step/pallas_call | solution.py:476
  86.0 16.1 %collective-permute-done.15.other_ref = bf16[1,768,256]{2,1,0:T(8,128)(2,1)S(1)} collective-permute-done((bf16[1,768,256]{2,1,0:T(8,128)(2,1)S(1)}, bf16[1,768,256]{2,1,0:T(8,128)(2,1)S(1)}, u32[]{:S(2)}, u32[]{:S(2)}) %collective-permute-start.15) | collective-permute-done | bytes 393248 | tf_op jit(solution)/shard_map/ppermute | solution.py:28
  103.7 2.5 %second_layer.4 = (f32[8,768]{1,0:T(8,128)S(1)}, f32[48,256]{1,0:T(8,128)S(1)}) custom-call(bf16[768,1024]{1,0:T(8,128)(2,1)S(1)} %get-tuple-element.57.left_ref.x_ref, f32[8,768]{1,0:T(8,128)S(1)} %add.74.l0, f32[8,768]{1,0:T(8,128)S(1)} %collective-permute-done.3.l1, f32[8,768]{1,0:T(8,128)S(1)} %add.76.s0, f32[8,768]{1,0:T(8,128)S(1)} %copy-done.14, ...), custom_call_target="tpu_custom_call" | custom-call | flops 1000 | bytes 1000 | tf_op jit(solution)/shard_map/second_layer/pallas_call | solution.py:396
  106.2 2.5 %second_layer.5 = (f32[8,768]{1,0:T(8,128)S(1)}, f32[48,256]{1,0:T(8,128)S(1)}) custom-call(bf16[768,1024]{1,0:T(8,128)(2,1)S(1)} %get-tuple-element.57.left_ref.x_ref, f32[8,768]{1,0:T(8,128)S(1)} %add.74.l0, f32[8,768]{1,0:T(8,128)S(1)} %collective-permute-done.3.l1, f32[8,768]{1,0:T(8,128)S(1)} %add.76.s0, f32[8,768]{1,0:T(8,128)S(1)} %copy-done.14, ...), custom_call_target="tpu_custom_call" | custom-call | flops 1000 | bytes 1000 | tf_op jit(solution)/shard_map/second_layer/pallas_call | solution.py:396
  108.8 2.5 %second_layer.6 = (f32[8,768]{1,0:T(8,128)S(1)}, f32[48,256]{1,0:T(8,128)S(1)}) custom-call(bf16[768,1024]{1,0:T(8,128)(2,1)S(1)} %get-tuple-element.57.left_ref.x_ref, f32[8,768]{1,0:T(8,128)S(1)} %add.74.l0, f32[8,768]{1,0:T(8,128)S(1)} %collective-permute-done.3.l1, f32[8,768]{1,0:T(8,128)S(1)} %add.76.s0, f32[8,768]{1,0:T(8,128)S(1)} %copy-done.14, ...), custom_call_target="tpu_custom_call" | custom-call | flops 1000 | bytes 1000 | tf_op jit(solution)/shard_map/second_layer/pallas_call | solution.py:396
  111.2 1.7 %second_layer.7 = (f32[8,768]{1,0:T(8,128)S(1)}, f32[48,256]{1,0:T(8,128)S(1)}) custom-call(bf16[768,1024]{1,0:T(8,128)(2,1)S(1)} %get-tuple-element.57.left_ref.x_ref, f32[8,768]{1,0:T(8,128)S(1)} %add.74.l0, f32[8,768]{1,0:T(8,128)S(1)} %collective-permute-done.3.l1, f32[8,768]{1,0:T(8,128)S(1)} %add.76.s0, f32[8,768]{1,0:T(8,128)S(1)} %copy-done.14, ...), custom_call_target="tpu_custom_call" | custom-call | flops 1000 | bytes 1000 | tf_op jit(solution)/shard_map/second_layer/pallas_call | solution.py:396
  114.3 2.0 %collective-permute-start.17 = (f32[8,768]{1,0:T(8,128)S(1)}, f32[8,768]{1,0:T(8,128)S(1)}, u32[]{:S(2)}, u32[]{:S(2)}) collective-permute-start(f32[8,768]{1,0:T(8,128)S(1)} %add.81), channel_id=1, source_target_pairs={{0,2},{2,0},{1,3},{3,1},{4,6},{6,4},{5,7},{7,5},{8,10},{10,8},{9,1... | collective-permute-start | bytes 73736 | tf_op jit(solution)/shard_map/ppermute | solution.py:28
  116.3 2.2 %collective-permute-done.17 = f32[8,768]{1,0:T(8,128)S(1)} collective-permute-done((f32[8,768]{1,0:T(8,128)S(1)}, f32[8,768]{1,0:T(8,128)S(1)}, u32[]{:S(2)}, u32[]{:S(2)}) %collective-permute-start.17) | collective-permute-done | bytes 24608 | tf_op jit(solution)/shard_map/ppermute | solution.py:28
  (137 shorter events, 39.1 us)
Async XLA Ops:
  1.8 48.5 %copy-start.25 = (s32[5]{0:T(128)}, s32[5]{0:T(128)S(1)}, u32[]{:S(2)}) copy-start(s32[5]{0:T(128)S(1)} %stack.43.where_ref) | copy-start | bytes 64
  9.6 4.4 %collective-permute-start = (bf16[4,256,512]{2,1,0:T(8,128)(2,1)}, bf16[4,256,512]{2,1,0:T(8,128)(2,1)}, u32[]{:S(2)}, u32[]{:S(2)}) collective-permute-start(bf16[4,256,512]{2,1,0:T(8,128)(2,1)} %get-tuple-element.46), channel_id=1, source_target_pairs={{0,1},{1,0},{2,3},{3,2},{4,5},{5,4},{6,7},{7,6},{8,9},{9,8},{10,11... | collective-permute-start | bytes 3145736 | tf_op jit(solution)/shard_map/ppermute | solution.py:28
  12.5 5.4 %collective-permute-start.2 = (f32[8,768]{1,0:T(8,128)S(1)}, f32[8,768]{1,0:T(8,128)S(1)}, u32[]{:S(2)}, u32[]{:S(2)}) collective-permute-start(f32[8,768]{1,0:T(8,128)S(1)} %low.1), channel_id=1, source_target_pairs={{0,1},{1,0},{2,3},{3,2},{4,5},{5,4},{6,7},{7,6},{8,9},{9,8},{10,11... | collective-permute-start | bytes 73736 | tf_op jit(solution)/shard_map/ppermute | solution.py:28
  12.6 5.3 %collective-permute-start.10 = (s32[12]{0:T(128)S(1)}, s32[12]{0:T(128)S(1)}, u32[]{:S(2)}, u32[]{:S(2)}) collective-permute-start(s32[12]{0:T(128)S(1)} %copy-done.32), channel_id=1, source_target_pairs={{0,16},{16,0},{1,17},{17,1},{2,18},{18,2},{3,19},{19,3},{4,20},{20... | collective-permute-start | bytes 152 | tf_op jit(solution)/shard_map/ppermute | solution.py:28
  15.3 14.3 %collective-permute-start.1 = (bf16[2,256,512]{2,1,0:T(8,128)(2,1)S(1)}, bf16[2,256,512]{2,1,0:T(8,128)(2,1)S(1)}, u32[]{:S(2)}, u32[]{:S(2)}) collective-permute-start(bf16[2,256,512]{2,1,0:T(8,128)(2,1)S(1)} %add_convert_fusion.2), channel_id=1, source_target_pairs={{0,2},{2,0},{1,3},{3,1},{4,6},{6,4},{5,7},{7,5},{8,10},{10,8},{9,1... | collective-permute-start | bytes 1572872 | tf_op jit(solution)/shard_map/ppermute | solution.py:28
  20.8 53.3 %all-to-all-start = ((bf16[16,880,128]{2,1,0:T(8,128)(2,1)}), bf16[16,880,128]{2,1,0:T(8,128)(2,1)}, u32[]{:S(2)}, u32[]{:S(2)}) async-start(bf16[16,880,128]{2,1,0:T(8,128)(2,1)} %copy-done), calls=%async_computation | async-start | bytes 7208960 | tf_op jit(solution)/shard_map/all_to_all | solution.py:538
  28.8 4.3 %collective-permute-start.3 = (f32[8,768]{1,0:T(8,128)S(1)}, f32[8,768]{1,0:T(8,128)S(1)}, u32[]{:S(2)}, u32[]{:S(2)}) collective-permute-start(f32[8,768]{1,0:T(8,128)S(1)} %add.74.l0), channel_id=1, source_target_pairs={{0,2},{2,0},{1,3},{3,1},{4,6},{6,4},{5,7},{7,5},{8,10},{10,8},{9,1... | collective-permute-start | bytes 73736 | tf_op jit(solution)/shard_map/ppermute | solution.py:28
  36.6 3.3 %collective-permute-start.4 = (f32[8,768]{1,0:T(8,128)S(1)}, f32[8,768]{1,0:T(8,128)S(1)}, u32[]{:S(2)}, u32[]{:S(2)}) collective-permute-start(f32[8,768]{1,0:T(8,128)S(1)} %constant_dynamic-update-slice_fusion), channel_id=1, source_target_pairs={{0,1},{1,0},{2,3},{3,2},{4,5},{5,4},{6,7},{7,6},{8,9},{9,8},{10,11... | collective-permute-start | bytes 73736 | tf_op jit(solution)/shard_map/ppermute | solution.py:28
  39.9 4.6 %collective-permute-start.5 = (f32[8,768]{1,0:T(8,128)S(1)}, f32[8,768]{1,0:T(8,128)S(1)}, u32[]{:S(2)}, u32[]{:S(2)}) collective-permute-start(f32[8,768]{1,0:T(8,128)S(1)} %add.76.s0), channel_id=1, source_target_pairs={{0,2},{2,0},{1,3},{3,1},{4,6},{6,4},{5,7},{7,5},{8,10},{10,8},{9,1... | collective-permute-start | bytes 73736 | tf_op jit(solution)/shard_map/ppermute | solution.py:28
  49.1 4.8 %collective-permute-start.6 = (bf16[3,768,256]{2,1,0:T(8,128)(2,1)S(1)}, bf16[3,768,256]{2,1,0:T(8,128)(2,1)S(1)}, u32[]{:S(2)}, u32[]{:S(2)}) collective-permute-start(bf16[3,768,256]{2,1,0:T(8,128)(2,1)S(1)} %get-tuple-element.60), channel_id=1, source_target_pairs={{0,1},{1,0},{2,3},{3,2},{4,5},{5,4},{6,7},{7,6},{8,9},{9,8},{10,11... | collective-permute-start | bytes 3538952 | tf_op jit(solution)/shard_map/ppermute | solution.py:28
  51.8 2.0 %collective-permute-start.7 = (bf16[1,768,256]{2,1,0:T(8,128)(2,1)S(1)}, bf16[1,768,256]{2,1,0:T(8,128)(2,1)S(1)}, u32[]{:S(2)}, u32[]{:S(2)}) collective-permute-start(bf16[1,768,256]{2,1,0:T(8,128)(2,1)S(1)} %get-tuple-element.62), channel_id=1, source_target_pairs={{0,1},{1,0},{2,3},{3,2},{4,5},{5,4},{6,7},{7,6},{8,9},{9,8},{10,11... | collective-permute-start | bytes 1179656 | tf_op jit(solution)/shard_map/ppermute | solution.py:28
  56.8 1.7 %collective-permute-start.8 = (bf16[1,768,256]{2,1,0:T(8,128)(2,1)S(1)}, bf16[1,768,256]{2,1,0:T(8,128)(2,1)S(1)}, u32[]{:S(2)}, u32[]{:S(2)}) collective-permute-start(bf16[1,768,256]{2,1,0:T(8,128)(2,1)S(1)} %get-tuple-element.64), channel_id=1, source_target_pairs={{0,1},{1,0},{2,3},{3,2},{4,5},{5,4},{6,7},{7,6},{8,9},{9,8},{10,11... | collective-permute-start | bytes 1179656 | tf_op jit(solution)/shard_map/ppermute | solution.py:28
  60.8 1.7 %collective-permute-start.11 = (bf16[1,768,256]{2,1,0:T(8,128)(2,1)S(1)}, bf16[1,768,256]{2,1,0:T(8,128)(2,1)S(1)}, u32[]{:S(2)}, u32[]{:S(2)}) collective-permute-start(bf16[1,768,256]{2,1,0:T(8,128)(2,1)S(1)} %get-tuple-element.67), channel_id=1, source_target_pairs={{0,1},{1,0},{2,3},{3,2},{4,5},{5,4},{6,7},{7,6},{8,9},{9,8},{10,11... | collective-permute-start | bytes 1179656 | tf_op jit(solution)/shard_map/ppermute | solution.py:28
  64.8 1.7 %collective-permute-start.12 = (bf16[1,768,256]{2,1,0:T(8,128)(2,1)S(1)}, bf16[1,768,256]{2,1,0:T(8,128)(2,1)S(1)}, u32[]{:S(2)}, u32[]{:S(2)}) collective-permute-start(bf16[1,768,256]{2,1,0:T(8,128)(2,1)S(1)} %get-tuple-element.68), channel_id=1, source_target_pairs={{0,1},{1,0},{2,3},{3,2},{4,5},{5,4},{6,7},{7,6},{8,9},{9,8},{10,11... | collective-permute-start | bytes 1179656 | tf_op jit(solution)/shard_map/ppermute | solution.py:28
  65.0 38.6 %collective-permute-start.9 = (bf16[3,768,256]{2,1,0:T(8,128)(2,1)S(1)}, bf16[3,768,256]{2,1,0:T(8,128)(2,1)}, u32[]{:S(2)}, u32[]{:S(2)}) collective-permute-start(bf16[3,768,256]{2,1,0:T(8,128)(2,1)S(1)} %add_convert_fusion.refs_0_), channel_id=1, source_target_pairs={{0,2},{2,0},{1,3},{3,1},{4,6},{6,4},{5,7},{7,5},{8,10},{10,8},{9,1... | collective-permute-start | bytes 3538952 | tf_op jit(solution)/shard_map/ppermute | solution.py:28
  74.0 29.6 %copy-start.14 = (f32[8,768]{1,0:T(8,128)S(1)}, f32[8,768]{1,0:T(8,128)}, u32[]{:S(2)}) copy-start(f32[8,768]{1,0:T(8,128)} %copy-done.13) | copy-start | bytes 73732
  74.1 29.6 %copy-start.16 = (bf16[1,768,256]{2,1,0:T(8,128)(2,1)S(1)}, bf16[1,768,256]{2,1,0:T(8,128)(2,1)}, u32[]{:S(2)}) copy-start(bf16[1,768,256]{2,1,0:T(8,128)(2,1)} %copy-done.15) | copy-start | bytes 1179652
  74.1 29.6 %copy-start.24 = (f32[1024]{0:T(1024)S(1)}, f32[1024]{0:T(1024)}, u32[]{:S(2)}) copy-start(f32[1024]{0:T(1024)} %param.17) | copy-start | bytes 12292
  75.2 5.1 %collective-permute-start.13 = (bf16[16,112,128]{2,1,0:T(8,128)(2,1)S(1)}, bf16[16,112,128]{2,1,0:T(8,128)(2,1)S(1)}, u32[]{:S(2)}, u32[]{:S(2)}) collective-permute-start(bf16[16,112,128]{2,1,0:T(8,128)(2,1)S(1)} %slice.47), channel_id=1, source_target_pairs={{0,1},{1,0},{2,3},{3,2},{4,5},{5,4},{6,7},{7,6},{8,9},{9,8},{10,11... | collective-permute-start | bytes 1376264 | tf_op jit(solution)/shard_map/ppermute | solution.py:28
  78.9 23.2 %collective-permute-start.15 = (bf16[1,768,256]{2,1,0:T(8,128)(2,1)S(1)}, bf16[1,768,256]{2,1,0:T(8,128)(2,1)S(1)}, u32[]{:S(2)}, u32[]{:S(2)}) collective-permute-start(bf16[1,768,256]{2,1,0:T(8,128)(2,1)S(1)} %add_convert_fusion.3.refs_1_), channel_id=1, source_target_pairs={{0,2},{2,0},{1,3},{3,1},{4,6},{6,4},{5,7},{7,5},{8,10},{10,8},{9,1... | collective-permute-start | bytes 1179656 | tf_op jit(solution)/shard_map/ppermute | solution.py:28
  102.1 16.4 %collective-permute-start.18 = (bf16[2,1024,128]{2,1,0:T(8,128)(2,1)S(1)}, bf16[2,1024,128]{2,1,0:T(8,128)(2,1)S(1)}, u32[]{:S(2)}, u32[]{:S(2)}) collective-permute-start(bf16[2,1024,128]{2,1,0:T(8,128)(2,1)S(1)} %get-tuple-element.85), channel_id=1, source_target_pairs={{0,16},{16,0},{1,17},{17,1},{2,18},{18,2},{3,19},{19,3},{4,20},{20... | collective-permute-start | bytes 1572872 | tf_op jit(solution)/shard_map/ppermute | solution.py:28
  102.1 9.1 %collective-permute-start.14 = (bf16[1,768,256]{2,1,0:T(8,128)(2,1)S(1)}, bf16[1,768,256]{2,1,0:T(8,128)(2,1)S(1)}, u32[]{:S(2)}, u32[]{:S(2)}) collective-permute-start(bf16[1,768,256]{2,1,0:T(8,128)(2,1)S(1)} %copy-done.28), channel_id=1, source_target_pairs={{0,1},{1,0},{2,3},{3,2},{4,5},{5,4},{6,7},{7,6},{8,9},{9,8},{10,11... | collective-permute-start | bytes 1179656 | tf_op jit(solution)/shard_map/ppermute | solution.py:28
  113.0 1.3 %collective-permute-start.16 = (f32[8,768]{1,0:T(8,128)S(1)}, f32[8,768]{1,0:T(8,128)S(1)}, u32[]{:S(2)}, u32[]{:S(2)}) collective-permute-start(f32[8,768]{1,0:T(8,128)S(1)} %get-tuple-element.83), channel_id=1, source_target_pairs={{0,1},{1,0},{2,3},{3,2},{4,5},{5,4},{6,7},{7,6},{8,9},{9,8},{10,11... | collective-permute-start | bytes 73736 | tf_op jit(solution)/shard_map/ppermute | solution.py:28
  114.3 4.2 %collective-permute-start.17 = (f32[8,768]{1,0:T(8,128)S(1)}, f32[8,768]{1,0:T(8,128)S(1)}, u32[]{:S(2)}, u32[]{:S(2)}) collective-permute-start(f32[8,768]{1,0:T(8,128)S(1)} %add.81), channel_id=1, source_target_pairs={{0,2},{2,0},{1,3},{3,1},{4,6},{6,4},{5,7},{7,5},{8,10},{10,8},{9,1... | collective-permute-start | bytes 73736 | tf_op jit(solution)/shard_map/ppermute | solution.py:28
  (29 other events, 150.7 us)
